TPU v7x, 256 devices: a whole 4x4x8 slice. The times are simulated.
256 devices in a mesh: pipe: 4 (over y), expert: 16 (over z, core), dp: 4 (over x).
Axes of the slice: x: 4, y: 4, z: 8, core: 2. Of those that a mesh axis runs over, the one named last changes fastest.
Arguments:
- normed: bfloat16 [4, 4, 3072, 4096], P('pipe', None, ('expert', 'dp')), may hold values from -1.5 to 1.5
- saved_out: bfloat16 [4, 4, 3072, 2, 4096], P('pipe', None, ('expert', 'dp')), may hold values from -0.59765625 to 0.59765625
- expert_grads: bfloat16 [4, 4, 4, 16, 16, 9, 4096], P('pipe', None, 'dp', 'expert'), may hold values from -24 to 24
- routes: int32 [4, 4, 3072, 2], P('pipe', None, ('expert', 'dp')), may hold values from 0 to 15, all different within a row; in each aligned block of 48 rows (0 to 47, 48 to 95, ..., all dimensions but the last counted through in order) at most 9 rows name the same one
- router_weight: bfloat16 [4, 4096, 16], P('pipe'), may hold values from -0.375 to 0.375
- upstream: bfloat16 [4, 3072, 4096], P(None, ('expert', 'dp')), may hold values from -6 to 6
Outputs:
- grad_input: bfloat16 [4, 4, 3072, 4096], P('pipe', None, ('expert', 'dp'))
- router_grad: float32 [4, 4096, 16], P('pipe')
Inputs may be any that keep to these rules, and one draw needn't show every extreme that they name: `routes`: the two experts of a row differ. Within the 48 rows of one device for one section and micro-batch no expert is named more than 9 times, a bound that some expert reaches in some of these blocks.
All inputs are finite; a program needn't handle non-finite values.
Results may differ from a plain program's by a relative error of at most 0.007.
Values may be sent and summed in bfloat16 or wider, within the bound.
No kernel may reach another device: no remote copies, remote signals or barrier semaphores. Data moves between devices by JAX's collectives and lax.ppermute only.
A program may use at most 128 MiB of HBM per device.

v0:
```python
import jax
import jax.numpy as jnp
from jax import lax
from jax.sharding import PartitionSpec as P


def shifted(block, axis, distance):
    devices = range(lax.axis_size(axis))
    route = [(i - distance, i) for i in devices if i - distance in devices]
    return lax.ppermute(block, axis, route)


def slot_index(flat, experts, capacity):
    onehot = (flat[..., None] == jnp.arange(experts, dtype=jnp.int32)).astype(jnp.int32)
    before = jnp.cumsum(onehot, axis=-2) - onehot
    position = jnp.sum(before * onehot, axis=-1)
    return flat * capacity + position


def block_grad(incoming, normed_rows, saved_rows, route_rows, returned, index_rows, router_w):
    experts = router_w.shape[1]
    rows_dev = normed_rows.shape[0]
    width = normed_rows.shape[1]
    logits = jnp.dot(normed_rows, router_w, preferred_element_type=jnp.float32)
    expl = jnp.exp(logits)
    probs = expl / jnp.sum(expl, axis=-1, keepdims=True)
    chosen = (route_rows[..., None] == jnp.arange(experts, dtype=jnp.int32)).astype(jnp.float32)
    gates = jnp.einsum("tke,te->tk", chosen, probs)
    dot_grads = jnp.einsum("td,tkd->tk", incoming, saved_rows, preferred_element_type=jnp.float32)
    weighted = dot_grads * gates
    dense_f = (
        jnp.einsum("tke,tk->te", chosen, weighted) - probs * jnp.sum(weighted, axis=-1)[:, None]
    )
    dense = dense_f.astype(jnp.bfloat16)
    router_term = lax.dot_general(
        dense, router_w, (((1,), (1,)), ((), ())), preferred_element_type=jnp.float32
    )
    back_rows = returned[index_rows].reshape(rows_dev, 2, width).astype(jnp.float32)
    total = (
        incoming.astype(jnp.float32)
        + gates[:, 0, None] * back_rows[:, 0]
        + gates[:, 1, None] * back_rows[:, 1]
        + router_term
    )
    weight_part = lax.dot_general(
        normed_rows, dense, (((0,), (0,)), ((), ())), preferred_element_type=jnp.float32
    )
    return (total.astype(jnp.bfloat16), weight_part)


def on_device(normed, saved_out, expert_grads, routes, router_weight, upstream):
    micro = normed.shape[1]
    rows_dev = normed.shape[2]
    width = normed.shape[3]
    sections = lax.axis_size("pipe")
    section_idx = lax.axis_index("pipe")
    router_w = router_weight[0]
    experts = router_w.shape[1]
    capacity = expert_grads.shape[5]
    slot_rows = slot_index(routes[0].reshape(micro, -1), experts, capacity)
    local_grads = expert_grads[0, :, 0]
    returned_list = []
    for block_num in range(micro):
        received = lax.all_to_all(
            local_grads[block_num], "expert", split_axis=1, concat_axis=0, tiled=True
        )
        returned_list.append(received.reshape(experts * capacity, width))
    returned_all = jnp.stack(returned_list)
    grad_buffer = jnp.zeros((micro, rows_dev, width), jnp.bfloat16)
    weight_sum = jnp.zeros((width, experts), jnp.float32)
    passed = jnp.zeros((rows_dev, width), jnp.bfloat16)
    for tick_num in range(micro + sections - 1):
        if tick_num > 0:
            passed = shifted(passed, "pipe", -1)
        block_num = tick_num - (sections - 1 - section_idx)
        is_active = (block_num >= 0) & (block_num < micro)
        block_idx = jnp.clip(block_num, 0, micro - 1)
        returned = lax.dynamic_index_in_dim(returned_all, block_idx, 0, keepdims=False)
        from_top = lax.dynamic_index_in_dim(upstream, block_idx, 0, keepdims=False)
        incoming = jnp.where(section_idx == sections - 1, from_top, passed)
        new_grad, weight_part = block_grad(
            incoming,
            lax.dynamic_index_in_dim(normed[0], block_idx, 0, keepdims=False),
            lax.dynamic_index_in_dim(saved_out[0], block_idx, 0, keepdims=False),
            lax.dynamic_index_in_dim(routes[0], block_idx, 0, keepdims=False),
            returned,
            lax.dynamic_index_in_dim(slot_rows, block_idx, 0, keepdims=False),
            router_w,
        )
        updated = lax.dynamic_update_index_in_dim(grad_buffer, new_grad, block_idx, 0)
        grad_buffer = jnp.where(is_active, updated, grad_buffer)
        weight_sum = weight_sum + jnp.where(is_active, weight_part, 0.0)
        passed = new_grad
    router_grad = lax.psum(weight_sum / micro, ("expert", "dp"))
    return (grad_buffer[None], router_grad[None])


def solution(mesh):
    in_specs = (
        P("pipe", None, ("expert", "dp"), None),
        P("pipe", None, ("expert", "dp"), None, None),
        P("pipe", None, "dp", "expert", None, None, None),
        P("pipe", None, ("expert", "dp"), None),
        P("pipe", None, None),
        P(None, ("expert", "dp"), None),
    )
    out_specs = (P("pipe", None, ("expert", "dp"), None), P("pipe", None, None))
    return jax.shard_map(
        on_device, mesh=mesh, in_specs=in_specs, out_specs=out_specs, check_vma=False
    )
```

profile of v0, /device:TPU:8, one launch (start us, length us, event | category | flops | bytes accessed | tf_op | source)
XLA Modules:
  0.0 633.7 jit_solution(2353032965511129839)
XLA Ops:
  7.2 4.4 fusion.196
  13.7 8.8 %all-to-all-start = ((bf16[1,16,9,4096]{3,2,0,1:T(8,128)(2,1)}), bf16[1,16,9,4096]{3,2,0,1:T(8,128)(2,1)}, u32[]{:S(2)}, u32[]{:S(2)}) async-start(bf16[1,16,9,4096]{3,2,0,1:T(8,128)(2,1)} %bitcast.551), calls=%async_computation | async-start | bytes 4194304 | tf_op jit(solution)/shard_map/all_to_all | solution.py:64
  38.0 33.6 %all-to-all-done = bf16[1,16,9,4096]{3,2,0,1:T(8,128)(2,1)} async-done(((bf16[1,16,9,4096]{3,2,0,1:T(8,128)(2,1)}), bf16[1,16,9,4096]{3,2,0,1:T(8,128)(2,1)}, u32[]{:S(2)}, u32[]{:S(2)}) %all-to-all-start) | async-done | bytes 1179680 | tf_op jit(solution)/shard_map/all_to_all | solution.py:64
  71.7 4.8 all-to-all-start.1
  96.1 29.6 %all-to-all-done.1 = bf16[1,16,9,4096]{3,2,0,1:T(8,128)(2,1)} async-done(((bf16[1,16,9,4096]{3,2,0,1:T(8,128)(2,1)}), bf16[1,16,9,4096]{3,2,0,1:T(8,128)(2,1)}, u32[]{:S(2)}, u32[]{:S(2)}) %all-to-all-start.1) | async-done | bytes 1179680 | tf_op jit(solution)/shard_map/all_to_all | solution.py:64
  125.7 4.8 all-to-all-start.2
  141.9 37.9 %all-to-all-done.2 = bf16[1,16,9,4096]{3,2,0,1:T(8,128)(2,1)} async-done(((bf16[1,16,9,4096]{3,2,0,1:T(8,128)(2,1)}), bf16[1,16,9,4096]{3,2,0,1:T(8,128)(2,1)}, u32[]{:S(2)}, u32[]{:S(2)}) %all-to-all-start.2) | async-done | bytes 1179680 | tf_op jit(solution)/shard_map/all_to_all | solution.py:64
  179.8 4.9 all-to-all-start.3
  200.0 33.9 %all-to-all-done.3 = bf16[1,16,9,4096]{3,2,0,1:T(8,128)(2,1)} async-done(((bf16[1,16,9,4096]{3,2,0,1:T(8,128)(2,1)}), bf16[1,16,9,4096]{3,2,0,1:T(8,128)(2,1)}, u32[]{:S(2)}, u32[]{:S(2)}) %all-to-all-start.3) | async-done | bytes 1179680 | tf_op jit(solution)/shard_map/all_to_all | solution.py:64
  239.0 6.8 %dynamic-slice_bitcast_fusion = (bf16[144,4096]{1,0:T(8,128)(2,1)}, bf16[144,4096]{1,0:T(8,128)(2,1)}, bf16[144,4096]{1,0:T(8,128)(2,1)}, bf16[144,4096]{1,0:T(8...) fusion(bf16[4,144,4096]{2,1,0:T(8,128)(2,1)} %constant_dynamic-update-slice_fusion, ...), kind=kLoop, calls=%fused_computation.28 | loop fusion | bytes 16515100 | tf_op jit(solution)/shard_map/jit(dynamic_index_in_dim)/squeeze | solution.py:78
  245.8 4.1 gather_fusion
  263.7 4.2 gather_fusion.1
  270.8 4.7 fusion.202
  275.6 4.2 gather_fusion.2
  282.8 4.7 fusion.201
  287.5 4.2 gather_fusion.3
  294.8 4.7 fusion.200
  299.5 4.3 gather_fusion.4
  327.6 4.2 gather_fusion.5
  356.9 4.3 gather_fusion.6
  387.6 4.5 collective-permute-done.3
  402.9 8.4 %collective-permute-done.4 = bf16[48,4096]{1,0:T(8,128)(2,1)S(1)} collective-permute-done((bf16[48,4096]{1,0:T(8,128)(2,1)S(1)}, bf16[48,4096]{1,0:T(8,128)(2,1)S(1)}, u32[]{:S(2)}, u32[]{:S(2)}) %collective-permute-start.4) | collective-permute-done | bytes 393248 | tf_op jit(solution)/shard_map/ppermute | solution.py:10
  432.9 4.8 collective-permute-done.5
  455.9 168.8 %all-reduce.2.cloned.1.call-done = f32[1,4096,16]{1,2,0:T(8,128)} async-done(((f32[1,4096,16]{1,2,0:T(8,128)}), f32[1,4096,16]{1,2,0:T(8,128)}) %all-reduce.2.cloned.1.call-update) | async-done | bytes 262160 | tf_op jit(solution)/shard_map/psum | solution.py:94
  (294 shorter events, 218.7 us)
Async XLA Ops:
  7.2 19.4 %copy-start = (bf16[1,4,48,2,4096]{4,3,2,1,0:T(2,128)(2,1)S(1)}, bf16[1,4,48,2,4096]{4,3,2,1,0:T(2,128)(2,1)}, u32[]{:S(2)}) copy-start(bf16[1,4,48,2,4096]{4,3,2,1,0:T(2,128)(2,1)} %param.7) | copy-start | bytes 9437188
  13.7 9.6 %copy-start.1 = (bf16[1,4096,16]{1,2,0:T(8,128)(2,1)S(1)}, bf16[1,4096,16]{1,2,0:T(8,128)(2,1)}, u32[]{:S(2)}) copy-start(bf16[1,4096,16]{1,2,0:T(8,128)(2,1)} %param.10) | copy-start | bytes 393220
  13.7 58.0 %all-to-all-start = ((bf16[1,16,9,4096]{3,2,0,1:T(8,128)(2,1)}), bf16[1,16,9,4096]{3,2,0,1:T(8,128)(2,1)}, u32[]{:S(2)}, u32[]{:S(2)}) async-start(bf16[1,16,9,4096]{3,2,0,1:T(8,128)(2,1)} %bitcast.551), calls=%async_computation | async-start | bytes 4194304 | tf_op jit(solution)/shard_map/all_to_all | solution.py:64
  32.9 38.8 %copy-start.41 = (s32[4,96]{1,0:T(4,128)}, s32[4,96]{1,0:T(4,128)S(1)}, u32[]{:S(2)}) copy-start(s32[4,96]{1,0:T(4,128)S(1)} %copy.75) | copy-start | bytes 4612
  33.0 38.7 %copy-start.20 = (s32[48,2]{1,0:T(8,128)}, s32[48,2]{1,0:T(8,128)S(1)}, u32[]{:S(2)}) copy-start(s32[48,2]{1,0:T(8,128)S(1)} %copy.79) | copy-start | bytes 1156
  34.9 41.6 %copy-start.18 = (s32[48,2]{1,0:T(8,128)}, s32[48,2]{1,0:T(8,128)S(1)}, u32[]{:S(2)}) copy-start(s32[48,2]{1,0:T(8,128)S(1)} %copy.82) | copy-start | bytes 1156
  71.7 54.0 %all-to-all-start.1 = ((bf16[1,16,9,4096]{3,2,0,1:T(8,128)(2,1)}), bf16[1,16,9,4096]{3,2,0,1:T(8,128)(2,1)}, u32[]{:S(2)}, u32[]{:S(2)}) async-start(bf16[1,16,9,4096]{3,2,0,1:T(8,128)(2,1)} %bitcast.550), calls=%async_computation.1 | async-start | bytes 4194304 | tf_op jit(solution)/shard_map/all_to_all | solution.py:64
  94.8 35.7 %copy-start.14 = (s32[48,2]{1,0:T(8,128)}, s32[48,2]{1,0:T(8,128)S(1)}, u32[]{:S(2)}) copy-start(s32[48,2]{1,0:T(8,128)S(1)} %copy.94) | copy-start | bytes 1156
  96.0 29.7 %copy-start.48 = (f32[48]{0:T(128)}, f32[48]{0:T(128)S(1)}, u32[]{:S(2)}) copy-start(f32[48]{0:T(128)S(1)} %get-tuple-element.93) | copy-start | bytes 580
  125.7 54.0 %all-to-all-start.2 = ((bf16[1,16,9,4096]{3,2,0,1:T(8,128)(2,1)}), bf16[1,16,9,4096]{3,2,0,1:T(8,128)(2,1)}, u32[]{:S(2)}, u32[]{:S(2)}) async-start(bf16[1,16,9,4096]{3,2,0,1:T(8,128)(2,1)} %bitcast.549), calls=%async_computation.2 | async-start | bytes 4194304 | tf_op jit(solution)/shard_map/all_to_all | solution.py:64
  130.8 54.2 %copy-start.44 = (f32[48,2]{0,1:T(2,128)}, f32[48,2]{0,1:T(2,128)S(1)}, u32[]{:S(2)}) copy-start(f32[48,2]{0,1:T(2,128)S(1)} %copy.167) | copy-start | bytes 1156
  179.8 54.2 %all-to-all-start.3 = ((bf16[1,16,9,4096]{3,2,0,1:T(8,128)(2,1)}), bf16[1,16,9,4096]{3,2,0,1:T(8,128)(2,1)}, u32[]{:S(2)}, u32[]{:S(2)}) async-start(bf16[1,16,9,4096]{3,2,0,1:T(8,128)(2,1)} %bitcast.548), calls=%async_computation.3 | async-start | bytes 4194304 | tf_op jit(solution)/shard_map/all_to_all | solution.py:64
  184.7 440.0 %all-reduce.2.cloned.1.call-start = ((), (), s32[]{:S(2)}) async-start(), calls=%async_computation.4 | async-start | bytes 524288 | tf_op jit(solution)/shard_map/psum | solution.py:94
  260.7 46.0 %collective-permute-start = (bf16[48,4096]{1,0:T(8,128)(2,1)}, bf16[48,4096]{1,0:T(8,128)(2,1)}, u32[]{:S(2)}, u32[]{:S(2)}) collective-permute-start(bf16[48,4096]{1,0:T(8,128)(2,1)} %get-tuple-element.72), channel_id=1, source_target_pairs={{64,0},{128,64},{192,128},{65,1},{129,65},{193,129},{66,2},{130,66... | collective-permute-start | bytes 1179656 | tf_op jit(solution)/shard_map/ppermute | solution.py:10
  307.9 10.3 %copy-start.30 = (f32[48,16]{0,1:T(8,128)S(1)}, f32[48,16]{0,1:T(8,128)}, u32[]{:S(2)}) copy-start(f32[48,16]{0,1:T(8,128)} %copy-done.29) | copy-start | bytes 9220
  322.7 13.1 %collective-permute-start.1 = (bf16[48,4096]{1,0:T(8,128)(2,1)}, bf16[48,4096]{1,0:T(8,128)(2,1)}, u32[]{:S(2)}, u32[]{:S(2)}) collective-permute-start(bf16[48,4096]{1,0:T(8,128)(2,1)} %get-tuple-element.76), channel_id=1, source_target_pairs={{64,0},{128,64},{192,128},{65,1},{129,65},{193,129},{66,2},{130,66... | collective-permute-start | bytes 1179656 | tf_op jit(solution)/shard_map/ppermute | solution.py:10
  337.0 10.3 %copy-start.26 = (f32[48,16]{0,1:T(8,128)S(1)}, f32[48,16]{0,1:T(8,128)}, u32[]{:S(2)}) copy-start(f32[48,16]{0,1:T(8,128)} %copy-done.25) | copy-start | bytes 9220
  351.8 12.4 %collective-permute-start.2 = (bf16[48,4096]{1,0:T(8,128)(2,1)}, bf16[48,4096]{1,0:T(8,128)(2,1)}, u32[]{:S(2)}, u32[]{:S(2)}) collective-permute-start(bf16[48,4096]{1,0:T(8,128)(2,1)} %get-tuple-element.80), channel_id=1, source_target_pairs={{64,0},{128,64},{192,128},{65,1},{129,65},{193,129},{66,2},{130,66... | collective-permute-start | bytes 1179656 | tf_op jit(solution)/shard_map/ppermute | solution.py:10
  365.3 10.3 %copy-start.28 = (f32[48,16]{0,1:T(8,128)S(1)}, f32[48,16]{0,1:T(8,128)}, u32[]{:S(2)}) copy-start(f32[48,16]{0,1:T(8,128)} %copy-done.27) | copy-start | bytes 9220
  380.0 12.1 %collective-permute-start.3 = (bf16[48,4096]{1,0:T(8,128)(2,1)S(1)}, bf16[48,4096]{1,0:T(8,128)(2,1)S(1)}, u32[]{:S(2)}, u32[]{:S(2)}) collective-permute-start(bf16[48,4096]{1,0:T(8,128)(2,1)S(1)} %get-tuple-element.84), channel_id=1, source_target_pairs={{64,0},{128,64},{192,128},{65,1},{129,65},{193,129},{66,2},{130,66... | collective-permute-start | bytes 1179656 | tf_op jit(solution)/shard_map/ppermute | solution.py:10
  400.3 11.0 %collective-permute-start.4 = (bf16[48,4096]{1,0:T(8,128)(2,1)S(1)}, bf16[48,4096]{1,0:T(8,128)(2,1)S(1)}, u32[]{:S(2)}, u32[]{:S(2)}) collective-permute-start(bf16[48,4096]{1,0:T(8,128)(2,1)S(1)} %get-tuple-element.88), channel_id=1, source_target_pairs={{64,0},{128,64},{192,128},{65,1},{129,65},{193,129},{66,2},{130,66... | collective-permute-start | bytes 1179656 | tf_op jit(solution)/shard_map/ppermute | solution.py:10
  413.1 10.1 %copy-start.22 = (f32[48,16]{0,1:T(8,128)S(1)}, f32[48,16]{0,1:T(8,128)}, u32[]{:S(2)}) copy-start(f32[48,16]{0,1:T(8,128)} %copy-done.21) | copy-start | bytes 9220
  427.5 10.1 %collective-permute-start.5 = (bf16[48,4096]{1,0:T(8,128)(2,1)S(1)}, bf16[48,4096]{1,0:T(8,128)(2,1)S(1)}, u32[]{:S(2)}, u32[]{:S(2)}) collective-permute-start(bf16[48,4096]{1,0:T(8,128)(2,1)S(1)} %get-tuple-element.92), channel_id=1, source_target_pairs={{64,0},{128,64},{192,128},{65,1},{129,65},{193,129},{66,2},{130,66... | collective-permute-start | bytes 1179656 | tf_op jit(solution)/shard_map/ppermute | solution.py:10
  439.5 10.3 %copy-start.49 = (f32[48]{0:T(128)S(1)}, f32[48]{0:T(128)}, u32[]{:S(2)}) copy-start(f32[48]{0:T(128)} %copy-done.48) | copy-start | bytes 580
  (50 other events, 157.4 us)
Sparse Core Ops, SparseCore 0:
  452.5 172.1 all-reduce.1
where the time goes:
time: 646 us; the launch traced here: 634 us
  waiting for transfers between devices  322 us (50%)
  local copies, waits for them, and re-layouts  165 us (26%)
  matrix products  57.4 us (9%)
  starting transfers between devices  37.7 us (6%)
  other arithmetic  35.6 us (6%)
  between operations  15.3 us (2%)
    psum x1, waiting for transfers between devices, on_device(): router_grad = lax.psum(weight_sum / micro, ('expert', 'dp'))  169 us
    all_to_all x4, waiting for transfers between devices, on_device(): lax.all_to_all(local_grads[block_num], 'expert', split_axis=1, concat_axi...  135 us
    unnamed x150, local copies, waits for them, and re-layouts  34.3 us
    gather x7, local copies, waits for them, and re-layouts, block_grad(): returned[index_rows].reshape(rows_dev, 2, width).astype(jnp.float32)  29.6 us
    slice x7, local copies, waits for them, and re-layouts, block_grad(): back_rows[:, 0]  26.5 us
    dot_general x7, matrix products, block_grad(): lax.dot_general(dense, router_w, (((1,), (1,)), ((), ())), preferred_elem...  25 us
    all_to_all x4, starting transfers between devices, on_device(): lax.all_to_all(local_grads[block_num], 'expert', split_axis=1, concat_axi...  23.3 us
    convert_element_type x7, local copies, waits for them, and re-layouts, block_grad(): returned[index_rows].reshape(rows_dev, 2, width).astype(jnp.float32)  20.9 us
  transfers between devices with their start and end apart: 11, of which 9 were waited for; matrix products, arithmetic and copies ran while one was open for 21% of the time, Pallas kernels for 0%

commit v1 on v0

v1 whole, which is shorter than its diff:
```python
import jax
import jax.numpy as jnp
from jax import lax
from jax.experimental import pallas as pl
from jax.experimental.pallas import tpu as pltpu
from jax.sharding import PartitionSpec as P

F32 = jnp.float32
BF16 = jnp.bfloat16
NT = (((1,), (1,)), ((), ()))
TN = (((0,), (0,)), ((), ()))


def params(mib):
    return pltpu.CompilerParams(vmem_limit_bytes=mib << 20)


def pack_kernel(main_ref, last_ref, out_ref):
    unit = pl.program_id(0)
    units = pl.num_programs(0)
    micro, _, dests, width = last_ref.shape
    half = width // 2

    @pl.when(unit < units - 1)
    def _():
        slots = main_ref.shape[1]
        n = slots * dests
        out_row = lax.broadcasted_iota(jnp.int32, (n, n), 0)
        in_row = lax.broadcasted_iota(jnp.int32, (n, n), 1)
        swap = (in_row == (out_row % slots) * dests + out_row // slots).astype(BF16)
        rows = main_ref[0].reshape(n, half)
        moved = jnp.dot(swap, rows, preferred_element_type=F32)
        out_ref[...] = moved.reshape(dests, slots, half).astype(BF16)

    @pl.when(unit == units - 1)
    def _():
        n_in = micro * dests
        n_out = 2 * micro * dests
        out_row = lax.broadcasted_iota(jnp.int32, (n_out, n_in), 0)
        in_row = lax.broadcasted_iota(jnp.int32, (n_out, n_in), 1)
        within = out_row % (2 * micro)
        source = (within % micro) * dests + out_row // (2 * micro)
        total = jnp.zeros((n_out, half), F32)
        for h in range(2):
            pick = ((in_row == source) & (within // micro == h)).astype(BF16)
            rows = last_ref[:, 0, :, h * half : (h + 1) * half].reshape(n_in, half)
            total = total + jnp.dot(pick, rows, preferred_element_type=F32)
        out_ref[...] = total.reshape(dests, 2 * micro, half).astype(BF16)


def pack(grads):
    micro, cap, dests, width = grads.shape
    half = width // 2
    units = 2 * micro + 1
    last_unit = 2 * micro - 1
    return pl.pallas_call(
        pack_kernel,
        grid=(units,),
        in_specs=[
            pl.BlockSpec(
                (1, cap - 1, dests, half),
                lambda u: (jnp.minimum(u, last_unit) // 2, 0, 0, jnp.minimum(u, last_unit) % 2),
            ),
            pl.BlockSpec((micro, 1, dests, width), lambda u: (0, cap - 1, 0, 0)),
        ],
        out_specs=pl.BlockSpec((dests, 8, half), lambda u: (0, u, 0)),
        out_shape=jax.ShapeDtypeStruct((dests, units * 8, half), BF16),
        compiler_params=params(40),
        name="pack_slots",
    )(grads, grads)


def gate_kernel(normed_ref, w_ref, routes_ref, v_ref, gate_ref, place_ref):
    m = pl.program_id(0)
    logits = lax.dot_general(w_ref[...], normed_ref[0], NT, preferred_element_type=F32)
    experts, rows = logits.shape
    expl = jnp.exp(logits)
    probs = expl / jnp.sum(expl, axis=0, keepdims=True)
    ids = lax.broadcasted_iota(jnp.int32, (experts, rows), 0)
    first = lax.broadcasted_iota(jnp.int32, (rows, rows), 0)
    second = lax.broadcasted_iota(jnp.int32, (rows, rows), 1)
    earlier = (first < second).astype(BF16)
    named = [ids == routes_ref[0, k : k + 1, :] for k in range(2)]
    both = jnp.where(named[0] | named[1], 1.0, 0.0).astype(BF16)
    before = jnp.dot(both, earlier, preferred_element_type=F32)
    for k in range(2):
        gate = jnp.sum(jnp.where(named[k], probs, 0.0), axis=0, keepdims=True)
        v_ref[0, k * experts : (k + 1) * experts, :] = gate * (jnp.where(named[k], 1.0, 0.0) - probs)
        gate_ref[0, k : k + 1, :] = gate
        slot = jnp.sum(jnp.where(named[k], before, 0.0), axis=0, keepdims=True).astype(jnp.int32)
        start = routes_ref[0, k : k + 1, :] * 8
        place_ref[0, k : k + 1, :] = jnp.where(slot < 8, start + slot, experts * 8 + start + m)


def gates_of(normed, w, routes):
    micro, rows, width = normed.shape
    experts = w.shape[0]
    return pl.pallas_call(
        gate_kernel,
        grid=(micro,),
        in_specs=[
            pl.BlockSpec((1, rows, width), lambda m: (m, 0, 0)),
            pl.BlockSpec((experts, width), lambda m: (0, 0)),
            pl.BlockSpec((1, 2, rows), lambda m: (m, 0, 0)),
        ],
        out_specs=[
            pl.BlockSpec((1, 2 * experts, rows), lambda m: (m, 0, 0)),
            pl.BlockSpec((1, 2, rows), lambda m: (m, 0, 0)),
            pl.BlockSpec((1, 2, rows), lambda m: (m, 0, 0)),
        ],
        out_shape=[
            jax.ShapeDtypeStruct((micro, 2 * experts, rows), F32),
            jax.ShapeDtypeStruct((micro, 2, rows), F32),
            jax.ShapeDtypeStruct((micro, 2, rows), jnp.int32),
        ],
        compiler_params=params(32),
        name="gates",
    )(normed, w, routes)


def pairs(sections):
    found = []
    for s in range(sections - 1):
        for k in range(2):
            for upper in range(s + 1, sections):
                for k2 in range(2):
                    found.append((s, k, upper, k2))
    return {key: row for row, key in enumerate(found)}


def couple_kernel(p_ref, saved_ref, w_ref, v_ref, out_ref):
    p = p_ref[0]
    sections, experts, _ = w_ref.shape
    for s in range(sections - 1):
        j = (s - p) & (sections - 1)
        for k in range(2):
            saved = saved_ref[j, k, 0]
            for upper in range(s + 1, sections):
                j2 = (upper - p) & (sections - 1)
                part = lax.dot_general(w_ref[j2], saved, NT, preferred_element_type=F32)
                for k2 in range(2):
                    row = pairs(sections)[(s, k, upper, k2)]
                    v = v_ref[j2, 0, k2 * experts : (k2 + 1) * experts, :]
                    out_ref[0, row : row + 1, :] = jnp.sum(part * v, axis=0, keepdims=True)


def coupling(p, saved, w, v):
    sections, _, micro, rows, quarter = saved.shape
    experts = w.shape[1]
    n = len(pairs(sections))
    return pl.pallas_call(
        couple_kernel,
        grid_spec=pltpu.PrefetchScalarGridSpec(
            num_scalar_prefetch=1,
            grid=(micro,),
            in_specs=[
                pl.BlockSpec((sections, 2, 1, rows, quarter), lambda m, p: (0, 0, m, 0, 0)),
                pl.BlockSpec((sections, experts, quarter), lambda m, p: (0, 0, 0)),
                pl.BlockSpec((sections, 1, 2 * experts, rows), lambda m, p: (0, m, 0, 0)),
            ],
            out_specs=pl.BlockSpec((1, n, rows), lambda m, p: (m, 0, 0)),
        ),
        out_shape=jax.ShapeDtypeStruct((micro, n, rows), F32),
        compiler_params=params(32),
        name="coupling",
    )(p, saved, w, v)


def combine_kernel(main_ref, last_ref, gate_ref, place_ref, out_ref):
    h = pl.program_id(0)
    experts, _, half = main_ref.shape
    lanes = gate_ref.shape[2]
    rows = lanes // 2
    n = experts * 8
    micro = pl.num_programs(1)
    index = lax.broadcasted_iota(jnp.int32, (2 * n, lanes), 0)
    pick = jnp.zeros((2 * n, lanes), F32)
    for k in range(2):
        place = place_ref[0, k : k + 1, :]
        place = place + jnp.where(place >= n, h * micro, 0)
        pick = pick + jnp.where(index == place, gate_ref[0, k : k + 1, :], 0.0)
    high = pick.astype(BF16)
    low = (pick - high.astype(F32)).astype(BF16)
    is_low = lax.broadcasted_iota(jnp.int32, (2 * n, lanes), 1) >= rows
    pick = jnp.where(is_low, low.astype(F32), high.astype(F32)).astype(BF16)
    both = lax.dot_general(
        pick[:n], main_ref[...].reshape(n, half), TN, preferred_element_type=F32
    ) + lax.dot_general(pick[n:], last_ref[...].reshape(n, half), TN, preferred_element_type=F32)
    total = (both[:rows] + both[rows:]).astype(BF16)
    out_ref[0, 0] = total[:, : half // 2]
    out_ref[1, 0] = total[:, half // 2 :]


def combine(received, gates, places):
    experts, packed, half = received.shape
    units = packed // 8
    micro = (units - 1) // 2
    lanes = gates.shape[2]
    rows = lanes // 2
    return pl.pallas_call(
        combine_kernel,
        grid=(2, micro),
        in_specs=[
            pl.BlockSpec((experts, 8, half), lambda h, m: (0, 2 * m + h, 0)),
            pl.BlockSpec((experts, 8, half), lambda h, m: (0, units - 1, 0)),
            pl.BlockSpec((1, 2, lanes), lambda h, m: (m, 0, 0)),
            pl.BlockSpec((1, 2, lanes), lambda h, m: (m, 0, 0)),
        ],
        out_specs=pl.BlockSpec((2, 1, rows, half // 2), lambda h, m: (h, m, 0, 0)),
        out_shape=jax.ShapeDtypeStruct((4, micro, rows, half // 2), BF16),
        compiler_params=params(40),
        name="combine",
    )(received, received, gates, places)


def dots_kernel(p_ref, up_ref, back_ref, saved_ref, out_ref):
    p = p_ref[0]
    sections, _, rows, quarter = back_ref.shape
    base = up_ref[0].astype(F32)
    ones = jnp.ones((8, 128), F32)
    for s in reversed(range(sections)):
        j = (s - p) & (sections - 1)
        for k in range(2):
            product = base * saved_ref[j, k, 0].astype(F32)
            lane = product[:, :128]
            for c in range(1, quarter // 128):
                lane = lane + product[:, c * 128 : (c + 1) * 128]
            row = lax.dot_general(
                ones, lane, NT, precision=lax.Precision.HIGHEST, preferred_element_type=F32
            )
            out_ref[0, 2 * s + k : 2 * s + k + 1, :] = row[:1]
        if s > 0:
            base = base + back_ref[s, 0].astype(F32)


def partial_dots(p, upstream, back, saved):
    sections, micro, rows, quarter = back.shape
    return pl.pallas_call(
        dots_kernel,
        grid_spec=pltpu.PrefetchScalarGridSpec(
            num_scalar_prefetch=1,
            grid=(micro,),
            in_specs=[
                pl.BlockSpec((1, rows, quarter), lambda m, p: (m, 0, p[0])),
                pl.BlockSpec((sections, 1, rows, quarter), lambda m, p: (0, m, 0, 0)),
                pl.BlockSpec((sections, 2, 1, rows, quarter), lambda m, p: (0, 0, m, 0, 0)),
            ],
            out_specs=pl.BlockSpec((1, 2 * sections, rows), lambda m, p: (m, 0, 0)),
        ),
        out_shape=jax.ShapeDtypeStruct((micro, 2 * sections, rows), F32),
        compiler_params=params(32),
        name="dots",
    )(p, upstream, back, saved)


def dense_kernel(p_ref, dots_ref, couple_ref, v_ref, normed_ref, dense_ref, part_ref):
    p = p_ref[0]
    sections, micro, _, rows = dots_ref.shape
    experts = v_ref.shape[2] // 2
    width = normed_ref.shape[2]
    table = pairs(sections)
    total = jnp.zeros((experts, width), F32)
    for m in range(micro):
        given = dots_ref[0, m]
        for source in range(1, sections):
            given = given + dots_ref[source, m]
        links = couple_ref[m]
        dots = {}
        own = jnp.zeros((experts, rows), F32)
        for s in reversed(range(sections)):
            j = (s - p) & (sections - 1)
            dense = jnp.zeros((experts, rows), F32)
            for k in range(2):
                value = given[2 * s + k : 2 * s + k + 1, :]
                for upper in range(s + 1, sections):
                    for k2 in range(2):
                        row = table[(s, k, upper, k2)]
                        value = value + links[row : row + 1, :] * dots[(upper, k2)]
                dots[(s, k)] = value
                dense = dense + value * v_ref[j, m, k * experts : (k + 1) * experts, :]
            dense_ref[m, s * experts : (s + 1) * experts, :] = dense.astype(BF16)
            own = jnp.where(p == s, dense, own)
        total = total + jnp.dot(own.astype(BF16), normed_ref[m], preferred_element_type=F32)
    total = total * (1.0 / micro)
    cols = width // 128
    for r in range(experts // 8):
        for c in range(cols):
            part_ref[r * cols + c] = total[r * 8 : (r + 1) * 8, c * 128 : (c + 1) * 128]


def dense_terms(p, dots, links, v, normed):
    sections, micro, _, rows = dots.shape
    experts = v.shape[2] // 2
    width = normed.shape[2]
    blocks = experts // 8 * (width // 128)
    whole = pl.BlockSpec(memory_space=pltpu.MemorySpace.VMEM)
    return pl.pallas_call(
        dense_kernel,
        in_specs=[pl.BlockSpec(memory_space=pltpu.MemorySpace.SMEM)] + [whole] * 4,
        out_specs=[whole] * 2,
        out_shape=[
            jax.ShapeDtypeStruct((micro, sections * experts, rows), BF16),
            jax.ShapeDtypeStruct((blocks, 8, 128), F32),
        ],
        compiler_params=params(32),
        name="dense",
    )(p, dots, links, v, normed)


def grads_kernel(p_ref, up_ref, back_ref, dense_ref, w_ref, out_ref):
    p = p_ref[0]
    sections = back_ref.shape[0]
    experts = w_ref.shape[1]
    total = up_ref[0].astype(F32)
    for s in reversed(range(sections)):
        j = (s - p) & (sections - 1)
        dense = dense_ref[0, s * experts : (s + 1) * experts, :]
        term = lax.dot_general(dense, w_ref[j], TN, preferred_element_type=F32)
        total = total + back_ref[s, 0].astype(F32) + term
        out_ref[s, 0] = total.astype(BF16)


def grads_of(p, upstream, back, dense, w):
    sections, micro, rows, quarter = back.shape
    experts = w.shape[1]
    return pl.pallas_call(
        grads_kernel,
        grid_spec=pltpu.PrefetchScalarGridSpec(
            num_scalar_prefetch=1,
            grid=(micro,),
            in_specs=[
                pl.BlockSpec((1, rows, quarter), lambda m, p: (m, 0, p[0])),
                pl.BlockSpec((sections, 1, rows, quarter), lambda m, p: (0, m, 0, 0)),
                pl.BlockSpec((1, sections * experts, rows), lambda m, p: (m, 0, 0)),
                pl.BlockSpec((sections, experts, quarter), lambda m, p: (0, 0, 0)),
            ],
            out_specs=pl.BlockSpec((sections, 1, rows, quarter), lambda m, p: (0, m, 0, 0)),
        ),
        out_shape=jax.ShapeDtypeStruct((sections, micro, rows, quarter), BF16),
        compiler_params=params(32),
        name="grads",
    )(p, upstream, back, dense, w)


def join_kernel(p_ref, *refs):
    step = pl.program_id(0)
    out_ref = refs[-1]
    for d in range(len(refs) - 1):

        @pl.when(step == d)
        def _():
            out_ref[...] = refs[d][...]


def join(p, blocks):
    n = len(blocks)
    micro, rows, quarter = blocks[0].shape
    return pl.pallas_call(
        join_kernel,
        grid_spec=pltpu.PrefetchScalarGridSpec(
            num_scalar_prefetch=1,
            grid=(n,),
            in_specs=[pl.BlockSpec((micro, rows, quarter), lambda d, p: (0, 0, 0))] * n,
            out_specs=pl.BlockSpec((micro, rows, quarter), lambda d, p: (0, 0, (p[0] - d) & (n - 1))),
        ),
        out_shape=jax.ShapeDtypeStruct((micro, rows, n * quarter), BF16),
        compiler_params=params(32),
        name="join",
    )(p, *blocks)


def turned(block, distance):
    n = lax.axis_size("pipe")
    return lax.ppermute(block, "pipe", [(i, (i + distance) % n) for i in range(n)])


def gathered(block):
    n = lax.axis_size("pipe")
    return [block] + [turned(block, n - j) for j in range(1, n)]


def on_device(normed, saved_out, expert_grads, routes, router_weight, upstream):
    sections = lax.axis_size("pipe")
    section = lax.axis_index("pipe")
    p = section.astype(jnp.int32).reshape(1)
    normed = normed[0]
    micro, rows, width = normed.shape
    quarter = width // sections
    w = router_weight[0].T
    experts = w.shape[0]

    send = pack(jnp.transpose(expert_grads[0, :, 0, 0], (0, 2, 1, 3)))
    received = lax.all_to_all(send, "expert", 0, 0, tiled=True)

    v, gates, places = gates_of(normed, w, jnp.transpose(routes[0], (0, 2, 1)))
    gates = jnp.concatenate([gates, gates], axis=-1)
    places = jnp.concatenate([places, places], axis=-1)

    def part_for(array, distance, axis):
        start = ((section + distance) % sections) * quarter
        return lax.dynamic_slice_in_dim(array, start, quarter, axis)

    def spread(array, axis):
        blocks = [part_for(array, 0, axis)]
        for j in range(1, sections):
            blocks.append(turned(part_for(array, sections - j, axis), sections - j))
        return jnp.stack(blocks)

    v_all = jnp.stack(gathered(v))
    w_all = spread(w, 1)
    saved_all = spread(jnp.transpose(saved_out[0], (2, 0, 1, 3)), 3)
    links = coupling(p, saved_all, w_all, v_all)
    links = sum(gathered(links))

    back = combine(received, gates, places)
    back = lax.all_to_all(back, "pipe", 0, 0, tiled=True)
    dots = partial_dots(p, upstream, back, saved_all)
    dots = jnp.broadcast_to(dots[None], (sections,) + dots.shape)
    dots = lax.all_to_all(dots, "pipe", 0, 0, tiled=True)
    dense, part = dense_terms(p, dots, links, v_all, normed)

    axes = ("expert", "dp")
    part = lax.all_to_all(part, axes, 0, 0, tiled=True)
    part = jnp.broadcast_to(jnp.sum(part, axis=0, keepdims=True), part.shape)
    part = lax.all_to_all(part, axes, 0, 0, tiled=True)
    cols = width // 128
    router_grad = part.reshape(experts // 8, cols, 8, 128).transpose(0, 2, 1, 3)
    router_grad = router_grad.reshape(experts, width).T

    outs = grads_of(p, upstream, back, dense, w_all)
    blocks = [lax.dynamic_index_in_dim(outs, section, 0, keepdims=False)]
    for d in range(1, sections):
        block = lax.dynamic_index_in_dim(outs, (section + d) % sections, 0, keepdims=False)
        blocks.append(turned(block, d))
    grad_input = join(p, blocks)
    return (grad_input[None], router_grad[None])


def solution(mesh):
    in_specs = (
        P("pipe", None, ("expert", "dp"), None),
        P("pipe", None, ("expert", "dp"), None, None),
        P("pipe", None, "dp", "expert", None, None, None),
        P("pipe", None, ("expert", "dp"), None),
        P("pipe", None, None),
        P(None, ("expert", "dp"), None),
    )
    out_specs = (P("pipe", None, ("expert", "dp"), None), P("pipe", None, None))
    return jax.shard_map(
        on_device, mesh=mesh, in_specs=in_specs, out_specs=out_specs, check_vma=False
    )
```

time: 646 us -> 284 us (0.44); the launches traced: 634 us -> 282 us
  local copies, waits for them, and re-layouts: 165 us -> 16.1 us
  waiting for transfers between devices: 322 us -> 181 us
  matrix products: 57.4 us -> 0 us
  other arithmetic: 35.6 us -> 3.25 us
  Pallas kernels: 0 us -> 24.4 us
  starting transfers between devices: 37.7 us -> 55.7 us
  between operations: 15.3 us -> 0.97 us
    psum x1 -> x0, waiting for transfers between devices: 169 us -> none  [on_device(): router_grad = lax.psum(weight_sum / micro, ('expert', 'dp'))]
    dot_general x28 -> x0, matrix products: 57.4 us -> none  [the longest x7 25 us: block_grad(): lax.dot_general(dense, router_w, (((1,), (1,)), ((), ())), preferred_elem...]
    ppermute x6 -> x15, waiting for transfers between devices: 18.5 us -> 64.3 us  [turned(): lax.ppermute(block, 'pipe', [(i, (i + distance) % n) for i in range(n)])]
    slice x8 -> x0, local copies, waits for them, and re-layouts: 31 us -> none  [the longest x7 26.5 us: block_grad(): back_rows[:, 0]]
    gather x7 -> x0, local copies, waits for them, and re-layouts: 29.6 us -> none  [block_grad(): returned[index_rows].reshape(rows_dev, 2, width).astype(jnp.float32)]
    pallas_call x0 -> x8, Pallas kernels: none -> 24.4 us  [the longest x1 7.63 us: combine(): pl.pallas_call(combine_kernel, grid=(2, micro), in_specs=[pl.BlockSpec((e...]
    unnamed x150 -> x23, local copies, waits for them, and re-layouts: 34.3 us -> 10.3 us
    convert_element_type x7 -> x0, local copies, waits for them, and re-layouts: 20.9 us -> none  [block_grad(): returned[index_rows].reshape(rows_dev, 2, width).astype(jnp.float32)]
  transfers between devices with their start and end apart: 11 -> 20, of which waited for: 9 -> 10; matrix products, arithmetic and copies ran while one was open for 21% -> 2% of each run, Pallas kernels for 0% -> 4%
where the time goes in v1:
time: 284 us; the launch traced here: 282 us
  waiting for transfers between devices  181 us (64%)
  starting transfers between devices  55.7 us (20%)
  Pallas kernels  24.4 us (9%)
  local copies, waits for them, and re-layouts  16.1 us (6%)
  other arithmetic  3.25 us (1%)
    all_to_all x1, waiting for transfers between devices, on_device(): received = lax.all_to_all(send, 'expert', 0, 0, tiled=True)  104 us
    ppermute x15, waiting for transfers between devices, turned(): lax.ppermute(block, 'pipe', [(i, (i + distance) % n) for i in range(n)])  64.3 us
    ppermute x15, starting transfers between devices, turned(): lax.ppermute(block, 'pipe', [(i, (i + distance) % n) for i in range(n)])  25.3 us
    all_to_all x2, starting transfers between devices, on_device(): part = lax.all_to_all(part, axes, 0, 0, tiled=True)  13 us
    unnamed x23, local copies, waits for them, and re-layouts  10.3 us
    all_to_all x2, waiting for transfers between devices, on_device(): part = lax.all_to_all(part, axes, 0, 0, tiled=True)  9.75 us
    all_to_all x1, starting transfers between devices, on_device(): received = lax.all_to_all(send, 'expert', 0, 0, tiled=True)  8.75 us
    pallas_call x1, Pallas kernels, combine(): pl.pallas_call(combine_kernel, grid=(2, micro), in_specs=[pl.BlockSpec((e...  7.63 us
  transfers between devices with their start and end apart: 20, of which 10 were waited for; matrix products, arithmetic and copies ran while one was open for 2% of the time, Pallas kernels for 4%

profile of v1, /device:TPU:8, one launch (start us, length us, event | category | flops | bytes accessed | tf_op | source)
XLA Modules:
  0.0 281.9 jit_solution(2283534110271761225)
XLA Ops:
  3.0 3.7 %pack_slots.1 = bf16[16,72,2048]{2,1,0:T(8,128)(2,1)S(1)} custom-call(bf16[4,9,16,4096]{3,2,1,0:T(8,128)(2,1)S(1)} %bitcast.79, bf16[4,9,16,4096]{3,2,1,0:T(8,128)(2,1)S(1)} %bitcast.80), custom_call_target="tpu_custom_call" | custom-call | tf_op jit(solution)/shard_map/pack_slots/pallas_call | solution.py:56
  8.9 8.8 %all-to-all-start = ((bf16[16,72,2048]{2,1,0:T(8,128)(2,1)}), bf16[16,72,2048]{2,1,0:T(8,128)(2,1)}, u32[]{:S(2)}, u32[]{:S(2)}) async-start(bf16[16,72,2048]{2,1,0:T(8,128)(2,1)} %copy-done.1), calls=%async_computation | async-start | bytes 9437184 | tf_op jit(solution)/shard_map/all_to_all | solution.py:393
  18.9 104.3 %all-to-all-done.main_ref.last_ref = bf16[16,72,2048]{2,1,0:T(8,128)(2,1)} async-done(((bf16[16,72,2048]{2,1,0:T(8,128)(2,1)}), bf16[16,72,2048]{2,1,0:T(8,128)(2,1)}, u32[]{:S(2)}, u32[]{:S(2)}) %all-to-all-start) | async-done | bytes 4718624 | tf_op jit(solution)/shard_map/all_to_all | solution.py:393
  123.2 7.6 %combine.1 = bf16[4,4,48,1024]{3,2,1,0:T(8,128)(2,1)} custom-call(bf16[16,72,2048]{2,1,0:T(8,128)(2,1)} %all-to-all-done.main_ref.last_ref, bf16[16,72,2048]{2,1,0:T(8,128)(2,1)} %all-to-all-done.main_ref.last_ref, f32[4,2,96]{2,1,0:T(2,128)S(1)} %pad_maximum_fusion.3.gate_ref, s32[4,2,96]{2,1,0:T(2,128)S(1)} %pad_add_fusion.place_ref), custom_call_target="tpu_custom_call" | custom-call | tf_op jit(solution)/shard_map/combine/pallas_call | solution.py:200
  130.8 4.9 %all-to-all-start.1 = ((bf16[4,4,48,1024]{3,2,1,0:T(8,128)(2,1)}), bf16[4,4,48,1024]{3,2,1,0:T(8,128)(2,1)}, u32[]{:S(2)}, u32[]{:S(2)}) async-start(bf16[4,4,48,1024]{3,2,1,0:T(8,128)(2,1)} %combine.1), calls=%async_computation.1 | async-start | bytes 3145728 | tf_op jit(solution)/shard_map/all_to_all | solution.py:416
  135.7 3.6 %constant_dynamic-slice_fusion.3 = (bf16[1,4,48,2,1024]{4,3,2,1,0:T(2,128)(2,1)S(1)}, bf16[1,4,48,2,1024]{4,3,2,1,0:T(2,128)(2,1)S(1)}, bf16[1,4,48,2,1024]{4,3,...) fusion(bf16[1,4,48,2,4096]{4,3,2,1,0:T(2,128)(2,1)} %param.7, s32[]{:T(128)S(6)} %select_n.63, s32[]{:T(128)S(6)} %select_n.65, ...), kind=kLoop, calls=%fused_computation.21 | loop fusion | bytes 6291472 | tf_op jit(solution)/shard_map/dynamic-slice.8
  142.2 2.7 collective-permute-start
  144.9 3.5 %collective-permute-start.7 = (f32[4,32,48]{2,1,0:T(8,128)S(1)}, f32[4,32,48]{2,1,0:T(8,128)S(1)}, u32[]{:S(2)}, u32[]{:S(2)}) collective-permute-start(f32[4,32,48]{2,1,0:T(8,128)S(1)} %get-tuple-element.9), channel_id=1, source_target_pairs={{0,128},{64,192},{128,0},{192,64},{1,129},{65,193},{129,1},{193,65... | collective-permute-start | bytes 73736 | tf_op jit(solution)/shard_map/ppermute | solution.py:374
  148.4 40.7 %collective-permute-done.8 = f32[4,32,48]{2,1,0:T(8,128)S(1)} collective-permute-done((f32[4,32,48]{2,1,0:T(8,128)S(1)}, f32[4,32,48]{2,1,0:T(8,128)S(1)}, u32[]{:S(2)}, u32[]{:S(2)}) %collective-permute-start.8) | collective-permute-done | bytes 24608 | tf_op jit(solution)/shard_map/ppermute | solution.py:374
  189.2 2.6 collective-permute-start.5
  193.4 2.6 collective-permute-done.6
  196.0 4.5 %collective-permute-start.4 = (bf16[16,1024]{1,0:T(8,128)(2,1)S(1)}, bf16[16,1024]{1,0:T(8,128)(2,1)S(1)}, u32[]{:S(2)}, u32[]{:S(2)}) collective-permute-start(bf16[16,1024]{1,0:T(8,128)(2,1)S(1)} %get-tuple-element.23), channel_id=1, source_target_pairs={{0,128},{64,192},{128,0},{192,64},{1,129},{65,193},{129,1},{193,65... | collective-permute-start | bytes 98312 | tf_op jit(solution)/shard_map/ppermute | solution.py:374
  204.9 2.7 coupling.1
  207.6 2.4 collective-permute-start.10
  213.2 3.5 %dots.1 = f32[4,8,48]{2,1,0:T(8,128)S(1)} custom-call(s32[1]{0:T(128)} %bitcast.p_ref, bf16[4,48,4096]{2,1,0:T(8,128)(2,1)S(1)} %copy-done.2, bf16[4,4,48,1024]{3,2,1,0:T(8,128)(2,1)} %all-to-all-done.1.back_ref, bf16[4,2,4,48,1024]{4,3,2,1,0:T(8,128)(2,1)S(1)} %pad_maximum_fusion.saved_ref), custom_call_target="tpu_custom_call" | custom-call | tf_op jit(solution)/shard_map/dots/pallas_call | solution.py:238
  217.5 3.7 %all-to-all-start.2 = ((f32[4,1,1536]{2,1,0:T(1,128)}), f32[4,1,1536]{2,1,0:T(1,128)S(1)}, u32[]{:S(2)}, u32[]{:S(2)}) async-start(f32[4,1,1536]{2,1,0:T(1,128)} %reshape.50), calls=%async_computation.2 | async-start | bytes 49152 | tf_op jit(solution)/shard_map/all_to_all | solution.py:419
  222.1 3.1 %all-to-all-done.2 = f32[4,1,1536]{2,1,0:T(1,128)S(1)} async-done(((f32[4,1,1536]{2,1,0:T(1,128)}), f32[4,1,1536]{2,1,0:T(1,128)S(1)}, u32[]{:S(2)}, u32[]{:S(2)}) %all-to-all-start.2) | async-done | bytes 24608 | tf_op jit(solution)/shard_map/all_to_all | solution.py:419
  229.6 8.4 %all-to-all-start.3 = ((f32[64,8,128]{2,1,0:T(8,128)}), f32[64,8,128]{2,1,0:T(8,128)}, u32[]{:S(2)}, u32[]{:S(2)}) async-start(f32[64,8,128]{2,1,0:T(8,128)} %get-tuple-element.11), calls=%async_computation.3 | async-start | bytes 524288 | tf_op jit(solution)/shard_map/all_to_all | solution.py:423
  238.9 3.1 %grads.1 = bf16[4,4,48,1024]{3,2,1,0:T(8,128)(2,1)S(1)} custom-call(s32[1]{0:T(128)} %bitcast.p_ref, bf16[4,48,4096]{2,1,0:T(8,128)(2,1)S(1)} %copy-done.3, bf16[4,4,48,1024]{3,2,1,0:T(8,128)(2,1)} %all-to-all-done.1.back_ref, bf16[4,64,48]{2,1,0:T(8,128)(2,1)S(1)} %copy-done.8, bf16[4,16,1024]{2,1,0:T(8,128)(2,1)S(1)} %pad_maximum_fusion.2.w_ref), custom_call_target="tpu_custom_call" | custom-call | tf_op jit(solution)/shard_map/grads/pallas_call | solution.py:326
  241.9 9.8 %all-to-all-done.3 = f32[64,8,128]{2,1,0:T(8,128)} async-done(((f32[64,8,128]{2,1,0:T(8,128)}), f32[64,8,128]{2,1,0:T(8,128)}, u32[]{:S(2)}, u32[]{:S(2)}) %all-to-all-start.3) | async-done | bytes 262176 | tf_op jit(solution)/shard_map/all_to_all | solution.py:423
  253.4 4.6 %all-to-all-start.4 = ((f32[64,8,128]{2,1,0:T(8,128)}), f32[64,8,128]{2,1,0:T(8,128)S(1)}, u32[]{:S(2)}, u32[]{:S(2)}) async-start(f32[64,8,128]{2,1,0:T(8,128)} %broadcast_in_dim.20), calls=%async_computation.4 | async-start | bytes 524288 | tf_op jit(solution)/shard_map/all_to_all | solution.py:425
  258.8 3.0 %collective-permute-start.13 = (bf16[4,48,1024]{2,1,0:T(8,128)(2,1)S(1)}, bf16[4,48,1024]{2,1,0:T(8,128)(2,1)S(1)}, u32[]{:S(2)}, u32[]{:S(2)}) collective-permute-start(bf16[4,48,1024]{2,1,0:T(8,128)(2,1)S(1)} %get-tuple-element.17), channel_id=1, source_target_pairs={{0,128},{64,192},{128,0},{192,64},{1,129},{65,193},{129,1},{193,65... | collective-permute-start | bytes 1179656 | tf_op jit(solution)/shard_map/ppermute | solution.py:374
  262.4 7.9 %collective-permute-done.12.refs_1_ = bf16[4,48,1024]{2,1,0:T(8,128)(2,1)S(1)} collective-permute-done((bf16[4,48,1024]{2,1,0:T(8,128)(2,1)S(1)}, bf16[4,48,1024]{2,1,0:T(8,128)(2,1)S(1)}, u32[]{:S(2)}, u32[]{:S(2)}) %collective-permute-start.12) | collective-permute-done | bytes 393248 | tf_op jit(solution)/shard_map/ppermute | solution.py:374
  272.4 7.1 %collective-permute-done.14.refs_3_ = bf16[4,48,1024]{2,1,0:T(8,128)(2,1)S(1)} collective-permute-done((bf16[4,48,1024]{2,1,0:T(8,128)(2,1)S(1)}, bf16[4,48,1024]{2,1,0:T(8,128)(2,1)S(1)}, u32[]{:S(2)}, u32[]{:S(2)}) %collective-permute-start.14) | collective-permute-done | bytes 393248 | tf_op jit(solution)/shard_map/ppermute | solution.py:374
  (65 shorter events, 32.2 us)
Async XLA Ops:
  8.9 8.8 %copy-start.4 = (bf16[1,4,48,4096]{3,2,1,0:T(8,128)(2,1)S(1)}, bf16[1,4,48,4096]{3,2,1,0:T(8,128)(2,1)}, u32[]{:S(2)}) copy-start(bf16[1,4,48,4096]{3,2,1,0:T(8,128)(2,1)} %param.6) | copy-start | bytes 4718596
  8.9 8.8 %copy-start.6 = (bf16[1,4096,16]{1,2,0:T(8,128)(2,1)S(1)}, bf16[1,4096,16]{1,2,0:T(8,128)(2,1)}, u32[]{:S(2)}) copy-start(bf16[1,4096,16]{1,2,0:T(8,128)(2,1)} %param.10) | copy-start | bytes 393220
  8.9 8.8 %copy-start.9 = (s32[1,4,48,2]{2,3,1,0:T(2,128)S(1)}, s32[1,4,48,2]{2,3,1,0:T(2,128)}, u32[]{:S(2)}) copy-start(s32[1,4,48,2]{2,3,1,0:T(2,128)} %param.9) | copy-start | bytes 4612
  8.9 114.3 %all-to-all-start = ((bf16[16,72,2048]{2,1,0:T(8,128)(2,1)}), bf16[16,72,2048]{2,1,0:T(8,128)(2,1)}, u32[]{:S(2)}, u32[]{:S(2)}) async-start(bf16[16,72,2048]{2,1,0:T(8,128)(2,1)} %copy-done.1), calls=%async_computation | async-start | bytes 9437184 | tf_op jit(solution)/shard_map/all_to_all | solution.py:393
  130.8 81.0 %all-to-all-start.1 = ((bf16[4,4,48,1024]{3,2,1,0:T(8,128)(2,1)}), bf16[4,4,48,1024]{3,2,1,0:T(8,128)(2,1)}, u32[]{:S(2)}, u32[]{:S(2)}) async-start(bf16[4,4,48,1024]{3,2,1,0:T(8,128)(2,1)} %combine.1), calls=%async_computation.1 | async-start | bytes 3145728 | tf_op jit(solution)/shard_map/all_to_all | solution.py:416
  139.5 64.9 %collective-permute-start.2 = (bf16[2,4,48,1024]{3,2,1,0:T(8,128)(2,1)S(1)}, bf16[2,4,48,1024]{3,2,1,0:T(8,128)(2,1)S(1)}, u32[]{:S(2)}, u32[]{:S(2)}) collective-permute-start(bf16[2,4,48,1024]{3,2,1,0:T(8,128)(2,1)S(1)} %bitcast.92), channel_id=1, source_target_pairs={{0,64},{64,128},{128,192},{192,0},{1,65},{65,129},{129,193},{193,1... | collective-permute-start | bytes 2359304 | tf_op jit(solution)/shard_map/ppermute | solution.py:374
  141.3 63.2 %collective-permute-start.1 = (bf16[2,4,48,1024]{3,2,1,0:T(8,128)(2,1)S(1)}, bf16[2,4,48,1024]{3,2,1,0:T(8,128)(2,1)S(1)}, u32[]{:S(2)}, u32[]{:S(2)}) collective-permute-start(bf16[2,4,48,1024]{3,2,1,0:T(8,128)(2,1)S(1)} %bitcast.93), channel_id=1, source_target_pairs={{0,128},{64,192},{128,0},{192,64},{1,129},{65,193},{129,1},{193,65... | collective-permute-start | bytes 2359304 | tf_op jit(solution)/shard_map/ppermute | solution.py:374
  142.2 62.2 %collective-permute-start = (bf16[2,4,48,1024]{3,2,1,0:T(8,128)(2,1)S(1)}, bf16[2,4,48,1024]{3,2,1,0:T(8,128)(2,1)S(1)}, u32[]{:S(2)}, u32[]{:S(2)}) collective-permute-start(bf16[2,4,48,1024]{3,2,1,0:T(8,128)(2,1)S(1)} %bitcast.94), channel_id=1, source_target_pairs={{0,192},{64,0},{128,64},{192,128},{1,193},{65,1},{129,65},{193,129... | collective-permute-start | bytes 2359304 | tf_op jit(solution)/shard_map/ppermute | solution.py:374
  144.9 44.3 %collective-permute-start.8 = (f32[4,32,48]{2,1,0:T(8,128)S(1)}, f32[4,32,48]{2,1,0:T(8,128)S(1)}, u32[]{:S(2)}, u32[]{:S(2)}) collective-permute-start(f32[4,32,48]{2,1,0:T(8,128)S(1)} %get-tuple-element.9), channel_id=1, source_target_pairs={{0,64},{64,128},{128,192},{192,0},{1,65},{65,129},{129,193},{193,1... | collective-permute-start | bytes 73736 | tf_op jit(solution)/shard_map/ppermute | solution.py:374
  144.9 46.8 %collective-permute-start.7 = (f32[4,32,48]{2,1,0:T(8,128)S(1)}, f32[4,32,48]{2,1,0:T(8,128)S(1)}, u32[]{:S(2)}, u32[]{:S(2)}) collective-permute-start(f32[4,32,48]{2,1,0:T(8,128)S(1)} %get-tuple-element.9), channel_id=1, source_target_pairs={{0,128},{64,192},{128,0},{192,64},{1,129},{65,193},{129,1},{193,65... | collective-permute-start | bytes 73736 | tf_op jit(solution)/shard_map/ppermute | solution.py:374
  189.2 11.3 %collective-permute-start.5 = (bf16[16,1024]{1,0:T(8,128)(2,1)S(1)}, bf16[16,1024]{1,0:T(8,128)(2,1)S(1)}, u32[]{:S(2)}, u32[]{:S(2)}) collective-permute-start(bf16[16,1024]{1,0:T(8,128)(2,1)S(1)} %get-tuple-element.22), channel_id=1, source_target_pairs={{0,64},{64,128},{128,192},{192,0},{1,65},{65,129},{129,193},{193,1... | collective-permute-start | bytes 98312 | tf_op jit(solution)/shard_map/ppermute | solution.py:374
  191.7 4.3 %collective-permute-start.6 = (f32[4,32,48]{2,1,0:T(8,128)S(1)}, f32[4,32,48]{2,1,0:T(8,128)S(1)}, u32[]{:S(2)}, u32[]{:S(2)}) collective-permute-start(f32[4,32,48]{2,1,0:T(8,128)S(1)} %get-tuple-element.9), channel_id=1, source_target_pairs={{0,192},{64,0},{128,64},{192,128},{1,193},{65,1},{129,65},{193,129... | collective-permute-start | bytes 73736 | tf_op jit(solution)/shard_map/ppermute | solution.py:374
  196.0 6.4 %collective-permute-start.4 = (bf16[16,1024]{1,0:T(8,128)(2,1)S(1)}, bf16[16,1024]{1,0:T(8,128)(2,1)S(1)}, u32[]{:S(2)}, u32[]{:S(2)}) collective-permute-start(bf16[16,1024]{1,0:T(8,128)(2,1)S(1)} %get-tuple-element.23), channel_id=1, source_target_pairs={{0,128},{64,192},{128,0},{192,64},{1,129},{65,193},{129,1},{193,65... | collective-permute-start | bytes 98312 | tf_op jit(solution)/shard_map/ppermute | solution.py:374
  200.5 3.9 %collective-permute-start.3 = (bf16[16,1024]{1,0:T(8,128)(2,1)S(1)}, bf16[16,1024]{1,0:T(8,128)(2,1)S(1)}, u32[]{:S(2)}, u32[]{:S(2)}) collective-permute-start(bf16[16,1024]{1,0:T(8,128)(2,1)S(1)} %get-tuple-element.21), channel_id=1, source_target_pairs={{0,192},{64,0},{128,64},{192,128},{1,193},{65,1},{129,65},{193,129... | collective-permute-start | bytes 98312 | tf_op jit(solution)/shard_map/ppermute | solution.py:374
  207.6 13.6 %collective-permute-start.11 = (f32[4,24,48]{2,1,0:T(8,128)}, f32[4,24,48]{2,1,0:T(8,128)}, u32[]{:S(2)}, u32[]{:S(2)}) collective-permute-start(f32[4,24,48]{2,1,0:T(8,128)} %coupling.1), channel_id=1, source_target_pairs={{0,64},{64,128},{128,192},{192,0},{1,65},{65,129},{129,193},{193,1... | collective-permute-start | bytes 55304 | tf_op jit(solution)/shard_map/ppermute | solution.py:374
  207.6 13.6 %collective-permute-start.10 = (f32[4,24,48]{2,1,0:T(8,128)}, f32[4,24,48]{2,1,0:T(8,128)}, u32[]{:S(2)}, u32[]{:S(2)}) collective-permute-start(f32[4,24,48]{2,1,0:T(8,128)} %coupling.1), channel_id=1, source_target_pairs={{0,128},{64,192},{128,0},{192,64},{1,129},{65,193},{129,1},{193,65... | collective-permute-start | bytes 55304 | tf_op jit(solution)/shard_map/ppermute | solution.py:374
  210.0 11.2 %collective-permute-start.9 = (f32[4,24,48]{2,1,0:T(8,128)}, f32[4,24,48]{2,1,0:T(8,128)}, u32[]{:S(2)}, u32[]{:S(2)}) collective-permute-start(f32[4,24,48]{2,1,0:T(8,128)} %coupling.1), channel_id=1, source_target_pairs={{0,192},{64,0},{128,64},{192,128},{1,193},{65,1},{129,65},{193,129... | collective-permute-start | bytes 55304 | tf_op jit(solution)/shard_map/ppermute | solution.py:374
  216.7 21.3 %copy-start.3 = (bf16[4,48,4096]{2,1,0:T(8,128)(2,1)S(1)}, bf16[4,48,4096]{2,1,0:T(8,128)(2,1)}, u32[]{:S(2)}) copy-start(bf16[4,48,4096]{2,1,0:T(8,128)(2,1)} %up_ref.3) | copy-start | bytes 4718596
  217.5 7.7 %all-to-all-start.2 = ((f32[4,1,1536]{2,1,0:T(1,128)}), f32[4,1,1536]{2,1,0:T(1,128)S(1)}, u32[]{:S(2)}, u32[]{:S(2)}) async-start(f32[4,1,1536]{2,1,0:T(1,128)} %reshape.50), calls=%async_computation.2 | async-start | bytes 49152 | tf_op jit(solution)/shard_map/all_to_all | solution.py:419
  229.6 22.1 %all-to-all-start.3 = ((f32[64,8,128]{2,1,0:T(8,128)}), f32[64,8,128]{2,1,0:T(8,128)}, u32[]{:S(2)}, u32[]{:S(2)}) async-start(f32[64,8,128]{2,1,0:T(8,128)} %get-tuple-element.11), calls=%async_computation.3 | async-start | bytes 524288 | tf_op jit(solution)/shard_map/all_to_all | solution.py:423
  253.4 27.7 %all-to-all-start.4 = ((f32[64,8,128]{2,1,0:T(8,128)}), f32[64,8,128]{2,1,0:T(8,128)S(1)}, u32[]{:S(2)}, u32[]{:S(2)}) async-start(f32[64,8,128]{2,1,0:T(8,128)} %broadcast_in_dim.20), calls=%async_computation.4 | async-start | bytes 524288 | tf_op jit(solution)/shard_map/all_to_all | solution.py:425
  258.2 12.1 %collective-permute-start.12 = (bf16[4,48,1024]{2,1,0:T(8,128)(2,1)S(1)}, bf16[4,48,1024]{2,1,0:T(8,128)(2,1)S(1)}, u32[]{:S(2)}, u32[]{:S(2)}) collective-permute-start(bf16[4,48,1024]{2,1,0:T(8,128)(2,1)S(1)} %get-tuple-element.18), channel_id=1, source_target_pairs={{0,64},{64,128},{128,192},{192,0},{1,65},{65,129},{129,193},{193,1... | collective-permute-start | bytes 1179656 | tf_op jit(solution)/shard_map/ppermute | solution.py:374
  258.8 13.6 %collective-permute-start.13 = (bf16[4,48,1024]{2,1,0:T(8,128)(2,1)S(1)}, bf16[4,48,1024]{2,1,0:T(8,128)(2,1)S(1)}, u32[]{:S(2)}, u32[]{:S(2)}) collective-permute-start(bf16[4,48,1024]{2,1,0:T(8,128)(2,1)S(1)} %get-tuple-element.17), channel_id=1, source_target_pairs={{0,128},{64,192},{128,0},{192,64},{1,129},{65,193},{129,1},{193,65... | collective-permute-start | bytes 1179656 | tf_op jit(solution)/shard_map/ppermute | solution.py:374
  261.8 17.6 %collective-permute-start.14 = (bf16[4,48,1024]{2,1,0:T(8,128)(2,1)S(1)}, bf16[4,48,1024]{2,1,0:T(8,128)(2,1)S(1)}, u32[]{:S(2)}, u32[]{:S(2)}) collective-permute-start(bf16[4,48,1024]{2,1,0:T(8,128)(2,1)S(1)} %get-tuple-element.16), channel_id=1, source_target_pairs={{0,192},{64,0},{128,64},{192,128},{1,193},{65,1},{129,65},{193,129... | collective-permute-start | bytes 1179656 | tf_op jit(solution)/shard_map/ppermute | solution.py:374
  (6 other events, 8.8 us)

commit v2 on v1

--- a/solution.py
+++ b/solution.py
@@ -1,3 +1,5 @@
+import functools
+
 import jax
 import jax.numpy as jnp
 from jax import lax
@@ -15,13 +17,16 @@
     return pltpu.CompilerParams(vmem_limit_bytes=mib << 20)
 
 
-def pack_kernel(main_ref, last_ref, out_ref):
-    unit = pl.program_id(0)
-    units = pl.num_programs(0)
+def in_hbm(array):
+    return pltpu.with_memory_space_constraint(array, pltpu.MemorySpace.HBM)
+
+
+def pack_kernel(first, main_ref, last_ref, out_ref):
+    unit = pl.program_id(0) + first
     micro, _, dests, width = last_ref.shape
     half = width // 2
 
-    @pl.when(unit < units - 1)
+    @pl.when(unit > 0)
     def _():
         slots = main_ref.shape[1]
         n = slots * dests
@@ -32,7 +37,7 @@
         moved = jnp.dot(swap, rows, preferred_element_type=F32)
         out_ref[...] = moved.reshape(dests, slots, half).astype(BF16)
 
-    @pl.when(unit == units - 1)
+    @pl.when(unit == 0)
     def _():
         n_in = micro * dests
         n_out = 2 * micro * dests
@@ -48,23 +53,22 @@
         out_ref[...] = total.reshape(dests, 2 * micro, half).astype(BF16)
 
 
-def pack(grads):
+def pack(grads, first, last):
     micro, cap, dests, width = grads.shape
     half = width // 2
-    units = 2 * micro + 1
-    last_unit = 2 * micro - 1
-    return pl.pallas_call(
-        pack_kernel,
-        grid=(units,),
+
+    def main(u):
+        return jnp.maximum(u + first - 1, 0)
+
+    return pl.pallas_call(
+        functools.partial(pack_kernel, first),
+        grid=(last - first,),
         in_specs=[
-            pl.BlockSpec(
-                (1, cap - 1, dests, half),
-                lambda u: (jnp.minimum(u, last_unit) // 2, 0, 0, jnp.minimum(u, last_unit) % 2),
-            ),
+            pl.BlockSpec((1, cap - 1, dests, half), lambda u: (main(u) // 2, 0, 0, main(u) % 2)),
             pl.BlockSpec((micro, 1, dests, width), lambda u: (0, cap - 1, 0, 0)),
         ],
         out_specs=pl.BlockSpec((dests, 8, half), lambda u: (0, u, 0)),
-        out_shape=jax.ShapeDtypeStruct((dests, units * 8, half), BF16),
+        out_shape=pltpu.HBM((dests, (last - first) * 8, half), BF16),
         compiler_params=params(40),
         name="pack_slots",
     )(grads, grads)
@@ -166,13 +170,12 @@
     )(p, saved, w, v)
 
 
-def combine_kernel(main_ref, last_ref, gate_ref, place_ref, out_ref):
+def combine_kernel(micro, main_ref, last_ref, gate_ref, place_ref, out_ref):
     h = pl.program_id(0)
     experts, _, half = main_ref.shape
     lanes = gate_ref.shape[2]
     rows = lanes // 2
     n = experts * 8
-    micro = pl.num_programs(1)
     index = lax.broadcasted_iota(jnp.int32, (2 * n, lanes), 0)
     pick = jnp.zeros((2 * n, lanes), F32)
     for k in range(2):
@@ -191,29 +194,27 @@
     out_ref[1, 0] = total[:, half // 2 :]
 
 
-def combine(received, gates, places):
-    experts, packed, half = received.shape
-    units = packed // 8
-    micro = (units - 1) // 2
-    lanes = gates.shape[2]
+def combine(main, last, gates, places, first_m, count, first_unit):
+    experts, _, half = main.shape
+    micro, _, lanes = gates.shape
     rows = lanes // 2
     return pl.pallas_call(
-        combine_kernel,
-        grid=(2, micro),
+        functools.partial(combine_kernel, micro),
+        grid=(2, count),
         in_specs=[
-            pl.BlockSpec((experts, 8, half), lambda h, m: (0, 2 * m + h, 0)),
-            pl.BlockSpec((experts, 8, half), lambda h, m: (0, units - 1, 0)),
-            pl.BlockSpec((1, 2, lanes), lambda h, m: (m, 0, 0)),
-            pl.BlockSpec((1, 2, lanes), lambda h, m: (m, 0, 0)),
+            pl.BlockSpec((experts, 8, half), lambda h, m: (0, first_unit + 2 * m + h, 0)),
+            pl.BlockSpec((experts, 8, half), lambda h, m: (0, 0, 0)),
+            pl.BlockSpec((1, 2, lanes), lambda h, m: (first_m + m, 0, 0)),
+            pl.BlockSpec((1, 2, lanes), lambda h, m: (first_m + m, 0, 0)),
         ],
         out_specs=pl.BlockSpec((2, 1, rows, half // 2), lambda h, m: (h, m, 0, 0)),
-        out_shape=jax.ShapeDtypeStruct((4, micro, rows, half // 2), BF16),
+        out_shape=jax.ShapeDtypeStruct((4, count, rows, half // 2), BF16),
         compiler_params=params(40),
         name="combine",
-    )(received, received, gates, places)
-
-
-def dots_kernel(p_ref, up_ref, back_ref, saved_ref, out_ref):
+    )(main, last, gates, places)
+
+
+def dots_kernel(turned_order, p_ref, up_ref, back_ref, saved_ref, out_ref):
     p = p_ref[0]
     sections, _, rows, quarter = back_ref.shape
     base = up_ref[0].astype(F32)
@@ -230,24 +231,24 @@
             )
             out_ref[0, 2 * s + k : 2 * s + k + 1, :] = row[:1]
         if s > 0:
-            base = base + back_ref[s, 0].astype(F32)
-
-
-def partial_dots(p, upstream, back, saved):
-    sections, micro, rows, quarter = back.shape
-    return pl.pallas_call(
-        dots_kernel,
+            base = base + back_ref[j if turned_order else s, 0].astype(F32)
+
+
+def partial_dots(p, upstream, back, saved, first_m, turned_order):
+    sections, count, rows, quarter = back.shape
+    return pl.pallas_call(
+        functools.partial(dots_kernel, turned_order),
         grid_spec=pltpu.PrefetchScalarGridSpec(
             num_scalar_prefetch=1,
-            grid=(micro,),
+            grid=(count,),
             in_specs=[
-                pl.BlockSpec((1, rows, quarter), lambda m, p: (m, 0, p[0])),
+                pl.BlockSpec((1, rows, quarter), lambda m, p: (first_m + m, 0, p[0])),
                 pl.BlockSpec((sections, 1, rows, quarter), lambda m, p: (0, m, 0, 0)),
-                pl.BlockSpec((sections, 2, 1, rows, quarter), lambda m, p: (0, 0, m, 0, 0)),
+                pl.BlockSpec((sections, 2, 1, rows, quarter), lambda m, p: (0, 0, first_m + m, 0, 0)),
             ],
             out_specs=pl.BlockSpec((1, 2 * sections, rows), lambda m, p: (m, 0, 0)),
         ),
-        out_shape=jax.ShapeDtypeStruct((micro, 2 * sections, rows), F32),
+        out_shape=jax.ShapeDtypeStruct((count, 2 * sections, rows), F32),
         compiler_params=params(32),
         name="dots",
     )(p, upstream, back, saved)
@@ -285,7 +286,8 @@
     cols = width // 128
     for r in range(experts // 8):
         for c in range(cols):
-            part_ref[r * cols + c] = total[r * 8 : (r + 1) * 8, c * 128 : (c + 1) * 128]
+            tile = total[r * 8 : (r + 1) * 8, c * 128 : (c + 1) * 128]
+            part_ref[r * cols + c] = tile.astype(BF16)
 
 
 def dense_terms(p, dots, links, v, normed):
@@ -300,14 +302,14 @@
         out_specs=[whole] * 2,
         out_shape=[
             jax.ShapeDtypeStruct((micro, sections * experts, rows), BF16),
-            jax.ShapeDtypeStruct((blocks, 8, 128), F32),
+            jax.ShapeDtypeStruct((blocks, 8, 128), BF16),
         ],
         compiler_params=params(32),
         name="dense",
     )(p, dots, links, v, normed)
 
 
-def grads_kernel(p_ref, up_ref, back_ref, dense_ref, w_ref, out_ref):
+def grads_kernel(turned_order, p_ref, up_ref, back_ref, dense_ref, w_ref, out_ref):
     p = p_ref[0]
     sections = back_ref.shape[0]
     experts = w_ref.shape[1]
@@ -316,27 +318,27 @@
         j = (s - p) & (sections - 1)
         dense = dense_ref[0, s * experts : (s + 1) * experts, :]
         term = lax.dot_general(dense, w_ref[j], TN, preferred_element_type=F32)
-        total = total + back_ref[s, 0].astype(F32) + term
-        out_ref[s, 0] = total.astype(BF16)
-
-
-def grads_of(p, upstream, back, dense, w):
-    sections, micro, rows, quarter = back.shape
+        total = total + back_ref[j if turned_order else s, 0].astype(F32) + term
+        out_ref[j, 0] = total.astype(BF16)
+
+
+def grads_of(p, upstream, back, dense, w, first_m, turned_order):
+    sections, count, rows, quarter = back.shape
     experts = w.shape[1]
     return pl.pallas_call(
-        grads_kernel,
+        functools.partial(grads_kernel, turned_order),
         grid_spec=pltpu.PrefetchScalarGridSpec(
             num_scalar_prefetch=1,
-            grid=(micro,),
+            grid=(count,),
             in_specs=[
-                pl.BlockSpec((1, rows, quarter), lambda m, p: (m, 0, p[0])),
+                pl.BlockSpec((1, rows, quarter), lambda m, p: (first_m + m, 0, p[0])),
                 pl.BlockSpec((sections, 1, rows, quarter), lambda m, p: (0, m, 0, 0)),
-                pl.BlockSpec((1, sections * experts, rows), lambda m, p: (m, 0, 0)),
+                pl.BlockSpec((1, sections * experts, rows), lambda m, p: (first_m + m, 0, 0)),
                 pl.BlockSpec((sections, experts, quarter), lambda m, p: (0, 0, 0)),
             ],
             out_specs=pl.BlockSpec((sections, 1, rows, quarter), lambda m, p: (0, m, 0, 0)),
         ),
-        out_shape=jax.ShapeDtypeStruct((sections, micro, rows, quarter), BF16),
+        out_shape=jax.ShapeDtypeStruct((sections, count, rows, quarter), BF16),
         compiler_params=params(32),
         name="grads",
     )(p, upstream, back, dense, w)
@@ -389,8 +391,11 @@
     w = router_weight[0].T
     experts = w.shape[0]
 
-    send = pack(jnp.transpose(expert_grads[0, :, 0, 0], (0, 2, 1, 3)))
-    received = lax.all_to_all(send, "expert", 0, 0, tiled=True)
+    grads = in_hbm(jnp.transpose(expert_grads[0, :, 0, 0], (0, 2, 1, 3)))
+    units = 2 * micro + 1
+    cut = units - 2
+    lead = lax.all_to_all(pack(grads, 0, cut), "expert", 0, 0, tiled=True)
+    tail_send = pack(grads, cut, units)
 
     v, gates, places = gates_of(normed, w, jnp.transpose(routes[0], (0, 2, 1)))
     gates = jnp.concatenate([gates, gates], axis=-1)
@@ -411,27 +416,45 @@
     saved_all = spread(jnp.transpose(saved_out[0], (2, 0, 1, 3)), 3)
     links = coupling(p, saved_all, w_all, v_all)
     links = sum(gathered(links))
-
-    back = combine(received, gates, places)
-    back = lax.all_to_all(back, "pipe", 0, 0, tiled=True)
-    dots = partial_dots(p, upstream, back, saved_all)
+    gates, places, links, saved_all, w_all, v_all, tail_send = lax.optimization_barrier(
+        (gates, places, links, saved_all, w_all, v_all, tail_send)
+    )
+
+    def spread_back(back):
+        def block(distance):
+            return lax.dynamic_index_in_dim(back, (section + distance) % sections, 0, False)
+
+        blocks = [block(0)] + [turned(block(sections - j), sections - j) for j in range(1, sections)]
+        return jnp.stack(blocks)
+
+    lead, tail_send = lax.optimization_barrier((lead, tail_send))
+    tail = lax.all_to_all(tail_send, "expert", 0, 0, tiled=True)
+    back_lead = spread_back(combine(lead, lead, gates, places, 0, micro - 1, 1))
+    dots_lead = partial_dots(p, upstream, back_lead, saved_all, 0, True)
+    dots_lead, back_lead, gates = lax.optimization_barrier((dots_lead, back_lead, gates))
+    back_tail = combine(tail, lead, gates, places, micro - 1, 1, 0)
+    back_tail = lax.all_to_all(back_tail, "pipe", 0, 0, tiled=True)
+    dots_tail = partial_dots(p, upstream, back_tail, saved_all, micro - 1, False)
+
+    dots = jnp.concatenate([dots_lead, dots_tail])
     dots = jnp.broadcast_to(dots[None], (sections,) + dots.shape)
     dots = lax.all_to_all(dots, "pipe", 0, 0, tiled=True)
     dense, part = dense_terms(p, dots, links, v_all, normed)
 
     axes = ("expert", "dp")
     part = lax.all_to_all(part, axes, 0, 0, tiled=True)
-    part = jnp.broadcast_to(jnp.sum(part, axis=0, keepdims=True), part.shape)
-    part = lax.all_to_all(part, axes, 0, 0, tiled=True)
+
+    outs_lead = grads_of(p, upstream, back_lead, dense, w_all, 0, True)
+    outs_tail = grads_of(p, upstream, back_tail, dense, w_all, micro - 1, False)
+    outs = jnp.concatenate([outs_lead, outs_tail], axis=1)
+    blocks = [outs[0]] + [turned(outs[d], d) for d in range(1, sections)]
+
+    total = jnp.sum(part.astype(F32), axis=0, keepdims=True).astype(BF16)
+    total, blocks[1], blocks[3] = lax.optimization_barrier((total, blocks[1], blocks[3]))
+    part = lax.all_to_all(jnp.broadcast_to(total, part.shape), axes, 0, 0, tiled=True)
     cols = width // 128
-    router_grad = part.reshape(experts // 8, cols, 8, 128).transpose(0, 2, 1, 3)
+    router_grad = part.astype(F32).reshape(experts // 8, cols, 8, 128).transpose(0, 2, 1, 3)
     router_grad = router_grad.reshape(experts, width).T
-
-    outs = grads_of(p, upstream, back, dense, w_all)
-    blocks = [lax.dynamic_index_in_dim(outs, section, 0, keepdims=False)]
-    for d in range(1, sections):
-        block = lax.dynamic_index_in_dim(outs, (section + d) % sections, 0, keepdims=False)
-        blocks.append(turned(block, d))
     grad_input = join(p, blocks)
     return (grad_input[None], router_grad[None])
 

time: 284 us -> 206 us (0.73)
  waiting for transfers between devices: 181 us -> 86.6 us
  blocking collectives: 0 us -> 20.3 us
  local copies, waits for them, and re-layouts: 16.1 us -> 12.1 us
    all_to_all x3, waiting for transfers between devices: 107 us -> 29 us  [the longest x1 18.6 us: on_device(): lead = lax.all_to_all(pack(grads, 0, cut), 'expert', 0, 0, tiled=True)]
    all_to_all x0 -> x2, blocking collectives: none -> 20.3 us  [the longest x1 12.4 us: on_device(): back_tail = lax.all_to_all(back_tail, 'pipe', 0, 0, tiled=True)]
    ppermute x15 -> x18, waiting for transfers between devices: 64.3 us -> 47.8 us  [turned(): lax.ppermute(block, 'pipe', [(i, (i + distance) % n) for i in range(n)])]
    all_to_all x2 -> x1, starting transfers between devices: 13 us -> 7.96 us  [on_device(): part = lax.all_to_all(part, axes, 0, 0, tiled=True)]
    unnamed x23 -> x32, local copies, waits for them, and re-layouts: 10.3 us -> 6.74 us
    pallas_call x4 -> x8, Pallas kernels: 17.8 us -> 20.8 us  [the longest x2 9.87 us: pack(): pl.pallas_call(functools.partial(pack_kernel, first), grid=(last - first,...]
    ppermute x15 -> x18, starting transfers between devices: 25.3 us -> 26.7 us  [turned(): lax.ppermute(block, 'pipe', [(i, (i + distance) % n) for i in range(n)])]
    all_to_all x2 -> x1, waiting for transfers between devices: 9.75 us -> 9.77 us  [on_device(): part = lax.all_to_all(part, axes, 0, 0, tiled=True)]
  transfers between devices with their start and end apart: 20 -> 22, of which waited for: 10 -> 12; matrix products, arithmetic and copies ran while one was open for 2% -> 3% of each run, Pallas kernels for 4% -> 7%
where the time goes in v2:
time: 206 us; the launch traced here: 203 us
  waiting for transfers between devices  86.6 us (42%)
  starting transfers between devices  52.9 us (26%)
  Pallas kernels  26.6 us (13%)
  blocking collectives  20.3 us (10%)
  local copies, waits for them, and re-layouts  12.1 us (6%)
  other arithmetic  3.92 us (2%)
    ppermute x18, waiting for transfers between devices, turned(): lax.ppermute(block, 'pipe', [(i, (i + distance) % n) for i in range(n)])  47.8 us
    ppermute x18, starting transfers between devices, turned(): lax.ppermute(block, 'pipe', [(i, (i + distance) % n) for i in range(n)])  26.7 us
    all_to_all x1, waiting for transfers between devices, on_device(): lead = lax.all_to_all(pack(grads, 0, cut), 'expert', 0, 0, tiled=True)  18.6 us
    all_to_all x1, blocking collectives, on_device(): back_tail = lax.all_to_all(back_tail, 'pipe', 0, 0, tiled=True)  12.4 us
    pallas_call x2, Pallas kernels, pack(): pl.pallas_call(functools.partial(pack_kernel, first), grid=(last - first,...  9.87 us
    all_to_all x1, waiting for transfers between devices, on_device(): part = lax.all_to_all(part, axes, 0, 0, tiled=True)  9.77 us
    all_to_all x1, waiting for transfers between devices, on_device(): lax.all_to_all(jnp.broadcast_to(total, part.shape), axes, 0, 0, tiled=True)  9.65 us
    all_to_all x1, starting transfers between devices, on_device(): lead = lax.all_to_all(pack(grads, 0, cut), 'expert', 0, 0, tiled=True)  8.91 us
  transfers between devices with their start and end apart: 22, of which 12 were waited for; matrix products, arithmetic and copies ran while one was open for 3% of the time, Pallas kernels for 7%

profile of v2, /device:TPU:8, one launch (start us, length us, event | category | flops | bytes accessed | tf_op | source)
XLA Modules:
  0.0 203.5 jit_solution(11794760027868880757)
XLA Ops:
  0.6 7.2 %pack_slots.2 = bf16[16,56,2048]{2,1,0:T(8,128)(2,1)} custom-call(bf16[4,9,16,4096]{3,2,1,0:T(8,128)(2,1)} %bitcast.96, bf16[4,9,16,4096]{3,2,1,0:T(8,128)(2,1)} %bitcast.97), custom_call_target="tpu_custom_call" | custom-call | tf_op jit(solution)/shard_map/pack_slots/pallas_call | solution.py:63
  7.8 8.9 %all-to-all-start = ((bf16[16,56,2048]{2,1,0:T(8,128)(2,1)}), bf16[16,56,2048]{2,1,0:T(8,128)(2,1)}, u32[]{:S(2)}, u32[]{:S(2)}) async-start(bf16[16,56,2048]{2,1,0:T(8,128)(2,1)} %pack_slots.2), calls=%async_computation | async-start | bytes 7340032 | tf_op jit(solution)/shard_map/all_to_all | solution.py:397
  16.8 3.2 %constant_dynamic-slice_fusion.4 = (bf16[1,4,48,2,1024]{4,3,2,1,0:T(2,128)(2,1)S(1)}, bf16[1,4,48,2,1024]{4,3,2,1,0:T(2,128)(2,1)S(1)}, bf16[1,4,48,2,1024]{4,3,...) fusion(bf16[1,4,48,2,4096]{4,3,2,1,0:T(2,128)(2,1)S(1)} %copy-done.14, s32[]{:T(128)S(6)} %select_n.65, s32[]{:T(128)S(6)} %select_n.67, ...), kind=kLoop, calls=%fused_computation.38 | loop fusion | bytes 6291472 | tf_op jit(solution)/shard_map/dynamic-slice.8
  23.3 2.5 %collective-permute-start = (bf16[2,4,48,1024]{3,2,1,0:T(8,128)(2,1)S(1)}, bf16[2,4,48,1024]{3,2,1,0:T(8,128)(2,1)S(1)}, u32[]{:S(2)}, u32[]{:S(2)}) collective-permute-start(bf16[2,4,48,1024]{3,2,1,0:T(8,128)(2,1)S(1)} %bitcast.107), channel_id=1, source_target_pairs={{0,192},{64,0},{128,64},{192,128},{1,193},{65,1},{129,65},{193,129... | collective-permute-start | bytes 2359304 | tf_op jit(solution)/shard_map/ppermute | solution.py:376
  27.0 3.4 %collective-permute-start.7 = (f32[4,32,48]{2,1,0:T(8,128)S(1)}, f32[4,32,48]{2,1,0:T(8,128)S(1)}, u32[]{:S(2)}, u32[]{:S(2)}) collective-permute-start(f32[4,32,48]{2,1,0:T(8,128)S(1)} %get-tuple-element.24), channel_id=1, source_target_pairs={{0,128},{64,192},{128,0},{192,64},{1,129},{65,193},{129,1},{193,65... | collective-permute-start | bytes 73736 | tf_op jit(solution)/shard_map/ppermute | solution.py:376
  30.4 28.6 %collective-permute-done.8 = f32[4,32,48]{2,1,0:T(8,128)S(1)} collective-permute-done((f32[4,32,48]{2,1,0:T(8,128)S(1)}, f32[4,32,48]{2,1,0:T(8,128)S(1)}, u32[]{:S(2)}, u32[]{:S(2)}) %collective-permute-start.8) | collective-permute-done | bytes 24608 | tf_op jit(solution)/shard_map/ppermute | solution.py:376
  63.5 3.2 %collective-permute-start.4 = (bf16[16,1024]{1,0:T(8,128)(2,1)S(1)}, bf16[16,1024]{1,0:T(8,128)(2,1)S(1)}, u32[]{:S(2)}, u32[]{:S(2)}) collective-permute-start(bf16[16,1024]{1,0:T(8,128)(2,1)S(1)} %get-tuple-element.57), channel_id=1, source_target_pairs={{0,128},{64,192},{128,0},{192,64},{1,129},{65,193},{129,1},{193,65... | collective-permute-start | bytes 98312 | tf_op jit(solution)/shard_map/ppermute | solution.py:376
  71.3 2.0 coupling.1
  73.7 2.8 %collective-permute-start.10 = (f32[4,24,48]{2,1,0:T(8,128)S(1)}, f32[4,24,48]{2,1,0:T(8,128)S(1)}, u32[]{:S(2)}, u32[]{:S(2)}) collective-permute-start(f32[4,24,48]{2,1,0:T(8,128)S(1)} %coupling.1), channel_id=1, source_target_pairs={{0,128},{64,192},{128,0},{192,64},{1,129},{65,193},{129,1},{193,65... | collective-permute-start | bytes 55304 | tf_op jit(solution)/shard_map/ppermute | solution.py:376
  78.0 2.7 %pack_slots.3 = bf16[16,16,2048]{2,1,0:T(8,128)(2,1)} custom-call(bf16[4,9,16,4096]{3,2,1,0:T(8,128)(2,1)} %bitcast.98, bf16[4,9,16,4096]{3,2,1,0:T(8,128)(2,1)} %bitcast.99), custom_call_target="tpu_custom_call" | custom-call | tf_op jit(solution)/shard_map/pack_slots/pallas_call | solution.py:63
  81.3 18.6 %all-to-all-done.main_ref.last_ref = bf16[16,56,2048]{2,1,0:T(8,128)(2,1)} async-done(((bf16[16,56,2048]{2,1,0:T(8,128)(2,1)}), bf16[16,56,2048]{2,1,0:T(8,128)(2,1)}, u32[]{:S(2)}, u32[]{:S(2)}) %all-to-all-start) | async-done | bytes 3670048 | tf_op jit(solution)/shard_map/all_to_all | solution.py:397
  99.9 4.8 %all-to-all-start.1 = ((bf16[16,16,2048]{2,1,0:T(8,128)(2,1)}), bf16[16,16,2048]{2,1,0:T(8,128)(2,1)}, u32[]{:S(2)}, u32[]{:S(2)}) async-start(bf16[16,16,2048]{2,1,0:T(8,128)(2,1)} %pack_slots.3), calls=%async_computation.1 | async-start | bytes 2097152 | tf_op jit(solution)/shard_map/all_to_all | solution.py:431
  104.7 5.2 %combine.2 = bf16[4,3,48,1024]{3,2,1,0:T(8,128)(2,1)S(1)} custom-call(bf16[16,56,2048]{2,1,0:T(8,128)(2,1)} %all-to-all-done.main_ref.last_ref, bf16[16,56,2048]{2,1,0:T(8,128)(2,1)} %all-to-all-done.main_ref.last_ref, f32[4,2,96]{2,1,0:T(2,128)S(1)} %pad_maximum_fusion.6.gate_ref, s32[4,2,96]{2,1,0:T(2,128)S(1)} %pad_add_fusion.place_ref), custom_call_target="tpu_custom_call" | custom-call | tf_op jit(solution)/shard_map/combine/pallas_call | solution.py:201
  112.5 2.4 %collective-permute-start.12 = (bf16[3,48,1024]{2,1,0:T(8,128)(2,1)S(1)}, bf16[3,48,1024]{2,1,0:T(8,128)(2,1)S(1)}, u32[]{:S(2)}, u32[]{:S(2)}) collective-permute-start(bf16[3,48,1024]{2,1,0:T(8,128)(2,1)S(1)} %get-tuple-element.53), channel_id=1, source_target_pairs={{0,192},{64,0},{128,64},{192,128},{1,193},{65,1},{129,65},{193,129... | collective-permute-start | bytes 884744 | tf_op jit(solution)/shard_map/ppermute | solution.py:376
  115.0 4.9 %collective-permute-done.14 = bf16[3,48,1024]{2,1,0:T(8,128)(2,1)S(1)} collective-permute-done((bf16[3,48,1024]{2,1,0:T(8,128)(2,1)S(1)}, bf16[3,48,1024]{2,1,0:T(8,128)(2,1)S(1)}, u32[]{:S(2)}, u32[]{:S(2)}) %collective-permute-start.14) | collective-permute-done | bytes 294944 | tf_op jit(solution)/shard_map/ppermute | solution.py:376
  119.9 3.2 %collective-permute-done.13 = bf16[3,48,1024]{2,1,0:T(8,128)(2,1)S(1)} collective-permute-done((bf16[3,48,1024]{2,1,0:T(8,128)(2,1)S(1)}, bf16[3,48,1024]{2,1,0:T(8,128)(2,1)S(1)}, u32[]{:S(2)}, u32[]{:S(2)}) %collective-permute-start.13) | collective-permute-done | bytes 294944 | tf_op jit(solution)/shard_map/ppermute | solution.py:376
  123.0 4.7 %collective-permute-done.12 = bf16[3,48,1024]{2,1,0:T(8,128)(2,1)S(1)} collective-permute-done((bf16[3,48,1024]{2,1,0:T(8,128)(2,1)S(1)}, bf16[3,48,1024]{2,1,0:T(8,128)(2,1)S(1)}, u32[]{:S(2)}, u32[]{:S(2)}) %collective-permute-start.12) | collective-permute-done | bytes 294944 | tf_op jit(solution)/shard_map/ppermute | solution.py:376
  131.4 2.2 %combine.3 = bf16[4,1,48,1024]{3,2,1,0:T(8,128)(2,1)S(1)} custom-call(bf16[16,16,2048]{2,1,0:T(8,128)(2,1)} %all-to-all-done.1.main_ref, bf16[16,56,2048]{2,1,0:T(8,128)(2,1)} %all-to-all-done.main_ref.last_ref, f32[4,2,96]{2,1,0:T(2,128)S(1)} %pad_maximum_fusion.6.gate_ref, s32[4,2,96]{2,1,0:T(2,128)S(1)} %pad_add_fusion.place_ref), custom_call_target="tpu_custom_call" | custom-call | tf_op jit(solution)/shard_map/combine/pallas_call | solution.py:201
  133.5 12.4 %all_to_all.30.back_ref = bf16[4,1,48,1024]{3,2,1,0:T(8,128)(2,1)S(1)} all-to-all(bf16[4,1,48,1024]{3,2,1,0:T(8,128)(2,1)S(1)} %combine.3), channel_id=1, replica_groups=mesh['pipe'=4,'expert'=16,'dp'=4] {'pipe'}, dimensions={0} | all-to-all | bytes 786432 | tf_op jit(solution)/shard_map/all_to_all | solution.py:436
  146.6 7.9 %all_to_all.31 = f32[4,1,1536]{2,1,0:T(1,128)S(1)} all-to-all(f32[4,1,1536]{2,1,0:T(1,128)S(1)} %reshape.63), channel_id=1, replica_groups=mesh['pipe'=4,'expert'=16,'dp'=4] {'pipe'}, dimensions={0} | all-to-all | bytes 49152 | tf_op jit(solution)/shard_map/all_to_all | solution.py:441
  166.6 8.0 %all-to-all-start.4 = ((bf16[64,8,128]{2,1,0:T(8,128)(2,1)}), bf16[64,8,128]{2,1,0:T(8,128)(2,1)S(1)}, u32[]{:S(2)}, u32[]{:S(2)}) async-start(bf16[64,8,128]{2,1,0:T(8,128)(2,1)} %get-tuple-element.38), calls=%async_computation.4 | async-start | bytes 262144 | tf_op jit(solution)/shard_map/all_to_all | solution.py:445
  176.2 9.8 %all-to-all-done.4 = bf16[64,8,128]{2,1,0:T(8,128)(2,1)S(1)} async-done(((bf16[64,8,128]{2,1,0:T(8,128)(2,1)}), bf16[64,8,128]{2,1,0:T(8,128)(2,1)S(1)}, u32[]{:S(2)}, u32[]{:S(2)}) %all-to-all-start.4) | async-done | bytes 131104 | tf_op jit(solution)/shard_map/all_to_all | solution.py:445
  186.7 4.6 %all-to-all-start.5 = ((bf16[64,8,128]{2,1,0:T(8,128)(2,1)}), bf16[64,8,128]{2,1,0:T(8,128)(2,1)S(1)}, u32[]{:S(2)}, u32[]{:S(2)}) async-start(bf16[64,8,128]{2,1,0:T(8,128)(2,1)} %broadcast_in_dim.26), calls=%async_computation.5 | async-start | bytes 262144 | tf_op jit(solution)/shard_map/all_to_all | solution.py:454
  193.1 9.7 %all-to-all-done.5 = bf16[64,8,128]{2,1,0:T(8,128)(2,1)S(1)} async-done(((bf16[64,8,128]{2,1,0:T(8,128)(2,1)}), bf16[64,8,128]{2,1,0:T(8,128)(2,1)S(1)}, u32[]{:S(2)}, u32[]{:S(2)}) %all-to-all-start.5) | async-done | bytes 131104 | tf_op jit(solution)/shard_map/all_to_all | solution.py:454
  (88 shorter events, 39.9 us)
Async XLA Ops:
  7.8 92.0 %all-to-all-start = ((bf16[16,56,2048]{2,1,0:T(8,128)(2,1)}), bf16[16,56,2048]{2,1,0:T(8,128)(2,1)}, u32[]{:S(2)}, u32[]{:S(2)}) async-start(bf16[16,56,2048]{2,1,0:T(8,128)(2,1)} %pack_slots.2), calls=%async_computation | async-start | bytes 7340032 | tf_op jit(solution)/shard_map/all_to_all | solution.py:397
  20.2 50.5 %collective-permute-start.2 = (bf16[2,4,48,1024]{3,2,1,0:T(8,128)(2,1)S(1)}, bf16[2,4,48,1024]{3,2,1,0:T(8,128)(2,1)S(1)}, u32[]{:S(2)}, u32[]{:S(2)}) collective-permute-start(bf16[2,4,48,1024]{3,2,1,0:T(8,128)(2,1)S(1)} %bitcast.105), channel_id=1, source_target_pairs={{0,64},{64,128},{128,192},{192,0},{1,65},{65,129},{129,193},{193,1... | collective-permute-start | bytes 2359304 | tf_op jit(solution)/shard_map/ppermute | solution.py:376
  22.1 48.6 %collective-permute-start.1 = (bf16[2,4,48,1024]{3,2,1,0:T(8,128)(2,1)S(1)}, bf16[2,4,48,1024]{3,2,1,0:T(8,128)(2,1)S(1)}, u32[]{:S(2)}, u32[]{:S(2)}) collective-permute-start(bf16[2,4,48,1024]{3,2,1,0:T(8,128)(2,1)S(1)} %bitcast.106), channel_id=1, source_target_pairs={{0,128},{64,192},{128,0},{192,64},{1,129},{65,193},{129,1},{193,65... | collective-permute-start | bytes 2359304 | tf_op jit(solution)/shard_map/ppermute | solution.py:376
  23.3 47.4 %collective-permute-start = (bf16[2,4,48,1024]{3,2,1,0:T(8,128)(2,1)S(1)}, bf16[2,4,48,1024]{3,2,1,0:T(8,128)(2,1)S(1)}, u32[]{:S(2)}, u32[]{:S(2)}) collective-permute-start(bf16[2,4,48,1024]{3,2,1,0:T(8,128)(2,1)S(1)} %bitcast.107), channel_id=1, source_target_pairs={{0,192},{64,0},{128,64},{192,128},{1,193},{65,1},{129,65},{193,129... | collective-permute-start | bytes 2359304 | tf_op jit(solution)/shard_map/ppermute | solution.py:376
  26.9 32.1 %collective-permute-start.8 = (f32[4,32,48]{2,1,0:T(8,128)S(1)}, f32[4,32,48]{2,1,0:T(8,128)S(1)}, u32[]{:S(2)}, u32[]{:S(2)}) collective-permute-start(f32[4,32,48]{2,1,0:T(8,128)S(1)} %get-tuple-element.24), channel_id=1, source_target_pairs={{0,64},{64,128},{128,192},{192,0},{1,65},{65,129},{129,193},{193,1... | collective-permute-start | bytes 73736 | tf_op jit(solution)/shard_map/ppermute | solution.py:376
  27.0 34.6 %collective-permute-start.7 = (f32[4,32,48]{2,1,0:T(8,128)S(1)}, f32[4,32,48]{2,1,0:T(8,128)S(1)}, u32[]{:S(2)}, u32[]{:S(2)}) collective-permute-start(f32[4,32,48]{2,1,0:T(8,128)S(1)} %get-tuple-element.24), channel_id=1, source_target_pairs={{0,128},{64,192},{128,0},{192,64},{1,129},{65,193},{129,1},{193,65... | collective-permute-start | bytes 73736 | tf_op jit(solution)/shard_map/ppermute | solution.py:376
  59.0 4.6 %collective-permute-start.6 = (f32[4,32,48]{2,1,0:T(8,128)S(1)}, f32[4,32,48]{2,1,0:T(8,128)S(1)}, u32[]{:S(2)}, u32[]{:S(2)}) collective-permute-start(f32[4,32,48]{2,1,0:T(8,128)S(1)} %get-tuple-element.24), channel_id=1, source_target_pairs={{0,192},{64,0},{128,64},{192,128},{1,193},{65,1},{129,65},{193,129... | collective-permute-start | bytes 73736 | tf_op jit(solution)/shard_map/ppermute | solution.py:376
  61.6 5.2 %collective-permute-start.5 = (bf16[16,1024]{1,0:T(8,128)(2,1)S(1)}, bf16[16,1024]{1,0:T(8,128)(2,1)S(1)}, u32[]{:S(2)}, u32[]{:S(2)}) collective-permute-start(bf16[16,1024]{1,0:T(8,128)(2,1)S(1)} %get-tuple-element.56), channel_id=1, source_target_pairs={{0,64},{64,128},{128,192},{192,0},{1,65},{65,129},{129,193},{193,1... | collective-permute-start | bytes 98312 | tf_op jit(solution)/shard_map/ppermute | solution.py:376
  63.5 5.4 %collective-permute-start.4 = (bf16[16,1024]{1,0:T(8,128)(2,1)S(1)}, bf16[16,1024]{1,0:T(8,128)(2,1)S(1)}, u32[]{:S(2)}, u32[]{:S(2)}) collective-permute-start(bf16[16,1024]{1,0:T(8,128)(2,1)S(1)} %get-tuple-element.57), channel_id=1, source_target_pairs={{0,128},{64,192},{128,0},{192,64},{1,129},{65,193},{129,1},{193,65... | collective-permute-start | bytes 98312 | tf_op jit(solution)/shard_map/ppermute | solution.py:376
  66.8 3.9 %collective-permute-start.3 = (bf16[16,1024]{1,0:T(8,128)(2,1)S(1)}, bf16[16,1024]{1,0:T(8,128)(2,1)S(1)}, u32[]{:S(2)}, u32[]{:S(2)}) collective-permute-start(bf16[16,1024]{1,0:T(8,128)(2,1)S(1)} %get-tuple-element.55), channel_id=1, source_target_pairs={{0,192},{64,0},{128,64},{192,128},{1,193},{65,1},{129,65},{193,129... | collective-permute-start | bytes 98312 | tf_op jit(solution)/shard_map/ppermute | solution.py:376
  73.3 7.3 %collective-permute-start.11 = (f32[4,24,48]{2,1,0:T(8,128)S(1)}, f32[4,24,48]{2,1,0:T(8,128)S(1)}, u32[]{:S(2)}, u32[]{:S(2)}) collective-permute-start(f32[4,24,48]{2,1,0:T(8,128)S(1)} %coupling.1), channel_id=1, source_target_pairs={{0,64},{64,128},{128,192},{192,0},{1,65},{65,129},{129,193},{193,1... | collective-permute-start | bytes 55304 | tf_op jit(solution)/shard_map/ppermute | solution.py:376
  73.7 6.9 %collective-permute-start.10 = (f32[4,24,48]{2,1,0:T(8,128)S(1)}, f32[4,24,48]{2,1,0:T(8,128)S(1)}, u32[]{:S(2)}, u32[]{:S(2)}) collective-permute-start(f32[4,24,48]{2,1,0:T(8,128)S(1)} %coupling.1), channel_id=1, source_target_pairs={{0,128},{64,192},{128,0},{192,64},{1,129},{65,193},{129,1},{193,65... | collective-permute-start | bytes 55304 | tf_op jit(solution)/shard_map/ppermute | solution.py:376
  76.5 4.1 %collective-permute-start.9 = (f32[4,24,48]{2,1,0:T(8,128)S(1)}, f32[4,24,48]{2,1,0:T(8,128)S(1)}, u32[]{:S(2)}, u32[]{:S(2)}) collective-permute-start(f32[4,24,48]{2,1,0:T(8,128)S(1)} %coupling.1), channel_id=1, source_target_pairs={{0,192},{64,0},{128,64},{192,128},{1,193},{65,1},{129,65},{193,129... | collective-permute-start | bytes 55304 | tf_op jit(solution)/shard_map/ppermute | solution.py:376
  99.9 31.5 %all-to-all-start.1 = ((bf16[16,16,2048]{2,1,0:T(8,128)(2,1)}), bf16[16,16,2048]{2,1,0:T(8,128)(2,1)}, u32[]{:S(2)}, u32[]{:S(2)}) async-start(bf16[16,16,2048]{2,1,0:T(8,128)(2,1)} %pack_slots.3), calls=%async_computation.1 | async-start | bytes 2097152 | tf_op jit(solution)/shard_map/all_to_all | solution.py:431
  109.9 17.9 %copy-start = (bf16[4,48,4096]{2,1,0:T(8,128)(2,1)S(1)}, bf16[4,48,4096]{2,1,0:T(8,128)(2,1)}, u32[]{:S(2)}) copy-start(bf16[4,48,4096]{2,1,0:T(8,128)(2,1)} %up_ref.7) | copy-start | bytes 4718596
  110.0 9.9 %collective-permute-start.14 = (bf16[3,48,1024]{2,1,0:T(8,128)(2,1)S(1)}, bf16[3,48,1024]{2,1,0:T(8,128)(2,1)S(1)}, u32[]{:S(2)}, u32[]{:S(2)}) collective-permute-start(bf16[3,48,1024]{2,1,0:T(8,128)(2,1)S(1)} %get-tuple-element.51), channel_id=1, source_target_pairs={{0,64},{64,128},{128,192},{192,0},{1,65},{65,129},{129,193},{193,1... | collective-permute-start | bytes 884744 | tf_op jit(solution)/shard_map/ppermute | solution.py:376
  111.6 11.4 %collective-permute-start.13 = (bf16[3,48,1024]{2,1,0:T(8,128)(2,1)S(1)}, bf16[3,48,1024]{2,1,0:T(8,128)(2,1)S(1)}, u32[]{:S(2)}, u32[]{:S(2)}) collective-permute-start(bf16[3,48,1024]{2,1,0:T(8,128)(2,1)S(1)} %get-tuple-element.52), channel_id=1, source_target_pairs={{0,128},{64,192},{128,0},{192,64},{1,129},{65,193},{129,1},{193,65... | collective-permute-start | bytes 884744 | tf_op jit(solution)/shard_map/ppermute | solution.py:376
  112.5 15.2 %collective-permute-start.12 = (bf16[3,48,1024]{2,1,0:T(8,128)(2,1)S(1)}, bf16[3,48,1024]{2,1,0:T(8,128)(2,1)S(1)}, u32[]{:S(2)}, u32[]{:S(2)}) collective-permute-start(bf16[3,48,1024]{2,1,0:T(8,128)(2,1)S(1)} %get-tuple-element.53), channel_id=1, source_target_pairs={{0,192},{64,0},{128,64},{192,128},{1,193},{65,1},{129,65},{193,129... | collective-permute-start | bytes 884744 | tf_op jit(solution)/shard_map/ppermute | solution.py:376
  131.3 14.6 %copy-start.1 = (bf16[4,48,4096]{2,1,0:T(8,128)(2,1)S(1)}, bf16[4,48,4096]{2,1,0:T(8,128)(2,1)}, u32[]{:S(2)}) copy-start(bf16[4,48,4096]{2,1,0:T(8,128)(2,1)} %up_ref.7) | copy-start | bytes 4718596
  164.6 21.4 %collective-permute-start.15 = (bf16[4,48,1024]{2,1,0:T(8,128)(2,1)}, bf16[4,48,1024]{2,1,0:T(8,128)(2,1)S(1)}, u32[]{:S(2)}, u32[]{:S(2)}) collective-permute-start(bf16[4,48,1024]{2,1,0:T(8,128)(2,1)} %get-tuple-element.48), channel_id=1, source_target_pairs={{0,64},{64,128},{128,192},{192,0},{1,65},{65,129},{129,193},{193,1... | collective-permute-start | bytes 1179656 | tf_op jit(solution)/shard_map/ppermute | solution.py:376
  165.1 20.9 %collective-permute-start.16 = (bf16[4,48,1024]{2,1,0:T(8,128)(2,1)}, bf16[4,48,1024]{2,1,0:T(8,128)(2,1)S(1)}, u32[]{:S(2)}, u32[]{:S(2)}) collective-permute-start(bf16[4,48,1024]{2,1,0:T(8,128)(2,1)} %get-tuple-element.49), channel_id=1, source_target_pairs={{0,192},{64,0},{128,64},{192,128},{1,193},{65,1},{129,65},{193,129... | collective-permute-start | bytes 1179656 | tf_op jit(solution)/shard_map/ppermute | solution.py:376
  166.6 19.3 %all-to-all-start.4 = ((bf16[64,8,128]{2,1,0:T(8,128)(2,1)}), bf16[64,8,128]{2,1,0:T(8,128)(2,1)S(1)}, u32[]{:S(2)}, u32[]{:S(2)}) async-start(bf16[64,8,128]{2,1,0:T(8,128)(2,1)} %get-tuple-element.38), calls=%async_computation.4 | async-start | bytes 262144 | tf_op jit(solution)/shard_map/all_to_all | solution.py:445
  174.6 16.8 %collective-permute-start.17 = (bf16[4,48,1024]{2,1,0:T(8,128)(2,1)S(1)}, bf16[4,48,1024]{2,1,0:T(8,128)(2,1)S(1)}, u32[]{:S(2)}, u32[]{:S(2)}) collective-permute-start(bf16[4,48,1024]{2,1,0:T(8,128)(2,1)S(1)} %get-tuple-element.46), channel_id=1, source_target_pairs={{0,128},{64,192},{128,0},{192,64},{1,129},{65,193},{129,1},{193,65... | collective-permute-start | bytes 1179656 | tf_op jit(solution)/shard_map/ppermute | solution.py:376
  186.7 16.0 %all-to-all-start.5 = ((bf16[64,8,128]{2,1,0:T(8,128)(2,1)}), bf16[64,8,128]{2,1,0:T(8,128)(2,1)S(1)}, u32[]{:S(2)}, u32[]{:S(2)}) async-start(bf16[64,8,128]{2,1,0:T(8,128)(2,1)} %broadcast_in_dim.26), calls=%async_computation.5 | async-start | bytes 262144 | tf_op jit(solution)/shard_map/all_to_all | solution.py:454
  (13 other events, 44.8 us)

commit v3 on v1

v3 whole, which is shorter than its diff:
```python
import functools

import jax
import jax.numpy as jnp
from jax import lax
from jax.experimental import pallas as pl
from jax.experimental.pallas import tpu as pltpu
from jax.sharding import PartitionSpec as P

F32 = jnp.float32
BF16 = jnp.bfloat16
NT = (((1,), (1,)), ((), ()))
TN = (((0,), (0,)), ((), ()))

TILE = 8


def params(mib):
    return pltpu.CompilerParams(vmem_limit_bytes=mib << 20)


def in_hbm(array):
    return pltpu.with_memory_space_constraint(array, pltpu.MemorySpace.HBM)


def iotas(shape):
    return [lax.broadcasted_iota(jnp.int32, shape, d) for d in range(2)]


def swap_matrix(slots, dests):
    out_row, in_row = iotas((slots * dests, slots * dests))
    return (in_row == (out_row % slots) * dests + out_row // slots).astype(BF16)


def lead_pack_kernel(grads_ref, out_ref):
    _, slots, dests, width = grads_ref.shape
    half = width // 2
    swap = swap_matrix(slots, dests)
    for h in range(2):
        rows = grads_ref[0, :, :, h * half : (h + 1) * half].reshape(slots * dests, half)
        moved = jnp.dot(swap, rows, preferred_element_type=F32)
        out_ref[:, h * slots : (h + 1) * slots, :] = moved.reshape(dests, slots, half).astype(BF16)


def lead_pack(grads, count):
    _, _, dests, width = grads.shape
    half = width // 2
    return pl.pallas_call(
        lead_pack_kernel,
        grid=(count,),
        in_specs=[pl.BlockSpec((1, TILE, dests, width), lambda m: (m, 0, 0, 0))],
        out_specs=pl.BlockSpec((dests, 2 * TILE, half), lambda m: (0, m, 0)),
        out_shape=pltpu.HBM((dests, 2 * TILE * count, half), BF16),
        compiler_params=params(40),
        name="lead_pack",
    )(grads)


def tail_pack_kernel(*refs):
    out_ref = refs[-1]
    kept, dests, quarter = refs[0].shape
    micro = kept - TILE
    swap = swap_matrix(TILE, dests)
    out_row, in_row = iotas((2 * micro * dests, micro * dests))
    within = out_row % (2 * micro)
    source = (within % micro) * dests + out_row // (2 * micro)
    for c in range(2):
        total = jnp.zeros((2 * micro * dests, quarter), F32)
        columns = slice(c * quarter, (c + 1) * quarter)
        for h in range(2):
            ref = refs[2 * h + c]
            moved = jnp.dot(swap, ref[:TILE].reshape(TILE * dests, quarter), preferred_element_type=F32)
            moved = moved.reshape(dests, TILE, quarter).astype(BF16)
            out_ref[:, h * TILE : (h + 1) * TILE, columns] = moved
            pick = ((in_row == source) & (within // micro == h)).astype(BF16)
            rows = ref[TILE:].reshape(micro * dests, quarter)
            total = total + jnp.dot(pick, rows, preferred_element_type=F32)
        out_ref[:, 2 * TILE :, columns] = total.reshape(dests, 2 * micro, quarter).astype(BF16)


def tail_pack(blocks):
    kept, dests, quarter = blocks[0].shape
    return pl.pallas_call(
        tail_pack_kernel,
        out_shape=jax.ShapeDtypeStruct((dests, 2 * TILE + 2 * (kept - TILE), 2 * quarter), BF16),
        compiler_params=params(40),
        name="tail_pack",
    )(*blocks)


def gate_kernel(normed_ref, w_ref, routes_ref, info_ref):
    m = pl.program_id(0)
    logits = lax.dot_general(w_ref[...], normed_ref[0], NT, preferred_element_type=F32)
    experts, rows = logits.shape
    expl = jnp.exp(logits)
    probs = expl / jnp.sum(expl, axis=0, keepdims=True)
    ids = lax.broadcasted_iota(jnp.int32, (experts, rows), 0)
    first, second = iotas((rows, rows))
    earlier = (first < second).astype(BF16)
    named = [ids == routes_ref[0, k : k + 1, :] for k in range(2)]
    both = jnp.where(named[0] | named[1], 1.0, 0.0).astype(BF16)
    before = jnp.dot(both, earlier, preferred_element_type=F32)
    found = []
    gates = []
    places = []
    for k in range(2):
        gate = jnp.sum(jnp.where(named[k], probs, 0.0), axis=0, keepdims=True)
        found.append(gate * (jnp.where(named[k], 1.0, 0.0) - probs))
        gates.append(gate)
        slot = jnp.sum(jnp.where(named[k], before, 0.0), axis=0, keepdims=True).astype(jnp.int32)
        start = routes_ref[0, k : k + 1, :] * TILE
        place = jnp.where(slot < TILE, start + slot, experts * TILE + start + m)
        places.append(place.astype(F32))
    found.append(jnp.concatenate(gates + places + [jnp.zeros((4, rows), F32)], axis=0))
    info = jnp.concatenate(found, axis=0)
    info_ref[0, :, :rows] = info
    info_ref[0, :, rows:] = info


def gate_info(normed, w, routes):
    micro, rows, width = normed.shape
    experts = w.shape[0]
    height = 2 * experts + 8
    return pl.pallas_call(
        gate_kernel,
        grid=(micro,),
        in_specs=[
            pl.BlockSpec((1, rows, width), lambda m: (m, 0, 0)),
            pl.BlockSpec((experts, width), lambda m: (0, 0)),
            pl.BlockSpec((1, 2, rows), lambda m: (m, 0, 0)),
        ],
        out_specs=pl.BlockSpec((1, height, 2 * rows), lambda m: (m, 0, 0)),
        out_shape=jax.ShapeDtypeStruct((micro, height, 2 * rows), F32),
        compiler_params=params(32),
        name="gates",
    )(normed, w, routes)


def pairs(sections):
    found = []
    for s in range(sections - 1):
        for k in range(2):
            for upper in range(s + 1, sections):
                for k2 in range(2):
                    found.append((s, k, upper, k2))
    return {key: row for row, key in enumerate(found)}


def couple_kernel(p_ref, saved_ref, w_ref, info_ref, out_ref):
    p = p_ref[0]
    sections, experts, _ = w_ref.shape
    rows = saved_ref.shape[3]
    table = pairs(sections)
    for s in range(sections - 1):
        j = (s - p) & (sections - 1)
        for k in range(2):
            saved = saved_ref[j, k, 0]
            for upper in range(s + 1, sections):
                j2 = (upper - p) & (sections - 1)
                part = lax.dot_general(w_ref[j2], saved, NT, preferred_element_type=F32)
                for k2 in range(2):
                    row = table[(s, k, upper, k2)]
                    v = info_ref[j2, 0, k2 * experts : (k2 + 1) * experts, :rows]
                    out_ref[0, row : row + 1, :] = jnp.sum(part * v, axis=0, keepdims=True)


def coupling(p, saved, w, info):
    sections, _, micro, rows, quarter = saved.shape
    experts = w.shape[1]
    n = len(pairs(sections))
    return pl.pallas_call(
        couple_kernel,
        grid_spec=pltpu.PrefetchScalarGridSpec(
            num_scalar_prefetch=1,
            grid=(micro,),
            in_specs=[
                pl.BlockSpec((sections, 2, 1, rows, quarter), lambda m, p: (0, 0, m, 0, 0)),
                pl.BlockSpec((sections, experts, quarter), lambda m, p: (0, 0, 0)),
                pl.BlockSpec((sections, 1) + info.shape[2:], lambda m, p: (0, m, 0, 0)),
            ],
            out_specs=pl.BlockSpec((1, n, rows), lambda m, p: (m, 0, 0)),
        ),
        out_shape=jax.ShapeDtypeStruct((micro, n, rows), F32),
        compiler_params=params(32),
        name="coupling",
    )(p, saved, w, info)


def picked(info, experts, rows, value, first, received):
    n = received.shape[0]
    index = lax.broadcasted_iota(jnp.int32, (n, 2 * rows), 0)
    pick = jnp.zeros((n, 2 * rows), F32)
    for k in range(2):
        gate = info[2 * experts + k : 2 * experts + k + 1, :]
        place = info[2 * experts + 2 + k : 2 * experts + 3 + k, :].astype(jnp.int32)
        inside = (place >= first) & (place < first + n)
        row = jnp.where(inside, place - first + value, -1)
        pick = pick + jnp.where(index == row, gate, 0.0)
    high = pick.astype(BF16).astype(F32)
    is_low = lax.broadcasted_iota(jnp.int32, (n, 2 * rows), 1) >= rows
    pick = jnp.where(is_low, pick - high, high).astype(BF16)
    both = lax.dot_general(pick, received, TN, preferred_element_type=F32)
    return both[:rows] + both[rows:]


def lead_kernel(experts, main_ref, info_ref, out_ref):
    half = main_ref.shape[2]
    rows = info_ref.shape[2] // 2
    received = main_ref[...].reshape(experts * TILE, half)
    total = picked(info_ref[0], experts, rows, 0, 0, received).astype(BF16)
    out_ref[0, 0] = total[:, : half // 2]
    out_ref[1, 0] = total[:, half // 2 :]


def lead_combine(received, info):
    experts, packed, half = received.shape
    count = packed // (2 * TILE)
    rows = info.shape[2] // 2
    return pl.pallas_call(
        functools.partial(lead_kernel, experts),
        grid=(2, count),
        in_specs=[
            pl.BlockSpec((experts, TILE, half), lambda h, m: (0, 2 * m + h, 0)),
            pl.BlockSpec((1,) + info.shape[1:], lambda h, m: (m, 0, 0)),
        ],
        out_specs=pl.BlockSpec((2, 1, rows, half // 2), lambda h, m: (h, m, 0, 0)),
        out_shape=jax.ShapeDtypeStruct((4, count, rows, half // 2), BF16),
        compiler_params=params(40),
        name="lead_combine",
    )(received, info)


def tail_kernel(
    p_ref, received_ref, info_ref, up_ref, lead_ref, saved_ref, back_ref, dots_ref, last_ref, sum_ref
):
    m = pl.program_id(0)
    micro = pl.num_programs(0)
    p = p_ref[0]
    experts, _, half = received_ref.shape
    sections, _, rows, quarter = sum_ref.shape[:1] + (1,) + sum_ref.shape[1:]
    n = experts * TILE

    @pl.when(m == 0)
    def _():
        last_ref[...] = received_ref[:, 2 * TILE :, :].reshape(n, half)

    for j in range(sections):
        h, c = divmod(j, 2)
        columns = slice(c * quarter, (c + 1) * quarter)
        info = info_ref[j, 0]
        extra = picked(info, experts, rows, h * (TILE // 2), n, last_ref[:, columns])

        @pl.when(m < micro - 1)
        def _():
            sum_ref[j] = extra + lead_ref[j, 0].astype(F32)

        @pl.when(m == micro - 1)
        def _():
            main = received_ref[:, h * TILE : (h + 1) * TILE, columns].reshape(n, quarter)
            sum_ref[j] = extra + picked(info, experts, rows, 0, 0, main)

        back_ref[j, 0] = sum_ref[j].astype(BF16)

    base = up_ref[0].astype(F32)
    ones = jnp.ones((8, 128), F32)
    found = {}
    for s in reversed(range(sections)):
        j = (s - p) & (sections - 1)
        for k in range(2):
            product = base * saved_ref[j, k, 0].astype(F32)
            lane = product[:, :128]
            for c in range(1, quarter // 128):
                lane = lane + product[:, c * 128 : (c + 1) * 128]
            row = lax.dot_general(
                ones, lane, NT, precision=lax.Precision.HIGHEST, preferred_element_type=F32
            )
            found[2 * s + k] = row[:1]
        if s > 0:
            base = base + sum_ref[j]
    dots = jnp.concatenate([found[i] for i in range(2 * sections)], axis=0)
    for dest in range(sections):
        dots_ref[dest, 0, :, :rows] = dots


def tail_combine(p, received, info, upstream, lead, saved):
    sections, _, micro, rows, quarter = saved.shape
    experts, packed, half = received.shape
    last_lead = lead.shape[1] - 1
    part = (sections, 1, rows, quarter)
    return pl.pallas_call(
        tail_kernel,
        grid_spec=pltpu.PrefetchScalarGridSpec(
            num_scalar_prefetch=1,
            grid=(micro,),
            in_specs=[
                pl.BlockSpec((experts, packed, half), lambda m, p: (0, 0, 0)),
                pl.BlockSpec((sections, 1) + info.shape[2:], lambda m, p: (0, m, 0, 0)),
                pl.BlockSpec((1, rows, quarter), lambda m, p: (m, 0, p[0])),
                pl.BlockSpec(part, lambda m, p: (0, jnp.minimum(m, last_lead), 0, 0)),
                pl.BlockSpec((sections, 2, 1, rows, quarter), lambda m, p: (0, 0, m, 0, 0)),
            ],
            out_specs=[
                pl.BlockSpec(part, lambda m, p: (0, m, 0, 0)),
                pl.BlockSpec((sections, 1, 2 * sections, 128), lambda m, p: (0, m, 0, 0)),
            ],
            scratch_shapes=[
                pltpu.VMEM((experts * TILE, half), BF16),
                pltpu.VMEM((sections, rows, quarter), F32),
            ],
        ),
        out_shape=[
            jax.ShapeDtypeStruct((sections, micro, rows, quarter), BF16),
            jax.ShapeDtypeStruct((sections, micro, 2 * sections, 128), F32),
        ],
        compiler_params=params(48),
        name="tail_combine",
    )(p, received, info, upstream, lead, saved)


def dense_kernel(p_ref, dots_ref, couple_ref, info_ref, normed_ref, dense_ref, part_ref, total_ref):
    m = pl.program_id(0)
    micro = pl.num_programs(0)
    p = p_ref[0]
    sections = dots_ref.shape[0]
    rows = normed_ref.shape[1]
    experts, width = total_ref.shape
    table = pairs(sections)
    given = dots_ref[0, 0, :, :rows]
    for source in range(1, sections):
        given = given + dots_ref[source, 0, :, :rows]
    links = couple_ref[0]
    dots = {}
    own = jnp.zeros((experts, rows), F32)
    for s in reversed(range(sections)):
        j = (s - p) & (sections - 1)
        dense = jnp.zeros((experts, rows), F32)
        for k in range(2):
            value = given[2 * s + k : 2 * s + k + 1, :]
            for upper in range(s + 1, sections):
                for k2 in range(2):
                    row = table[(s, k, upper, k2)]
                    value = value + links[row : row + 1, :] * dots[(upper, k2)]
            dots[(s, k)] = value
            dense = dense + value * info_ref[j, 0, k * experts : (k + 1) * experts, :rows]
        dense_ref[0, s * experts : (s + 1) * experts, :] = dense.astype(BF16)
        own = jnp.where(p == s, dense, own)
    part = jnp.dot(own.astype(BF16), normed_ref[0], preferred_element_type=F32)

    @pl.when(m == 0)
    def _():
        total_ref[...] = part

    @pl.when(m > 0)
    def _():
        total_ref[...] += part

    @pl.when(m == micro - 1)
    def _():
        total = total_ref[...] * (1.0 / micro)
        cols = width // 128
        for r in range(experts // 8):
            for c in range(cols):
                tile = total[r * 8 : (r + 1) * 8, c * 128 : (c + 1) * 128]
                part_ref[r * cols + c] = tile.astype(BF16)


def dense_terms(p, dots, links, info, normed):
    sections, micro = dots.shape[:2]
    _, rows, width = normed.shape
    experts = (info.shape[2] - 8) // 2
    blocks = experts // 8 * (width // 128)
    return pl.pallas_call(
        dense_kernel,
        grid_spec=pltpu.PrefetchScalarGridSpec(
            num_scalar_prefetch=1,
            grid=(micro,),
            in_specs=[
                pl.BlockSpec((sections, 1) + dots.shape[2:], lambda m, p: (0, m, 0, 0)),
                pl.BlockSpec((1,) + links.shape[1:], lambda m, p: (m, 0, 0)),
                pl.BlockSpec((sections, 1) + info.shape[2:], lambda m, p: (0, m, 0, 0)),
                pl.BlockSpec((1, rows, width), lambda m, p: (m, 0, 0)),
            ],
            out_specs=[
                pl.BlockSpec((1, sections * experts, rows), lambda m, p: (m, 0, 0)),
                pl.BlockSpec((blocks, 8, 128), lambda m, p: (0, 0, 0)),
            ],
            scratch_shapes=[pltpu.VMEM((experts, width), F32)],
        ),
        out_shape=[
            jax.ShapeDtypeStruct((micro, sections * experts, rows), BF16),
            jax.ShapeDtypeStruct((blocks, 8, 128), BF16),
        ],
        compiler_params=params(32),
        name="dense",
    )(p, dots, links, info, normed)


def grads_kernel(p_ref, up_ref, back_ref, dense_ref, w_ref, *refs):
    p = p_ref[0]
    total_ref = refs[-1]
    sections = back_ref.shape[0]
    experts = w_ref.shape[1]
    total = up_ref[0].astype(F32)
    for s in reversed(range(sections)):
        j = (s - p) & (sections - 1)
        dense = dense_ref[0, s * experts : (s + 1) * experts, :]
        term = lax.dot_general(dense, w_ref[j], TN, preferred_element_type=F32)
        total = total + back_ref[j, 0].astype(F32) + term
        total_ref[j] = total.astype(BF16)
    for j in range(sections):
        refs[j][0] = total_ref[j]


def grads_of(p, upstream, back, dense, w):
    sections, micro, rows, quarter = back.shape
    experts = w.shape[1]
    return pl.pallas_call(
        grads_kernel,
        grid_spec=pltpu.PrefetchScalarGridSpec(
            num_scalar_prefetch=1,
            grid=(micro,),
            in_specs=[
                pl.BlockSpec((1, rows, quarter), lambda m, p: (m, 0, p[0])),
                pl.BlockSpec((sections, 1, rows, quarter), lambda m, p: (0, m, 0, 0)),
                pl.BlockSpec((1, sections * experts, rows), lambda m, p: (m, 0, 0)),
                pl.BlockSpec((sections, experts, quarter), lambda m, p: (0, 0, 0)),
            ],
            out_specs=[pl.BlockSpec((1, rows, quarter), lambda m, p: (m, 0, 0))] * sections,
            scratch_shapes=[pltpu.VMEM((sections, rows, quarter), BF16)],
        ),
        out_shape=[jax.ShapeDtypeStruct((micro, rows, quarter), BF16)] * sections,
        compiler_params=params(32),
        name="grads",
    )(p, upstream, back, dense, w)


def join_kernel(p_ref, *refs):
    step = pl.program_id(0)
    out_ref = refs[-1]
    for d in range(len(refs) - 1):

        @pl.when(step == d)
        def _():
            out_ref[...] = refs[d][...]


def join(p, blocks):
    n = len(blocks)
    micro, rows, quarter = blocks[0].shape
    return pl.pallas_call(
        join_kernel,
        grid_spec=pltpu.PrefetchScalarGridSpec(
            num_scalar_prefetch=1,
            grid=(n,),
            in_specs=[pl.BlockSpec((micro, rows, quarter), lambda d, p: (0, 0, 0))] * n,
            out_specs=pl.BlockSpec((micro, rows, quarter), lambda d, p: (0, 0, (p[0] - d) & (n - 1))),
        ),
        out_shape=jax.ShapeDtypeStruct((micro, rows, n * quarter), BF16),
        compiler_params=params(32),
        name="join",
    )(p, *blocks)


def turned(block, distance):
    n = lax.axis_size("pipe")
    return lax.ppermute(block, "pipe", [(i, (i + distance) % n) for i in range(n)])


def gathered(block):
    n = lax.axis_size("pipe")
    return [block] + [turned(block, n - j) for j in range(1, n)]


def on_device(normed, saved_out, expert_grads, routes, router_weight, upstream):
    sections = lax.axis_size("pipe")
    section = lax.axis_index("pipe")
    p = section.astype(jnp.int32).reshape(1)
    normed = in_hbm(normed[0])
    upstream = in_hbm(upstream)
    micro, rows, width = normed.shape
    quarter = width // sections
    w = router_weight[0].T
    experts = w.shape[0]

    def spread(array, axis):
        blocks = []
        for j in range(sections):
            start = ((section - j) % sections) * quarter
            block = lax.dynamic_slice_in_dim(array, start, quarter, axis)
            blocks.append(turned(block, sections - j) if j else block)
        return blocks

    grads = jnp.transpose(expert_grads[0, :, 0, 0], (0, 2, 1, 3))
    lead = lax.all_to_all(lead_pack(in_hbm(grads), micro - 1), "expert", 0, 0, tiled=True)
    late = spread(jnp.concatenate([grads[micro - 1, :TILE], grads[:, TILE]]), 2)
    info = gate_info(normed, w, jnp.transpose(routes[0], (0, 2, 1)))
    tail_send = tail_pack(late)
    saved_out, tail_send = lax.optimization_barrier((saved_out, tail_send))

    info_all = jnp.stack(gathered(info))
    w_all = jnp.stack(spread(w, 1))
    saved = spread(jnp.transpose(saved_out[0], (2, 0, 1, 3)), 3)
    lead, tail_send, saved[1], saved[2], w_all, info_all = lax.optimization_barrier(
        (lead, tail_send, saved[1], saved[2], w_all, info_all)
    )
    saved_all = jnp.stack(saved)
    links = sum(gathered(coupling(p, saved_all, w_all, info_all)))

    tail = lax.all_to_all(tail_send, "expert", 0, 0, tiled=True)
    back = lead_combine(lead, info)

    def back_for(distance):
        return lax.dynamic_index_in_dim(back, (section + distance) % sections, 0, False)

    lead = jnp.stack(
        [turned(back_for(sections - j), sections - j) if j else back_for(0) for j in range(sections)]
    )
    lead, info_all, w_all, saved_all, links = lax.optimization_barrier(
        (lead, info_all, w_all, saved_all, links)
    )
    back, dots = tail_combine(p, tail, info_all, upstream, lead, saved_all)
    dots = lax.all_to_all(dots, "pipe", 0, 0, tiled=True)
    dense, part = dense_terms(p, dots, links, info_all, normed)

    axes = ("expert", "dp")
    part = lax.all_to_all(part, axes, 0, 0, tiled=True)
    outs = grads_of(p, upstream, back, dense, w_all)
    blocks = [turned(outs[d], d) if d else outs[0] for d in range(sections)]
    total = jnp.sum(part.astype(F32), axis=0, keepdims=True).astype(BF16)
    part = lax.all_to_all(jnp.broadcast_to(total, part.shape), axes, 0, 0, tiled=True)
    cols = width // 128
    router_grad = part.astype(F32).reshape(experts // 8, cols, 8, 128).transpose(0, 2, 1, 3)
    router_grad = router_grad.reshape(experts, width).T
    grad_input = join(p, blocks)
    return (grad_input[None], router_grad[None])


def solution(mesh):
    in_specs = (
        P("pipe", None, ("expert", "dp"), None),
        P("pipe", None, ("expert", "dp"), None, None),
        P("pipe", None, "dp", "expert", None, None, None),
        P("pipe", None, ("expert", "dp"), None),
        P("pipe", None, None),
        P(None, ("expert", "dp"), None),
    )
    out_specs = (P("pipe", None, ("expert", "dp"), None), P("pipe", None, None))
    return jax.shard_map(
        on_device, mesh=mesh, in_specs=in_specs, out_specs=out_specs, check_vma=False
    )
```

time: 284 us -> 211 us (0.74)
  waiting for transfers between devices: 181 us -> 76.6 us
  starting transfers between devices: 55.7 us -> 68.6 us
  blocking collectives: 0 us -> 9.72 us
  Pallas kernels: 24.4 us -> 31 us
    all_to_all x3, waiting for transfers between devices: 107 us -> 4.39 us  [the longest x1 4.38 us: on_device(): lax.all_to_all(jnp.broadcast_to(total, part.shape), axes, 0, 0, tiled=True)]
    ppermute x15 -> x21, starting transfers between devices: 25.3 us -> 35.5 us  [turned(): lax.ppermute(block, 'pipe', [(i, (i + distance) % n) for i in range(n)])]
    all_to_all x0 -> x1, blocking collectives: none -> 9.72 us  [on_device(): dots = lax.all_to_all(dots, 'pipe', 0, 0, tiled=True)]
    pallas_call x5 -> x6, Pallas kernels: 16.9 us -> 23.6 us  [the longest x1 9.13 us: tail_combine(): pl.pallas_call(tail_kernel, grid_spec=pltpu.PrefetchScalarGridSpec(num_sc...]
    all_to_all x2 -> x1, waiting for transfers between devices: 9.75 us -> 3.31 us  [on_device(): part = lax.all_to_all(part, axes, 0, 0, tiled=True)]
    all_to_all x3, starting transfers between devices: 17.4 us -> 22.5 us  [the longest x1 8.57 us: on_device(): lax.all_to_all(lead_pack(in_hbm(grads), micro - 1), 'expert', 0, 0, tiled...]
    ppermute x15 -> x21, waiting for transfers between devices: 64.3 us -> 68.9 us  [turned(): lax.ppermute(block, 'pipe', [(i, (i + distance) % n) for i in range(n)])]
    another operation x6, local copies, waits for them, and re-layouts: 4.39 us -> 8.04 us
  transfers between devices with their start and end apart: 20 -> 25, of which waited for: 10 -> 13; matrix products, arithmetic and copies ran while one was open for 2% -> 9% of each run, Pallas kernels for 4% -> 6%
where the time goes in v3:
time: 211 us; the launch traced here: 210 us
  waiting for transfers between devices  76.6 us (36%)
  starting transfers between devices  68.6 us (33%)
  Pallas kernels  31 us (15%)
  local copies, waits for them, and re-layouts  18.4 us (9%)
  blocking collectives  9.72 us (5%)
  other arithmetic  4.33 us (2%)
    ppermute x21, waiting for transfers between devices, turned(): lax.ppermute(block, 'pipe', [(i, (i + distance) % n) for i in range(n)])  68.9 us
    ppermute x21, starting transfers between devices, turned(): lax.ppermute(block, 'pipe', [(i, (i + distance) % n) for i in range(n)])  35.5 us
    all_to_all x1, starting transfers between devices, on_device(): part = lax.all_to_all(part, axes, 0, 0, tiled=True)  10.6 us
    all_to_all x1, blocking collectives, on_device(): dots = lax.all_to_all(dots, 'pipe', 0, 0, tiled=True)  9.72 us
    pallas_call x1, Pallas kernels, tail_combine(): pl.pallas_call(tail_kernel, grid_spec=pltpu.PrefetchScalarGridSpec(num_sc...  9.13 us
    all_to_all x1, starting transfers between devices, on_device(): lax.all_to_all(lead_pack(in_hbm(grads), micro - 1), 'expert', 0, 0, tiled...  8.57 us
    another operation x5, local copies, waits for them, and re-layouts  8.02 us
    unnamed x17, local copies, waits for them, and re-layouts  7.14 us
  transfers between devices with their start and end apart: 25, of which 13 were waited for; matrix products, arithmetic and copies ran while one was open for 9% of the time, Pallas kernels for 6%

profile of v3, /device:TPU:8, one launch (start us, length us, event | category | flops | bytes accessed | tf_op | source)
XLA Modules:
  0.0 209.6 jit_solution(6643408237687677230)
XLA Ops:
  0.6 5.1 %lead_pack.1 = bf16[16,48,2048]{2,1,0:T(8,128)(2,1)} custom-call(bf16[4,9,16,4096]{3,2,1,0:T(8,128)(2,1)} %bitcast.91), custom_call_target="tpu_custom_call" | custom-call | tf_op jit(solution)/shard_map/lead_pack/pallas_call | solution.py:48
  5.7 8.6 %all-to-all-start = ((bf16[16,48,2048]{2,1,0:T(8,128)(2,1)}), bf16[16,48,2048]{2,1,0:T(8,128)(2,1)S(1)}, u32[]{:S(2)}, u32[]{:S(2)}) async-start(bf16[16,48,2048]{2,1,0:T(8,128)(2,1)} %lead_pack.1), calls=%async_computation | async-start | bytes 6291456 | tf_op jit(solution)/shard_map/all_to_all | solution.py:494
  14.3 5.0 %copy.20 = bf16[1,4,1,1,16,9,4096]{6,4,1,5,3,2,0:T(8,128)(2,1)} copy(bf16[1,4,1,1,16,9,4096]{6,4,5,3,2,1,0:T(8,128)(2,1)} %param.8) | data formatting | bytes 9437184 | tf_op args[2]
  27.0 6.5 %collective-permute-done.refs_1_ = bf16[12,16,1024]{2,1,0:T(8,128)(2,1)S(1)} collective-permute-done((bf16[12,16,1024]{2,1,0:T(8,128)(2,1)S(1)}, bf16[12,16,1024]{2,1,0:T(8,128)(2,1)S(1)}, u32[]{:S(2)}, u32[]{:S(2)}) %collective-permute-start) | collective-permute-done | bytes 393248 | tf_op jit(solution)/shard_map/ppermute | solution.py:466
  33.4 9.4 %collective-permute-done.1.refs_2_ = bf16[12,16,1024]{2,1,0:T(8,128)(2,1)S(1)} collective-permute-done((bf16[12,16,1024]{2,1,0:T(8,128)(2,1)S(1)}, bf16[12,16,1024]{2,1,0:T(8,128)(2,1)S(1)}, u32[]{:S(2)}, u32[]{:S(2)}) %collective-permute-start.1) | collective-permute-done | bytes 393248 | tf_op jit(solution)/shard_map/ppermute | solution.py:466
  45.6 4.0 %constant_dynamic-slice_fusion.1 = (bf16[1,4,48,2,1024]{4,3,2,1,0:T(2,128)(2,1)}, bf16[1,4,48,2,1024]{4,3,2,1,0:T(2,128)(2,1)}, bf16[1,4,48,2,1024]{4,3,2,1,0:T(2,128)(2,1)S(1)}, bf16[1,4,48,2,1024]{4,3,2,1,0:T(2,128)(2,1)S(1)}) fusion(bf16[1,4,48,2,4096]{4,3,2,1,0:T(2,128)(2,1)S(1)} %copy-done.5, s32[]{:T(128)S(6)} %select_n.83, s32[]{:T(128)S(6)} %select_n.89, ...), kind=kLoop, calls=%fused_computation.33 | loop fusion | bytes 6291472 | tf_op jit(solution)/shard_map/dynamic-slice.14
  59.3 3.0 %gates.1.info_ref = f32[4,40,96]{2,1,0:T(8,128)S(1)} custom-call(bf16[4,48,4096]{2,1,0:T(8,128)(2,1)} %bitcast.94, bf16[16,4096]{1,0:T(8,128)(2,1)S(1)} %bitcast.89, s32[4,2,48]{2,1,0:T(2,128)S(1)} %bitcast.90), custom_call_target="tpu_custom_call" | custom-call | tf_op jit(solution)/shard_map/gates/pallas_call | solution.py:124
  62.3 9.9 %collective-permute-done.7 = bf16[16,1024]{1,0:T(8,128)(2,1)S(1)} collective-permute-done((bf16[16,1024]{1,0:T(8,128)(2,1)S(1)}, bf16[16,1024]{1,0:T(8,128)(2,1)S(1)}, u32[]{:S(2)}, u32[]{:S(2)}) %collective-permute-start.7) | collective-permute-done | bytes 32800 | tf_op jit(solution)/shard_map/ppermute | solution.py:466
  73.6 14.5 %collective-permute-done.6 = bf16[16,1024]{1,0:T(8,128)(2,1)S(1)} collective-permute-done((bf16[16,1024]{1,0:T(8,128)(2,1)S(1)}, bf16[16,1024]{1,0:T(8,128)(2,1)S(1)}, u32[]{:S(2)}, u32[]{:S(2)}) %collective-permute-start.6) | collective-permute-done | bytes 32800 | tf_op jit(solution)/shard_map/ppermute | solution.py:466
  88.1 3.5 %collective-permute-start.9 = (f32[4,40,96]{2,1,0:T(8,128)S(1)}, f32[4,40,96]{2,1,0:T(8,128)S(1)}, u32[]{:S(2)}, u32[]{:S(2)}) collective-permute-start(f32[4,40,96]{2,1,0:T(8,128)S(1)} %gates.1.info_ref), channel_id=1, source_target_pairs={{0,128},{64,192},{128,0},{192,64},{1,129},{65,193},{129,1},{193,65... | collective-permute-start | bytes 184328 | tf_op jit(solution)/shard_map/ppermute | solution.py:466
  97.0 7.0 %all-to-all-start.1 = ((bf16[16,24,2048]{2,1,0:T(8,128)(2,1)}), bf16[16,24,2048]{2,1,0:T(8,128)(2,1)}, u32[]{:S(2)}, u32[]{:S(2)}) async-start(bf16[16,24,2048]{2,1,0:T(8,128)(2,1)} %copy-done.1), calls=%async_computation.1 | async-start | bytes 3145728 | tf_op jit(solution)/shard_map/all_to_all | solution.py:509
  115.7 11.3 %collective-permute-done.14 = bf16[2,4,48,1024]{3,2,1,0:T(8,128)(2,1)} collective-permute-done((bf16[2,4,48,1024]{3,2,1,0:T(8,128)(2,1)}, bf16[2,4,48,1024]{3,2,1,0:T(8,128)(2,1)}, u32[]{:S(2)}, u32[]{:S(2)}) %collective-permute-start.14) | collective-permute-done | bytes 786464 | tf_op jit(solution)/shard_map/ppermute | solution.py:466
  130.9 4.0 %collective-permute-start.16 = (f32[4,24,48]{2,1,0:T(8,128)S(1)}, f32[4,24,48]{2,1,0:T(8,128)S(1)}, u32[]{:S(2)}, u32[]{:S(2)}) collective-permute-start(f32[4,24,48]{2,1,0:T(8,128)S(1)} %coupling.1), channel_id=1, source_target_pairs={{0,128},{64,192},{128,0},{192,64},{1,129},{65,193},{129,1},{193,65... | collective-permute-start | bytes 55304 | tf_op jit(solution)/shard_map/ppermute | solution.py:466
  134.8 5.7 %collective-permute-done.17 = f32[4,24,48]{2,1,0:T(8,128)S(1)} collective-permute-done((f32[4,24,48]{2,1,0:T(8,128)S(1)}, f32[4,24,48]{2,1,0:T(8,128)S(1)}, u32[]{:S(2)}, u32[]{:S(2)}) %collective-permute-start.17) | collective-permute-done | bytes 18464 | tf_op jit(solution)/shard_map/ppermute | solution.py:466
  144.9 9.1 %tail_combine.1 = (bf16[4,4,48,1024]{3,2,1,0:T(8,128)(2,1)S(1)}, f32[4,4,8,128]{3,2,1,0:T(8,128)S(1)}) custom-call(s32[1]{0:T(128)} %bitcast.p_ref, bf16[16,24,2048]{2,1,0:T(8,128)(2,1)} %all-to-all-done.1.received_ref, f32[4,4,40,96]{3,2,1,0:T(8,128)S(1)} %pad_maximum_fusion.2.info_ref, bf16[4,48,4096]{2,1,0:T(8,128)(2,1)} %up_ref.3, ...), custom_call_target="tpu_custom_call" | custom-call | tf_op jit(solution)/shard_map/tail_combine/pallas_call | solution.py:290
  154.0 9.7 %all_to_all.25.dots_ref = f32[4,4,8,128]{3,2,1,0:T(8,128)S(1)} all-to-all(f32[4,4,8,128]{3,2,1,0:T(8,128)S(1)} %get-tuple-element.35), channel_id=1, replica_groups=mesh['pipe'=4,'expert'=16,'dp'=4] {'pipe'}, dimensions={0} | all-to-all | bytes 131072 | tf_op jit(solution)/shard_map/all_to_all | solution.py:522
  163.7 3.4 %dense.1 = (bf16[4,64,48]{2,1,0:T(8,128)(2,1)S(1)}, bf16[64,8,128]{2,1,0:T(8,128)(2,1)}) custom-call(s32[1]{0:T(128)} %bitcast.p_ref, f32[4,4,8,128]{3,2,1,0:T(8,128)S(1)} %all_to_all.25.dots_ref, f32[4,24,48]{2,1,0:T(8,128)S(1)} %add_add_fusion.couple_ref, f32[4,4,40,96]{3,2,1,0:T(8,128)S(1)} %pad_maximum_fusion.2.info_ref, bf16[4,48,4096]{2,1,0:T(8,128)(2,1)} %bitcast.95), custom_call_target="tpu_custom_call" | custom-call | tf_op jit(solution)/shard_map/dense/pallas_call | solution.py:372
  167.1 10.6 %all-to-all-start.3 = ((bf16[64,8,128]{2,1,0:T(8,128)(2,1)}), bf16[64,8,128]{2,1,0:T(8,128)(2,1)}, u32[]{:S(2)}, u32[]{:S(2)}) async-start(bf16[64,8,128]{2,1,0:T(8,128)(2,1)} %get-tuple-element.43), calls=%async_computation.3 | async-start | bytes 262144 | tf_op jit(solution)/shard_map/all_to_all | solution.py:526
  177.7 3.8 %grads.1 = (bf16[4,48,1024]{2,1,0:T(8,128)(2,1)S(1)}, bf16[4,48,1024]{2,1,0:T(8,128)(2,1)}, bf16[4,48,1024]{2,1,0:T(8,128)(2,1)}, bf16[4,48,1024]{2,1,0:T(8,128)(2,1)S(1)}) custom-call(s32[1]{0:T(128)} %bitcast.p_ref, bf16[4,48,4096]{2,1,0:T(8,128)(2,1)} %up_ref.3, bf16[4,4,48,1024]{3,2,1,0:T(8,128)(2,1)S(1)} %get-tuple-element.34.back_ref, ...), custom_call_target="tpu_custom_call" | custom-call | tf_op jit(solution)/shard_map/grads/pallas_call | solution.py:417
  181.9 3.1 %collective-permute-start.19 = (bf16[4,48,1024]{2,1,0:T(8,128)(2,1)}, bf16[4,48,1024]{2,1,0:T(8,128)(2,1)S(1)}, u32[]{:S(2)}, u32[]{:S(2)}) collective-permute-start(bf16[4,48,1024]{2,1,0:T(8,128)(2,1)} %get-tuple-element.41), channel_id=1, source_target_pairs={{0,128},{64,192},{128,0},{192,64},{1,129},{65,193},{129,1},{193,65... | collective-permute-start | bytes 1179656 | tf_op jit(solution)/shard_map/ppermute | solution.py:466
  185.6 3.3 %all-to-all-done.3 = bf16[64,8,128]{2,1,0:T(8,128)(2,1)} async-done(((bf16[64,8,128]{2,1,0:T(8,128)(2,1)}), bf16[64,8,128]{2,1,0:T(8,128)(2,1)}, u32[]{:S(2)}, u32[]{:S(2)}) %all-to-all-start.3) | async-done | bytes 131104 | tf_op jit(solution)/shard_map/all_to_all | solution.py:526
  190.6 6.9 %all-to-all-start.4 = ((bf16[64,8,128]{2,1,0:T(8,128)(2,1)}), bf16[64,8,128]{2,1,0:T(8,128)(2,1)S(1)}, u32[]{:S(2)}, u32[]{:S(2)}) async-start(bf16[64,8,128]{2,1,0:T(8,128)(2,1)} %broadcast_in_dim.16), calls=%async_computation.4 | async-start | bytes 262144 | tf_op jit(solution)/shard_map/all_to_all | solution.py:530
  197.5 5.3 %collective-permute-done.20.refs_3_ = bf16[4,48,1024]{2,1,0:T(8,128)(2,1)S(1)} collective-permute-done((bf16[4,48,1024]{2,1,0:T(8,128)(2,1)S(1)}, bf16[4,48,1024]{2,1,0:T(8,128)(2,1)S(1)}, u32[]{:S(2)}, u32[]{:S(2)}) %collective-permute-start.20) | collective-permute-done | bytes 393248 | tf_op jit(solution)/shard_map/ppermute | solution.py:466
  204.5 4.4 %all-to-all-done.4 = bf16[64,8,128]{2,1,0:T(8,128)(2,1)S(1)} async-done(((bf16[64,8,128]{2,1,0:T(8,128)(2,1)}), bf16[64,8,128]{2,1,0:T(8,128)(2,1)S(1)}, u32[]{:S(2)}, u32[]{:S(2)}) %all-to-all-start.4) | async-done | bytes 131104 | tf_op jit(solution)/shard_map/all_to_all | solution.py:530
  (71 shorter events, 51.5 us)
Async XLA Ops:
  5.7 91.3 %all-to-all-start = ((bf16[16,48,2048]{2,1,0:T(8,128)(2,1)}), bf16[16,48,2048]{2,1,0:T(8,128)(2,1)S(1)}, u32[]{:S(2)}, u32[]{:S(2)}) async-start(bf16[16,48,2048]{2,1,0:T(8,128)(2,1)} %lead_pack.1), calls=%async_computation | async-start | bytes 6291456 | tf_op jit(solution)/shard_map/all_to_all | solution.py:494
  21.9 11.5 %collective-permute-start = (bf16[12,16,1024]{2,1,0:T(8,128)(2,1)S(1)}, bf16[12,16,1024]{2,1,0:T(8,128)(2,1)S(1)}, u32[]{:S(2)}, u32[]{:S(2)}) collective-permute-start(bf16[12,16,1024]{2,1,0:T(8,128)(2,1)S(1)} %get-tuple-element.50), channel_id=1, source_target_pairs={{0,192},{64,0},{128,64},{192,128},{1,193},{65,1},{129,65},{193,129... | collective-permute-start | bytes 1179656 | tf_op jit(solution)/shard_map/ppermute | solution.py:466
  22.5 20.4 %collective-permute-start.1 = (bf16[12,16,1024]{2,1,0:T(8,128)(2,1)S(1)}, bf16[12,16,1024]{2,1,0:T(8,128)(2,1)S(1)}, u32[]{:S(2)}, u32[]{:S(2)}) collective-permute-start(bf16[12,16,1024]{2,1,0:T(8,128)(2,1)S(1)} %get-tuple-element.51), channel_id=1, source_target_pairs={{0,128},{64,192},{128,0},{192,64},{1,129},{65,193},{129,1},{193,65... | collective-permute-start | bytes 1179656 | tf_op jit(solution)/shard_map/ppermute | solution.py:466
  25.1 18.6 %collective-permute-start.2 = (bf16[12,16,1024]{2,1,0:T(8,128)(2,1)S(1)}, bf16[12,16,1024]{2,1,0:T(8,128)(2,1)S(1)}, u32[]{:S(2)}, u32[]{:S(2)}) collective-permute-start(bf16[12,16,1024]{2,1,0:T(8,128)(2,1)S(1)} %get-tuple-element.48), channel_id=1, source_target_pairs={{0,64},{64,128},{128,192},{192,0},{1,65},{65,129},{129,193},{193,1... | collective-permute-start | bytes 1179656 | tf_op jit(solution)/shard_map/ppermute | solution.py:466
  49.8 46.3 %collective-permute-start.3 = (bf16[2,4,48,1024]{3,2,1,0:T(8,128)(2,1)S(1)}, bf16[2,4,48,1024]{3,2,1,0:T(8,128)(2,1)S(1)}, u32[]{:S(2)}, u32[]{:S(2)}) collective-permute-start(bf16[2,4,48,1024]{3,2,1,0:T(8,128)(2,1)S(1)} %bitcast.99), channel_id=1, source_target_pairs={{0,192},{64,0},{128,64},{192,128},{1,193},{65,1},{129,65},{193,129... | collective-permute-start | bytes 2359304 | tf_op jit(solution)/shard_map/ppermute | solution.py:466
  53.0 44.0 %collective-permute-start.4 = (bf16[2,4,48,1024]{3,2,1,0:T(8,128)(2,1)S(1)}, bf16[2,4,48,1024]{3,2,1,0:T(8,128)(2,1)}, u32[]{:S(2)}, u32[]{:S(2)}) collective-permute-start(bf16[2,4,48,1024]{3,2,1,0:T(8,128)(2,1)S(1)} %bitcast.100), channel_id=1, source_target_pairs={{0,128},{64,192},{128,0},{192,64},{1,129},{65,193},{129,1},{193,65... | collective-permute-start | bytes 2359304 | tf_op jit(solution)/shard_map/ppermute | solution.py:466
  53.1 19.1 %collective-permute-start.7 = (bf16[16,1024]{1,0:T(8,128)(2,1)S(1)}, bf16[16,1024]{1,0:T(8,128)(2,1)S(1)}, u32[]{:S(2)}, u32[]{:S(2)}) collective-permute-start(bf16[16,1024]{1,0:T(8,128)(2,1)S(1)} %get-tuple-element.59), channel_id=1, source_target_pairs={{0,64},{64,128},{128,192},{192,0},{1,65},{65,129},{129,193},{193,1... | collective-permute-start | bytes 98312 | tf_op jit(solution)/shard_map/ppermute | solution.py:466
  55.2 32.9 %collective-permute-start.6 = (bf16[16,1024]{1,0:T(8,128)(2,1)S(1)}, bf16[16,1024]{1,0:T(8,128)(2,1)S(1)}, u32[]{:S(2)}, u32[]{:S(2)}) collective-permute-start(bf16[16,1024]{1,0:T(8,128)(2,1)S(1)} %get-tuple-element.57), channel_id=1, source_target_pairs={{0,128},{64,192},{128,0},{192,64},{1,129},{65,193},{129,1},{193,65... | collective-permute-start | bytes 98312 | tf_op jit(solution)/shard_map/ppermute | solution.py:466
  56.8 34.9 %collective-permute-start.5 = (bf16[16,1024]{1,0:T(8,128)(2,1)S(1)}, bf16[16,1024]{1,0:T(8,128)(2,1)S(1)}, u32[]{:S(2)}, u32[]{:S(2)}) collective-permute-start(bf16[16,1024]{1,0:T(8,128)(2,1)S(1)} %get-tuple-element.58), channel_id=1, source_target_pairs={{0,192},{64,0},{128,64},{192,128},{1,193},{65,1},{129,65},{193,129... | collective-permute-start | bytes 98312 | tf_op jit(solution)/shard_map/ppermute | solution.py:466
  72.2 20.1 %collective-permute-start.10 = (f32[4,40,96]{2,1,0:T(8,128)S(1)}, f32[4,40,96]{2,1,0:T(8,128)S(1)}, u32[]{:S(2)}, u32[]{:S(2)}) collective-permute-start(f32[4,40,96]{2,1,0:T(8,128)S(1)} %gates.1.info_ref), channel_id=1, source_target_pairs={{0,64},{64,128},{128,192},{192,0},{1,65},{65,129},{129,193},{193,1... | collective-permute-start | bytes 184328 | tf_op jit(solution)/shard_map/ppermute | solution.py:466
  88.1 6.1 %collective-permute-start.9 = (f32[4,40,96]{2,1,0:T(8,128)S(1)}, f32[4,40,96]{2,1,0:T(8,128)S(1)}, u32[]{:S(2)}, u32[]{:S(2)}) collective-permute-start(f32[4,40,96]{2,1,0:T(8,128)S(1)} %gates.1.info_ref), channel_id=1, source_target_pairs={{0,128},{64,192},{128,0},{192,64},{1,129},{65,193},{129,1},{193,65... | collective-permute-start | bytes 184328 | tf_op jit(solution)/shard_map/ppermute | solution.py:466
  91.6 4.4 %collective-permute-start.8 = (f32[4,40,96]{2,1,0:T(8,128)S(1)}, f32[4,40,96]{2,1,0:T(8,128)S(1)}, u32[]{:S(2)}, u32[]{:S(2)}) collective-permute-start(f32[4,40,96]{2,1,0:T(8,128)S(1)} %gates.1.info_ref), channel_id=1, source_target_pairs={{0,192},{64,0},{128,64},{192,128},{1,193},{65,1},{129,65},{193,129... | collective-permute-start | bytes 184328 | tf_op jit(solution)/shard_map/ppermute | solution.py:466
  97.0 47.9 %all-to-all-start.1 = ((bf16[16,24,2048]{2,1,0:T(8,128)(2,1)}), bf16[16,24,2048]{2,1,0:T(8,128)(2,1)}, u32[]{:S(2)}, u32[]{:S(2)}) async-start(bf16[16,24,2048]{2,1,0:T(8,128)(2,1)} %copy-done.1), calls=%async_computation.1 | async-start | bytes 3145728 | tf_op jit(solution)/shard_map/all_to_all | solution.py:509
  106.3 20.7 %collective-permute-start.14 = (bf16[2,4,48,1024]{3,2,1,0:T(8,128)(2,1)}, bf16[2,4,48,1024]{3,2,1,0:T(8,128)(2,1)}, u32[]{:S(2)}, u32[]{:S(2)}) collective-permute-start(bf16[2,4,48,1024]{3,2,1,0:T(8,128)(2,1)} %bitcast.84), channel_id=1, source_target_pairs={{0,64},{64,128},{128,192},{192,0},{1,65},{65,129},{129,193},{193,1... | collective-permute-start | bytes 2359304 | tf_op jit(solution)/shard_map/ppermute | solution.py:466
  110.0 34.6 %collective-permute-start.13 = (bf16[3,48,1024]{2,1,0:T(8,128)(2,1)S(1)}, bf16[3,48,1024]{2,1,0:T(8,128)(2,1)S(1)}, u32[]{:S(2)}, u32[]{:S(2)}) collective-permute-start(bf16[3,48,1024]{2,1,0:T(8,128)(2,1)S(1)} %get-tuple-element.53), channel_id=1, source_target_pairs={{0,64},{64,128},{128,192},{192,0},{1,65},{65,129},{129,193},{193,1... | collective-permute-start | bytes 884744 | tf_op jit(solution)/shard_map/ppermute | solution.py:466
  112.8 31.9 %collective-permute-start.12 = (bf16[3,48,1024]{2,1,0:T(8,128)(2,1)S(1)}, bf16[3,48,1024]{2,1,0:T(8,128)(2,1)S(1)}, u32[]{:S(2)}, u32[]{:S(2)}) collective-permute-start(bf16[3,48,1024]{2,1,0:T(8,128)(2,1)S(1)} %get-tuple-element.54), channel_id=1, source_target_pairs={{0,128},{64,192},{128,0},{192,64},{1,129},{65,193},{129,1},{193,65... | collective-permute-start | bytes 884744 | tf_op jit(solution)/shard_map/ppermute | solution.py:466
  114.2 30.5 %collective-permute-start.11 = (bf16[3,48,1024]{2,1,0:T(8,128)(2,1)S(1)}, bf16[3,48,1024]{2,1,0:T(8,128)(2,1)S(1)}, u32[]{:S(2)}, u32[]{:S(2)}) collective-permute-start(bf16[3,48,1024]{2,1,0:T(8,128)(2,1)S(1)} %get-tuple-element.55), channel_id=1, source_target_pairs={{0,192},{64,0},{128,64},{192,128},{1,193},{65,1},{129,65},{193,129... | collective-permute-start | bytes 884744 | tf_op jit(solution)/shard_map/ppermute | solution.py:466
  130.6 9.9 %collective-permute-start.17 = (f32[4,24,48]{2,1,0:T(8,128)S(1)}, f32[4,24,48]{2,1,0:T(8,128)S(1)}, u32[]{:S(2)}, u32[]{:S(2)}) collective-permute-start(f32[4,24,48]{2,1,0:T(8,128)S(1)} %coupling.1), channel_id=1, source_target_pairs={{0,64},{64,128},{128,192},{192,0},{1,65},{65,129},{129,193},{193,1... | collective-permute-start | bytes 55304 | tf_op jit(solution)/shard_map/ppermute | solution.py:466
  130.9 12.0 %collective-permute-start.16 = (f32[4,24,48]{2,1,0:T(8,128)S(1)}, f32[4,24,48]{2,1,0:T(8,128)S(1)}, u32[]{:S(2)}, u32[]{:S(2)}) collective-permute-start(f32[4,24,48]{2,1,0:T(8,128)S(1)} %coupling.1), channel_id=1, source_target_pairs={{0,128},{64,192},{128,0},{192,64},{1,129},{65,193},{129,1},{193,65... | collective-permute-start | bytes 55304 | tf_op jit(solution)/shard_map/ppermute | solution.py:466
  167.1 21.8 %all-to-all-start.3 = ((bf16[64,8,128]{2,1,0:T(8,128)(2,1)}), bf16[64,8,128]{2,1,0:T(8,128)(2,1)}, u32[]{:S(2)}, u32[]{:S(2)}) async-start(bf16[64,8,128]{2,1,0:T(8,128)(2,1)} %get-tuple-element.43), calls=%async_computation.3 | async-start | bytes 262144 | tf_op jit(solution)/shard_map/all_to_all | solution.py:526
  181.5 16.0 %collective-permute-start.18 = (bf16[4,48,1024]{2,1,0:T(8,128)(2,1)}, bf16[4,48,1024]{2,1,0:T(8,128)(2,1)S(1)}, u32[]{:S(2)}, u32[]{:S(2)}) collective-permute-start(bf16[4,48,1024]{2,1,0:T(8,128)(2,1)} %get-tuple-element.40), channel_id=1, source_target_pairs={{0,64},{64,128},{128,192},{192,0},{1,65},{65,129},{129,193},{193,1... | collective-permute-start | bytes 1179656 | tf_op jit(solution)/shard_map/ppermute | solution.py:466
  181.9 15.6 %collective-permute-start.19 = (bf16[4,48,1024]{2,1,0:T(8,128)(2,1)}, bf16[4,48,1024]{2,1,0:T(8,128)(2,1)S(1)}, u32[]{:S(2)}, u32[]{:S(2)}) collective-permute-start(bf16[4,48,1024]{2,1,0:T(8,128)(2,1)} %get-tuple-element.41), channel_id=1, source_target_pairs={{0,128},{64,192},{128,0},{192,64},{1,129},{65,193},{129,1},{193,65... | collective-permute-start | bytes 1179656 | tf_op jit(solution)/shard_map/ppermute | solution.py:466
  185.1 17.7 %collective-permute-start.20 = (bf16[4,48,1024]{2,1,0:T(8,128)(2,1)S(1)}, bf16[4,48,1024]{2,1,0:T(8,128)(2,1)S(1)}, u32[]{:S(2)}, u32[]{:S(2)}) collective-permute-start(bf16[4,48,1024]{2,1,0:T(8,128)(2,1)S(1)} %get-tuple-element.42), channel_id=1, source_target_pairs={{0,192},{64,0},{128,64},{192,128},{1,193},{65,1},{129,65},{193,129... | collective-permute-start | bytes 1179656 | tf_op jit(solution)/shard_map/ppermute | solution.py:466
  190.6 18.3 %all-to-all-start.4 = ((bf16[64,8,128]{2,1,0:T(8,128)(2,1)}), bf16[64,8,128]{2,1,0:T(8,128)(2,1)S(1)}, u32[]{:S(2)}, u32[]{:S(2)}) async-start(bf16[64,8,128]{2,1,0:T(8,128)(2,1)} %broadcast_in_dim.16), calls=%async_computation.4 | async-start | bytes 262144 | tf_op jit(solution)/shard_map/all_to_all | solution.py:530
  (9 other events, 44.8 us)

commit v4 on v3

v4 whole, which is shorter than its diff:
```python
import functools

import jax
import jax.numpy as jnp
from jax import lax
from jax.experimental import pallas as pl
from jax.experimental.pallas import tpu as pltpu
from jax.sharding import PartitionSpec as P

F32 = jnp.float32
BF16 = jnp.bfloat16
NT = (((1,), (1,)), ((), ()))
TN = (((0,), (0,)), ((), ()))

TILE = 8


def params(mib):
    return pltpu.CompilerParams(vmem_limit_bytes=mib << 20)


def in_hbm(array):
    return pltpu.with_memory_space_constraint(array, pltpu.MemorySpace.HBM)


def iotas(shape):
    return [lax.broadcasted_iota(jnp.int32, shape, d) for d in range(2)]


def swap_matrix(slots, dests):
    out_row, in_row = iotas((slots * dests, slots * dests))
    return (in_row == (out_row % slots) * dests + out_row // slots).astype(BF16)


def lead_pack_kernel(grads_ref, out_ref):
    _, slots, dests, width = grads_ref.shape
    half = width // 2
    swap = swap_matrix(slots, dests)
    for h in range(2):
        rows = grads_ref[0, :, :, h * half : (h + 1) * half].reshape(slots * dests, half)
        moved = jnp.dot(swap, rows, preferred_element_type=F32)
        out_ref[:, h * slots : (h + 1) * slots, :] = moved.reshape(dests, slots, half).astype(BF16)


def lead_pack(grads, count):
    _, _, dests, width = grads.shape
    half = width // 2
    return pl.pallas_call(
        lead_pack_kernel,
        grid=(count,),
        in_specs=[pl.BlockSpec((1, TILE, dests, width), lambda m: (m, 0, 0, 0))],
        out_specs=pl.BlockSpec((dests, 2 * TILE, half), lambda m: (0, m, 0)),
        out_shape=pltpu.HBM((dests, 2 * TILE * count, half), BF16),
        compiler_params=params(40),
        name="lead_pack",
    )(grads)


def tail_pack_kernel(*refs):
    out_ref = refs[-1]
    kept, dests, quarter = refs[0].shape
    micro = kept - TILE
    swap = swap_matrix(TILE, dests)
    out_row, in_row = iotas((2 * micro * dests, micro * dests))
    within = out_row % (2 * micro)
    source = (within % micro) * dests + out_row // (2 * micro)
    for c in range(2):
        total = jnp.zeros((2 * micro * dests, quarter), F32)
        columns = slice(c * quarter, (c + 1) * quarter)
        for h in range(2):
            ref = refs[2 * h + c]
            moved = jnp.dot(swap, ref[:TILE].reshape(TILE * dests, quarter), preferred_element_type=F32)
            moved = moved.reshape(dests, TILE, quarter).astype(BF16)
            out_ref[:, h * TILE : (h + 1) * TILE, columns] = moved
            pick = ((in_row == source) & (within // micro == h)).astype(BF16)
            rows = ref[TILE:].reshape(micro * dests, quarter)
            total = total + jnp.dot(pick, rows, preferred_element_type=F32)
        out_ref[:, 2 * TILE :, columns] = total.reshape(dests, 2 * micro, quarter).astype(BF16)


def tail_pack(blocks):
    kept, dests, quarter = blocks[0].shape
    return pl.pallas_call(
        tail_pack_kernel,
        out_shape=jax.ShapeDtypeStruct((dests, 2 * TILE + 2 * (kept - TILE), 2 * quarter), BF16),
        compiler_params=params(40),
        name="tail_pack",
    )(*blocks)


def late_kernel(p_ref, main_ref, last_ref, *out_refs):
    step = pl.program_id(0)
    for j in range(len(out_refs)):

        @pl.when(step == j)
        def _():
            out_refs[j][:TILE] = main_ref[0]
            out_refs[j][TILE:] = last_ref[:, 0]


def late_blocks(p, grads, sections):
    micro, cap, dests, width = grads.shape
    quarter = width // sections
    shape = (TILE + micro, dests, quarter)
    return pl.pallas_call(
        late_kernel,
        grid_spec=pltpu.PrefetchScalarGridSpec(
            num_scalar_prefetch=1,
            grid=(sections,),
            in_specs=[
                pl.BlockSpec(
                    (1, TILE, dests, quarter),
                    lambda j, p: (micro - 1, 0, 0, (p[0] - j) & (sections - 1)),
                ),
                pl.BlockSpec(
                    (micro, 1, dests, quarter),
                    lambda j, p: (0, cap - 1, 0, (p[0] - j) & (sections - 1)),
                ),
            ],
            out_specs=[pl.BlockSpec(shape, lambda j, p: (0, 0, 0))] * sections,
        ),
        out_shape=[jax.ShapeDtypeStruct(shape, BF16)] * sections,
        compiler_params=params(32),
        name="late_blocks",
    )(p, grads, grads)


def gate_kernel(micro, normed_ref, w_ref, routes_ref, info_ref, near_ref):
    logits = lax.dot_general(w_ref[...], normed_ref[...], NT, preferred_element_type=F32)
    experts, tokens = logits.shape
    rows = tokens // micro
    expl = jnp.exp(logits)
    probs = expl / jnp.sum(expl, axis=0, keepdims=True)
    ids = lax.broadcasted_iota(jnp.int32, (experts, tokens), 0)
    first, second = iotas((tokens, tokens))
    lane = lax.broadcasted_iota(jnp.int32, (1, tokens), 1)
    block = jnp.zeros((1, tokens), jnp.int32)
    same = first >= 0
    for m in range(1, micro):
        block = block + (lane >= m * rows).astype(jnp.int32)
        same = same & ((first >= m * rows) == (second >= m * rows))
    earlier = ((first < second) & same).astype(BF16)
    named = [ids == routes_ref[k : k + 1, :] for k in range(2)]
    both = jnp.where(named[0] | named[1], 1.0, 0.0).astype(BF16)
    before = jnp.dot(both, earlier, preferred_element_type=F32)
    found = []
    gates = []
    places = []
    for k in range(2):
        gate = jnp.sum(jnp.where(named[k], probs, 0.0), axis=0, keepdims=True)
        found.append(gate * (jnp.where(named[k], 1.0, 0.0) - probs))
        gates.append(gate)
        slot = jnp.sum(jnp.where(named[k], before, 0.0), axis=0, keepdims=True).astype(jnp.int32)
        expert = routes_ref[k : k + 1, :]
        place = jnp.where(slot < TILE, expert * TILE + slot, experts * TILE + block * experts + expert)
        places.append(place.astype(F32))
    near = jnp.concatenate(gates + places + [jnp.zeros((4, tokens), F32)], axis=0)
    info_ref[...] = jnp.concatenate(found + [near], axis=0)
    for m in range(micro):
        part = near[:, m * rows : (m + 1) * rows]
        near_ref[m, :, :rows] = part
        near_ref[m, :, rows:] = part


def gate_info(normed, w, routes, micro):
    tokens, width = normed.shape
    experts = w.shape[0]
    return pl.pallas_call(
        functools.partial(gate_kernel, micro),
        out_shape=[
            jax.ShapeDtypeStruct((2 * experts + 8, tokens), F32),
            jax.ShapeDtypeStruct((micro, 8, 2 * tokens // micro), F32),
        ],
        compiler_params=params(32),
        name="gates",
    )(normed, w, routes)


def pairs(sections):
    found = []
    for s in range(sections - 1):
        for k in range(2):
            for upper in range(s + 1, sections):
                for k2 in range(2):
                    found.append((s, k, upper, k2))
    return {key: row for row, key in enumerate(found)}


def couple_kernel(p_ref, saved_ref, w_ref, info_ref, out_ref):
    p = p_ref[0]
    sections, experts, quarter = w_ref.shape
    tokens = saved_ref.shape[2]
    table = pairs(sections)
    for s in range(sections - 1):
        j = (s - p) & (sections - 1)
        for k in range(2):
            saved = saved_ref[j, k]
            for upper in range(s + 1, sections):
                j2 = (upper - p) & (sections - 1)
                part = lax.dot_general(w_ref[j2], saved, NT, preferred_element_type=F32)
                for k2 in range(2):
                    row = table[(s, k, upper, k2)]
                    v = info_ref[j2, k2 * experts : (k2 + 1) * experts, :]
                    out_ref[row : row + 1, :] = jnp.sum(part * v, axis=0, keepdims=True)


SCALAR = pl.BlockSpec(memory_space=pltpu.MemorySpace.SMEM)
WHOLE = pl.BlockSpec(memory_space=pltpu.MemorySpace.VMEM)
STAYS = pl.BlockSpec(memory_space=pl.ANY)


def coupling(p, saved, w, info):
    sections, _, tokens, _ = saved.shape
    return pl.pallas_call(
        couple_kernel,
        in_specs=[SCALAR, WHOLE, WHOLE, WHOLE],
        out_specs=WHOLE,
        out_shape=jax.ShapeDtypeStruct((len(pairs(sections)), tokens), F32),
        compiler_params=params(32),
        name="coupling",
    )(p, saved, w, info)


def picked(gates, places, first, received):
    n = received.shape[0]
    lanes = gates[0].shape[1]
    index, lane = iotas((n, lanes))
    pick = jnp.zeros((n, lanes), F32)
    for k in range(2):
        pick = pick + jnp.where(index + first == places[k], gates[k], 0.0)
    high = pick.astype(BF16).astype(F32)
    pick = jnp.where(lane >= lanes // 2, pick - high, high).astype(BF16)
    both = lax.dot_general(pick, received, TN, preferred_element_type=F32)
    return both[: lanes // 2] + both[lanes // 2 :]


def lead_kernel(main_ref, near_ref, out_ref):
    experts, _, half = main_ref.shape
    received = main_ref[...].reshape(experts * TILE, half)
    gates = [near_ref[0, k : k + 1, :] for k in range(2)]
    places = [near_ref[0, 2 + k : 3 + k, :].astype(jnp.int32) for k in range(2)]
    total = picked(gates, places, 0, received).astype(BF16)
    out_ref[0, 0] = total[:, : half // 2]
    out_ref[1, 0] = total[:, half // 2 :]


def lead_combine(received, near):
    experts, packed, half = received.shape
    count = packed // (2 * TILE)
    rows = near.shape[2] // 2
    return pl.pallas_call(
        lead_kernel,
        grid=(2, count),
        in_specs=[
            pl.BlockSpec((experts, TILE, half), lambda h, m: (0, 2 * m + h, 0)),
            pl.BlockSpec((1,) + near.shape[1:], lambda h, m: (m, 0, 0)),
        ],
        out_specs=pl.BlockSpec((2, 1, rows, half // 2), lambda h, m: (h, m, 0, 0)),
        out_shape=jax.ShapeDtypeStruct((4, count, rows, half // 2), BF16),
        compiler_params=params(40),
        name="lead_combine",
    )(received, near)


def tail_kernel(
    p_ref, received_ref, info_ref, up_ref, lead_ref, saved_ref, links_ref,
    back_ref, sent_ref, block_ref, last_ref, sum_ref, sems,
):
    p = p_ref[0]
    sections, rows, quarter = sum_ref.shape
    _, experts, _, half = block_ref.shape
    micro = up_ref.shape[0]
    n = experts * TILE
    copies = [
        pltpu.make_async_copy(
            received_ref.at[:, pl.ds(TILE * unit, TILE), :], block_ref.at[unit], sems.at[unit]
        )
        for unit in range(3)
    ]
    copies[2].start()
    copies[0].start()
    copies[1].start()
    out_row, in_row = iotas((n, n))
    order = (in_row == (out_row % experts) * TILE + out_row // experts).astype(BF16)
    lane = lax.broadcasted_iota(jnp.int32, (rows, 128), 1)
    row, column = iotas((2 * sections, 128))
    eye = (row == column).astype(F32)
    copies[2].wait()
    last = block_ref[2].reshape(n, half)
    last_ref[...] = jnp.dot(order, last, preferred_element_type=F32).astype(BF16)
    for m in range(micro):
        if m == micro - 1:
            copies[0].wait()
            copies[1].wait()
        for j in range(sections):
            h, c = divmod(j, 2)
            columns = slice(c * quarter, (c + 1) * quarter)
            facts = info_ref[j, 2 * experts :, m * rows : (m + 1) * rows]
            facts = jnp.concatenate([facts, facts], axis=1)
            gates = [facts[k : k + 1] for k in range(2)]
            places = [facts[2 + k : 3 + k].astype(jnp.int32) for k in range(2)]
            start = (h * micro + m) * experts
            total = picked(gates, places, n + m * experts, last_ref[start : start + experts, columns])
            if m == micro - 1:
                main = block_ref[h, :, :, columns].reshape(n, quarter)
                total = total + picked(gates, places, 0, main)
            else:
                total = total + lead_ref[j, m].astype(F32)
            sum_ref[j] = total
            back_ref[j, m] = total.astype(BF16)
        base = up_ref[m].astype(F32)
        dots = jnp.zeros((rows, 128), F32)
        for s in reversed(range(sections)):
            j = (s - p) & (sections - 1)
            for k in range(2):
                product = base * saved_ref[j, k, m * rows : (m + 1) * rows, :].astype(F32)
                part = product[:, :128]
                for t in range(1, quarter // 128):
                    part = part + product[:, t * 128 : (t + 1) * 128]
                part = jnp.sum(part, axis=1, keepdims=True)
                dots = jnp.where(lane == 2 * s + k, part, dots)
            if s > 0:
                base = base + sum_ref[j]
        dots = lax.dot_general(
            eye, dots, NT, precision=lax.Precision.HIGHEST, preferred_element_type=F32
        )
        for dest in range(sections):
            sent_ref[dest, : 2 * sections, m * rows : (m + 1) * rows] = dots
    for dest in range(sections):
        sent_ref[dest, 2 * sections :, :] = links_ref[...]


def tail_combine(p, received, info, upstream, lead, saved, links):
    sections, _, tokens, quarter = saved.shape
    micro, rows, _ = upstream.shape
    experts, packed, half = received.shape
    return pl.pallas_call(
        tail_kernel,
        in_specs=[SCALAR, STAYS] + [WHOLE] * 5,
        out_specs=[WHOLE] * 2,
        out_shape=[
            jax.ShapeDtypeStruct((sections, micro, rows, quarter), BF16),
            jax.ShapeDtypeStruct((sections, 2 * sections + links.shape[0], tokens), F32),
        ],
        scratch_shapes=[
            pltpu.VMEM((3, experts, TILE, half), BF16),
            pltpu.VMEM((experts * TILE, half), BF16),
            pltpu.VMEM((sections, rows, quarter), F32),
            pltpu.SemaphoreType.DMA((3,)),
        ],
        compiler_params=params(48),
        name="tail_combine",
    )(p, received, info, upstream, lead, saved, links)


def dense_kernel(micro, p_ref, sent_ref, info_ref, normed_ref, dense_ref, part_ref, rows_ref, sem):
    copy = pltpu.make_async_copy(normed_ref, rows_ref, sem)
    copy.start()
    p = p_ref[0]
    sections = sent_ref.shape[0]
    tokens, width = rows_ref.shape
    experts = (info_ref.shape[1] - 8) // 2
    table = pairs(sections)
    given = sent_ref[0]
    for source in range(1, sections):
        given = given + sent_ref[source]
    dots = {}
    own = jnp.zeros((experts, tokens), F32)
    for s in reversed(range(sections)):
        j = (s - p) & (sections - 1)
        dense = jnp.zeros((experts, tokens), F32)
        for k in range(2):
            value = given[2 * s + k : 2 * s + k + 1, :]
            for upper in range(s + 1, sections):
                for k2 in range(2):
                    row = 2 * sections + table[(s, k, upper, k2)]
                    value = value + given[row : row + 1, :] * dots[(upper, k2)]
            dots[(s, k)] = value
            dense = dense + value * info_ref[j, k * experts : (k + 1) * experts, :]
        dense_ref[s * experts : (s + 1) * experts, :] = dense.astype(BF16)
        own = jnp.where(p == s, dense, own)
    copy.wait()
    total = jnp.dot(own.astype(BF16), rows_ref[...], preferred_element_type=F32) * (1.0 / micro)
    cols = width // 128
    for r in range(experts // 8):
        for c in range(cols):
            tile = total[r * 8 : (r + 1) * 8, c * 128 : (c + 1) * 128]
            part_ref[r * cols + c] = tile.astype(BF16)


def dense_terms(p, sent, info, normed, micro):
    sections, _, tokens = sent.shape
    width = normed.shape[1]
    experts = (info.shape[1] - 8) // 2
    blocks = experts // 8 * (width // 128)
    return pl.pallas_call(
        functools.partial(dense_kernel, micro),
        in_specs=[SCALAR, WHOLE, WHOLE, STAYS],
        out_specs=[WHOLE] * 2,
        out_shape=[
            jax.ShapeDtypeStruct((sections * experts, tokens), BF16),
            jax.ShapeDtypeStruct((blocks, 8, 128), BF16),
        ],
        scratch_shapes=[pltpu.VMEM((tokens, width), BF16), pltpu.SemaphoreType.DMA],
        compiler_params=params(32),
        name="dense",
    )(p, sent, info, normed)


def grads_kernel(p_ref, up_ref, back_ref, dense_ref, w_ref, *refs):
    p = p_ref[0]
    outs, total_ref, turn_ref = refs[:-2], refs[-2], refs[-1]
    sections, micro, rows, quarter = back_ref.shape
    experts = w_ref.shape[1]
    total_ref[...] = up_ref[...].astype(F32)
    for s in reversed(range(sections)):
        j = (s - p) & (sections - 1)
        dense = dense_ref[s * experts : (s + 1) * experts, :]
        term = lax.dot_general(dense, w_ref[j], TN, preferred_element_type=F32)
        for m in range(micro):
            total = total_ref[m] + back_ref[j, m].astype(F32) + term[m * rows : (m + 1) * rows]
            total_ref[m] = total
            turn_ref[j, m] = total.astype(BF16)
    for j in range(sections):
        outs[j][...] = turn_ref[j]


def grads_of(p, upstream, back, dense, w):
    sections, micro, rows, quarter = back.shape
    return pl.pallas_call(
        grads_kernel,
        in_specs=[SCALAR] + [WHOLE] * 4,
        out_specs=[WHOLE] * sections,
        out_shape=[jax.ShapeDtypeStruct((micro, rows, quarter), BF16)] * sections,
        scratch_shapes=[
            pltpu.VMEM((micro, rows, quarter), F32),
            pltpu.VMEM((sections, micro, rows, quarter), BF16),
        ],
        compiler_params=params(40),
        name="grads",
    )(p, upstream, back, dense, w)


def join_kernel(p_ref, *refs):
    step = pl.program_id(0)
    out_ref = refs[-1]
    for d in range(len(refs) - 1):

        @pl.when(step == d)
        def _():
            out_ref[...] = refs[d][...]


def join(p, blocks):
    n = len(blocks)
    micro, rows, quarter = blocks[0].shape
    return pl.pallas_call(
        join_kernel,
        grid_spec=pltpu.PrefetchScalarGridSpec(
            num_scalar_prefetch=1,
            grid=(n,),
            in_specs=[pl.BlockSpec((micro, rows, quarter), lambda d, p: (0, 0, 0))] * n,
            out_specs=pl.BlockSpec((micro, rows, quarter), lambda d, p: (0, 0, (p[0] - d) & (n - 1))),
        ),
        out_shape=jax.ShapeDtypeStruct((micro, rows, n * quarter), BF16),
        compiler_params=params(32),
        name="join",
    )(p, *blocks)


def turned(block, distance):
    n = lax.axis_size("pipe")
    return lax.ppermute(block, "pipe", [(i, (i + distance) % n) for i in range(n)])


def gathered(block):
    n = lax.axis_size("pipe")
    return [block] + [turned(block, n - j) for j in range(1, n)]


def on_device(normed, saved_out, expert_grads, routes, router_weight, upstream):
    sections = lax.axis_size("pipe")
    section = lax.axis_index("pipe")
    p = section.astype(jnp.int32).reshape(1)
    _, micro, rows, width = normed.shape
    tokens = micro * rows
    quarter = width // sections
    normed = normed.reshape(tokens, width)
    w = router_weight[0].T
    experts = w.shape[0]

    def part(array, j, axis):
        return lax.dynamic_slice_in_dim(array, ((section - j) % sections) * quarter, quarter, axis)

    def spread(blocks):
        return [turned(block, sections - j) if j else block for j, block in enumerate(blocks)]

    grads = in_hbm(jnp.transpose(expert_grads[0, :, 0, 0], (0, 2, 1, 3)))
    lead = lax.all_to_all(lead_pack(grads, micro - 1), "expert", 0, 0, tiled=True)
    late = spread(late_blocks(p, grads, sections))
    info, near = gate_info(normed, w, jnp.transpose(routes[0], (2, 0, 1)).reshape(2, tokens), micro)
    info_all = jnp.stack(spread([info] * sections))
    w_all = jnp.stack(spread([part(w, j, 1) for j in range(sections)]))
    tail_send = tail_pack(late)
    saved_out, tail_send, info_all, w_all = lax.optimization_barrier(
        (saved_out, tail_send, info_all, w_all)
    )

    saved = jnp.transpose(saved_out[0], (2, 0, 1, 3))
    early = spread([part(saved[:, : micro - 1], j, 3) for j in range(sections)])
    lead, tail_send, *early = lax.optimization_barrier((lead, tail_send, *early))
    tail = lax.all_to_all(tail_send, "expert", 0, 0, tiled=True)
    rest = spread([part(saved[:, micro - 1 :], j, 3) for j in range(sections)])
    back = lead_combine(lead, near)
    lead = [
        lax.dynamic_index_in_dim(back, (section - j) % sections, 0, False) for j in range(sections)
    ]
    lead = jnp.stack(spread(lead))
    saved = jnp.concatenate([jnp.stack(early), jnp.stack(rest)], axis=2)
    saved = saved.reshape(sections, 2, tokens, quarter)
    links = coupling(p, saved, w_all, info_all)
    up = part(upstream, 0, 2)
    lead, info_all, w_all, saved, links, up = lax.optimization_barrier(
        (lead, info_all, w_all, saved, links, up)
    )
    back, sent = tail_combine(p, tail, info_all, up, lead, saved, links)
    sent = lax.all_to_all(sent, "pipe", 0, 0, tiled=True)
    dense, partial = dense_terms(p, sent, info_all, normed, micro)

    axes = ("expert", "dp")
    partial = lax.all_to_all(partial, axes, 0, 0, tiled=True)
    outs = grads_of(p, up, back, dense, w_all)
    blocks = [turned(out, d) if d else out for d, out in enumerate(outs)]
    total = jnp.sum(partial.astype(F32), axis=0, keepdims=True).astype(BF16)
    total = lax.all_to_all(jnp.broadcast_to(total, partial.shape), axes, 0, 0, tiled=True)
    total = total.astype(F32).reshape(experts // 8, width // 128, 8, 128).transpose(0, 2, 1, 3)
    router_grad = total.reshape(experts, width).T
    return (join(p, blocks)[None], router_grad[None])


def solution(mesh):
    in_specs = (
        P("pipe", None, ("expert", "dp"), None),
        P("pipe", None, ("expert", "dp"), None, None),
        P("pipe", None, "dp", "expert", None, None, None),
        P("pipe", None, ("expert", "dp"), None),
        P("pipe", None, None),
        P(None, ("expert", "dp"), None),
    )
    out_specs = (P("pipe", None, ("expert", "dp"), None), P("pipe", None, None))
    return jax.shard_map(
        on_device, mesh=mesh, in_specs=in_specs, out_specs=out_specs, check_vma=False
    )
```

time: 211 us -> 203 us (0.962)
  waiting for transfers between devices: 76.6 us -> 61.8 us
  other arithmetic: 4.33 us -> 12.1 us
  local copies, waits for them, and re-layouts: 18.4 us -> 22.9 us
  starting transfers between devices: 68.6 us -> 65.6 us
  Pallas kernels: 31 us -> 28.7 us
    ppermute x21, waiting for transfers between devices: 68.9 us -> 49.8 us  [turned(): lax.ppermute(block, 'pipe', [(i, (i + distance) % n) for i in range(n)])]
    concatenate x1, other arithmetic: 0.17 us -> 7.86 us  [on_device(): saved = jnp.concatenate([jnp.stack(early), jnp.stack(rest)], axis=2)]
    another operation x6 -> x2, local copies, waits for them, and re-layouts: 8.04 us -> 0.77 us  [the longest x1 0.76 us: on_device(): saved = jnp.concatenate([jnp.stack(early), jnp.stack(rest)], axis=2)]
    all_to_all x1, waiting for transfers between devices: 0.01 us -> 6.97 us  [on_device(): tail = lax.all_to_all(tail_send, 'expert', 0, 0, tiled=True)]
    unnamed x17 -> x46, local copies, waits for them, and re-layouts: 7.14 us -> 13 us
    pallas_call x6 -> x7, Pallas kernels: 23.6 us -> 18.5 us  [the longest x1 6.31 us: tail_combine(): pl.pallas_call(tail_kernel, in_specs=[SCALAR, STAYS] + [WHOLE] * 5, out_s...]
    slice x0 -> x2, local copies, waits for them, and re-layouts: none -> 4.04 us  [the longest x1 2.25 us: on_device(): early = spread([part(saved[:, :micro - 1], j, 3) for j in range(sections)])]
    dynamic_slice x1 -> x3, local copies, waits for them, and re-layouts: 0.12 us -> 3.31 us  [the longest x2 3.22 us: part(): lax.dynamic_slice_in_dim(array, (section - j) % sections * quarter, quart...]
  transfers between devices with their start and end apart: 25 -> 25, of which waited for: 13 -> 10; matrix products, arithmetic and copies ran while one was open for 9% -> 11% of each run, Pallas kernels for 6% -> 8%
where the time goes in v4:
time: 203 us; the launch traced here: 202 us
  starting transfers between devices  65.6 us (32%)
  waiting for transfers between devices  61.8 us (30%)
  Pallas kernels  28.7 us (14%)
  local copies, waits for them, and re-layouts  22.9 us (11%)
  other arithmetic  12.1 us (6%)
  blocking collectives  9.6 us (5%)
    ppermute x21, waiting for transfers between devices, turned(): lax.ppermute(block, 'pipe', [(i, (i + distance) % n) for i in range(n)])  49.8 us
    ppermute x21, starting transfers between devices, turned(): lax.ppermute(block, 'pipe', [(i, (i + distance) % n) for i in range(n)])  33.4 us
    unnamed x46, local copies, waits for them, and re-layouts  13 us
    all_to_all x1, blocking collectives, on_device(): sent = lax.all_to_all(sent, 'pipe', 0, 0, tiled=True)  9.6 us
    all_to_all x1, starting transfers between devices, on_device(): lax.all_to_all(jnp.broadcast_to(total, partial.shape), axes, 0, 0, tiled=...  8.67 us
    all_to_all x1, starting transfers between devices, on_device(): lax.all_to_all(lead_pack(grads, micro - 1), 'expert', 0, 0, tiled=True)  8.62 us
    all_to_all x1, starting transfers between devices, on_device(): partial = lax.all_to_all(partial, axes, 0, 0, tiled=True)  7.92 us
    concatenate x1, other arithmetic, on_device(): saved = jnp.concatenate([jnp.stack(early), jnp.stack(rest)], axis=2)  7.86 us
  transfers between devices with their start and end apart: 25, of which 10 were waited for; matrix products, arithmetic and copies ran while one was open for 11% of the time, Pallas kernels for 8%

profile of v4, /device:TPU:8, one launch (start us, length us, event | category | flops | bytes accessed | tf_op | source)
XLA Modules:
  0.0 201.6 jit_solution(18162173323672124522)
XLA Ops:
  0.6 5.2 %lead_pack.1 = bf16[16,48,2048]{2,1,0:T(8,128)(2,1)} custom-call(bf16[4,9,16,4096]{3,2,1,0:T(8,128)(2,1)} %bitcast.75), custom_call_target="tpu_custom_call" | custom-call | tf_op jit(solution)/shard_map/lead_pack/pallas_call | solution.py:48
  5.9 8.6 %all-to-all-start = ((bf16[16,48,2048]{2,1,0:T(8,128)(2,1)}), bf16[16,48,2048]{2,1,0:T(8,128)(2,1)}, u32[]{:S(2)}, u32[]{:S(2)}) async-start(bf16[16,48,2048]{2,1,0:T(8,128)(2,1)} %lead_pack.1), calls=%async_computation | async-start | bytes 6291456 | tf_op jit(solution)/shard_map/all_to_all | solution.py:499
  14.5 3.4 %late_blocks.1 = (bf16[12,16,1024]{2,1,0:T(8,128)(2,1)S(1)}, bf16[12,16,1024]{2,1,0:T(8,128)(2,1)}, bf16[12,16,1024]{2,1,0:T(8,128)(2,1)}, bf16[12,16,1024]{2,1,0:T(8,128)(2,1)}) custom-call(s32[1]{0:T(128)} %bitcast.p_ref, bf16[4,9,16,4096]{3,2,1,0:T(8,128)(2,1)} %bitcast.76, bf16[4,9,16,4096]{3,2,1,0:T(8,128)(2,1)} %bitcast.77), custom_call_target="tpu_custom_call" | custom-call | tf_op jit(solution)/shard_map/late_blocks/pallas_call | solution.py:105
  19.2 2.6 %collective-permute-start.1 = (bf16[12,16,1024]{2,1,0:T(8,128)(2,1)}, bf16[12,16,1024]{2,1,0:T(8,128)(2,1)}, u32[]{:S(2)}, u32[]{:S(2)}) collective-permute-start(bf16[12,16,1024]{2,1,0:T(8,128)(2,1)} %get-tuple-element.34), channel_id=1, source_target_pairs={{0,128},{64,192},{128,0},{192,64},{1,129},{65,193},{129,1},{193,65... | collective-permute-start | bytes 1179656 | tf_op jit(solution)/shard_map/ppermute | solution.py:473
  26.6 15.3 %collective-permute-done.5 = f32[40,192]{1,0:T(8,128)S(1)} collective-permute-done((f32[40,192]{1,0:T(8,128)S(1)}, f32[40,192]{1,0:T(8,128)S(1)}, u32[]{:S(2)}, u32[]{:S(2)}) %collective-permute-start.5) | collective-permute-done | bytes 30752 | tf_op jit(solution)/shard_map/ppermute | solution.py:473
  47.3 4.7 %collective-permute-start.7 = (bf16[16,1024]{1,0:T(8,128)(2,1)S(1)}, bf16[16,1024]{1,0:T(8,128)(2,1)S(1)}, u32[]{:S(2)}, u32[]{:S(2)}) collective-permute-start(bf16[16,1024]{1,0:T(8,128)(2,1)S(1)} %get-tuple-element.77), channel_id=1, source_target_pairs={{0,128},{64,192},{128,0},{192,64},{1,129},{65,193},{129,1},{193,65... | collective-permute-start | bytes 98312 | tf_op jit(solution)/shard_map/ppermute | solution.py:473
  57.6 3.2 %tail_pack.1 = bf16[16,24,2048]{2,1,0:T(8,128)(2,1)} custom-call(bf16[12,16,1024]{2,1,0:T(8,128)(2,1)S(1)} %copy-done.12, bf16[12,16,1024]{2,1,0:T(8,128)(2,1)} %collective-permute-done.refs_1_, bf16[12,16,1024]{2,1,0:T(8,128)(2,1)} %collective-permute-done.1.refs_2_, bf16[12,16,1024]{2,1,0:T(8,128)(2,1)} %collective-permute-done.2.refs_3_), custom_call_target="tpu_custom_call" | custom-call | tf_op jit(solution)/shard_map/tail_pack/pallas_call | solution.py:83
  60.8 2.2 %slice.6 = bf16[2,3,48,4096]{3,0,2,1:T(2,128)(2,1)S(1)} slice(bf16[2,4,48,4096]{3,0,2,1:T(2,128)(2,1)S(1)} %bitcast.79), slice={[0:2], [0:3], [0:48], [0:4096]} | slice | bytes 4718592 | tf_op jit(solution)/shard_map/slice | solution.py:510
  63.1 3.2 %constant_dynamic-slice_fusion.5 = (bf16[2,3,48,1024]{3,0,2,1:T(2,128)(2,1)S(1)}, bf16[2,3,48,1024]{3,0,2,1:T(2,128)(2,1)S(1)}, bf16[2,3,48,1024]{3,0,2,1:T(2,128)(2,1)S(1)}, bf16[2,3,48,1024]{3,0,2,1:T(2,128)(2,1)}) fusion(bf16[2,3,48,4096]{3,0,2,1:T(2,128)(2,1)S(1)} %slice.6, s32[]{:T(128)S(6)} %select_n.86, s32[]{:T(128)S(6)} %select_n.84, ...), kind=kLoop, calls=%fused_computation.18 | loop fusion | bytes 4718608 | tf_op jit(solution)/shard_map/dynamic_slice | solution.py:493
  67.9 2.6 %collective-permute-start.11 = (bf16[2,3,48,1024]{3,0,2,1:T(2,128)(2,1)S(1)}, bf16[2,3,48,1024]{3,0,2,1:T(2,128)(2,1)}, u32[]{:S(2)}, u32[]{:S(2)}) collective-permute-start(bf16[2,3,48,1024]{3,0,2,1:T(2,128)(2,1)S(1)} %get-tuple-element.62), channel_id=1, source_target_pairs={{0,64},{64,128},{128,192},{192,0},{1,65},{65,129},{129,193},{193,1... | collective-permute-start | bytes 1769480 | tf_op jit(solution)/shard_map/ppermute | solution.py:473
  70.5 22.2 %collective-permute-done.9 = bf16[2,3,48,1024]{3,0,2,1:T(2,128)(2,1)} collective-permute-done((bf16[2,3,48,1024]{3,0,2,1:T(2,128)(2,1)S(1)}, bf16[2,3,48,1024]{3,0,2,1:T(2,128)(2,1)}, u32[]{:S(2)}, u32[]{:S(2)}) %collective-permute-start.9) | collective-permute-done | bytes 589856 | tf_op jit(solution)/shard_map/ppermute | solution.py:473
  94.5 7.0 %all-to-all-start.1 = ((bf16[16,24,2048]{2,1,0:T(8,128)(2,1)}), bf16[16,24,2048]{2,1,0:T(8,128)(2,1)}, u32[]{:S(2)}, u32[]{:S(2)}) async-start(bf16[16,24,2048]{2,1,0:T(8,128)(2,1)} %tail_pack.1), calls=%async_computation.1 | async-start | bytes 3145728 | tf_op jit(solution)/shard_map/all_to_all | solution.py:512
  105.6 2.6 %collective-permute-start.16 = (bf16[2,1,48,1024]{3,0,2,1:T(2,128)(2,1)S(1)}, bf16[2,1,48,1024]{3,0,2,1:T(2,128)(2,1)S(1)}, u32[]{:S(2)}, u32[]{:S(2)}) collective-permute-start(bf16[2,1,48,1024]{3,0,2,1:T(2,128)(2,1)S(1)} %get-tuple-element.72), channel_id=1, source_target_pairs={{0,128},{64,192},{128,0},{192,64},{1,129},{65,193},{129,1},{193,65... | collective-permute-start | bytes 589832 | tf_op jit(solution)/shard_map/ppermute | solution.py:473
  108.3 4.6 %lead_combine.1 = bf16[4,3,48,1024]{3,2,1,0:T(8,128)(2,1)S(1)} custom-call(bf16[16,48,2048]{2,1,0:T(8,128)(2,1)} %all-to-all-done.main_ref, f32[4,8,96]{2,1,0:T(8,128)S(1)} %get-tuple-element.40.near_ref), custom_call_target="tpu_custom_call" | custom-call | tf_op jit(solution)/shard_map/lead_combine/pallas_call | solution.py:251
  113.0 2.3 %collective-permute-start.14 = (bf16[3,48,1024]{2,1,0:T(8,128)(2,1)S(1)}, bf16[3,48,1024]{2,1,0:T(8,128)(2,1)S(1)}, u32[]{:S(2)}, u32[]{:S(2)}) collective-permute-start(bf16[3,48,1024]{2,1,0:T(8,128)(2,1)S(1)} %get-tuple-element.67), channel_id=1, source_target_pairs={{0,64},{64,128},{128,192},{192,0},{1,65},{65,129},{129,193},{193,1... | collective-permute-start | bytes 884744 | tf_op jit(solution)/shard_map/ppermute | solution.py:473
  118.8 7.9 %maximum_maximum_fusion = bf16[4,2,4,48,1024]{4,1,3,2,0:T(2,128)(2,1)S(1)} fusion(bf16[1,2,1,48,1024]{4,1,3,2,0:T(2,128)(2,1)S(1)} %bitcast.86, bf16[1,2,1,48,1024]{4,1,3,2,0:T(2,128)(2,1)S(1)} %bitcast.87, bf16[1,2,1,48,1024]{4,1,3,2,0:T(2,128)(2,1)S(1)} %bitcast.88, bf16[1,2,1,48,1024]{4,1,3,2,0:T(2,128)(2,1)S(1)} %get-tuple-element.70, ...), kind=kLoop, calls=%fused_computation | loop fusion | flops 11010048 | bytes 6291456 | tf_op jit(solution)/shard_map/concatenate | solution.py:519
  132.5 7.0 %all-to-all-done.1.received_ref = bf16[16,24,2048]{2,1,0:T(8,128)(2,1)} async-done(((bf16[16,24,2048]{2,1,0:T(8,128)(2,1)}), bf16[16,24,2048]{2,1,0:T(8,128)(2,1)}, u32[]{:S(2)}, u32[]{:S(2)}) %all-to-all-start.1) | async-done | bytes 1572896 | tf_op jit(solution)/shard_map/all_to_all | solution.py:512
  142.4 6.3 %tail_combine.1 = (bf16[4,4,48,1024]{3,2,1,0:T(8,128)(2,1)S(1)}, f32[4,32,192]{2,1,0:T(8,128)S(1)}) custom-call(s32[1]{0:T(128)} %bitcast.p_ref, bf16[16,24,2048]{2,1,0:T(8,128)(2,1)} %all-to-all-done.1.received_ref, f32[4,40,192]{2,1,0:T(8,128)S(1)} %copy-done.5, bf16[4,48,1024]{2,1,0:T(8,128)(2,1)S(1)} %constant_dynamic-slice_fusion.up_ref, ...), custom_call_target="tpu_custom_call" | custom-call | tf_op jit(solution)/shard_map/tail_combine/pallas_call | solution.py:337
  148.7 9.6 %all_to_all.25.sent_ref = f32[4,32,192]{2,1,0:T(8,128)S(1)} all-to-all(f32[4,32,192]{2,1,0:T(8,128)S(1)} %get-tuple-element.54), channel_id=1, replica_groups=mesh['pipe'=4,'expert'=16,'dp'=4] {'pipe'}, dimensions={0} | all-to-all | bytes 196608 | tf_op jit(solution)/shard_map/all_to_all | solution.py:527
  160.1 7.9 %all-to-all-start.3 = ((bf16[64,8,128]{2,1,0:T(8,128)(2,1)}), bf16[64,8,128]{2,1,0:T(8,128)(2,1)}, u32[]{:S(2)}, u32[]{:S(2)}) async-start(bf16[64,8,128]{2,1,0:T(8,128)(2,1)} %copy-done.15), calls=%async_computation.3 | async-start | bytes 262144 | tf_op jit(solution)/shard_map/all_to_all | solution.py:531
  173.8 3.3 %collective-permute-start.19 = (bf16[4,48,1024]{2,1,0:T(8,128)(2,1)}, bf16[4,48,1024]{2,1,0:T(8,128)(2,1)S(1)}, u32[]{:S(2)}, u32[]{:S(2)}) collective-permute-start(bf16[4,48,1024]{2,1,0:T(8,128)(2,1)} %get-tuple-element.59), channel_id=1, source_target_pairs={{0,128},{64,192},{128,0},{192,64},{1,129},{65,193},{129,1},{193,65... | collective-permute-start | bytes 1179656 | tf_op jit(solution)/shard_map/ppermute | solution.py:473
  180.9 8.7 %all-to-all-start.4 = ((bf16[64,8,128]{2,1,0:T(8,128)(2,1)}), bf16[64,8,128]{2,1,0:T(8,128)(2,1)S(1)}, u32[]{:S(2)}, u32[]{:S(2)}) async-start(bf16[64,8,128]{2,1,0:T(8,128)(2,1)} %broadcast_in_dim.16), calls=%async_computation.4 | async-start | bytes 262144 | tf_op jit(solution)/shard_map/all_to_all | solution.py:535
  189.6 5.2 %collective-permute-done.20.refs_3_ = bf16[4,48,1024]{2,1,0:T(8,128)(2,1)S(1)} collective-permute-done((bf16[4,48,1024]{2,1,0:T(8,128)(2,1)}, bf16[4,48,1024]{2,1,0:T(8,128)(2,1)S(1)}, u32[]{:S(2)}, u32[]{:S(2)}) %collective-permute-start.20) | collective-permute-done | bytes 393248 | tf_op jit(solution)/shard_map/ppermute | solution.py:473
  197.4 3.5 %all-to-all-done.4 = bf16[64,8,128]{2,1,0:T(8,128)(2,1)S(1)} async-done(((bf16[64,8,128]{2,1,0:T(8,128)(2,1)}), bf16[64,8,128]{2,1,0:T(8,128)(2,1)S(1)}, u32[]{:S(2)}, u32[]{:S(2)}) %all-to-all-start.4) | async-done | bytes 131104 | tf_op jit(solution)/shard_map/all_to_all | solution.py:535
  (100 shorter events, 51.5 us)
Async XLA Ops:
  5.9 88.6 %all-to-all-start = ((bf16[16,48,2048]{2,1,0:T(8,128)(2,1)}), bf16[16,48,2048]{2,1,0:T(8,128)(2,1)}, u32[]{:S(2)}, u32[]{:S(2)}) async-start(bf16[16,48,2048]{2,1,0:T(8,128)(2,1)} %lead_pack.1), calls=%async_computation | async-start | bytes 6291456 | tf_op jit(solution)/shard_map/all_to_all | solution.py:499
  18.7 37.9 %collective-permute-start = (bf16[12,16,1024]{2,1,0:T(8,128)(2,1)}, bf16[12,16,1024]{2,1,0:T(8,128)(2,1)}, u32[]{:S(2)}, u32[]{:S(2)}) collective-permute-start(bf16[12,16,1024]{2,1,0:T(8,128)(2,1)} %get-tuple-element.33), channel_id=1, source_target_pairs={{0,192},{64,0},{128,64},{192,128},{1,193},{65,1},{129,65},{193,129... | collective-permute-start | bytes 1179656 | tf_op jit(solution)/shard_map/ppermute | solution.py:473
  19.2 37.4 %collective-permute-start.1 = (bf16[12,16,1024]{2,1,0:T(8,128)(2,1)}, bf16[12,16,1024]{2,1,0:T(8,128)(2,1)}, u32[]{:S(2)}, u32[]{:S(2)}) collective-permute-start(bf16[12,16,1024]{2,1,0:T(8,128)(2,1)} %get-tuple-element.34), channel_id=1, source_target_pairs={{0,128},{64,192},{128,0},{192,64},{1,129},{65,193},{129,1},{193,65... | collective-permute-start | bytes 1179656 | tf_op jit(solution)/shard_map/ppermute | solution.py:473
  21.7 34.9 %collective-permute-start.2 = (bf16[12,16,1024]{2,1,0:T(8,128)(2,1)}, bf16[12,16,1024]{2,1,0:T(8,128)(2,1)}, u32[]{:S(2)}, u32[]{:S(2)}) collective-permute-start(bf16[12,16,1024]{2,1,0:T(8,128)(2,1)} %get-tuple-element.35), channel_id=1, source_target_pairs={{0,64},{64,128},{128,192},{192,0},{1,65},{65,129},{129,193},{193,1... | collective-permute-start | bytes 1179656 | tf_op jit(solution)/shard_map/ppermute | solution.py:473
  24.4 17.5 %collective-permute-start.5 = (f32[40,192]{1,0:T(8,128)S(1)}, f32[40,192]{1,0:T(8,128)S(1)}, u32[]{:S(2)}, u32[]{:S(2)}) collective-permute-start(f32[40,192]{1,0:T(8,128)S(1)} %get-tuple-element.36), channel_id=1, source_target_pairs={{0,64},{64,128},{128,192},{192,0},{1,65},{65,129},{129,193},{193,1... | collective-permute-start | bytes 92168 | tf_op jit(solution)/shard_map/ppermute | solution.py:473
  24.4 18.9 %collective-permute-start.4 = (f32[40,192]{1,0:T(8,128)S(1)}, f32[40,192]{1,0:T(8,128)S(1)}, u32[]{:S(2)}, u32[]{:S(2)}) collective-permute-start(f32[40,192]{1,0:T(8,128)S(1)} %get-tuple-element.36), channel_id=1, source_target_pairs={{0,128},{64,192},{128,0},{192,64},{1,129},{65,193},{129,1},{193,65... | collective-permute-start | bytes 92168 | tf_op jit(solution)/shard_map/ppermute | solution.py:473
  41.9 10.1 %collective-permute-start.8 = (bf16[16,1024]{1,0:T(8,128)(2,1)S(1)}, bf16[16,1024]{1,0:T(8,128)(2,1)S(1)}, u32[]{:S(2)}, u32[]{:S(2)}) collective-permute-start(bf16[16,1024]{1,0:T(8,128)(2,1)S(1)} %get-tuple-element.76), channel_id=1, source_target_pairs={{0,64},{64,128},{128,192},{192,0},{1,65},{65,129},{129,193},{193,1... | collective-permute-start | bytes 98312 | tf_op jit(solution)/shard_map/ppermute | solution.py:473
  43.3 4.0 %collective-permute-start.3 = (f32[40,192]{1,0:T(8,128)S(1)}, f32[40,192]{1,0:T(8,128)S(1)}, u32[]{:S(2)}, u32[]{:S(2)}) collective-permute-start(f32[40,192]{1,0:T(8,128)S(1)} %get-tuple-element.36), channel_id=1, source_target_pairs={{0,192},{64,0},{128,64},{192,128},{1,193},{65,1},{129,65},{193,129... | collective-permute-start | bytes 92168 | tf_op jit(solution)/shard_map/ppermute | solution.py:473
  47.3 6.7 %collective-permute-start.7 = (bf16[16,1024]{1,0:T(8,128)(2,1)S(1)}, bf16[16,1024]{1,0:T(8,128)(2,1)S(1)}, u32[]{:S(2)}, u32[]{:S(2)}) collective-permute-start(bf16[16,1024]{1,0:T(8,128)(2,1)S(1)} %get-tuple-element.77), channel_id=1, source_target_pairs={{0,128},{64,192},{128,0},{192,64},{1,129},{65,193},{129,1},{193,65... | collective-permute-start | bytes 98312 | tf_op jit(solution)/shard_map/ppermute | solution.py:473
  66.3 26.4 %collective-permute-start.9 = (bf16[2,3,48,1024]{3,0,2,1:T(2,128)(2,1)S(1)}, bf16[2,3,48,1024]{3,0,2,1:T(2,128)(2,1)}, u32[]{:S(2)}, u32[]{:S(2)}) collective-permute-start(bf16[2,3,48,1024]{3,0,2,1:T(2,128)(2,1)S(1)} %get-tuple-element.64), channel_id=1, source_target_pairs={{0,192},{64,0},{128,64},{192,128},{1,193},{65,1},{129,65},{193,129... | collective-permute-start | bytes 1769480 | tf_op jit(solution)/shard_map/ppermute | solution.py:473
  66.6 26.0 %collective-permute-start.10 = (bf16[2,3,48,1024]{3,0,2,1:T(2,128)(2,1)S(1)}, bf16[2,3,48,1024]{3,0,2,1:T(2,128)(2,1)}, u32[]{:S(2)}, u32[]{:S(2)}) collective-permute-start(bf16[2,3,48,1024]{3,0,2,1:T(2,128)(2,1)S(1)} %get-tuple-element.63), channel_id=1, source_target_pairs={{0,128},{64,192},{128,0},{192,64},{1,129},{65,193},{129,1},{193,65... | collective-permute-start | bytes 1769480 | tf_op jit(solution)/shard_map/ppermute | solution.py:473
  67.9 26.6 %collective-permute-start.11 = (bf16[2,3,48,1024]{3,0,2,1:T(2,128)(2,1)S(1)}, bf16[2,3,48,1024]{3,0,2,1:T(2,128)(2,1)}, u32[]{:S(2)}, u32[]{:S(2)}) collective-permute-start(bf16[2,3,48,1024]{3,0,2,1:T(2,128)(2,1)S(1)} %get-tuple-element.62), channel_id=1, source_target_pairs={{0,64},{64,128},{128,192},{192,0},{1,65},{65,129},{129,193},{193,1... | collective-permute-start | bytes 1769480 | tf_op jit(solution)/shard_map/ppermute | solution.py:473
  94.5 44.9 %all-to-all-start.1 = ((bf16[16,24,2048]{2,1,0:T(8,128)(2,1)}), bf16[16,24,2048]{2,1,0:T(8,128)(2,1)}, u32[]{:S(2)}, u32[]{:S(2)}) async-start(bf16[16,24,2048]{2,1,0:T(8,128)(2,1)} %tail_pack.1), calls=%async_computation.1 | async-start | bytes 3145728 | tf_op jit(solution)/shard_map/all_to_all | solution.py:512
  104.1 13.3 %collective-permute-start.17 = (bf16[2,1,48,1024]{3,0,2,1:T(2,128)(2,1)S(1)}, bf16[2,1,48,1024]{3,0,2,1:T(2,128)(2,1)S(1)}, u32[]{:S(2)}, u32[]{:S(2)}) collective-permute-start(bf16[2,1,48,1024]{3,0,2,1:T(2,128)(2,1)S(1)} %get-tuple-element.71), channel_id=1, source_target_pairs={{0,64},{64,128},{128,192},{192,0},{1,65},{65,129},{129,193},{193,1... | collective-permute-start | bytes 589832 | tf_op jit(solution)/shard_map/ppermute | solution.py:473
  105.6 13.1 %collective-permute-start.16 = (bf16[2,1,48,1024]{3,0,2,1:T(2,128)(2,1)S(1)}, bf16[2,1,48,1024]{3,0,2,1:T(2,128)(2,1)S(1)}, u32[]{:S(2)}, u32[]{:S(2)}) collective-permute-start(bf16[2,1,48,1024]{3,0,2,1:T(2,128)(2,1)S(1)} %get-tuple-element.72), channel_id=1, source_target_pairs={{0,128},{64,192},{128,0},{192,64},{1,129},{65,193},{129,1},{193,65... | collective-permute-start | bytes 589832 | tf_op jit(solution)/shard_map/ppermute | solution.py:473
  108.3 10.5 %collective-permute-start.15 = (bf16[2,1,48,1024]{3,0,2,1:T(2,128)(2,1)S(1)}, bf16[2,1,48,1024]{3,0,2,1:T(2,128)(2,1)S(1)}, u32[]{:S(2)}, u32[]{:S(2)}) collective-permute-start(bf16[2,1,48,1024]{3,0,2,1:T(2,128)(2,1)S(1)} %get-tuple-element.73), channel_id=1, source_target_pairs={{0,192},{64,0},{128,64},{192,128},{1,193},{65,1},{129,65},{193,129... | collective-permute-start | bytes 589832 | tf_op jit(solution)/shard_map/ppermute | solution.py:473
  113.0 18.3 %collective-permute-start.14 = (bf16[3,48,1024]{2,1,0:T(8,128)(2,1)S(1)}, bf16[3,48,1024]{2,1,0:T(8,128)(2,1)S(1)}, u32[]{:S(2)}, u32[]{:S(2)}) collective-permute-start(bf16[3,48,1024]{2,1,0:T(8,128)(2,1)S(1)} %get-tuple-element.67), channel_id=1, source_target_pairs={{0,64},{64,128},{128,192},{192,0},{1,65},{65,129},{129,193},{193,1... | collective-permute-start | bytes 884744 | tf_op jit(solution)/shard_map/ppermute | solution.py:473
  115.3 16.0 %collective-permute-start.13 = (bf16[3,48,1024]{2,1,0:T(8,128)(2,1)S(1)}, bf16[3,48,1024]{2,1,0:T(8,128)(2,1)S(1)}, u32[]{:S(2)}, u32[]{:S(2)}) collective-permute-start(bf16[3,48,1024]{2,1,0:T(8,128)(2,1)S(1)} %get-tuple-element.68), channel_id=1, source_target_pairs={{0,128},{64,192},{128,0},{192,64},{1,129},{65,193},{129,1},{193,65... | collective-permute-start | bytes 884744 | tf_op jit(solution)/shard_map/ppermute | solution.py:473
  117.5 13.8 %collective-permute-start.12 = (bf16[3,48,1024]{2,1,0:T(8,128)(2,1)S(1)}, bf16[3,48,1024]{2,1,0:T(8,128)(2,1)S(1)}, u32[]{:S(2)}, u32[]{:S(2)}) collective-permute-start(bf16[3,48,1024]{2,1,0:T(8,128)(2,1)S(1)} %get-tuple-element.69), channel_id=1, source_target_pairs={{0,192},{64,0},{128,64},{192,128},{1,193},{65,1},{129,65},{193,129... | collective-permute-start | bytes 884744 | tf_op jit(solution)/shard_map/ppermute | solution.py:473
  160.1 19.1 %all-to-all-start.3 = ((bf16[64,8,128]{2,1,0:T(8,128)(2,1)}), bf16[64,8,128]{2,1,0:T(8,128)(2,1)}, u32[]{:S(2)}, u32[]{:S(2)}) async-start(bf16[64,8,128]{2,1,0:T(8,128)(2,1)} %copy-done.15), calls=%async_computation.3 | async-start | bytes 262144 | tf_op jit(solution)/shard_map/all_to_all | solution.py:531
  173.6 16.0 %collective-permute-start.18 = (bf16[4,48,1024]{2,1,0:T(8,128)(2,1)}, bf16[4,48,1024]{2,1,0:T(8,128)(2,1)S(1)}, u32[]{:S(2)}, u32[]{:S(2)}) collective-permute-start(bf16[4,48,1024]{2,1,0:T(8,128)(2,1)} %get-tuple-element.58), channel_id=1, source_target_pairs={{0,64},{64,128},{128,192},{192,0},{1,65},{65,129},{129,193},{193,1... | collective-permute-start | bytes 1179656 | tf_op jit(solution)/shard_map/ppermute | solution.py:473
  173.8 15.8 %collective-permute-start.19 = (bf16[4,48,1024]{2,1,0:T(8,128)(2,1)}, bf16[4,48,1024]{2,1,0:T(8,128)(2,1)S(1)}, u32[]{:S(2)}, u32[]{:S(2)}) collective-permute-start(bf16[4,48,1024]{2,1,0:T(8,128)(2,1)} %get-tuple-element.59), channel_id=1, source_target_pairs={{0,128},{64,192},{128,0},{192,64},{1,129},{65,193},{129,1},{193,65... | collective-permute-start | bytes 1179656 | tf_op jit(solution)/shard_map/ppermute | solution.py:473
  177.1 17.6 %collective-permute-start.20 = (bf16[4,48,1024]{2,1,0:T(8,128)(2,1)}, bf16[4,48,1024]{2,1,0:T(8,128)(2,1)S(1)}, u32[]{:S(2)}, u32[]{:S(2)}) collective-permute-start(bf16[4,48,1024]{2,1,0:T(8,128)(2,1)} %get-tuple-element.60), channel_id=1, source_target_pairs={{0,192},{64,0},{128,64},{192,128},{1,193},{65,1},{129,65},{193,129... | collective-permute-start | bytes 1179656 | tf_op jit(solution)/shard_map/ppermute | solution.py:473
  180.9 20.0 %all-to-all-start.4 = ((bf16[64,8,128]{2,1,0:T(8,128)(2,1)}), bf16[64,8,128]{2,1,0:T(8,128)(2,1)S(1)}, u32[]{:S(2)}, u32[]{:S(2)}) async-start(bf16[64,8,128]{2,1,0:T(8,128)(2,1)} %broadcast_in_dim.16), calls=%async_computation.4 | async-start | bytes 262144 | tf_op jit(solution)/shard_map/all_to_all | solution.py:535
  (24 other events, 178.0 us)

commit v5 on v4

--- a/solution.py
+++ b/solution.py
@@ -186,22 +186,26 @@
     return {key: row for row, key in enumerate(found)}
 
 
-def couple_kernel(p_ref, saved_ref, w_ref, info_ref, out_ref):
+def couple_kernel(p_ref, early_ref, rest_ref, w_ref, info_ref, out_ref):
     p = p_ref[0]
     sections, experts, quarter = w_ref.shape
-    tokens = saved_ref.shape[2]
     table = pairs(sections)
-    for s in range(sections - 1):
-        j = (s - p) & (sections - 1)
-        for k in range(2):
-            saved = saved_ref[j, k]
-            for upper in range(s + 1, sections):
-                j2 = (upper - p) & (sections - 1)
-                part = lax.dot_general(w_ref[j2], saved, NT, preferred_element_type=F32)
-                for k2 in range(2):
-                    row = table[(s, k, upper, k2)]
-                    v = info_ref[j2, k2 * experts : (k2 + 1) * experts, :]
-                    out_ref[row : row + 1, :] = jnp.sum(part * v, axis=0, keepdims=True)
+    start = 0
+    for saved_ref in (early_ref, rest_ref):
+        tokens = saved_ref.shape[2] * saved_ref.shape[3]
+        lanes = slice(start, start + tokens)
+        for s in range(sections - 1):
+            j = (s - p) & (sections - 1)
+            for k in range(2):
+                saved = saved_ref[j, k].reshape(tokens, quarter)
+                for upper in range(s + 1, sections):
+                    j2 = (upper - p) & (sections - 1)
+                    part = lax.dot_general(w_ref[j2], saved, NT, preferred_element_type=F32)
+                    for k2 in range(2):
+                        row = table[(s, k, upper, k2)]
+                        v = info_ref[j2, k2 * experts : (k2 + 1) * experts, lanes]
+                        out_ref[row : row + 1, lanes] = jnp.sum(part * v, axis=0, keepdims=True)
+        start += tokens
 
 
 SCALAR = pl.BlockSpec(memory_space=pltpu.MemorySpace.SMEM)
@@ -209,16 +213,17 @@
 STAYS = pl.BlockSpec(memory_space=pl.ANY)
 
 
-def coupling(p, saved, w, info):
-    sections, _, tokens, _ = saved.shape
+def coupling(p, early, rest, w, info):
+    sections = early.shape[0]
+    tokens = info.shape[2]
     return pl.pallas_call(
         couple_kernel,
-        in_specs=[SCALAR, WHOLE, WHOLE, WHOLE],
+        in_specs=[SCALAR, WHOLE, WHOLE, WHOLE, WHOLE],
         out_specs=WHOLE,
         out_shape=jax.ShapeDtypeStruct((len(pairs(sections)), tokens), F32),
         compiler_params=params(32),
         name="coupling",
-    )(p, saved, w, info)
+    )(p, early, rest, w, info)
 
 
 def picked(gates, places, first, received):
@@ -263,57 +268,88 @@
 
 
 def tail_kernel(
-    p_ref, received_ref, info_ref, up_ref, lead_ref, saved_ref, links_ref,
-    back_ref, sent_ref, block_ref, last_ref, sum_ref, sems,
+    p_ref, received_hbm, info_hbm, up_hbm, lead_hbm, early_hbm, rest_hbm, links_hbm, back_hbm, sent_ref,
+    block_ref, info_ref, up_ref, lead_ref, saved_ref, links_ref, last_ref, sum_ref, back_ref,
+    block_sems, info_sem, up_sem, links_sem, lead_sems, saved_sems, back_sems,
 ):
     p = p_ref[0]
     sections, rows, quarter = sum_ref.shape
     _, experts, _, half = block_ref.shape
     micro = up_ref.shape[0]
     n = experts * TILE
-    copies = [
+    blocks = [
         pltpu.make_async_copy(
-            received_ref.at[:, pl.ds(TILE * unit, TILE), :], block_ref.at[unit], sems.at[unit]
+            received_hbm.at[:, pl.ds(TILE * unit, TILE), :], block_ref.at[unit], block_sems.at[unit]
         )
         for unit in range(3)
     ]
-    copies[2].start()
-    copies[0].start()
-    copies[1].start()
-    out_row, in_row = iotas((n, n))
-    order = (in_row == (out_row % experts) * TILE + out_row // experts).astype(BF16)
+    lead = [
+        pltpu.make_async_copy(lead_hbm.at[:, m], lead_ref.at[m], lead_sems.at[m]) for m in range(micro - 1)
+    ]
+    saved = [
+        pltpu.make_async_copy(early_hbm.at[:, :, m], saved_ref.at[m], saved_sems.at[m])
+        for m in range(micro - 1)
+    ]
+    saved.append(
+        pltpu.make_async_copy(rest_hbm.at[:, :, 0], saved_ref.at[micro - 1], saved_sems.at[micro - 1])
+    )
+    info = pltpu.make_async_copy(info_hbm, info_ref, info_sem)
+    up = pltpu.make_async_copy(up_hbm, up_ref, up_sem)
+    links = pltpu.make_async_copy(links_hbm, links_ref, links_sem)
+    backs = [
+        pltpu.make_async_copy(back_ref.at[m], back_hbm.at[:, m], back_sems.at[m]) for m in range(micro)
+    ]
+    for copy in [blocks[2], info, lead[0], up, saved[0], lead[1], saved[1], lead[2], saved[2]]:
+        copy.start()
+    for copy in [blocks[0], blocks[1], saved[3], links]:
+        copy.start()
+    out_row, in_row = iotas((2 * n, n))
+    within = out_row % (2 * experts)
+    order = in_row == (within % experts) * TILE + out_row // (2 * experts)
+    order = order.astype(BF16)
     lane = lax.broadcasted_iota(jnp.int32, (rows, 128), 1)
     row, column = iotas((2 * sections, 128))
     eye = (row == column).astype(F32)
-    copies[2].wait()
+    blocks[2].wait()
     last = block_ref[2].reshape(n, half)
     last_ref[...] = jnp.dot(order, last, preferred_element_type=F32).astype(BF16)
+    info.wait()
     for m in range(micro):
         if m == micro - 1:
-            copies[0].wait()
-            copies[1].wait()
+            blocks[0].wait()
+            blocks[1].wait()
+        else:
+            lead[m].wait()
         for j in range(sections):
             h, c = divmod(j, 2)
             columns = slice(c * quarter, (c + 1) * quarter)
             facts = info_ref[j, 2 * experts :, m * rows : (m + 1) * rows]
-            facts = jnp.concatenate([facts, facts], axis=1)
             gates = [facts[k : k + 1] for k in range(2)]
             places = [facts[2 + k : 3 + k].astype(jnp.int32) for k in range(2)]
-            start = (h * micro + m) * experts
-            total = picked(gates, places, n + m * experts, last_ref[start : start + experts, columns])
+            start = (h * micro + m) * 2 * experts
+            pick = split_pick(gates, places, n + m * experts, experts)
+            received = last_ref[start : start + 2 * experts, columns]
+            total = lax.dot_general(pick, received, TN, preferred_element_type=F32)
             if m == micro - 1:
                 main = block_ref[h, :, :, columns].reshape(n, quarter)
-                total = total + picked(gates, places, 0, main)
+                pick = split_pick(gates, places, 0, n)
+                total = total + lax.dot_general(
+                    pick, jnp.concatenate([main, main], axis=0), TN, preferred_element_type=F32
+                )
             else:
-                total = total + lead_ref[j, m].astype(F32)
+                total = total + lead_ref[m, j].astype(F32)
             sum_ref[j] = total
-            back_ref[j, m] = total.astype(BF16)
+            back_ref[m, j] = total.astype(BF16)
+        backs[m].start()
+        if m == 0:
+            up.wait()
+        saved[m].wait()
         base = up_ref[m].astype(F32)
         dots = jnp.zeros((rows, 128), F32)
         for s in reversed(range(sections)):
             j = (s - p) & (sections - 1)
             for k in range(2):
-                product = base * saved_ref[j, k, m * rows : (m + 1) * rows, :].astype(F32)
+                product = base * saved_ref[m, j, k].astype(F32)
                 part = product[:, :128]
                 for t in range(1, quarter // 128):
                     part = part + product[:, t * 128 : (t + 1) * 128]
@@ -326,35 +362,57 @@
         )
         for dest in range(sections):
             sent_ref[dest, : 2 * sections, m * rows : (m + 1) * rows] = dots
+    links.wait()
     for dest in range(sections):
         sent_ref[dest, 2 * sections :, :] = links_ref[...]
-
-
-def tail_combine(p, received, info, upstream, lead, saved, links):
-    sections, _, tokens, quarter = saved.shape
-    micro, rows, _ = upstream.shape
+    for copy in backs:
+        copy.wait()
+
+
+def split_pick(gates, places, first, n):
+    index = lax.broadcasted_iota(jnp.int32, (n, gates[0].shape[1]), 0) + first
+    pick = jnp.zeros(index.shape, F32)
+    for k in range(2):
+        pick = pick + jnp.where(index == places[k], gates[k], 0.0)
+    high = pick.astype(BF16).astype(F32)
+    return jnp.concatenate([high, pick - high], axis=0).astype(BF16)
+
+
+def tail_combine(p, received, info, upstream, lead, early, rest, links):
+    sections = early.shape[0]
+    micro, rows, quarter = upstream.shape
     experts, packed, half = received.shape
+    part = (sections, rows, quarter)
+    dma = pltpu.SemaphoreType.DMA
     return pl.pallas_call(
         tail_kernel,
-        in_specs=[SCALAR, STAYS] + [WHOLE] * 5,
-        out_specs=[WHOLE] * 2,
+        in_specs=[SCALAR] + [STAYS] * 7,
+        out_specs=[STAYS, WHOLE],
         out_shape=[
-            jax.ShapeDtypeStruct((sections, micro, rows, quarter), BF16),
-            jax.ShapeDtypeStruct((sections, 2 * sections + links.shape[0], tokens), F32),
+            pltpu.HBM((sections, micro, rows, quarter), BF16),
+            jax.ShapeDtypeStruct((sections, 2 * sections + links.shape[0], micro * rows), F32),
         ],
         scratch_shapes=[
             pltpu.VMEM((3, experts, TILE, half), BF16),
-            pltpu.VMEM((experts * TILE, half), BF16),
-            pltpu.VMEM((sections, rows, quarter), F32),
-            pltpu.SemaphoreType.DMA((3,)),
+            pltpu.VMEM(info.shape, F32),
+            pltpu.VMEM(upstream.shape, BF16),
+            pltpu.VMEM((micro - 1,) + part, BF16),
+            pltpu.VMEM((micro, sections, 2, rows, quarter), BF16),
+            pltpu.VMEM(links.shape, F32),
+            pltpu.VMEM((2 * experts * TILE, half), BF16),
+            pltpu.VMEM(part, F32),
+            pltpu.VMEM((micro,) + part, BF16),
+            dma((3,)), dma, dma, dma, dma((micro - 1,)), dma((micro,)), dma((micro,)),
         ],
         compiler_params=params(48),
         name="tail_combine",
-    )(p, received, info, upstream, lead, saved, links)
-
-
-def dense_kernel(micro, p_ref, sent_ref, info_ref, normed_ref, dense_ref, part_ref, rows_ref, sem):
-    copy = pltpu.make_async_copy(normed_ref, rows_ref, sem)
+    )(p, *[in_hbm(array) for array in (received, info, upstream, lead, early, rest, links)])
+
+
+def dense_kernel(
+    micro, p_ref, sent_ref, info_ref, normed_hbm, dense_hbm, part_hbm, rows_ref, dense_ref, part_ref, sems
+):
+    copy = pltpu.make_async_copy(normed_hbm, rows_ref, sems.at[0])
     copy.start()
     p = p_ref[0]
     sections = sent_ref.shape[0]
@@ -379,6 +437,8 @@
             dense = dense + value * info_ref[j, k * experts : (k + 1) * experts, :]
         dense_ref[s * experts : (s + 1) * experts, :] = dense.astype(BF16)
         own = jnp.where(p == s, dense, own)
+    out_dense = pltpu.make_async_copy(dense_ref, dense_hbm, sems.at[1])
+    out_dense.start()
     copy.wait()
     total = jnp.dot(own.astype(BF16), rows_ref[...], preferred_element_type=F32) * (1.0 / micro)
     cols = width // 128
@@ -386,59 +446,81 @@
         for c in range(cols):
             tile = total[r * 8 : (r + 1) * 8, c * 128 : (c + 1) * 128]
             part_ref[r * cols + c] = tile.astype(BF16)
+    out_part = pltpu.make_async_copy(part_ref, part_hbm, sems.at[2])
+    out_part.start()
+    out_dense.wait()
+    out_part.wait()
 
 
 def dense_terms(p, sent, info, normed, micro):
     sections, _, tokens = sent.shape
     width = normed.shape[1]
     experts = (info.shape[1] - 8) // 2
-    blocks = experts // 8 * (width // 128)
+    dense = (sections * experts, tokens)
+    part = (experts // 8 * (width // 128), 8, 128)
     return pl.pallas_call(
         functools.partial(dense_kernel, micro),
         in_specs=[SCALAR, WHOLE, WHOLE, STAYS],
-        out_specs=[WHOLE] * 2,
-        out_shape=[
-            jax.ShapeDtypeStruct((sections * experts, tokens), BF16),
-            jax.ShapeDtypeStruct((blocks, 8, 128), BF16),
+        out_specs=[STAYS] * 2,
+        out_shape=[jax.ShapeDtypeStruct(dense, BF16), pltpu.HBM(part, BF16)],
+        scratch_shapes=[
+            pltpu.VMEM((tokens, width), BF16),
+            pltpu.VMEM(dense, BF16),
+            pltpu.VMEM(part, BF16),
+            pltpu.SemaphoreType.DMA((3,)),
         ],
-        scratch_shapes=[pltpu.VMEM((tokens, width), BF16), pltpu.SemaphoreType.DMA],
         compiler_params=params(32),
         name="dense",
-    )(p, sent, info, normed)
-
-
-def grads_kernel(p_ref, up_ref, back_ref, dense_ref, w_ref, *refs):
+    )(p, sent, info, in_hbm(normed))
+
+
+def grads_kernel(p_ref, up_ref, back_hbm, dense_ref, w_ref, *refs):
+    outs = refs[:-5]
+    back_ref, total_ref, turn_ref, back_sems, out_sems = refs[-5:]
     p = p_ref[0]
-    outs, total_ref, turn_ref = refs[:-2], refs[-2], refs[-1]
-    sections, micro, rows, quarter = back_ref.shape
+    sections, micro, rows, quarter = turn_ref.shape
     experts = w_ref.shape[1]
+    copies = [
+        pltpu.make_async_copy(back_hbm.at[:, m], back_ref.at[m], back_sems.at[m]) for m in range(micro)
+    ]
+    for copy in copies:
+        copy.start()
     total_ref[...] = up_ref[...].astype(F32)
     for s in reversed(range(sections)):
         j = (s - p) & (sections - 1)
         dense = dense_ref[s * experts : (s + 1) * experts, :]
         term = lax.dot_general(dense, w_ref[j], TN, preferred_element_type=F32)
         for m in range(micro):
-            total = total_ref[m] + back_ref[j, m].astype(F32) + term[m * rows : (m + 1) * rows]
+            if s == sections - 1:
+                copies[m].wait()
+            total = total_ref[m] + back_ref[m, j].astype(F32) + term[m * rows : (m + 1) * rows]
             total_ref[m] = total
             turn_ref[j, m] = total.astype(BF16)
-    for j in range(sections):
-        outs[j][...] = turn_ref[j]
+    copies = [pltpu.make_async_copy(turn_ref.at[j], outs[j], out_sems.at[j]) for j in range(sections)]
+    for copy in copies:
+        copy.start()
+    for copy in copies:
+        copy.wait()
 
 
 def grads_of(p, upstream, back, dense, w):
     sections, micro, rows, quarter = back.shape
+    part = (micro, rows, quarter)
     return pl.pallas_call(
         grads_kernel,
-        in_specs=[SCALAR] + [WHOLE] * 4,
-        out_specs=[WHOLE] * sections,
-        out_shape=[jax.ShapeDtypeStruct((micro, rows, quarter), BF16)] * sections,
+        in_specs=[SCALAR, WHOLE, STAYS, WHOLE, WHOLE],
+        out_specs=[STAYS] * sections,
+        out_shape=[pltpu.HBM(part, BF16)] * sections,
         scratch_shapes=[
-            pltpu.VMEM((micro, rows, quarter), F32),
-            pltpu.VMEM((sections, micro, rows, quarter), BF16),
+            pltpu.VMEM((micro, sections, rows, quarter), BF16),
+            pltpu.VMEM(part, F32),
+            pltpu.VMEM((sections,) + part, BF16),
+            pltpu.SemaphoreType.DMA((micro,)),
+            pltpu.SemaphoreType.DMA((sections,)),
         ],
         compiler_params=params(40),
         name="grads",
-    )(p, upstream, back, dense, w)
+    )(p, upstream, in_hbm(back), dense, w)
 
 
 def join_kernel(p_ref, *refs):
@@ -498,17 +580,18 @@
     grads = in_hbm(jnp.transpose(expert_grads[0, :, 0, 0], (0, 2, 1, 3)))
     lead = lax.all_to_all(lead_pack(grads, micro - 1), "expert", 0, 0, tiled=True)
     late = spread(late_blocks(p, grads, sections))
+    saved = jnp.transpose(saved_out[0], (2, 0, 1, 3))
+    early = [part(saved[:, : micro - 1], j, 3) for j in range(sections)]
+    *early, late[1], late[2], late[3] = lax.optimization_barrier((*early, *late[1:]))
+    early = spread(early)
+    tail_send = tail_pack(late)
     info, near = gate_info(normed, w, jnp.transpose(routes[0], (2, 0, 1)).reshape(2, tokens), micro)
     info_all = jnp.stack(spread([info] * sections))
     w_all = jnp.stack(spread([part(w, j, 1) for j in range(sections)]))
-    tail_send = tail_pack(late)
-    saved_out, tail_send, info_all, w_all = lax.optimization_barrier(
-        (saved_out, tail_send, info_all, w_all)
+
+    lead, tail_send, info_all, w_all, *early = lax.optimization_barrier(
+        (lead, tail_send, info_all, w_all, *early)
     )
-
-    saved = jnp.transpose(saved_out[0], (2, 0, 1, 3))
-    early = spread([part(saved[:, : micro - 1], j, 3) for j in range(sections)])
-    lead, tail_send, *early = lax.optimization_barrier((lead, tail_send, *early))
     tail = lax.all_to_all(tail_send, "expert", 0, 0, tiled=True)
     rest = spread([part(saved[:, micro - 1 :], j, 3) for j in range(sections)])
     back = lead_combine(lead, near)
@@ -516,14 +599,14 @@
         lax.dynamic_index_in_dim(back, (section - j) % sections, 0, False) for j in range(sections)
     ]
     lead = jnp.stack(spread(lead))
-    saved = jnp.concatenate([jnp.stack(early), jnp.stack(rest)], axis=2)
-    saved = saved.reshape(sections, 2, tokens, quarter)
-    links = coupling(p, saved, w_all, info_all)
+    early = jnp.stack(early)
+    rest = jnp.stack(rest)
+    links = coupling(p, early, rest, w_all, info_all)
     up = part(upstream, 0, 2)
-    lead, info_all, w_all, saved, links, up = lax.optimization_barrier(
-        (lead, info_all, w_all, saved, links, up)
+    lead, info_all, w_all, early, rest, links, up = lax.optimization_barrier(
+        (lead, info_all, w_all, early, rest, links, up)
     )
-    back, sent = tail_combine(p, tail, info_all, up, lead, saved, links)
+    back, sent = tail_combine(p, tail, info_all, up, lead, early, rest, links)
     sent = lax.all_to_all(sent, "pipe", 0, 0, tiled=True)
     dense, partial = dense_terms(p, sent, info_all, normed, micro)
 
@@ -535,6 +618,7 @@
     total = lax.all_to_all(jnp.broadcast_to(total, partial.shape), axes, 0, 0, tiled=True)
     total = total.astype(F32).reshape(experts // 8, width // 128, 8, 128).transpose(0, 2, 1, 3)
     router_grad = total.reshape(experts, width).T
+    blocks[0] = in_hbm(blocks[0])
     return (join(p, blocks)[None], router_grad[None])
 
 

time: 203 us -> 190 us (0.936)
  other arithmetic: 12.1 us -> 4.11 us
  local copies, waits for them, and re-layouts: 22.9 us -> 16.3 us
  starting transfers between devices: 65.6 us -> 60.8 us
  Pallas kernels: 28.7 us -> 32.9 us
  waiting for transfers between devices: 61.8 us -> 64 us
    concatenate x1 -> x0, other arithmetic: 7.86 us -> none  [on_device(): saved = jnp.concatenate([jnp.stack(early), jnp.stack(rest)], axis=2)]
    unnamed x46 -> x27, local copies, waits for them, and re-layouts: 13 us -> 6.49 us
    all_to_all x1, starting transfers between devices: 8.67 us -> 6.2 us  [on_device(): lax.all_to_all(jnp.broadcast_to(total, partial.shape), axes, 0, 0, tiled=...]
    ppermute x21, starting transfers between devices: 33.4 us -> 31 us  [turned(): lax.ppermute(block, 'pipe', [(i, (i + distance) % n) for i in range(n)])]
    all_to_all x1, waiting for transfers between devices: 1.54 us -> 3.86 us  [on_device(): partial = lax.all_to_all(partial, axes, 0, 0, tiled=True)]
    another operation x0 -> x2, other arithmetic: none -> 2.1 us  [the longest x1 2 us: on_device(): early = jnp.stack(early)]
  transfers between devices with their start and end apart: 25 -> 25, of which waited for: 10 -> 14; matrix products, arithmetic and copies ran while one was open for 11% -> 9% of each run, Pallas kernels for 8% -> 10%
where the time goes in v5:
time: 190 us; the launch traced here: 189 us
  waiting for transfers between devices  64 us (34%)
  starting transfers between devices  60.8 us (32%)
  Pallas kernels  32.9 us (17%)
  local copies, waits for them, and re-layouts  16.3 us (9%)
  blocking collectives  10 us (5%)
  other arithmetic  4.11 us (2%)
    ppermute x21, waiting for transfers between devices, turned(): lax.ppermute(block, 'pipe', [(i, (i + distance) % n) for i in range(n)])  51.6 us
    ppermute x21, starting transfers between devices, turned(): lax.ppermute(block, 'pipe', [(i, (i + distance) % n) for i in range(n)])  31 us
    all_to_all x1, blocking collectives, on_device(): sent = lax.all_to_all(sent, 'pipe', 0, 0, tiled=True)  10 us
    all_to_all x1, starting transfers between devices, on_device(): lax.all_to_all(lead_pack(grads, micro - 1), 'expert', 0, 0, tiled=True)  8.62 us
    all_to_all x1, starting transfers between devices, on_device(): partial = lax.all_to_all(partial, axes, 0, 0, tiled=True)  8 us
    all_to_all x1, starting transfers between devices, on_device(): tail = lax.all_to_all(tail_send, 'expert', 0, 0, tiled=True)  7.02 us
    pallas_call x1, Pallas kernels, tail_combine(): pl.pallas_call(tail_kernel, in_specs=[SCALAR] + [STAYS] * 7, out_specs=[S...  6.59 us
    unnamed x27, local copies, waits for them, and re-layouts  6.49 us
  transfers between devices with their start and end apart: 25, of which 14 were waited for; matrix products, arithmetic and copies ran while one was open for 9% of the time, Pallas kernels for 10%

profile of v5, /device:TPU:8, one launch (start us, length us, event | category | flops | bytes accessed | tf_op | source)
XLA Modules:
  0.0 189.0 jit_solution(17132635465658144125)
XLA Ops:
  0.6 5.2 %lead_pack.1 = bf16[16,48,2048]{2,1,0:T(8,128)(2,1)} custom-call(bf16[4,9,16,4096]{3,2,1,0:T(8,128)(2,1)} %bitcast.78), custom_call_target="tpu_custom_call" | custom-call | tf_op jit(solution)/shard_map/lead_pack/pallas_call | solution.py:48
  5.9 8.6 %all-to-all-start = ((bf16[16,48,2048]{2,1,0:T(8,128)(2,1)}), bf16[16,48,2048]{2,1,0:T(8,128)(2,1)}, u32[]{:S(2)}, u32[]{:S(2)}) async-start(bf16[16,48,2048]{2,1,0:T(8,128)(2,1)} %lead_pack.1), calls=%async_computation | async-start | bytes 6291456 | tf_op jit(solution)/shard_map/all_to_all | solution.py:581
  14.5 3.3 %late_blocks.1 = (bf16[12,16,1024]{2,1,0:T(8,128)(2,1)S(1)}, bf16[12,16,1024]{2,1,0:T(8,128)(2,1)}, bf16[12,16,1024]{2,1,0:T(8,128)(2,1)}, bf16[12,16,1024]{2,1,0:T(8,128)(2,1)}) custom-call(s32[1]{0:T(128)} %bitcast.p_ref, bf16[4,9,16,4096]{3,2,1,0:T(8,128)(2,1)} %bitcast.79, bf16[4,9,16,4096]{3,2,1,0:T(8,128)(2,1)} %bitcast.80), custom_call_target="tpu_custom_call" | custom-call | tf_op jit(solution)/shard_map/late_blocks/pallas_call | solution.py:105
  23.4 4.0 %copy.15 = bf16[1,4,48,2,4096]{4,2,3,1,0:T(8,128)(2,1)S(1)} copy(bf16[1,4,48,2,4096]{4,3,2,1,0:T(2,128)(2,1)} %param.7) | data formatting | bytes 6291456 | tf_op args[1]
  30.8 3.3 %constant_dynamic-slice_fusion.5 = (bf16[2,3,48,1024]{3,2,0,1:T(8,128)(2,1)}, bf16[2,3,48,1024]{3,2,0,1:T(8,128)(2,1)}, bf16[2,3,48,1024]{3,2,0,1:T(8,128)(2,1)}, bf16[2,3,48,1024]{3,2,0,1:T(8,128)(2,1)}) fusion(bf16[2,3,48,4096]{3,2,0,1:T(8,128)(2,1)} %slice.6, s32[]{:T(128)S(6)} %select_n.86, s32[]{:T(128)S(6)} %select_n.84, s32[]{:T(128)S(6)} %select_n.82, ...), kind=kLoop, calls=%fused_computation.20 | loop fusion | bytes 4718608 | tf_op jit(solution)/shard_map/dynamic_slice | solution.py:575
  34.1 5.6 %collective-permute-done.1.refs_2_ = bf16[12,16,1024]{2,1,0:T(8,128)(2,1)} collective-permute-done((bf16[12,16,1024]{2,1,0:T(8,128)(2,1)}, bf16[12,16,1024]{2,1,0:T(8,128)(2,1)}, u32[]{:S(2)}, u32[]{:S(2)}) %collective-permute-start.1) | collective-permute-done | bytes 393248 | tf_op jit(solution)/shard_map/ppermute | solution.py:555
  40.4 2.9 %collective-permute-start.9 = (bf16[2,3,48,1024]{3,2,0,1:T(8,128)(2,1)}, bf16[2,3,48,1024]{3,2,0,1:T(8,128)(2,1)}, u32[]{:S(2)}, u32[]{:S(2)}) collective-permute-start(bf16[2,3,48,1024]{3,2,0,1:T(8,128)(2,1)} %get-tuple-element.47), channel_id=1, source_target_pairs={{0,192},{64,0},{128,64},{192,128},{1,193},{65,1},{129,65},{193,129... | collective-permute-start | bytes 1769480 | tf_op jit(solution)/shard_map/ppermute | solution.py:555
  48.2 23.2 %collective-permute-done.5 = f32[40,192]{1,0:T(8,128)S(1)} collective-permute-done((f32[40,192]{1,0:T(8,128)S(1)}, f32[40,192]{1,0:T(8,128)S(1)}, u32[]{:S(2)}, u32[]{:S(2)}) %collective-permute-start.5) | collective-permute-done | bytes 30752 | tf_op jit(solution)/shard_map/ppermute | solution.py:555
  71.4 2.9 %collective-permute-start.6 = (bf16[16,1024]{1,0:T(8,128)(2,1)S(1)}, bf16[16,1024]{1,0:T(8,128)(2,1)S(1)}, u32[]{:S(2)}, u32[]{:S(2)}) collective-permute-start(bf16[16,1024]{1,0:T(8,128)(2,1)S(1)} %get-tuple-element.87), channel_id=1, source_target_pairs={{0,192},{64,0},{128,64},{192,128},{1,193},{65,1},{129,65},{193,129... | collective-permute-start | bytes 98312 | tf_op jit(solution)/shard_map/ppermute | solution.py:555
  74.8 3.4 %collective-permute-done.3 = f32[40,192]{1,0:T(8,128)S(1)} collective-permute-done((f32[40,192]{1,0:T(8,128)S(1)}, f32[40,192]{1,0:T(8,128)S(1)}, u32[]{:S(2)}, u32[]{:S(2)}) %collective-permute-start.3) | collective-permute-done | bytes 30752 | tf_op jit(solution)/shard_map/ppermute | solution.py:555
  83.7 3.1 %tail_pack.1 = bf16[16,24,2048]{2,1,0:T(8,128)(2,1)} custom-call(bf16[12,16,1024]{2,1,0:T(8,128)(2,1)S(1)} %copy-done.8, bf16[12,16,1024]{2,1,0:T(8,128)(2,1)} %collective-permute-done.refs_1_, bf16[12,16,1024]{2,1,0:T(8,128)(2,1)} %collective-permute-done.1.refs_2_, bf16[12,16,1024]{2,1,0:T(8,128)(2,1)} %collective-permute-done.2.refs_3_), custom_call_target="tpu_custom_call" | custom-call | tf_op jit(solution)/shard_map/tail_pack/pallas_call | solution.py:83
  86.8 7.0 %all-to-all-start.1 = ((bf16[16,24,2048]{2,1,0:T(8,128)(2,1)}), bf16[16,24,2048]{2,1,0:T(8,128)(2,1)}, u32[]{:S(2)}, u32[]{:S(2)}) async-start(bf16[16,24,2048]{2,1,0:T(8,128)(2,1)} %tail_pack.1), calls=%async_computation.1 | async-start | bytes 3145728 | tf_op jit(solution)/shard_map/all_to_all | solution.py:595
  101.2 4.5 %lead_combine.1 = bf16[4,3,48,1024]{3,2,1,0:T(8,128)(2,1)S(1)} custom-call(bf16[16,48,2048]{2,1,0:T(8,128)(2,1)} %all-to-all-done.main_ref, f32[4,8,96]{2,1,0:T(8,128)S(1)} %get-tuple-element.51.near_ref), custom_call_target="tpu_custom_call" | custom-call | tf_op jit(solution)/shard_map/lead_combine/pallas_call | solution.py:256
  118.3 4.5 %collective-permute-done.12 = bf16[3,48,1024]{2,1,0:T(8,128)(2,1)S(1)} collective-permute-done((bf16[3,48,1024]{2,1,0:T(8,128)(2,1)S(1)}, bf16[3,48,1024]{2,1,0:T(8,128)(2,1)S(1)}, u32[]{:S(2)}, u32[]{:S(2)}) %collective-permute-start.12) | collective-permute-done | bytes 294944 | tf_op jit(solution)/shard_map/ppermute | solution.py:555
  125.7 6.0 %all-to-all-done.1.received_hbm = bf16[16,24,2048]{2,1,0:T(8,128)(2,1)} async-done(((bf16[16,24,2048]{2,1,0:T(8,128)(2,1)}), bf16[16,24,2048]{2,1,0:T(8,128)(2,1)}, u32[]{:S(2)}, u32[]{:S(2)}) %all-to-all-start.1) | async-done | bytes 1572896 | tf_op jit(solution)/shard_map/all_to_all | solution.py:595
  131.7 6.6 %tail_combine.1 = (bf16[4,4,48,1024]{3,2,1,0:T(8,128)(2,1)}, f32[4,32,192]{2,1,0:T(8,128)S(1)}) custom-call(s32[1]{0:T(128)} %bitcast.p_ref, bf16[16,24,2048]{2,1,0:T(8,128)(2,1)} %all-to-all-done.1.received_hbm, f32[4,40,192]{2,1,0:T(8,128)} %copy-done.4, bf16[4,48,1024]{2,1,0:T(8,128)(2,1)} %constant_dynamic-slice_fusion.up_hbm.up_ref, ...), custom_call_target="tpu_custom_call" | custom-call | tf_op jit(solution)/shard_map/tail_combine/pallas_call | solution.py:387
  138.3 10.0 %all_to_all.25.sent_ref = f32[4,32,192]{2,1,0:T(8,128)S(1)} all-to-all(f32[4,32,192]{2,1,0:T(8,128)S(1)} %get-tuple-element.66), channel_id=1, replica_groups=mesh['pipe'=4,'expert'=16,'dp'=4] {'pipe'}, dimensions={0} | all-to-all | bytes 196608 | tf_op jit(solution)/shard_map/all_to_all | solution.py:610
  150.8 8.0 %all-to-all-start.3 = ((bf16[64,8,128]{2,1,0:T(8,128)(2,1)}), bf16[64,8,128]{2,1,0:T(8,128)(2,1)S(1)}, u32[]{:S(2)}, u32[]{:S(2)}) async-start(bf16[64,8,128]{2,1,0:T(8,128)(2,1)} %get-tuple-element.73), calls=%async_computation.3 | async-start | bytes 262144 | tf_op jit(solution)/shard_map/all_to_all | solution.py:614
  158.8 3.1 %grads.1 = (bf16[4,48,1024]{2,1,0:T(8,128)(2,1)}, bf16[4,48,1024]{2,1,0:T(8,128)(2,1)}, bf16[4,48,1024]{2,1,0:T(8,128)(2,1)}, bf16[4,48,1024]{2,1,0:T(8,128)(2,1)}) custom-call(s32[1]{0:T(128)} %bitcast.p_ref, bf16[4,48,1024]{2,1,0:T(8,128)(2,1)S(1)} %copy-done.3, bf16[4,4,48,1024]{3,2,1,0:T(8,128)(2,1)} %get-tuple-element.65.back_hbm, ...), custom_call_target="tpu_custom_call" | custom-call | tf_op jit(solution)/shard_map/grads/pallas_call | solution.py:509
  162.2 3.3 %collective-permute-start.19 = (bf16[4,48,1024]{2,1,0:T(8,128)(2,1)}, bf16[4,48,1024]{2,1,0:T(8,128)(2,1)S(1)}, u32[]{:S(2)}, u32[]{:S(2)}) collective-permute-start(bf16[4,48,1024]{2,1,0:T(8,128)(2,1)} %get-tuple-element.71), channel_id=1, source_target_pairs={{0,128},{64,192},{128,0},{192,64},{1,129},{65,193},{129,1},{193,65... | collective-permute-start | bytes 1179656 | tf_op jit(solution)/shard_map/ppermute | solution.py:555
  166.1 3.9 %all-to-all-done.3 = bf16[64,8,128]{2,1,0:T(8,128)(2,1)S(1)} async-done(((bf16[64,8,128]{2,1,0:T(8,128)(2,1)}), bf16[64,8,128]{2,1,0:T(8,128)(2,1)S(1)}, u32[]{:S(2)}, u32[]{:S(2)}) %all-to-all-start.3) | async-done | bytes 131104 | tf_op jit(solution)/shard_map/all_to_all | solution.py:614
  170.7 6.2 %all-to-all-start.4 = ((bf16[64,8,128]{2,1,0:T(8,128)(2,1)}), bf16[64,8,128]{2,1,0:T(8,128)(2,1)S(1)}, u32[]{:S(2)}, u32[]{:S(2)}) async-start(bf16[64,8,128]{2,1,0:T(8,128)(2,1)} %broadcast_in_dim.16), calls=%async_computation.4 | async-start | bytes 262144 | tf_op jit(solution)/shard_map/all_to_all | solution.py:618
  176.9 6.2 %collective-permute-done.20.refs_3_ = bf16[4,48,1024]{2,1,0:T(8,128)(2,1)S(1)} collective-permute-done((bf16[4,48,1024]{2,1,0:T(8,128)(2,1)}, bf16[4,48,1024]{2,1,0:T(8,128)(2,1)S(1)}, u32[]{:S(2)}, u32[]{:S(2)}) %collective-permute-start.20) | collective-permute-done | bytes 393248 | tf_op jit(solution)/shard_map/ppermute | solution.py:555
  183.1 2.7 %join.1 = bf16[4,48,4096]{2,1,0:T(8,128)(2,1)} custom-call(s32[1]{0:T(128)} %bitcast.p_ref, bf16[4,48,1024]{2,1,0:T(8,128)(2,1)} %get-tuple-element.69.refs_0_, bf16[4,48,1024]{2,1,0:T(8,128)(2,1)S(1)} %collective-permute-done.18.refs_1_, bf16[4,48,1024]{2,1,0:T(8,128)(2,1)S(1)} %collective-permute-done.19.refs_2_, ...), custom_call_target="tpu_custom_call" | custom-call | tf_op jit(solution)/shard_map/join/pallas_call | solution.py:539
  (83 shorter events, 50.8 us)
Async XLA Ops:
  5.9 80.9 %all-to-all-start = ((bf16[16,48,2048]{2,1,0:T(8,128)(2,1)}), bf16[16,48,2048]{2,1,0:T(8,128)(2,1)}, u32[]{:S(2)}, u32[]{:S(2)}) async-start(bf16[16,48,2048]{2,1,0:T(8,128)(2,1)} %lead_pack.1), calls=%async_computation | async-start | bytes 6291456 | tf_op jit(solution)/shard_map/all_to_all | solution.py:581
  18.5 15.6 %collective-permute-start = (bf16[12,16,1024]{2,1,0:T(8,128)(2,1)}, bf16[12,16,1024]{2,1,0:T(8,128)(2,1)}, u32[]{:S(2)}, u32[]{:S(2)}) collective-permute-start(bf16[12,16,1024]{2,1,0:T(8,128)(2,1)} %get-tuple-element.39), channel_id=1, source_target_pairs={{0,192},{64,0},{128,64},{192,128},{1,193},{65,1},{129,65},{193,129... | collective-permute-start | bytes 1179656 | tf_op jit(solution)/shard_map/ppermute | solution.py:555
  19.0 20.7 %collective-permute-start.1 = (bf16[12,16,1024]{2,1,0:T(8,128)(2,1)}, bf16[12,16,1024]{2,1,0:T(8,128)(2,1)}, u32[]{:S(2)}, u32[]{:S(2)}) collective-permute-start(bf16[12,16,1024]{2,1,0:T(8,128)(2,1)} %get-tuple-element.40), channel_id=1, source_target_pairs={{0,128},{64,192},{128,0},{192,64},{1,129},{65,193},{129,1},{193,65... | collective-permute-start | bytes 1179656 | tf_op jit(solution)/shard_map/ppermute | solution.py:555
  21.5 18.9 %collective-permute-start.2 = (bf16[12,16,1024]{2,1,0:T(8,128)(2,1)}, bf16[12,16,1024]{2,1,0:T(8,128)(2,1)}, u32[]{:S(2)}, u32[]{:S(2)}) collective-permute-start(bf16[12,16,1024]{2,1,0:T(8,128)(2,1)} %get-tuple-element.41), channel_id=1, source_target_pairs={{0,64},{64,128},{128,192},{192,0},{1,65},{65,129},{129,193},{193,1... | collective-permute-start | bytes 1179656 | tf_op jit(solution)/shard_map/ppermute | solution.py:555
  40.4 46.3 %collective-permute-start.9 = (bf16[2,3,48,1024]{3,2,0,1:T(8,128)(2,1)}, bf16[2,3,48,1024]{3,2,0,1:T(8,128)(2,1)}, u32[]{:S(2)}, u32[]{:S(2)}) collective-permute-start(bf16[2,3,48,1024]{3,2,0,1:T(8,128)(2,1)} %get-tuple-element.47), channel_id=1, source_target_pairs={{0,192},{64,0},{128,64},{192,128},{1,193},{65,1},{129,65},{193,129... | collective-permute-start | bytes 1769480 | tf_op jit(solution)/shard_map/ppermute | solution.py:555
  43.3 43.5 %collective-permute-start.10 = (bf16[2,3,48,1024]{3,2,0,1:T(8,128)(2,1)}, bf16[2,3,48,1024]{3,2,0,1:T(8,128)(2,1)}, u32[]{:S(2)}, u32[]{:S(2)}) collective-permute-start(bf16[2,3,48,1024]{3,2,0,1:T(8,128)(2,1)} %get-tuple-element.48), channel_id=1, source_target_pairs={{0,128},{64,192},{128,0},{192,64},{1,129},{65,193},{129,1},{193,65... | collective-permute-start | bytes 1769480 | tf_op jit(solution)/shard_map/ppermute | solution.py:555
  43.3 43.5 %collective-permute-start.11 = (bf16[2,3,48,1024]{3,2,0,1:T(8,128)(2,1)}, bf16[2,3,48,1024]{3,2,0,1:T(8,128)(2,1)}, u32[]{:S(2)}, u32[]{:S(2)}) collective-permute-start(bf16[2,3,48,1024]{3,2,0,1:T(8,128)(2,1)} %get-tuple-element.49), channel_id=1, source_target_pairs={{0,64},{64,128},{128,192},{192,0},{1,65},{65,129},{129,193},{193,1... | collective-permute-start | bytes 1769480 | tf_op jit(solution)/shard_map/ppermute | solution.py:555
  46.1 25.3 %collective-permute-start.5 = (f32[40,192]{1,0:T(8,128)S(1)}, f32[40,192]{1,0:T(8,128)S(1)}, u32[]{:S(2)}, u32[]{:S(2)}) collective-permute-start(f32[40,192]{1,0:T(8,128)S(1)} %get-tuple-element.45), channel_id=1, source_target_pairs={{0,64},{64,128},{128,192},{192,0},{1,65},{65,129},{129,193},{193,1... | collective-permute-start | bytes 92168 | tf_op jit(solution)/shard_map/ppermute | solution.py:555
  48.2 26.1 %collective-permute-start.4 = (f32[40,192]{1,0:T(8,128)S(1)}, f32[40,192]{1,0:T(8,128)S(1)}, u32[]{:S(2)}, u32[]{:S(2)}) collective-permute-start(f32[40,192]{1,0:T(8,128)S(1)} %get-tuple-element.45), channel_id=1, source_target_pairs={{0,128},{64,192},{128,0},{192,64},{1,129},{65,193},{129,1},{193,65... | collective-permute-start | bytes 92168 | tf_op jit(solution)/shard_map/ppermute | solution.py:555
  71.4 6.9 %collective-permute-start.6 = (bf16[16,1024]{1,0:T(8,128)(2,1)S(1)}, bf16[16,1024]{1,0:T(8,128)(2,1)S(1)}, u32[]{:S(2)}, u32[]{:S(2)}) collective-permute-start(bf16[16,1024]{1,0:T(8,128)(2,1)S(1)} %get-tuple-element.87), channel_id=1, source_target_pairs={{0,192},{64,0},{128,64},{192,128},{1,193},{65,1},{129,65},{193,129... | collective-permute-start | bytes 98312 | tf_op jit(solution)/shard_map/ppermute | solution.py:555
  74.2 4.0 %collective-permute-start.3 = (f32[40,192]{1,0:T(8,128)S(1)}, f32[40,192]{1,0:T(8,128)S(1)}, u32[]{:S(2)}, u32[]{:S(2)}) collective-permute-start(f32[40,192]{1,0:T(8,128)S(1)} %get-tuple-element.45), channel_id=1, source_target_pairs={{0,192},{64,0},{128,64},{192,128},{1,193},{65,1},{129,65},{193,129... | collective-permute-start | bytes 92168 | tf_op jit(solution)/shard_map/ppermute | solution.py:555
  78.2 5.4 %collective-permute-start.7 = (bf16[16,1024]{1,0:T(8,128)(2,1)S(1)}, bf16[16,1024]{1,0:T(8,128)(2,1)S(1)}, u32[]{:S(2)}, u32[]{:S(2)}) collective-permute-start(bf16[16,1024]{1,0:T(8,128)(2,1)S(1)} %get-tuple-element.89), channel_id=1, source_target_pairs={{0,128},{64,192},{128,0},{192,64},{1,129},{65,193},{129,1},{193,65... | collective-permute-start | bytes 98312 | tf_op jit(solution)/shard_map/ppermute | solution.py:555
  86.8 44.9 %all-to-all-start.1 = ((bf16[16,24,2048]{2,1,0:T(8,128)(2,1)}), bf16[16,24,2048]{2,1,0:T(8,128)(2,1)}, u32[]{:S(2)}, u32[]{:S(2)}) async-start(bf16[16,24,2048]{2,1,0:T(8,128)(2,1)} %tail_pack.1), calls=%async_computation.1 | async-start | bytes 3145728 | tf_op jit(solution)/shard_map/all_to_all | solution.py:595
  95.1 14.2 %collective-permute-start.17 = (bf16[2,1,48,1024]{3,2,0,1:T(8,128)(2,1)S(1)}, bf16[2,1,48,1024]{3,2,0,1:T(8,128)(2,1)S(1)}, u32[]{:S(2)}, u32[]{:S(2)}) collective-permute-start(bf16[2,1,48,1024]{3,2,0,1:T(8,128)(2,1)S(1)} %get-tuple-element.83), channel_id=1, source_target_pairs={{0,64},{64,128},{128,192},{192,0},{1,65},{65,129},{129,193},{193,1... | collective-permute-start | bytes 589832 | tf_op jit(solution)/shard_map/ppermute | solution.py:555
  97.0 12.3 %collective-permute-start.16 = (bf16[2,1,48,1024]{3,2,0,1:T(8,128)(2,1)S(1)}, bf16[2,1,48,1024]{3,2,0,1:T(8,128)(2,1)S(1)}, u32[]{:S(2)}, u32[]{:S(2)}) collective-permute-start(bf16[2,1,48,1024]{3,2,0,1:T(8,128)(2,1)S(1)} %get-tuple-element.84), channel_id=1, source_target_pairs={{0,128},{64,192},{128,0},{192,64},{1,129},{65,193},{129,1},{193,65... | collective-permute-start | bytes 589832 | tf_op jit(solution)/shard_map/ppermute | solution.py:555
  99.3 10.3 %collective-permute-start.15 = (bf16[2,1,48,1024]{3,2,0,1:T(8,128)(2,1)S(1)}, bf16[2,1,48,1024]{3,2,0,1:T(8,128)(2,1)S(1)}, u32[]{:S(2)}, u32[]{:S(2)}) collective-permute-start(bf16[2,1,48,1024]{3,2,0,1:T(8,128)(2,1)S(1)} %get-tuple-element.85), channel_id=1, source_target_pairs={{0,192},{64,0},{128,64},{192,128},{1,193},{65,1},{129,65},{193,129... | collective-permute-start | bytes 589832 | tf_op jit(solution)/shard_map/ppermute | solution.py:555
  105.9 10.0 %collective-permute-start.14 = (bf16[3,48,1024]{2,1,0:T(8,128)(2,1)S(1)}, bf16[3,48,1024]{2,1,0:T(8,128)(2,1)S(1)}, u32[]{:S(2)}, u32[]{:S(2)}) collective-permute-start(bf16[3,48,1024]{2,1,0:T(8,128)(2,1)S(1)} %get-tuple-element.79), channel_id=1, source_target_pairs={{0,64},{64,128},{128,192},{192,0},{1,65},{65,129},{129,193},{193,1... | collective-permute-start | bytes 884744 | tf_op jit(solution)/shard_map/ppermute | solution.py:555
  106.8 11.5 %collective-permute-start.13 = (bf16[3,48,1024]{2,1,0:T(8,128)(2,1)S(1)}, bf16[3,48,1024]{2,1,0:T(8,128)(2,1)S(1)}, u32[]{:S(2)}, u32[]{:S(2)}) collective-permute-start(bf16[3,48,1024]{2,1,0:T(8,128)(2,1)S(1)} %get-tuple-element.80), channel_id=1, source_target_pairs={{0,128},{64,192},{128,0},{192,64},{1,129},{65,193},{129,1},{193,65... | collective-permute-start | bytes 884744 | tf_op jit(solution)/shard_map/ppermute | solution.py:555
  109.3 13.5 %collective-permute-start.12 = (bf16[3,48,1024]{2,1,0:T(8,128)(2,1)S(1)}, bf16[3,48,1024]{2,1,0:T(8,128)(2,1)S(1)}, u32[]{:S(2)}, u32[]{:S(2)}) collective-permute-start(bf16[3,48,1024]{2,1,0:T(8,128)(2,1)S(1)} %get-tuple-element.81), channel_id=1, source_target_pairs={{0,192},{64,0},{128,64},{192,128},{1,193},{65,1},{129,65},{193,129... | collective-permute-start | bytes 884744 | tf_op jit(solution)/shard_map/ppermute | solution.py:555
  150.8 19.2 %all-to-all-start.3 = ((bf16[64,8,128]{2,1,0:T(8,128)(2,1)}), bf16[64,8,128]{2,1,0:T(8,128)(2,1)S(1)}, u32[]{:S(2)}, u32[]{:S(2)}) async-start(bf16[64,8,128]{2,1,0:T(8,128)(2,1)} %get-tuple-element.73), calls=%async_computation.3 | async-start | bytes 262144 | tf_op jit(solution)/shard_map/all_to_all | solution.py:614
  161.9 15.0 %collective-permute-start.18 = (bf16[4,48,1024]{2,1,0:T(8,128)(2,1)}, bf16[4,48,1024]{2,1,0:T(8,128)(2,1)S(1)}, u32[]{:S(2)}, u32[]{:S(2)}) collective-permute-start(bf16[4,48,1024]{2,1,0:T(8,128)(2,1)} %get-tuple-element.70), channel_id=1, source_target_pairs={{0,64},{64,128},{128,192},{192,0},{1,65},{65,129},{129,193},{193,1... | collective-permute-start | bytes 1179656 | tf_op jit(solution)/shard_map/ppermute | solution.py:555
  162.2 14.7 %collective-permute-start.19 = (bf16[4,48,1024]{2,1,0:T(8,128)(2,1)}, bf16[4,48,1024]{2,1,0:T(8,128)(2,1)S(1)}, u32[]{:S(2)}, u32[]{:S(2)}) collective-permute-start(bf16[4,48,1024]{2,1,0:T(8,128)(2,1)} %get-tuple-element.71), channel_id=1, source_target_pairs={{0,128},{64,192},{128,0},{192,64},{1,129},{65,193},{129,1},{193,65... | collective-permute-start | bytes 1179656 | tf_op jit(solution)/shard_map/ppermute | solution.py:555
  165.5 17.6 %collective-permute-start.20 = (bf16[4,48,1024]{2,1,0:T(8,128)(2,1)}, bf16[4,48,1024]{2,1,0:T(8,128)(2,1)S(1)}, u32[]{:S(2)}, u32[]{:S(2)}) collective-permute-start(bf16[4,48,1024]{2,1,0:T(8,128)(2,1)} %get-tuple-element.72), channel_id=1, source_target_pairs={{0,192},{64,0},{128,64},{192,128},{1,193},{65,1},{129,65},{193,129... | collective-permute-start | bytes 1179656 | tf_op jit(solution)/shard_map/ppermute | solution.py:555
  170.7 17.6 %all-to-all-start.4 = ((bf16[64,8,128]{2,1,0:T(8,128)(2,1)}), bf16[64,8,128]{2,1,0:T(8,128)(2,1)S(1)}, u32[]{:S(2)}, u32[]{:S(2)}) async-start(bf16[64,8,128]{2,1,0:T(8,128)(2,1)} %broadcast_in_dim.16), calls=%async_computation.4 | async-start | bytes 262144 | tf_op jit(solution)/shard_map/all_to_all | solution.py:618
  (14 other events, 279.3 us)

commit v6 on v5

--- a/solution.py
+++ b/solution.py
@@ -15,6 +15,11 @@
 TILE = 8
 
 
+SCALAR = pl.BlockSpec(memory_space=pltpu.MemorySpace.SMEM)
+WHOLE = pl.BlockSpec(memory_space=pltpu.MemorySpace.VMEM)
+STAYS = pl.BlockSpec(memory_space=pl.ANY)
+
+
 def params(mib):
     return pltpu.CompilerParams(vmem_limit_bytes=mib << 20)
 
@@ -32,14 +37,31 @@
     return (in_row == (out_row % slots) * dests + out_row // slots).astype(BF16)
 
 
-def lead_pack_kernel(grads_ref, out_ref):
-    _, slots, dests, width = grads_ref.shape
+def lead_pack_kernel(grads_hbm, out_hbm, grads_ref, out_ref, in_sems, out_sems):
+    count, slots, dests, width = grads_ref.shape
     half = width // 2
+    reads = [
+        pltpu.make_async_copy(grads_hbm.at[m, pl.ds(0, slots)], grads_ref.at[m], in_sems.at[m])
+        for m in range(count)
+    ]
+    for copy in reads:
+        copy.start()
     swap = swap_matrix(slots, dests)
-    for h in range(2):
-        rows = grads_ref[0, :, :, h * half : (h + 1) * half].reshape(slots * dests, half)
-        moved = jnp.dot(swap, rows, preferred_element_type=F32)
-        out_ref[:, h * slots : (h + 1) * slots, :] = moved.reshape(dests, slots, half).astype(BF16)
+    writes = []
+    for m in range(count):
+        reads[m].wait()
+        for h in range(2):
+            unit = 2 * m + h
+            rows = grads_ref[m, :, :, h * half : (h + 1) * half].reshape(slots * dests, half)
+            moved = jnp.dot(swap, rows, preferred_element_type=F32)
+            out_ref[unit] = moved.reshape(dests, slots, half).astype(BF16)
+            copy = pltpu.make_async_copy(
+                out_ref.at[unit], out_hbm.at[:, pl.ds(unit * slots, slots), :], out_sems.at[unit]
+            )
+            copy.start()
+            writes.append(copy)
+    for copy in writes:
+        copy.wait()
 
 
 def lead_pack(grads, count):
@@ -47,10 +69,15 @@
     half = width // 2
     return pl.pallas_call(
         lead_pack_kernel,
-        grid=(count,),
-        in_specs=[pl.BlockSpec((1, TILE, dests, width), lambda m: (m, 0, 0, 0))],
-        out_specs=pl.BlockSpec((dests, 2 * TILE, half), lambda m: (0, m, 0)),
+        in_specs=[STAYS],
+        out_specs=STAYS,
         out_shape=pltpu.HBM((dests, 2 * TILE * count, half), BF16),
+        scratch_shapes=[
+            pltpu.VMEM((count, TILE, dests, width), BF16),
+            pltpu.VMEM((2 * count, dests, TILE, half), BF16),
+            pltpu.SemaphoreType.DMA((count,)),
+            pltpu.SemaphoreType.DMA((2 * count,)),
+        ],
         compiler_params=params(40),
         name="lead_pack",
     )(grads)
@@ -186,9 +213,19 @@
     return {key: row for row, key in enumerate(found)}
 
 
-def couple_kernel(p_ref, early_ref, rest_ref, w_ref, info_ref, out_ref):
+def couple_kernel(p_ref, w_ref, info_ref, *refs):
+    sections, experts, quarter = w_ref.shape
+    early, rest = refs[:sections], refs[sections : 2 * sections]
+    out_ref, early_ref, rest_ref, sems = refs[2 * sections :]
+    copies = []
+    for j in range(sections):
+        copies.append(pltpu.make_async_copy(early[j], early_ref.at[j], sems.at[0, j]))
+        copies.append(pltpu.make_async_copy(rest[j], rest_ref.at[j], sems.at[1, j]))
+    for copy in copies:
+        copy.start()
+    for copy in copies:
+        copy.wait()
     p = p_ref[0]
-    sections, experts, quarter = w_ref.shape
     table = pairs(sections)
     start = 0
     for saved_ref in (early_ref, rest_ref):
@@ -208,22 +245,22 @@
         start += tokens
 
 
-SCALAR = pl.BlockSpec(memory_space=pltpu.MemorySpace.SMEM)
-WHOLE = pl.BlockSpec(memory_space=pltpu.MemorySpace.VMEM)
-STAYS = pl.BlockSpec(memory_space=pl.ANY)
-
-
 def coupling(p, early, rest, w, info):
-    sections = early.shape[0]
+    sections = len(early)
     tokens = info.shape[2]
     return pl.pallas_call(
         couple_kernel,
-        in_specs=[SCALAR, WHOLE, WHOLE, WHOLE, WHOLE],
+        in_specs=[SCALAR, WHOLE, WHOLE] + [STAYS] * (2 * sections),
         out_specs=WHOLE,
         out_shape=jax.ShapeDtypeStruct((len(pairs(sections)), tokens), F32),
+        scratch_shapes=[
+            pltpu.VMEM((sections,) + early[0].shape, BF16),
+            pltpu.VMEM((sections,) + rest[0].shape, BF16),
+            pltpu.SemaphoreType.DMA((2, sections)),
+        ],
         compiler_params=params(32),
         name="coupling",
-    )(p, early, rest, w, info)
+    )(p, w, info, *early, *rest)
 
 
 def picked(gates, places, first, received):
@@ -267,13 +304,14 @@
     )(received, near)
 
 
-def tail_kernel(
-    p_ref, received_hbm, info_hbm, up_hbm, lead_hbm, early_hbm, rest_hbm, links_hbm, back_hbm, sent_ref,
-    block_ref, info_ref, up_ref, lead_ref, saved_ref, links_ref, last_ref, sum_ref, back_ref,
-    block_sems, info_sem, up_sem, links_sem, lead_sems, saved_sems, back_sems,
-):
+def tail_kernel(p_ref, received_hbm, info_hbm, up_hbm, links_hbm, *refs):
+    sections = info_hbm.shape[0]
+    lead_hbm, early_hbm, rest_hbm = [refs[i * sections : (i + 1) * sections] for i in range(3)]
+    back_hbm, sent_ref, block_ref, info_ref, up_ref, lead_ref, saved_ref = refs[3 * sections :][:7]
+    links_ref, last_ref, sum_ref, back_ref = refs[3 * sections + 7 :][:4]
+    block_sems, info_sem, up_sem, links_sem, lead_sems, saved_sems, back_sems = refs[3 * sections + 11 :]
     p = p_ref[0]
-    sections, rows, quarter = sum_ref.shape
+    _, rows, quarter = sum_ref.shape
     _, experts, _, half = block_ref.shape
     micro = up_ref.shape[0]
     n = experts * TILE
@@ -284,24 +322,32 @@
         for unit in range(3)
     ]
     lead = [
-        pltpu.make_async_copy(lead_hbm.at[:, m], lead_ref.at[m], lead_sems.at[m]) for m in range(micro - 1)
+        [
+            pltpu.make_async_copy(lead_hbm[j].at[m], lead_ref.at[m, j], lead_sems.at[m, j])
+            for j in range(sections)
+        ]
+        for m in range(micro - 1)
     ]
     saved = [
-        pltpu.make_async_copy(early_hbm.at[:, :, m], saved_ref.at[m], saved_sems.at[m])
-        for m in range(micro - 1)
+        [
+            pltpu.make_async_copy(
+                early_hbm[j].at[:, m] if m < micro - 1 else rest_hbm[j].at[:, 0],
+                saved_ref.at[m, j],
+                saved_sems.at[m, j],
+            )
+            for j in range(sections)
+        ]
+        for m in range(micro)
     ]
-    saved.append(
-        pltpu.make_async_copy(rest_hbm.at[:, :, 0], saved_ref.at[micro - 1], saved_sems.at[micro - 1])
-    )
     info = pltpu.make_async_copy(info_hbm, info_ref, info_sem)
     up = pltpu.make_async_copy(up_hbm, up_ref, up_sem)
     links = pltpu.make_async_copy(links_hbm, links_ref, links_sem)
     backs = [
         pltpu.make_async_copy(back_ref.at[m], back_hbm.at[:, m], back_sems.at[m]) for m in range(micro)
     ]
-    for copy in [blocks[2], info, lead[0], up, saved[0], lead[1], saved[1], lead[2], saved[2]]:
+    for copy in [blocks[2], info] + lead[0] + [up] + saved[0] + lead[1] + saved[1] + lead[2] + saved[2]:
         copy.start()
-    for copy in [blocks[0], blocks[1], saved[3], links]:
+    for copy in blocks[:2] + saved[3] + [links]:
         copy.start()
     out_row, in_row = iotas((2 * n, n))
     within = out_row % (2 * experts)
@@ -318,8 +364,6 @@
         if m == micro - 1:
             blocks[0].wait()
             blocks[1].wait()
-        else:
-            lead[m].wait()
         for j in range(sections):
             h, c = divmod(j, 2)
             columns = slice(c * quarter, (c + 1) * quarter)
@@ -337,13 +381,15 @@
                     pick, jnp.concatenate([main, main], axis=0), TN, preferred_element_type=F32
                 )
             else:
+                lead[m][j].wait()
                 total = total + lead_ref[m, j].astype(F32)
             sum_ref[j] = total
             back_ref[m, j] = total.astype(BF16)
         backs[m].start()
         if m == 0:
             up.wait()
-        saved[m].wait()
+        for copy in saved[m]:
+            copy.wait()
         base = up_ref[m].astype(F32)
         dots = jnp.zeros((rows, 128), F32)
         for s in reversed(range(sections)):
@@ -378,15 +424,16 @@
     return jnp.concatenate([high, pick - high], axis=0).astype(BF16)
 
 
-def tail_combine(p, received, info, upstream, lead, early, rest, links):
-    sections = early.shape[0]
+def tail_combine(p, received, info, upstream, links, lead, early, rest):
+    sections = len(early)
     micro, rows, quarter = upstream.shape
     experts, packed, half = received.shape
     part = (sections, rows, quarter)
     dma = pltpu.SemaphoreType.DMA
+    operands = [received, info, upstream, links, *lead, *early, *rest]
     return pl.pallas_call(
         tail_kernel,
-        in_specs=[SCALAR] + [STAYS] * 7,
+        in_specs=[SCALAR] + [STAYS] * len(operands),
         out_specs=[STAYS, WHOLE],
         out_shape=[
             pltpu.HBM((sections, micro, rows, quarter), BF16),
@@ -402,18 +449,16 @@
             pltpu.VMEM((2 * experts * TILE, half), BF16),
             pltpu.VMEM(part, F32),
             pltpu.VMEM((micro,) + part, BF16),
-            dma((3,)), dma, dma, dma, dma((micro - 1,)), dma((micro,)), dma((micro,)),
+            dma((3,)), dma, dma, dma, dma((micro - 1, sections)), dma((micro, sections)), dma((micro,)),
         ],
         compiler_params=params(48),
         name="tail_combine",
-    )(p, *[in_hbm(array) for array in (received, info, upstream, lead, early, rest, links)])
+    )(p, *[in_hbm(array) for array in operands])
 
 
 def dense_kernel(
-    micro, p_ref, sent_ref, info_ref, normed_hbm, dense_hbm, part_hbm, rows_ref, dense_ref, part_ref, sems
+    micro, p_ref, sent_ref, info_ref, rows_ref, dense_hbm, part_hbm, dense_ref, part_ref, sems
 ):
-    copy = pltpu.make_async_copy(normed_hbm, rows_ref, sems.at[0])
-    copy.start()
     p = p_ref[0]
     sections = sent_ref.shape[0]
     tokens, width = rows_ref.shape
@@ -437,16 +482,15 @@
             dense = dense + value * info_ref[j, k * experts : (k + 1) * experts, :]
         dense_ref[s * experts : (s + 1) * experts, :] = dense.astype(BF16)
         own = jnp.where(p == s, dense, own)
-    out_dense = pltpu.make_async_copy(dense_ref, dense_hbm, sems.at[1])
+    out_dense = pltpu.make_async_copy(dense_ref, dense_hbm, sems.at[0])
     out_dense.start()
-    copy.wait()
     total = jnp.dot(own.astype(BF16), rows_ref[...], preferred_element_type=F32) * (1.0 / micro)
     cols = width // 128
     for r in range(experts // 8):
         for c in range(cols):
             tile = total[r * 8 : (r + 1) * 8, c * 128 : (c + 1) * 128]
             part_ref[r * cols + c] = tile.astype(BF16)
-    out_part = pltpu.make_async_copy(part_ref, part_hbm, sems.at[2])
+    out_part = pltpu.make_async_copy(part_ref, part_hbm, sems.at[1])
     out_part.start()
     out_dense.wait()
     out_part.wait()
@@ -460,18 +504,17 @@
     part = (experts // 8 * (width // 128), 8, 128)
     return pl.pallas_call(
         functools.partial(dense_kernel, micro),
-        in_specs=[SCALAR, WHOLE, WHOLE, STAYS],
+        in_specs=[SCALAR] + [WHOLE] * 3,
         out_specs=[STAYS] * 2,
-        out_shape=[jax.ShapeDtypeStruct(dense, BF16), pltpu.HBM(part, BF16)],
+        out_shape=[pltpu.HBM(dense, BF16), pltpu.HBM(part, BF16)],
         scratch_shapes=[
-            pltpu.VMEM((tokens, width), BF16),
             pltpu.VMEM(dense, BF16),
             pltpu.VMEM(part, BF16),
-            pltpu.SemaphoreType.DMA((3,)),
+            pltpu.SemaphoreType.DMA((2,)),
         ],
         compiler_params=params(32),
         name="dense",
-    )(p, sent, info, in_hbm(normed))
+    )(p, sent, info, normed)
 
 
 def grads_kernel(p_ref, up_ref, back_hbm, dense_ref, w_ref, *refs):
@@ -579,34 +622,33 @@
 
     grads = in_hbm(jnp.transpose(expert_grads[0, :, 0, 0], (0, 2, 1, 3)))
     lead = lax.all_to_all(lead_pack(grads, micro - 1), "expert", 0, 0, tiled=True)
-    late = spread(late_blocks(p, grads, sections))
+    info, near = gate_info(normed, w, jnp.transpose(routes[0], (2, 0, 1)).reshape(2, tokens), micro)
+    info_all = spread([info] * sections)
+    w_all = spread([part(w, j, 1) for j in range(sections)])
+    late = late_blocks(p, grads, sections)
+    late, info_all, w_all = lax.optimization_barrier((late, info_all, w_all))
+    late = spread(late)
+    info_all = jnp.stack(info_all)
+    w_all = jnp.stack(w_all)
     saved = jnp.transpose(saved_out[0], (2, 0, 1, 3))
     early = [part(saved[:, : micro - 1], j, 3) for j in range(sections)]
     *early, late[1], late[2], late[3] = lax.optimization_barrier((*early, *late[1:]))
     early = spread(early)
     tail_send = tail_pack(late)
-    info, near = gate_info(normed, w, jnp.transpose(routes[0], (2, 0, 1)).reshape(2, tokens), micro)
-    info_all = jnp.stack(spread([info] * sections))
-    w_all = jnp.stack(spread([part(w, j, 1) for j in range(sections)]))
-
-    lead, tail_send, info_all, w_all, *early = lax.optimization_barrier(
-        (lead, tail_send, info_all, w_all, *early)
-    )
+    tail_send, *early = lax.optimization_barrier((tail_send, *early))
     tail = lax.all_to_all(tail_send, "expert", 0, 0, tiled=True)
     rest = spread([part(saved[:, micro - 1 :], j, 3) for j in range(sections)])
     back = lead_combine(lead, near)
     lead = [
         lax.dynamic_index_in_dim(back, (section - j) % sections, 0, False) for j in range(sections)
     ]
-    lead = jnp.stack(spread(lead))
-    early = jnp.stack(early)
-    rest = jnp.stack(rest)
+    lead = spread(lead)
     links = coupling(p, early, rest, w_all, info_all)
     up = part(upstream, 0, 2)
     lead, info_all, w_all, early, rest, links, up = lax.optimization_barrier(
         (lead, info_all, w_all, early, rest, links, up)
     )
-    back, sent = tail_combine(p, tail, info_all, up, lead, early, rest, links)
+    back, sent = tail_combine(p, tail, info_all, up, links, lead, early, rest)
     sent = lax.all_to_all(sent, "pipe", 0, 0, tiled=True)
     dense, partial = dense_terms(p, sent, info_all, normed, micro)
 

time: 190 us -> 189 us (level)
  waiting for transfers between devices: 64 us -> 68.4 us
  other arithmetic: 4.11 us -> 0.83 us
    all_to_all x1, waiting for transfers between devices: 0.01 us -> 8.01 us  [on_device(): lax.all_to_all(lead_pack(grads, micro - 1), 'expert', 0, 0, tiled=True)]
    all_to_all x1, waiting for transfers between devices: 6.02 us -> 0.27 us  [on_device(): tail = lax.all_to_all(tail_send, 'expert', 0, 0, tiled=True)]
    ppermute x21, waiting for transfers between devices: 51.6 us -> 55.4 us  [turned(): lax.ppermute(block, 'pipe', [(i, (i + distance) % n) for i in range(n)])]
    another operation x5 -> x2, other arithmetic: 3.32 us -> 0.03 us  [the longest x1 0.02 us: on_device(): w_all = jnp.stack(w_all)]
    unnamed x27 -> x75, local copies, waits for them, and re-layouts: 6.49 us -> 9.15 us
    all_to_all x1, starting transfers between devices: 7.02 us -> 4.71 us  [on_device(): tail = lax.all_to_all(tail_send, 'expert', 0, 0, tiled=True)]
    dynamic_slice x2 -> x4, local copies, waits for them, and re-layouts: 4.04 us -> 3.88 us  [part(): lax.dynamic_slice_in_dim(array, (section - j) % sections * quarter, quart...]
  transfers between devices with their start and end apart: 25 -> 25, of which waited for: 14 -> 13; matrix products, arithmetic and copies ran while one was open for 9% -> 5% of each run, Pallas kernels for 10% -> 10%
where the time goes in v6:
time: 189 us
  waiting for transfers between devices  68.4 us (36%)
  starting transfers between devices  60.6 us (32%)
  Pallas kernels  32 us (17%)
  local copies, waits for them, and re-layouts  16 us (8%)
  blocking collectives  9.8 us (5%)
    ppermute x21, waiting for transfers between devices, turned(): lax.ppermute(block, 'pipe', [(i, (i + distance) % n) for i in range(n)])  55.4 us
    ppermute x21, starting transfers between devices, turned(): lax.ppermute(block, 'pipe', [(i, (i + distance) % n) for i in range(n)])  29.8 us
    all_to_all x1, blocking collectives, on_device(): sent = lax.all_to_all(sent, 'pipe', 0, 0, tiled=True)  9.8 us
    all_to_all x1, starting transfers between devices, on_device(): partial = lax.all_to_all(partial, axes, 0, 0, tiled=True)  9.39 us
    pallas_call x1, Pallas kernels, tail_combine(): pl.pallas_call(tail_kernel, in_specs=[SCALAR] + [STAYS] * len(operands),...  9.18 us
    unnamed x75, local copies, waits for them, and re-layouts  9.15 us
    all_to_all x1, starting transfers between devices, on_device(): lax.all_to_all(lead_pack(grads, micro - 1), 'expert', 0, 0, tiled=True)  8.77 us
    all_to_all x1, waiting for transfers between devices, on_device(): lax.all_to_all(lead_pack(grads, micro - 1), 'expert', 0, 0, tiled=True)  8.01 us
  transfers between devices with their start and end apart: 25, of which 13 were waited for; matrix products, arithmetic and copies ran while one was open for 5% of the time, Pallas kernels for 10%

profile of v6, /device:TPU:8, one launch (start us, length us, event | category | flops | bytes accessed | tf_op | source)
XLA Modules:
  0.0 188.8 jit_solution(499169119450282874)
XLA Ops:
  0.6 3.6 %lead_pack.1 = bf16[16,48,2048]{2,1,0:T(8,128)(2,1)} custom-call(bf16[4,9,16,4096]{3,2,1,0:T(8,128)(2,1)} %bitcast.63), custom_call_target="tpu_custom_call" | custom-call | tf_op jit(solution)/shard_map/lead_pack/pallas_call | solution.py:70
  4.3 8.8 %all-to-all-start = ((bf16[16,48,2048]{2,1,0:T(8,128)(2,1)}), bf16[16,48,2048]{2,1,0:T(8,128)(2,1)}, u32[]{:S(2)}, u32[]{:S(2)}) async-start(bf16[16,48,2048]{2,1,0:T(8,128)(2,1)} %lead_pack.1), calls=%async_computation | async-start | bytes 6291456 | tf_op jit(solution)/shard_map/all_to_all | solution.py:624
  14.9 3.0 %collective-permute-start.6 = (bf16[16,1024]{1,0:T(8,128)(2,1)S(1)}, bf16[16,1024]{1,0:T(8,128)(2,1)S(1)}, u32[]{:S(2)}, u32[]{:S(2)}) collective-permute-start(bf16[16,1024]{1,0:T(8,128)(2,1)S(1)} %get-tuple-element.123), channel_id=1, source_target_pairs={{0,192},{64,0},{128,64},{192,128},{1,193},{65,1},{129,65},{193,129... | collective-permute-start | bytes 98312 | tf_op jit(solution)/shard_map/ppermute | solution.py:598
  26.5 2.9 %collective-permute-start.9 = (bf16[12,16,1024]{2,1,0:T(8,128)(2,1)S(1)}, bf16[12,16,1024]{2,1,0:T(8,128)(2,1)S(1)}, u32[]{:S(2)}, u32[]{:S(2)}) collective-permute-start(bf16[12,16,1024]{2,1,0:T(8,128)(2,1)S(1)} %get-tuple-element.71), channel_id=1, source_target_pairs={{0,192},{64,0},{128,64},{192,128},{1,193},{65,1},{129,65},{193,129... | collective-permute-start | bytes 1179656 | tf_op jit(solution)/shard_map/ppermute | solution.py:598
  35.5 3.5 %collective-permute-done.9.refs_1_ = bf16[12,16,1024]{2,1,0:T(8,128)(2,1)S(1)} collective-permute-done((bf16[12,16,1024]{2,1,0:T(8,128)(2,1)S(1)}, bf16[12,16,1024]{2,1,0:T(8,128)(2,1)S(1)}, u32[]{:S(2)}, u32[]{:S(2)}) %collective-permute-start.9) | collective-permute-done | bytes 393248 | tf_op jit(solution)/shard_map/ppermute | solution.py:598
  39.0 6.1 %collective-permute-done.10.refs_2_ = bf16[12,16,1024]{2,1,0:T(8,128)(2,1)S(1)} collective-permute-done((bf16[12,16,1024]{2,1,0:T(8,128)(2,1)S(1)}, bf16[12,16,1024]{2,1,0:T(8,128)(2,1)S(1)}, u32[]{:S(2)}, u32[]{:S(2)}) %collective-permute-start.10) | collective-permute-done | bytes 393248 | tf_op jit(solution)/shard_map/ppermute | solution.py:598
  46.3 2.9 %collective-permute-start.12 = (bf16[2,3,48,1024]{3,2,1,0:T(8,128)(2,1)S(1)}, bf16[2,3,48,1024]{3,2,1,0:T(8,128)(2,1)S(1)}, u32[]{:S(2)}, u32[]{:S(2)}) collective-permute-start(bf16[2,3,48,1024]{3,2,1,0:T(8,128)(2,1)S(1)} %get-tuple-element.78), channel_id=1, source_target_pairs={{0,192},{64,0},{128,64},{192,128},{1,193},{65,1},{129,65},{193,129... | collective-permute-start | bytes 1769480 | tf_op jit(solution)/shard_map/ppermute | solution.py:598
  53.1 9.8 %collective-permute-done.12.refs_1_.refs_5_ = bf16[2,3,48,1024]{3,2,1,0:T(8,128)(2,1)S(1)} collective-permute-done((bf16[2,3,48,1024]{3,2,1,0:T(8,128)(2,1)S(1)}, bf16[2,3,48,1024]{3,2,1,0:T(8,128)(2,1)S(1)}, u32[]{:S(2)}, u32[]{:S(2)}) %collective-permute-start.12) | collective-permute-done | bytes 589856 | tf_op jit(solution)/shard_map/ppermute | solution.py:598
  63.7 11.5 %collective-permute-done.13.refs_2_.refs_6_ = bf16[2,3,48,1024]{3,2,1,0:T(8,128)(2,1)S(1)} collective-permute-done((bf16[2,3,48,1024]{3,2,1,0:T(8,128)(2,1)S(1)}, bf16[2,3,48,1024]{3,2,1,0:T(8,128)(2,1)S(1)}, u32[]{:S(2)}, u32[]{:S(2)}) %collective-permute-start.13) | collective-permute-done | bytes 589856 | tf_op jit(solution)/shard_map/ppermute | solution.py:598
  76.8 8.0 %all-to-all-done.main_ref = bf16[16,48,2048]{2,1,0:T(8,128)(2,1)} async-done(((bf16[16,48,2048]{2,1,0:T(8,128)(2,1)}), bf16[16,48,2048]{2,1,0:T(8,128)(2,1)}, u32[]{:S(2)}, u32[]{:S(2)}) %all-to-all-start) | async-done | bytes 3145760 | tf_op jit(solution)/shard_map/all_to_all | solution.py:624
  84.8 4.7 %all-to-all-start.1 = ((bf16[16,24,2048]{2,1,0:T(8,128)(2,1)}), bf16[16,24,2048]{2,1,0:T(8,128)(2,1)}, u32[]{:S(2)}, u32[]{:S(2)}) async-start(bf16[16,24,2048]{2,1,0:T(8,128)(2,1)} %tail_pack.1), calls=%async_computation.1 | async-start | bytes 3145728 | tf_op jit(solution)/shard_map/all_to_all | solution.py:639
  92.1 2.6 %collective-permute-start.16 = (bf16[2,1,48,1024]{3,2,1,0:T(8,128)(2,1)}, bf16[2,1,48,1024]{3,2,1,0:T(8,128)(2,1)}, u32[]{:S(2)}, u32[]{:S(2)}) collective-permute-start(bf16[2,1,48,1024]{3,2,1,0:T(8,128)(2,1)} %get-tuple-element.119), channel_id=1, source_target_pairs={{0,128},{64,192},{128,0},{192,64},{1,129},{65,193},{129,1},{193,65... | collective-permute-start | bytes 589832 | tf_op jit(solution)/shard_map/ppermute | solution.py:598
  94.7 4.5 %lead_combine.1 = bf16[4,3,48,1024]{3,2,1,0:T(8,128)(2,1)S(1)} custom-call(bf16[16,48,2048]{2,1,0:T(8,128)(2,1)} %all-to-all-done.main_ref, f32[4,8,96]{2,1,0:T(8,128)S(1)} %get-tuple-element.56.near_ref), custom_call_target="tpu_custom_call" | custom-call | tf_op jit(solution)/shard_map/lead_combine/pallas_call | solution.py:293
  106.2 15.1 %collective-permute-done.17.refs_7_.refs_11_ = bf16[2,1,48,1024]{3,2,1,0:T(8,128)(2,1)S(1)} collective-permute-done((bf16[2,1,48,1024]{3,2,1,0:T(8,128)(2,1)S(1)}, bf16[2,1,48,1024]{3,2,1,0:T(8,128)(2,1)S(1)}, u32[]{:S(2)}, u32[]{:S(2)}) %collective-permute-start.17) | collective-permute-done | bytes 196640 | tf_op jit(solution)/shard_map/ppermute | solution.py:598
  121.3 3.1 %coupling.1.links_hbm = f32[24,192]{1,0:T(8,128)S(1)} custom-call(s32[1]{0:T(128)} %bitcast.p_ref, bf16[4,16,1024]{2,1,0:T(8,128)(2,1)S(1)} %pad_maximum_fusion.1.w_ref, f32[4,40,192]{2,1,0:T(8,128)S(1)} %pad_maximum_fusion.info_ref.info_hbm, bf16[2,3,48,1024]{3,2,1,0:T(8,128)(2,1)S(1)} %copy-done.2, bf16[2,3,48,1024]{3,2,1,0:T(8,128)(2,1)S(1)} %copy-done.7, ...), custom_call_target="tpu_custom_call" | custom-call | tf_op jit(solution)/shard_map/coupling/pallas_call | solution.py:251
  127.5 9.2 %tail_combine.1 = (bf16[4,4,48,1024]{3,2,1,0:T(8,128)(2,1)}, f32[4,32,192]{2,1,0:T(8,128)S(1)}) custom-call(s32[1]{0:T(128)} %bitcast.p_ref, bf16[16,24,2048]{2,1,0:T(8,128)(2,1)} %all-to-all-done.1.received_hbm, f32[4,40,192]{2,1,0:T(8,128)} %copy-done.4, bf16[4,48,1024]{2,1,0:T(8,128)(2,1)} %constant_dynamic-slice_fusion.up_hbm.up_ref, ...), custom_call_target="tpu_custom_call" | custom-call | tf_op jit(solution)/shard_map/tail_combine/pallas_call | solution.py:434
  136.7 9.8 %all_to_all.25.sent_ref = f32[4,32,192]{2,1,0:T(8,128)S(1)} all-to-all(f32[4,32,192]{2,1,0:T(8,128)S(1)} %get-tuple-element.102), channel_id=1, replica_groups=mesh['pipe'=4,'expert'=16,'dp'=4] {'pipe'}, dimensions={0} | all-to-all | bytes 196608 | tf_op jit(solution)/shard_map/all_to_all | solution.py:652
  147.5 9.4 %all-to-all-start.3 = ((bf16[64,8,128]{2,1,0:T(8,128)(2,1)}), bf16[64,8,128]{2,1,0:T(8,128)(2,1)S(1)}, u32[]{:S(2)}, u32[]{:S(2)}) async-start(bf16[64,8,128]{2,1,0:T(8,128)(2,1)} %get-tuple-element.109), calls=%async_computation.3 | async-start | bytes 262144 | tf_op jit(solution)/shard_map/all_to_all | solution.py:656
  158.6 3.1 %grads.1 = (bf16[4,48,1024]{2,1,0:T(8,128)(2,1)}, bf16[4,48,1024]{2,1,0:T(8,128)(2,1)}, bf16[4,48,1024]{2,1,0:T(8,128)(2,1)}, bf16[4,48,1024]{2,1,0:T(8,128)(2,1)}) custom-call(s32[1]{0:T(128)} %bitcast.p_ref, bf16[4,48,1024]{2,1,0:T(8,128)(2,1)S(1)} %copy-done.3, bf16[4,4,48,1024]{3,2,1,0:T(8,128)(2,1)} %get-tuple-element.101.back_hbm, ...), custom_call_target="tpu_custom_call" | custom-call | tf_op jit(solution)/shard_map/grads/pallas_call | solution.py:552
  162.0 3.3 %collective-permute-start.19 = (bf16[4,48,1024]{2,1,0:T(8,128)(2,1)}, bf16[4,48,1024]{2,1,0:T(8,128)(2,1)S(1)}, u32[]{:S(2)}, u32[]{:S(2)}) collective-permute-start(bf16[4,48,1024]{2,1,0:T(8,128)(2,1)} %get-tuple-element.107), channel_id=1, source_target_pairs={{0,128},{64,192},{128,0},{192,64},{1,129},{65,193},{129,1},{193,65... | collective-permute-start | bytes 1179656 | tf_op jit(solution)/shard_map/ppermute | solution.py:598
  168.8 7.9 %all-to-all-start.4 = ((bf16[64,8,128]{2,1,0:T(8,128)(2,1)}), bf16[64,8,128]{2,1,0:T(8,128)(2,1)S(1)}, u32[]{:S(2)}, u32[]{:S(2)}) async-start(bf16[64,8,128]{2,1,0:T(8,128)(2,1)} %broadcast_in_dim.16), calls=%async_computation.4 | async-start | bytes 262144 | tf_op jit(solution)/shard_map/all_to_all | solution.py:660
  176.7 6.2 %collective-permute-done.20.refs_3_ = bf16[4,48,1024]{2,1,0:T(8,128)(2,1)S(1)} collective-permute-done((bf16[4,48,1024]{2,1,0:T(8,128)(2,1)}, bf16[4,48,1024]{2,1,0:T(8,128)(2,1)S(1)}, u32[]{:S(2)}, u32[]{:S(2)}) %collective-permute-start.20) | collective-permute-done | bytes 393248 | tf_op jit(solution)/shard_map/ppermute | solution.py:598
  182.9 2.7 %join.1 = bf16[4,48,4096]{2,1,0:T(8,128)(2,1)} custom-call(s32[1]{0:T(128)} %bitcast.p_ref, bf16[4,48,1024]{2,1,0:T(8,128)(2,1)} %get-tuple-element.105.refs_0_, bf16[4,48,1024]{2,1,0:T(8,128)(2,1)S(1)} %collective-permute-done.18.refs_1_, bf16[4,48,1024]{2,1,0:T(8,128)(2,1)S(1)} %collective-permute-done.19.refs_2_, ...), custom_call_target="tpu_custom_call" | custom-call | tf_op jit(solution)/shard_map/join/pallas_call | solution.py:582
  185.6 2.5 %all-to-all-done.4 = bf16[64,8,128]{2,1,0:T(8,128)(2,1)S(1)} async-done(((bf16[64,8,128]{2,1,0:T(8,128)(2,1)}), bf16[64,8,128]{2,1,0:T(8,128)(2,1)S(1)}, u32[]{:S(2)}, u32[]{:S(2)}) %all-to-all-start.4) | async-done | bytes 131104 | tf_op jit(solution)/shard_map/all_to_all | solution.py:660
  (126 shorter events, 43.6 us)
Async XLA Ops:
  4.3 80.6 %all-to-all-start = ((bf16[16,48,2048]{2,1,0:T(8,128)(2,1)}), bf16[16,48,2048]{2,1,0:T(8,128)(2,1)}, u32[]{:S(2)}, u32[]{:S(2)}) async-start(bf16[16,48,2048]{2,1,0:T(8,128)(2,1)} %lead_pack.1), calls=%async_computation | async-start | bytes 6291456 | tf_op jit(solution)/shard_map/all_to_all | solution.py:624
  13.8 7.6 %collective-permute-start.3 = (f32[40,192]{1,0:T(8,128)S(1)}, f32[40,192]{1,0:T(8,128)S(1)}, u32[]{:S(2)}, u32[]{:S(2)}) collective-permute-start(f32[40,192]{1,0:T(8,128)S(1)} %get-tuple-element.62), channel_id=1, source_target_pairs={{0,192},{64,0},{128,64},{192,128},{1,193},{65,1},{129,65},{193,129... | collective-permute-start | bytes 92168 | tf_op jit(solution)/shard_map/ppermute | solution.py:598
  14.9 11.6 %collective-permute-start.6 = (bf16[16,1024]{1,0:T(8,128)(2,1)S(1)}, bf16[16,1024]{1,0:T(8,128)(2,1)S(1)}, u32[]{:S(2)}, u32[]{:S(2)}) collective-permute-start(bf16[16,1024]{1,0:T(8,128)(2,1)S(1)} %get-tuple-element.123), channel_id=1, source_target_pairs={{0,192},{64,0},{128,64},{192,128},{1,193},{65,1},{129,65},{193,129... | collective-permute-start | bytes 98312 | tf_op jit(solution)/shard_map/ppermute | solution.py:598
  17.9 8.6 %collective-permute-start.7 = (bf16[16,1024]{1,0:T(8,128)(2,1)S(1)}, bf16[16,1024]{1,0:T(8,128)(2,1)S(1)}, u32[]{:S(2)}, u32[]{:S(2)}) collective-permute-start(bf16[16,1024]{1,0:T(8,128)(2,1)S(1)} %get-tuple-element.125), channel_id=1, source_target_pairs={{0,128},{64,192},{128,0},{192,64},{1,129},{65,193},{129,1},{193,65... | collective-permute-start | bytes 98312 | tf_op jit(solution)/shard_map/ppermute | solution.py:598
  17.9 8.6 %collective-permute-start.8 = (bf16[16,1024]{1,0:T(8,128)(2,1)S(1)}, bf16[16,1024]{1,0:T(8,128)(2,1)S(1)}, u32[]{:S(2)}, u32[]{:S(2)}) collective-permute-start(bf16[16,1024]{1,0:T(8,128)(2,1)S(1)} %get-tuple-element.122), channel_id=1, source_target_pairs={{0,64},{64,128},{128,192},{192,0},{1,65},{65,129},{129,193},{193,1... | collective-permute-start | bytes 98312 | tf_op jit(solution)/shard_map/ppermute | solution.py:598
  20.1 5.5 %collective-permute-start.4 = (f32[40,192]{1,0:T(8,128)S(1)}, f32[40,192]{1,0:T(8,128)S(1)}, u32[]{:S(2)}, u32[]{:S(2)}) collective-permute-start(f32[40,192]{1,0:T(8,128)S(1)} %get-tuple-element.62), channel_id=1, source_target_pairs={{0,128},{64,192},{128,0},{192,64},{1,129},{65,193},{129,1},{193,65... | collective-permute-start | bytes 92168 | tf_op jit(solution)/shard_map/ppermute | solution.py:598
  26.5 12.5 %collective-permute-start.9 = (bf16[12,16,1024]{2,1,0:T(8,128)(2,1)S(1)}, bf16[12,16,1024]{2,1,0:T(8,128)(2,1)S(1)}, u32[]{:S(2)}, u32[]{:S(2)}) collective-permute-start(bf16[12,16,1024]{2,1,0:T(8,128)(2,1)S(1)} %get-tuple-element.71), channel_id=1, source_target_pairs={{0,192},{64,0},{128,64},{192,128},{1,193},{65,1},{129,65},{193,129... | collective-permute-start | bytes 1179656 | tf_op jit(solution)/shard_map/ppermute | solution.py:598
  29.4 15.7 %collective-permute-start.10 = (bf16[12,16,1024]{2,1,0:T(8,128)(2,1)S(1)}, bf16[12,16,1024]{2,1,0:T(8,128)(2,1)S(1)}, u32[]{:S(2)}, u32[]{:S(2)}) collective-permute-start(bf16[12,16,1024]{2,1,0:T(8,128)(2,1)S(1)} %get-tuple-element.72), channel_id=1, source_target_pairs={{0,128},{64,192},{128,0},{192,64},{1,129},{65,193},{129,1},{193,65... | collective-permute-start | bytes 1179656 | tf_op jit(solution)/shard_map/ppermute | solution.py:598
  29.4 16.9 %collective-permute-start.11 = (bf16[12,16,1024]{2,1,0:T(8,128)(2,1)S(1)}, bf16[12,16,1024]{2,1,0:T(8,128)(2,1)S(1)}, u32[]{:S(2)}, u32[]{:S(2)}) collective-permute-start(bf16[12,16,1024]{2,1,0:T(8,128)(2,1)S(1)} %get-tuple-element.73), channel_id=1, source_target_pairs={{0,64},{64,128},{128,192},{192,0},{1,65},{65,129},{129,193},{193,1... | collective-permute-start | bytes 1179656 | tf_op jit(solution)/shard_map/ppermute | solution.py:598
  46.3 16.6 %collective-permute-start.12 = (bf16[2,3,48,1024]{3,2,1,0:T(8,128)(2,1)S(1)}, bf16[2,3,48,1024]{3,2,1,0:T(8,128)(2,1)S(1)}, u32[]{:S(2)}, u32[]{:S(2)}) collective-permute-start(bf16[2,3,48,1024]{3,2,1,0:T(8,128)(2,1)S(1)} %get-tuple-element.78), channel_id=1, source_target_pairs={{0,192},{64,0},{128,64},{192,128},{1,193},{65,1},{129,65},{193,129... | collective-permute-start | bytes 1769480 | tf_op jit(solution)/shard_map/ppermute | solution.py:598
  49.2 26.0 %collective-permute-start.13 = (bf16[2,3,48,1024]{3,2,1,0:T(8,128)(2,1)S(1)}, bf16[2,3,48,1024]{3,2,1,0:T(8,128)(2,1)S(1)}, u32[]{:S(2)}, u32[]{:S(2)}) collective-permute-start(bf16[2,3,48,1024]{3,2,1,0:T(8,128)(2,1)S(1)} %get-tuple-element.79), channel_id=1, source_target_pairs={{0,128},{64,192},{128,0},{192,64},{1,129},{65,193},{129,1},{193,65... | collective-permute-start | bytes 1769480 | tf_op jit(solution)/shard_map/ppermute | solution.py:598
  49.2 26.8 %collective-permute-start.14 = (bf16[2,3,48,1024]{3,2,1,0:T(8,128)(2,1)S(1)}, bf16[2,3,48,1024]{3,2,1,0:T(8,128)(2,1)S(1)}, u32[]{:S(2)}, u32[]{:S(2)}) collective-permute-start(bf16[2,3,48,1024]{3,2,1,0:T(8,128)(2,1)S(1)} %get-tuple-element.80), channel_id=1, source_target_pairs={{0,64},{64,128},{128,192},{192,0},{1,65},{65,129},{129,193},{193,1... | collective-permute-start | bytes 1769480 | tf_op jit(solution)/shard_map/ppermute | solution.py:598
  84.8 42.6 %all-to-all-start.1 = ((bf16[16,24,2048]{2,1,0:T(8,128)(2,1)}), bf16[16,24,2048]{2,1,0:T(8,128)(2,1)}, u32[]{:S(2)}, u32[]{:S(2)}) async-start(bf16[16,24,2048]{2,1,0:T(8,128)(2,1)} %tail_pack.1), calls=%async_computation.1 | async-start | bytes 3145728 | tf_op jit(solution)/shard_map/all_to_all | solution.py:639
  91.6 12.9 %collective-permute-start.15 = (bf16[2,1,48,1024]{3,2,1,0:T(8,128)(2,1)}, bf16[2,1,48,1024]{3,2,1,0:T(8,128)(2,1)}, u32[]{:S(2)}, u32[]{:S(2)}) collective-permute-start(bf16[2,1,48,1024]{3,2,1,0:T(8,128)(2,1)} %get-tuple-element.120), channel_id=1, source_target_pairs={{0,192},{64,0},{128,64},{192,128},{1,193},{65,1},{129,65},{193,129... | collective-permute-start | bytes 589832 | tf_op jit(solution)/shard_map/ppermute | solution.py:598
  92.1 14.1 %collective-permute-start.16 = (bf16[2,1,48,1024]{3,2,1,0:T(8,128)(2,1)}, bf16[2,1,48,1024]{3,2,1,0:T(8,128)(2,1)}, u32[]{:S(2)}, u32[]{:S(2)}) collective-permute-start(bf16[2,1,48,1024]{3,2,1,0:T(8,128)(2,1)} %get-tuple-element.119), channel_id=1, source_target_pairs={{0,128},{64,192},{128,0},{192,64},{1,129},{65,193},{129,1},{193,65... | collective-permute-start | bytes 589832 | tf_op jit(solution)/shard_map/ppermute | solution.py:598
  100.1 25.0 %collective-permute-start = (bf16[3,48,1024]{2,1,0:T(8,128)(2,1)S(1)}, bf16[3,48,1024]{2,1,0:T(8,128)(2,1)S(1)}, u32[]{:S(2)}, u32[]{:S(2)}) collective-permute-start(bf16[3,48,1024]{2,1,0:T(8,128)(2,1)S(1)} %get-tuple-element.116), channel_id=1, source_target_pairs={{0,192},{64,0},{128,64},{192,128},{1,193},{65,1},{129,65},{193,129... | collective-permute-start | bytes 884744 | tf_op jit(solution)/shard_map/ppermute | solution.py:598
  101.2 24.6 %collective-permute-start.1 = (bf16[3,48,1024]{2,1,0:T(8,128)(2,1)S(1)}, bf16[3,48,1024]{2,1,0:T(8,128)(2,1)S(1)}, u32[]{:S(2)}, u32[]{:S(2)}) collective-permute-start(bf16[3,48,1024]{2,1,0:T(8,128)(2,1)S(1)} %get-tuple-element.115), channel_id=1, source_target_pairs={{0,128},{64,192},{128,0},{192,64},{1,129},{65,193},{129,1},{193,65... | collective-permute-start | bytes 884744 | tf_op jit(solution)/shard_map/ppermute | solution.py:598
  103.5 23.0 %collective-permute-start.2 = (bf16[3,48,1024]{2,1,0:T(8,128)(2,1)S(1)}, bf16[3,48,1024]{2,1,0:T(8,128)(2,1)S(1)}, u32[]{:S(2)}, u32[]{:S(2)}) collective-permute-start(bf16[3,48,1024]{2,1,0:T(8,128)(2,1)S(1)} %get-tuple-element.114), channel_id=1, source_target_pairs={{0,64},{64,128},{128,192},{192,0},{1,65},{65,129},{129,193},{193,1... | collective-permute-start | bytes 884744 | tf_op jit(solution)/shard_map/ppermute | solution.py:598
  104.5 16.8 %collective-permute-start.17 = (bf16[2,1,48,1024]{3,2,1,0:T(8,128)(2,1)S(1)}, bf16[2,1,48,1024]{3,2,1,0:T(8,128)(2,1)S(1)}, u32[]{:S(2)}, u32[]{:S(2)}) collective-permute-start(bf16[2,1,48,1024]{3,2,1,0:T(8,128)(2,1)S(1)} %copy-done.24), channel_id=1, source_target_pairs={{0,64},{64,128},{128,192},{192,0},{1,65},{65,129},{129,193},{193,1... | collective-permute-start | bytes 589832 | tf_op jit(solution)/shard_map/ppermute | solution.py:598
  147.5 20.5 %all-to-all-start.3 = ((bf16[64,8,128]{2,1,0:T(8,128)(2,1)}), bf16[64,8,128]{2,1,0:T(8,128)(2,1)S(1)}, u32[]{:S(2)}, u32[]{:S(2)}) async-start(bf16[64,8,128]{2,1,0:T(8,128)(2,1)} %get-tuple-element.109), calls=%async_computation.3 | async-start | bytes 262144 | tf_op jit(solution)/shard_map/all_to_all | solution.py:656
  161.7 15.0 %collective-permute-start.18 = (bf16[4,48,1024]{2,1,0:T(8,128)(2,1)}, bf16[4,48,1024]{2,1,0:T(8,128)(2,1)S(1)}, u32[]{:S(2)}, u32[]{:S(2)}) collective-permute-start(bf16[4,48,1024]{2,1,0:T(8,128)(2,1)} %get-tuple-element.106), channel_id=1, source_target_pairs={{0,64},{64,128},{128,192},{192,0},{1,65},{65,129},{129,193},{193,1... | collective-permute-start | bytes 1179656 | tf_op jit(solution)/shard_map/ppermute | solution.py:598
  162.0 14.7 %collective-permute-start.19 = (bf16[4,48,1024]{2,1,0:T(8,128)(2,1)}, bf16[4,48,1024]{2,1,0:T(8,128)(2,1)S(1)}, u32[]{:S(2)}, u32[]{:S(2)}) collective-permute-start(bf16[4,48,1024]{2,1,0:T(8,128)(2,1)} %get-tuple-element.107), channel_id=1, source_target_pairs={{0,128},{64,192},{128,0},{192,64},{1,129},{65,193},{129,1},{193,65... | collective-permute-start | bytes 1179656 | tf_op jit(solution)/shard_map/ppermute | solution.py:598
  165.3 17.6 %collective-permute-start.20 = (bf16[4,48,1024]{2,1,0:T(8,128)(2,1)}, bf16[4,48,1024]{2,1,0:T(8,128)(2,1)S(1)}, u32[]{:S(2)}, u32[]{:S(2)}) collective-permute-start(bf16[4,48,1024]{2,1,0:T(8,128)(2,1)} %get-tuple-element.108), channel_id=1, source_target_pairs={{0,192},{64,0},{128,64},{192,128},{1,193},{65,1},{129,65},{193,129... | collective-permute-start | bytes 1179656 | tf_op jit(solution)/shard_map/ppermute | solution.py:598
  168.8 19.3 %all-to-all-start.4 = ((bf16[64,8,128]{2,1,0:T(8,128)(2,1)}), bf16[64,8,128]{2,1,0:T(8,128)(2,1)S(1)}, u32[]{:S(2)}, u32[]{:S(2)}) async-start(bf16[64,8,128]{2,1,0:T(8,128)(2,1)} %broadcast_in_dim.16), calls=%async_computation.4 | async-start | bytes 262144 | tf_op jit(solution)/shard_map/all_to_all | solution.py:660
  (38 other events, 428.4 us)

commit v7 on v6

--- a/solution.py
+++ b/solution.py
@@ -276,40 +276,64 @@
     return both[: lanes // 2] + both[lanes // 2 :]
 
 
-def lead_kernel(main_ref, near_ref, out_ref):
-    experts, _, half = main_ref.shape
-    received = main_ref[...].reshape(experts * TILE, half)
-    gates = [near_ref[0, k : k + 1, :] for k in range(2)]
-    places = [near_ref[0, 2 + k : 3 + k, :].astype(jnp.int32) for k in range(2)]
-    total = picked(gates, places, 0, received).astype(BF16)
-    out_ref[0, 0] = total[:, : half // 2]
-    out_ref[1, 0] = total[:, half // 2 :]
-
-
-def lead_combine(received, near):
+def lead_kernel(p_ref, received_hbm, near_ref, *refs):
+    outs = refs[:-4]
+    block_ref, out_ref, in_sems, out_sems = refs[-4:]
+    units, experts, _, half = block_ref.shape
+    reads = [
+        pltpu.make_async_copy(
+            received_hbm.at[:, pl.ds(TILE * unit, TILE), :], block_ref.at[unit], in_sems.at[unit]
+        )
+        for unit in range(units)
+    ]
+    for copy in reads:
+        copy.start()
+    for unit in range(units):
+        m, h = divmod(unit, 2)
+        reads[unit].wait()
+        received = block_ref[unit].reshape(experts * TILE, half)
+        gates = [near_ref[m, k : k + 1, :] for k in range(2)]
+        places = [near_ref[m, 2 + k : 3 + k, :].astype(jnp.int32) for k in range(2)]
+        total = picked(gates, places, 0, received).astype(BF16)
+        out_ref[2 * h, m] = total[:, : half // 2]
+        out_ref[2 * h + 1, m] = total[:, half // 2 :]
+    sections = len(outs)
+    writes = [
+        pltpu.make_async_copy(out_ref.at[(p_ref[0] - j) & (sections - 1)], outs[j], out_sems.at[j])
+        for j in range(sections)
+    ]
+    for copy in writes:
+        copy.start()
+    for copy in writes:
+        copy.wait()
+
+
+def lead_combine(p, received, near, sections):
     experts, packed, half = received.shape
-    count = packed // (2 * TILE)
-    rows = near.shape[2] // 2
+    units = packed // TILE
+    part = (units // 2, near.shape[2] // 2, 2 * half // sections)
     return pl.pallas_call(
         lead_kernel,
-        grid=(2, count),
-        in_specs=[
-            pl.BlockSpec((experts, TILE, half), lambda h, m: (0, 2 * m + h, 0)),
-            pl.BlockSpec((1,) + near.shape[1:], lambda h, m: (m, 0, 0)),
+        in_specs=[SCALAR, STAYS, WHOLE],
+        out_specs=[STAYS] * sections,
+        out_shape=[pltpu.HBM(part, BF16)] * sections,
+        scratch_shapes=[
+            pltpu.VMEM((units, experts, TILE, half), BF16),
+            pltpu.VMEM((sections,) + part, BF16),
+            pltpu.SemaphoreType.DMA((units,)),
+            pltpu.SemaphoreType.DMA((sections,)),
         ],
-        out_specs=pl.BlockSpec((2, 1, rows, half // 2), lambda h, m: (h, m, 0, 0)),
-        out_shape=jax.ShapeDtypeStruct((4, count, rows, half // 2), BF16),
-        compiler_params=params(40),
+        compiler_params=params(24),
         name="lead_combine",
-    )(received, near)
+    )(p, in_hbm(received), near)
 
 
 def tail_kernel(p_ref, received_hbm, info_hbm, up_hbm, links_hbm, *refs):
     sections = info_hbm.shape[0]
     lead_hbm, early_hbm, rest_hbm = [refs[i * sections : (i + 1) * sections] for i in range(3)]
-    back_hbm, sent_ref, block_ref, info_ref, up_ref, lead_ref, saved_ref = refs[3 * sections :][:7]
-    links_ref, last_ref, sum_ref, back_ref = refs[3 * sections + 7 :][:4]
-    block_sems, info_sem, up_sem, links_sem, lead_sems, saved_sems, back_sems = refs[3 * sections + 11 :]
+    back_hbm, sent_ref, block_ref, info_ref, up_ref, early_ref, rest_ref = refs[3 * sections :][:7]
+    lead_ref, links_ref, last_ref, sum_ref, back_ref = refs[3 * sections + 7 :][:5]
+    block_sems, info_sem, up_sem, links_sem, saved_sems, back_sems = refs[3 * sections + 12 :]
     p = p_ref[0]
     _, rows, quarter = sum_ref.shape
     _, experts, _, half = block_ref.shape
@@ -321,23 +345,14 @@
         )
         for unit in range(3)
     ]
+    early = [
+        pltpu.make_async_copy(early_hbm[j], early_ref.at[j], saved_sems.at[0, j]) for j in range(sections)
+    ]
+    rest = [
+        pltpu.make_async_copy(rest_hbm[j], rest_ref.at[j], saved_sems.at[1, j]) for j in range(sections)
+    ]
     lead = [
-        [
-            pltpu.make_async_copy(lead_hbm[j].at[m], lead_ref.at[m, j], lead_sems.at[m, j])
-            for j in range(sections)
-        ]
-        for m in range(micro - 1)
-    ]
-    saved = [
-        [
-            pltpu.make_async_copy(
-                early_hbm[j].at[:, m] if m < micro - 1 else rest_hbm[j].at[:, 0],
-                saved_ref.at[m, j],
-                saved_sems.at[m, j],
-            )
-            for j in range(sections)
-        ]
-        for m in range(micro)
+        pltpu.make_async_copy(lead_hbm[j], lead_ref.at[j], saved_sems.at[2, j]) for j in range(sections)
     ]
     info = pltpu.make_async_copy(info_hbm, info_ref, info_sem)
     up = pltpu.make_async_copy(up_hbm, up_ref, up_sem)
@@ -345,9 +360,7 @@
     backs = [
         pltpu.make_async_copy(back_ref.at[m], back_hbm.at[:, m], back_sems.at[m]) for m in range(micro)
     ]
-    for copy in [blocks[2], info] + lead[0] + [up] + saved[0] + lead[1] + saved[1] + lead[2] + saved[2]:
-        copy.start()
-    for copy in blocks[:2] + saved[3] + [links]:
+    for copy in [blocks[2], info] + lead + [up] + early + blocks[:2] + rest + [links]:
         copy.start()
     out_row, in_row = iotas((2 * n, n))
     within = out_row % (2 * experts)
@@ -381,21 +394,26 @@
                     pick, jnp.concatenate([main, main], axis=0), TN, preferred_element_type=F32
                 )
             else:
-                lead[m][j].wait()
-                total = total + lead_ref[m, j].astype(F32)
+                if m == 0:
+                    lead[j].wait()
+                total = total + lead_ref[j, m].astype(F32)
             sum_ref[j] = total
             back_ref[m, j] = total.astype(BF16)
         backs[m].start()
         if m == 0:
             up.wait()
-        for copy in saved[m]:
-            copy.wait()
+            for copy in early:
+                copy.wait()
+        if m == micro - 1:
+            for copy in rest:
+                copy.wait()
         base = up_ref[m].astype(F32)
         dots = jnp.zeros((rows, 128), F32)
         for s in reversed(range(sections)):
             j = (s - p) & (sections - 1)
             for k in range(2):
-                product = base * saved_ref[m, j, k].astype(F32)
+                saved = early_ref[j, k, m] if m < micro - 1 else rest_ref[j, k, 0]
+                product = base * saved.astype(F32)
                 part = product[:, :128]
                 for t in range(1, quarter // 128):
                     part = part + product[:, t * 128 : (t + 1) * 128]
@@ -430,10 +448,10 @@
     experts, packed, half = received.shape
     part = (sections, rows, quarter)
     dma = pltpu.SemaphoreType.DMA
-    operands = [received, info, upstream, links, *lead, *early, *rest]
+    fetched = [in_hbm(array) for array in (received, info, upstream, links, *lead, *early, *rest)]
     return pl.pallas_call(
         tail_kernel,
-        in_specs=[SCALAR] + [STAYS] * len(operands),
+        in_specs=[SCALAR] + [STAYS] * len(fetched),
         out_specs=[STAYS, WHOLE],
         out_shape=[
             pltpu.HBM((sections, micro, rows, quarter), BF16),
@@ -443,17 +461,18 @@
             pltpu.VMEM((3, experts, TILE, half), BF16),
             pltpu.VMEM(info.shape, F32),
             pltpu.VMEM(upstream.shape, BF16),
-            pltpu.VMEM((micro - 1,) + part, BF16),
-            pltpu.VMEM((micro, sections, 2, rows, quarter), BF16),
+            pltpu.VMEM((sections,) + early[0].shape, BF16),
+            pltpu.VMEM((sections,) + rest[0].shape, BF16),
+            pltpu.VMEM((sections,) + lead[0].shape, BF16),
             pltpu.VMEM(links.shape, F32),
             pltpu.VMEM((2 * experts * TILE, half), BF16),
             pltpu.VMEM(part, F32),
             pltpu.VMEM((micro,) + part, BF16),
-            dma((3,)), dma, dma, dma, dma((micro - 1, sections)), dma((micro, sections)), dma((micro,)),
+            dma((3,)), dma, dma, dma, dma((3, sections)), dma((micro,)),
         ],
-        compiler_params=params(48),
+        compiler_params=params(24),
         name="tail_combine",
-    )(p, *[in_hbm(array) for array in operands])
+    )(p, *fetched)
 
 
 def dense_kernel(
@@ -566,6 +585,30 @@
     )(p, upstream, in_hbm(back), dense, w)
 
 
+def total_kernel(parts_ref, out_hbm, out_ref, sem):
+    total = parts_ref[0].astype(F32)
+    for source in range(1, parts_ref.shape[0]):
+        total = total + parts_ref[source].astype(F32)
+    total = total.astype(BF16)
+    for dest in range(out_ref.shape[0]):
+        out_ref[dest] = total
+    copy = pltpu.make_async_copy(out_ref, out_hbm, sem)
+    copy.start()
+    copy.wait()
+
+
+def total_for_all(parts):
+    return pl.pallas_call(
+        total_kernel,
+        in_specs=[WHOLE],
+        out_specs=STAYS,
+        out_shape=pltpu.HBM(parts.shape, BF16),
+        scratch_shapes=[pltpu.VMEM(parts.shape, BF16), pltpu.SemaphoreType.DMA],
+        compiler_params=params(8),
+        name="router_total",
+    )(parts)
+
+
 def join_kernel(p_ref, *refs):
     step = pl.program_id(0)
     out_ref = refs[-1]
@@ -638,11 +681,7 @@
     tail_send, *early = lax.optimization_barrier((tail_send, *early))
     tail = lax.all_to_all(tail_send, "expert", 0, 0, tiled=True)
     rest = spread([part(saved[:, micro - 1 :], j, 3) for j in range(sections)])
-    back = lead_combine(lead, near)
-    lead = [
-        lax.dynamic_index_in_dim(back, (section - j) % sections, 0, False) for j in range(sections)
-    ]
-    lead = spread(lead)
+    lead = spread(lead_combine(p, lead, near, sections))
     links = coupling(p, early, rest, w_all, info_all)
     up = part(upstream, 0, 2)
     lead, info_all, w_all, early, rest, links, up = lax.optimization_barrier(
@@ -656,8 +695,7 @@
     partial = lax.all_to_all(partial, axes, 0, 0, tiled=True)
     outs = grads_of(p, up, back, dense, w_all)
     blocks = [turned(out, d) if d else out for d, out in enumerate(outs)]
-    total = jnp.sum(partial.astype(F32), axis=0, keepdims=True).astype(BF16)
-    total = lax.all_to_all(jnp.broadcast_to(total, partial.shape), axes, 0, 0, tiled=True)
+    total = lax.all_to_all(total_for_all(partial), axes, 0, 0, tiled=True)
     total = total.astype(F32).reshape(experts // 8, width // 128, 8, 128).transpose(0, 2, 1, 3)
     router_grad = total.reshape(experts, width).T
     blocks[0] = in_hbm(blocks[0])

time: 189 us -> 187 us (0.989)
  waiting for transfers between devices: 68.4 us -> 70.9 us
  Pallas kernels: 32 us -> 29.9 us
    all_to_all x1, waiting for transfers between devices: 0.27 us -> 2.62 us  [on_device(): tail = lax.all_to_all(tail_send, 'expert', 0, 0, tiled=True)]
    pallas_call x2 -> x3, Pallas kernels: 13.7 us -> 11.6 us  [the longest x1 6.87 us: tail_combine(): pl.pallas_call(tail_kernel, in_specs=[SCALAR] + [STAYS] * len(fetched), o...]
    unnamed x75 -> x55, local copies, waits for them, and re-layouts: 9.15 us -> 10.8 us
  transfers between devices with their start and end apart: 25 -> 25, of which waited for: 13 -> 13; matrix products, arithmetic and copies ran while one was open for 5% -> 3% of each run, Pallas kernels for 10% -> 10%
where the time goes in v7:
time: 187 us; the launch traced here: 186 us
  waiting for transfers between devices  70.9 us (38%)
  starting transfers between devices  59.3 us (32%)
  Pallas kernels  29.9 us (16%)
  local copies, waits for them, and re-layouts  14.3 us (8%)
  blocking collectives  9.8 us (5%)
    ppermute x21, waiting for transfers between devices, turned(): lax.ppermute(block, 'pipe', [(i, (i + distance) % n) for i in range(n)])  55 us
    ppermute x21, starting transfers between devices, turned(): lax.ppermute(block, 'pipe', [(i, (i + distance) % n) for i in range(n)])  29.9 us
    unnamed x55, local copies, waits for them, and re-layouts  10.8 us
    all_to_all x1, blocking collectives, on_device(): sent = lax.all_to_all(sent, 'pipe', 0, 0, tiled=True)  9.8 us
    all_to_all x1, starting transfers between devices, on_device(): lax.all_to_all(lead_pack(grads, micro - 1), 'expert', 0, 0, tiled=True)  8.77 us
    all_to_all x1, waiting for transfers between devices, on_device(): lax.all_to_all(lead_pack(grads, micro - 1), 'expert', 0, 0, tiled=True)  8.57 us
    all_to_all x1, starting transfers between devices, on_device(): partial = lax.all_to_all(partial, axes, 0, 0, tiled=True)  7.99 us
    all_to_all x1, starting transfers between devices, on_device(): total = lax.all_to_all(total_for_all(partial), axes, 0, 0, tiled=True)  7.91 us
  transfers between devices with their start and end apart: 25, of which 13 were waited for; matrix products, arithmetic and copies ran while one was open for 3% of the time, Pallas kernels for 10%

profile of v7, /device:TPU:8, one launch (start us, length us, event | category | flops | bytes accessed | tf_op | source)
XLA Modules:
  0.0 186.0 jit_solution(1532452969620538705)
XLA Ops:
  0.6 3.6 %lead_pack.1 = bf16[16,48,2048]{2,1,0:T(8,128)(2,1)} custom-call(bf16[4,9,16,4096]{3,2,1,0:T(8,128)(2,1)} %bitcast.55), custom_call_target="tpu_custom_call" | custom-call | tf_op jit(solution)/shard_map/lead_pack/pallas_call | solution.py:70
  4.3 8.8 %all-to-all-start = ((bf16[16,48,2048]{2,1,0:T(8,128)(2,1)}), bf16[16,48,2048]{2,1,0:T(8,128)(2,1)}, u32[]{:S(2)}, u32[]{:S(2)}) async-start(bf16[16,48,2048]{2,1,0:T(8,128)(2,1)} %lead_pack.1), calls=%async_computation | async-start | bytes 6291456 | tf_op jit(solution)/shard_map/all_to_all | solution.py:667
  14.3 3.1 %collective-permute-start.6 = (bf16[16,1024]{1,0:T(8,128)(2,1)S(1)}, bf16[16,1024]{1,0:T(8,128)(2,1)S(1)}, u32[]{:S(2)}, u32[]{:S(2)}) collective-permute-start(bf16[16,1024]{1,0:T(8,128)(2,1)S(1)} %get-tuple-element.127), channel_id=1, source_target_pairs={{0,192},{64,0},{128,64},{192,128},{1,193},{65,1},{129,65},{193,129... | collective-permute-start | bytes 98312 | tf_op jit(solution)/shard_map/ppermute | solution.py:641
  26.0 2.9 %collective-permute-start.9 = (bf16[12,16,1024]{2,1,0:T(8,128)(2,1)S(1)}, bf16[12,16,1024]{2,1,0:T(8,128)(2,1)S(1)}, u32[]{:S(2)}, u32[]{:S(2)}) collective-permute-start(bf16[12,16,1024]{2,1,0:T(8,128)(2,1)S(1)} %get-tuple-element.79), channel_id=1, source_target_pairs={{0,192},{64,0},{128,64},{192,128},{1,193},{65,1},{129,65},{193,129... | collective-permute-start | bytes 1179656 | tf_op jit(solution)/shard_map/ppermute | solution.py:641
  35.8 2.7 %collective-permute-done.9.refs_1_ = bf16[12,16,1024]{2,1,0:T(8,128)(2,1)S(1)} collective-permute-done((bf16[12,16,1024]{2,1,0:T(8,128)(2,1)S(1)}, bf16[12,16,1024]{2,1,0:T(8,128)(2,1)S(1)}, u32[]{:S(2)}, u32[]{:S(2)}) %collective-permute-start.9) | collective-permute-done | bytes 393248 | tf_op jit(solution)/shard_map/ppermute | solution.py:641
  38.4 6.1 %collective-permute-done.10.refs_2_ = bf16[12,16,1024]{2,1,0:T(8,128)(2,1)S(1)} collective-permute-done((bf16[12,16,1024]{2,1,0:T(8,128)(2,1)S(1)}, bf16[12,16,1024]{2,1,0:T(8,128)(2,1)S(1)}, u32[]{:S(2)}, u32[]{:S(2)}) %collective-permute-start.10) | collective-permute-done | bytes 393248 | tf_op jit(solution)/shard_map/ppermute | solution.py:641
  45.8 2.9 %collective-permute-start.12 = (bf16[2,3,48,1024]{3,2,1,0:T(8,128)(2,1)S(1)}, bf16[2,3,48,1024]{3,2,1,0:T(8,128)(2,1)S(1)}, u32[]{:S(2)}, u32[]{:S(2)}) collective-permute-start(bf16[2,3,48,1024]{3,2,1,0:T(8,128)(2,1)S(1)} %get-tuple-element.86), channel_id=1, source_target_pairs={{0,192},{64,0},{128,64},{192,128},{1,193},{65,1},{129,65},{193,129... | collective-permute-start | bytes 1769480 | tf_op jit(solution)/shard_map/ppermute | solution.py:641
  52.6 9.8 %collective-permute-done.12.refs_1_.refs_5_ = bf16[2,3,48,1024]{3,2,1,0:T(8,128)(2,1)S(1)} collective-permute-done((bf16[2,3,48,1024]{3,2,1,0:T(8,128)(2,1)S(1)}, bf16[2,3,48,1024]{3,2,1,0:T(8,128)(2,1)S(1)}, u32[]{:S(2)}, u32[]{:S(2)}) %collective-permute-start.12) | collective-permute-done | bytes 589856 | tf_op jit(solution)/shard_map/ppermute | solution.py:641
  63.2 11.5 %collective-permute-done.13.refs_2_.refs_6_ = bf16[2,3,48,1024]{3,2,1,0:T(8,128)(2,1)S(1)} collective-permute-done((bf16[2,3,48,1024]{3,2,1,0:T(8,128)(2,1)S(1)}, bf16[2,3,48,1024]{3,2,1,0:T(8,128)(2,1)S(1)}, u32[]{:S(2)}, u32[]{:S(2)}) %collective-permute-start.13) | collective-permute-done | bytes 589856 | tf_op jit(solution)/shard_map/ppermute | solution.py:641
  76.3 8.6 %all-to-all-done.received_hbm = bf16[16,48,2048]{2,1,0:T(8,128)(2,1)} async-done(((bf16[16,48,2048]{2,1,0:T(8,128)(2,1)}), bf16[16,48,2048]{2,1,0:T(8,128)(2,1)}, u32[]{:S(2)}, u32[]{:S(2)}) %all-to-all-start) | async-done | bytes 3145760 | tf_op jit(solution)/shard_map/all_to_all | solution.py:667
  84.9 4.7 %all-to-all-start.1 = ((bf16[16,24,2048]{2,1,0:T(8,128)(2,1)}), bf16[16,24,2048]{2,1,0:T(8,128)(2,1)}, u32[]{:S(2)}, u32[]{:S(2)}) async-start(bf16[16,24,2048]{2,1,0:T(8,128)(2,1)} %tail_pack.1), calls=%async_computation.1 | async-start | bytes 3145728 | tf_op jit(solution)/shard_map/all_to_all | solution.py:682
  91.5 2.6 %collective-permute-start.16 = (bf16[2,1,48,1024]{3,2,1,0:T(8,128)(2,1)S(1)}, bf16[2,1,48,1024]{3,2,1,0:T(8,128)(2,1)S(1)}, u32[]{:S(2)}, u32[]{:S(2)}) collective-permute-start(bf16[2,1,48,1024]{3,2,1,0:T(8,128)(2,1)S(1)} %get-tuple-element.123), channel_id=1, source_target_pairs={{0,128},{64,192},{128,0},{192,64},{1,129},{65,193},{129,1},{193,65... | collective-permute-start | bytes 589832 | tf_op jit(solution)/shard_map/ppermute | solution.py:641
  94.0 4.0 %lead_combine.1 = (bf16[3,48,1024]{2,1,0:T(8,128)(2,1)}, bf16[3,48,1024]{2,1,0:T(8,128)(2,1)}, bf16[3,48,1024]{2,1,0:T(8,128)(2,1)}, bf16[3,48,1024]{2,1,0:T(8,128)(2,1)}) custom-call(s32[1]{0:T(128)} %bitcast.p_ref, bf16[16,48,2048]{2,1,0:T(8,128)(2,1)} %all-to-all-done.received_hbm, f32[4,8,96]{2,1,0:T(8,128)S(1)} %get-tuple-element.60.near_ref), custom_call_target="tpu_custom_call" | custom-call | tf_op jit(solution)/shard_map/lead_combine/pallas_call | solution.py:315
  104.2 15.5 %collective-permute-done.17.refs_7_.refs_11_ = bf16[2,1,48,1024]{3,2,1,0:T(8,128)(2,1)S(1)} collective-permute-done((bf16[2,1,48,1024]{3,2,1,0:T(8,128)(2,1)S(1)}, bf16[2,1,48,1024]{3,2,1,0:T(8,128)(2,1)S(1)}, u32[]{:S(2)}, u32[]{:S(2)}) %collective-permute-start.17) | collective-permute-done | bytes 196640 | tf_op jit(solution)/shard_map/ppermute | solution.py:641
  119.7 3.0 %coupling.1.links_hbm = f32[24,192]{1,0:T(8,128)S(1)} custom-call(s32[1]{0:T(128)} %bitcast.p_ref, bf16[4,16,1024]{2,1,0:T(8,128)(2,1)S(1)} %pad_maximum_fusion.1.w_ref, f32[4,40,192]{2,1,0:T(8,128)S(1)} %pad_maximum_fusion.info_ref.info_hbm, bf16[2,3,48,1024]{3,2,1,0:T(8,128)(2,1)S(1)} %copy-done.2, bf16[2,3,48,1024]{3,2,1,0:T(8,128)(2,1)S(1)} %copy-done.7, ...), custom_call_target="tpu_custom_call" | custom-call | tf_op jit(solution)/shard_map/coupling/pallas_call | solution.py:251
  124.9 2.6 %all-to-all-done.1.received_hbm = bf16[16,24,2048]{2,1,0:T(8,128)(2,1)} async-done(((bf16[16,24,2048]{2,1,0:T(8,128)(2,1)}), bf16[16,24,2048]{2,1,0:T(8,128)(2,1)}, u32[]{:S(2)}, u32[]{:S(2)}) %all-to-all-start.1) | async-done | bytes 1572896 | tf_op jit(solution)/shard_map/all_to_all | solution.py:682
  127.5 6.9 %tail_combine.1 = (bf16[4,4,48,1024]{3,2,1,0:T(8,128)(2,1)}, f32[4,32,192]{2,1,0:T(8,128)S(1)}) custom-call(s32[1]{0:T(128)} %bitcast.p_ref, bf16[16,24,2048]{2,1,0:T(8,128)(2,1)} %all-to-all-done.1.received_hbm, f32[4,40,192]{2,1,0:T(8,128)} %copy-done.4, bf16[4,48,1024]{2,1,0:T(8,128)(2,1)} %constant_dynamic-slice_fusion.up_hbm.up_ref, ...), custom_call_target="tpu_custom_call" | custom-call | tf_op jit(solution)/shard_map/tail_combine/pallas_call | solution.py:452
  134.4 9.8 %all_to_all.25.sent_ref = f32[4,32,192]{2,1,0:T(8,128)S(1)} all-to-all(f32[4,32,192]{2,1,0:T(8,128)S(1)} %get-tuple-element.110), channel_id=1, replica_groups=mesh['pipe'=4,'expert'=16,'dp'=4] {'pipe'}, dimensions={0} | all-to-all | bytes 196608 | tf_op jit(solution)/shard_map/all_to_all | solution.py:691
  146.1 8.0 %all-to-all-start.3 = ((bf16[64,8,128]{2,1,0:T(8,128)(2,1)}), bf16[64,8,128]{2,1,0:T(8,128)(2,1)S(1)}, u32[]{:S(2)}, u32[]{:S(2)}) async-start(bf16[64,8,128]{2,1,0:T(8,128)(2,1)} %get-tuple-element.117), calls=%async_computation.3 | async-start | bytes 262144 | tf_op jit(solution)/shard_map/all_to_all | solution.py:695
  155.8 3.1 %grads.1 = (bf16[4,48,1024]{2,1,0:T(8,128)(2,1)}, bf16[4,48,1024]{2,1,0:T(8,128)(2,1)}, bf16[4,48,1024]{2,1,0:T(8,128)(2,1)}, bf16[4,48,1024]{2,1,0:T(8,128)(2,1)}) custom-call(s32[1]{0:T(128)} %bitcast.p_ref, bf16[4,48,1024]{2,1,0:T(8,128)(2,1)S(1)} %copy-done.3, bf16[4,4,48,1024]{3,2,1,0:T(8,128)(2,1)} %get-tuple-element.109.back_hbm, ...), custom_call_target="tpu_custom_call" | custom-call | tf_op jit(solution)/shard_map/grads/pallas_call | solution.py:571
  159.2 3.3 %collective-permute-start.19 = (bf16[4,48,1024]{2,1,0:T(8,128)(2,1)}, bf16[4,48,1024]{2,1,0:T(8,128)(2,1)S(1)}, u32[]{:S(2)}, u32[]{:S(2)}) collective-permute-start(bf16[4,48,1024]{2,1,0:T(8,128)(2,1)} %get-tuple-element.115), channel_id=1, source_target_pairs={{0,128},{64,192},{128,0},{192,64},{1,129},{65,193},{129,1},{193,65... | collective-permute-start | bytes 1179656 | tf_op jit(solution)/shard_map/ppermute | solution.py:641
  166.0 7.9 %all-to-all-start.4 = ((bf16[64,8,128]{2,1,0:T(8,128)(2,1)}), bf16[64,8,128]{2,1,0:T(8,128)(2,1)S(1)}, u32[]{:S(2)}, u32[]{:S(2)}) async-start(bf16[64,8,128]{2,1,0:T(8,128)(2,1)} %router_total.1), calls=%async_computation.4 | async-start | bytes 262144 | tf_op jit(solution)/shard_map/all_to_all | solution.py:698
  174.0 6.1 %collective-permute-done.20.refs_3_ = bf16[4,48,1024]{2,1,0:T(8,128)(2,1)S(1)} collective-permute-done((bf16[4,48,1024]{2,1,0:T(8,128)(2,1)}, bf16[4,48,1024]{2,1,0:T(8,128)(2,1)S(1)}, u32[]{:S(2)}, u32[]{:S(2)}) %collective-permute-start.20) | collective-permute-done | bytes 393248 | tf_op jit(solution)/shard_map/ppermute | solution.py:641
  180.1 2.7 %join.1 = bf16[4,48,4096]{2,1,0:T(8,128)(2,1)} custom-call(s32[1]{0:T(128)} %bitcast.p_ref, bf16[4,48,1024]{2,1,0:T(8,128)(2,1)} %get-tuple-element.113.refs_0_, bf16[4,48,1024]{2,1,0:T(8,128)(2,1)S(1)} %collective-permute-done.18.refs_1_, bf16[4,48,1024]{2,1,0:T(8,128)(2,1)S(1)} %collective-permute-done.19.refs_2_, ...), custom_call_target="tpu_custom_call" | custom-call | tf_op jit(solution)/shard_map/join/pallas_call | solution.py:625
  (104 shorter events, 45.0 us)
Async XLA Ops:
  4.3 80.6 %all-to-all-start = ((bf16[16,48,2048]{2,1,0:T(8,128)(2,1)}), bf16[16,48,2048]{2,1,0:T(8,128)(2,1)}, u32[]{:S(2)}, u32[]{:S(2)}) async-start(bf16[16,48,2048]{2,1,0:T(8,128)(2,1)} %lead_pack.1), calls=%async_computation | async-start | bytes 6291456 | tf_op jit(solution)/shard_map/all_to_all | solution.py:667
  13.8 7.1 %collective-permute-start.3 = (f32[40,192]{1,0:T(8,128)S(1)}, f32[40,192]{1,0:T(8,128)S(1)}, u32[]{:S(2)}, u32[]{:S(2)}) collective-permute-start(f32[40,192]{1,0:T(8,128)S(1)} %get-tuple-element.70), channel_id=1, source_target_pairs={{0,192},{64,0},{128,64},{192,128},{1,193},{65,1},{129,65},{193,129... | collective-permute-start | bytes 92168 | tf_op jit(solution)/shard_map/ppermute | solution.py:641
  14.3 11.7 %collective-permute-start.6 = (bf16[16,1024]{1,0:T(8,128)(2,1)S(1)}, bf16[16,1024]{1,0:T(8,128)(2,1)S(1)}, u32[]{:S(2)}, u32[]{:S(2)}) collective-permute-start(bf16[16,1024]{1,0:T(8,128)(2,1)S(1)} %get-tuple-element.127), channel_id=1, source_target_pairs={{0,192},{64,0},{128,64},{192,128},{1,193},{65,1},{129,65},{193,129... | collective-permute-start | bytes 98312 | tf_op jit(solution)/shard_map/ppermute | solution.py:641
  17.4 8.6 %collective-permute-start.7 = (bf16[16,1024]{1,0:T(8,128)(2,1)S(1)}, bf16[16,1024]{1,0:T(8,128)(2,1)S(1)}, u32[]{:S(2)}, u32[]{:S(2)}) collective-permute-start(bf16[16,1024]{1,0:T(8,128)(2,1)S(1)} %get-tuple-element.129), channel_id=1, source_target_pairs={{0,128},{64,192},{128,0},{192,64},{1,129},{65,193},{129,1},{193,65... | collective-permute-start | bytes 98312 | tf_op jit(solution)/shard_map/ppermute | solution.py:641
  17.4 8.6 %collective-permute-start.8 = (bf16[16,1024]{1,0:T(8,128)(2,1)S(1)}, bf16[16,1024]{1,0:T(8,128)(2,1)S(1)}, u32[]{:S(2)}, u32[]{:S(2)}) collective-permute-start(bf16[16,1024]{1,0:T(8,128)(2,1)S(1)} %get-tuple-element.126), channel_id=1, source_target_pairs={{0,64},{64,128},{128,192},{192,0},{1,65},{65,129},{129,193},{193,1... | collective-permute-start | bytes 98312 | tf_op jit(solution)/shard_map/ppermute | solution.py:641
  19.6 5.5 %collective-permute-start.4 = (f32[40,192]{1,0:T(8,128)S(1)}, f32[40,192]{1,0:T(8,128)S(1)}, u32[]{:S(2)}, u32[]{:S(2)}) collective-permute-start(f32[40,192]{1,0:T(8,128)S(1)} %get-tuple-element.70), channel_id=1, source_target_pairs={{0,128},{64,192},{128,0},{192,64},{1,129},{65,193},{129,1},{193,65... | collective-permute-start | bytes 92168 | tf_op jit(solution)/shard_map/ppermute | solution.py:641
  26.0 12.5 %collective-permute-start.9 = (bf16[12,16,1024]{2,1,0:T(8,128)(2,1)S(1)}, bf16[12,16,1024]{2,1,0:T(8,128)(2,1)S(1)}, u32[]{:S(2)}, u32[]{:S(2)}) collective-permute-start(bf16[12,16,1024]{2,1,0:T(8,128)(2,1)S(1)} %get-tuple-element.79), channel_id=1, source_target_pairs={{0,192},{64,0},{128,64},{192,128},{1,193},{65,1},{129,65},{193,129... | collective-permute-start | bytes 1179656 | tf_op jit(solution)/shard_map/ppermute | solution.py:641
  28.8 15.7 %collective-permute-start.10 = (bf16[12,16,1024]{2,1,0:T(8,128)(2,1)S(1)}, bf16[12,16,1024]{2,1,0:T(8,128)(2,1)S(1)}, u32[]{:S(2)}, u32[]{:S(2)}) collective-permute-start(bf16[12,16,1024]{2,1,0:T(8,128)(2,1)S(1)} %get-tuple-element.80), channel_id=1, source_target_pairs={{0,128},{64,192},{128,0},{192,64},{1,129},{65,193},{129,1},{193,65... | collective-permute-start | bytes 1179656 | tf_op jit(solution)/shard_map/ppermute | solution.py:641
  28.9 16.9 %collective-permute-start.11 = (bf16[12,16,1024]{2,1,0:T(8,128)(2,1)S(1)}, bf16[12,16,1024]{2,1,0:T(8,128)(2,1)S(1)}, u32[]{:S(2)}, u32[]{:S(2)}) collective-permute-start(bf16[12,16,1024]{2,1,0:T(8,128)(2,1)S(1)} %get-tuple-element.81), channel_id=1, source_target_pairs={{0,64},{64,128},{128,192},{192,0},{1,65},{65,129},{129,193},{193,1... | collective-permute-start | bytes 1179656 | tf_op jit(solution)/shard_map/ppermute | solution.py:641
  45.8 16.6 %collective-permute-start.12 = (bf16[2,3,48,1024]{3,2,1,0:T(8,128)(2,1)S(1)}, bf16[2,3,48,1024]{3,2,1,0:T(8,128)(2,1)S(1)}, u32[]{:S(2)}, u32[]{:S(2)}) collective-permute-start(bf16[2,3,48,1024]{3,2,1,0:T(8,128)(2,1)S(1)} %get-tuple-element.86), channel_id=1, source_target_pairs={{0,192},{64,0},{128,64},{192,128},{1,193},{65,1},{129,65},{193,129... | collective-permute-start | bytes 1769480 | tf_op jit(solution)/shard_map/ppermute | solution.py:641
  48.7 26.0 %collective-permute-start.13 = (bf16[2,3,48,1024]{3,2,1,0:T(8,128)(2,1)S(1)}, bf16[2,3,48,1024]{3,2,1,0:T(8,128)(2,1)S(1)}, u32[]{:S(2)}, u32[]{:S(2)}) collective-permute-start(bf16[2,3,48,1024]{3,2,1,0:T(8,128)(2,1)S(1)} %get-tuple-element.87), channel_id=1, source_target_pairs={{0,128},{64,192},{128,0},{192,64},{1,129},{65,193},{129,1},{193,65... | collective-permute-start | bytes 1769480 | tf_op jit(solution)/shard_map/ppermute | solution.py:641
  48.7 26.8 %collective-permute-start.14 = (bf16[2,3,48,1024]{3,2,1,0:T(8,128)(2,1)S(1)}, bf16[2,3,48,1024]{3,2,1,0:T(8,128)(2,1)S(1)}, u32[]{:S(2)}, u32[]{:S(2)}) collective-permute-start(bf16[2,3,48,1024]{3,2,1,0:T(8,128)(2,1)S(1)} %get-tuple-element.88), channel_id=1, source_target_pairs={{0,64},{64,128},{128,192},{192,0},{1,65},{65,129},{129,193},{193,1... | collective-permute-start | bytes 1769480 | tf_op jit(solution)/shard_map/ppermute | solution.py:641
  84.9 42.6 %all-to-all-start.1 = ((bf16[16,24,2048]{2,1,0:T(8,128)(2,1)}), bf16[16,24,2048]{2,1,0:T(8,128)(2,1)}, u32[]{:S(2)}, u32[]{:S(2)}) async-start(bf16[16,24,2048]{2,1,0:T(8,128)(2,1)} %tail_pack.1), calls=%async_computation.1 | async-start | bytes 3145728 | tf_op jit(solution)/shard_map/all_to_all | solution.py:682
  90.9 11.6 %collective-permute-start.15 = (bf16[2,1,48,1024]{3,2,1,0:T(8,128)(2,1)S(1)}, bf16[2,1,48,1024]{3,2,1,0:T(8,128)(2,1)S(1)}, u32[]{:S(2)}, u32[]{:S(2)}) collective-permute-start(bf16[2,1,48,1024]{3,2,1,0:T(8,128)(2,1)S(1)} %get-tuple-element.124), channel_id=1, source_target_pairs={{0,192},{64,0},{128,64},{192,128},{1,193},{65,1},{129,65},{193,129... | collective-permute-start | bytes 589832 | tf_op jit(solution)/shard_map/ppermute | solution.py:641
  91.5 12.7 %collective-permute-start.16 = (bf16[2,1,48,1024]{3,2,1,0:T(8,128)(2,1)S(1)}, bf16[2,1,48,1024]{3,2,1,0:T(8,128)(2,1)S(1)}, u32[]{:S(2)}, u32[]{:S(2)}) collective-permute-start(bf16[2,1,48,1024]{3,2,1,0:T(8,128)(2,1)S(1)} %get-tuple-element.123), channel_id=1, source_target_pairs={{0,128},{64,192},{128,0},{192,64},{1,129},{65,193},{129,1},{193,65... | collective-permute-start | bytes 589832 | tf_op jit(solution)/shard_map/ppermute | solution.py:641
  98.1 25.3 %collective-permute-start = (bf16[3,48,1024]{2,1,0:T(8,128)(2,1)}, bf16[3,48,1024]{2,1,0:T(8,128)(2,1)S(1)}, u32[]{:S(2)}, u32[]{:S(2)}) collective-permute-start(bf16[3,48,1024]{2,1,0:T(8,128)(2,1)} %get-tuple-element.62), channel_id=1, source_target_pairs={{0,192},{64,0},{128,64},{192,128},{1,193},{65,1},{129,65},{193,129... | collective-permute-start | bytes 884744 | tf_op jit(solution)/shard_map/ppermute | solution.py:641
  99.2 24.1 %collective-permute-start.1 = (bf16[3,48,1024]{2,1,0:T(8,128)(2,1)}, bf16[3,48,1024]{2,1,0:T(8,128)(2,1)S(1)}, u32[]{:S(2)}, u32[]{:S(2)}) collective-permute-start(bf16[3,48,1024]{2,1,0:T(8,128)(2,1)} %get-tuple-element.63), channel_id=1, source_target_pairs={{0,128},{64,192},{128,0},{192,64},{1,129},{65,193},{129,1},{193,65... | collective-permute-start | bytes 884744 | tf_op jit(solution)/shard_map/ppermute | solution.py:641
  101.5 21.9 %collective-permute-start.2 = (bf16[3,48,1024]{2,1,0:T(8,128)(2,1)}, bf16[3,48,1024]{2,1,0:T(8,128)(2,1)S(1)}, u32[]{:S(2)}, u32[]{:S(2)}) collective-permute-start(bf16[3,48,1024]{2,1,0:T(8,128)(2,1)} %get-tuple-element.64), channel_id=1, source_target_pairs={{0,64},{64,128},{128,192},{192,0},{1,65},{65,129},{129,193},{193,1... | collective-permute-start | bytes 884744 | tf_op jit(solution)/shard_map/ppermute | solution.py:641
  102.5 17.1 %collective-permute-start.17 = (bf16[2,1,48,1024]{3,2,1,0:T(8,128)(2,1)S(1)}, bf16[2,1,48,1024]{3,2,1,0:T(8,128)(2,1)S(1)}, u32[]{:S(2)}, u32[]{:S(2)}) collective-permute-start(bf16[2,1,48,1024]{3,2,1,0:T(8,128)(2,1)S(1)} %get-tuple-element.122), channel_id=1, source_target_pairs={{0,64},{64,128},{128,192},{192,0},{1,65},{65,129},{129,193},{193,1... | collective-permute-start | bytes 589832 | tf_op jit(solution)/shard_map/ppermute | solution.py:641
  146.1 19.1 %all-to-all-start.3 = ((bf16[64,8,128]{2,1,0:T(8,128)(2,1)}), bf16[64,8,128]{2,1,0:T(8,128)(2,1)S(1)}, u32[]{:S(2)}, u32[]{:S(2)}) async-start(bf16[64,8,128]{2,1,0:T(8,128)(2,1)} %get-tuple-element.117), calls=%async_computation.3 | async-start | bytes 262144 | tf_op jit(solution)/shard_map/all_to_all | solution.py:695
  158.9 15.0 %collective-permute-start.18 = (bf16[4,48,1024]{2,1,0:T(8,128)(2,1)}, bf16[4,48,1024]{2,1,0:T(8,128)(2,1)S(1)}, u32[]{:S(2)}, u32[]{:S(2)}) collective-permute-start(bf16[4,48,1024]{2,1,0:T(8,128)(2,1)} %get-tuple-element.114), channel_id=1, source_target_pairs={{0,64},{64,128},{128,192},{192,0},{1,65},{65,129},{129,193},{193,1... | collective-permute-start | bytes 1179656 | tf_op jit(solution)/shard_map/ppermute | solution.py:641
  159.2 14.7 %collective-permute-start.19 = (bf16[4,48,1024]{2,1,0:T(8,128)(2,1)}, bf16[4,48,1024]{2,1,0:T(8,128)(2,1)S(1)}, u32[]{:S(2)}, u32[]{:S(2)}) collective-permute-start(bf16[4,48,1024]{2,1,0:T(8,128)(2,1)} %get-tuple-element.115), channel_id=1, source_target_pairs={{0,128},{64,192},{128,0},{192,64},{1,129},{65,193},{129,1},{193,65... | collective-permute-start | bytes 1179656 | tf_op jit(solution)/shard_map/ppermute | solution.py:641
  162.5 17.6 %collective-permute-start.20 = (bf16[4,48,1024]{2,1,0:T(8,128)(2,1)}, bf16[4,48,1024]{2,1,0:T(8,128)(2,1)S(1)}, u32[]{:S(2)}, u32[]{:S(2)}) collective-permute-start(bf16[4,48,1024]{2,1,0:T(8,128)(2,1)} %get-tuple-element.116), channel_id=1, source_target_pairs={{0,192},{64,0},{128,64},{192,128},{1,193},{65,1},{129,65},{193,129... | collective-permute-start | bytes 1179656 | tf_op jit(solution)/shard_map/ppermute | solution.py:641
  166.0 19.3 %all-to-all-start.4 = ((bf16[64,8,128]{2,1,0:T(8,128)(2,1)}), bf16[64,8,128]{2,1,0:T(8,128)(2,1)S(1)}, u32[]{:S(2)}, u32[]{:S(2)}) async-start(bf16[64,8,128]{2,1,0:T(8,128)(2,1)} %router_total.1), calls=%async_computation.4 | async-start | bytes 262144 | tf_op jit(solution)/shard_map/all_to_all | solution.py:698
  (28 other events, 404.6 us)

commit v8 on v7

--- a/solution.py
+++ b/solution.py
@@ -335,7 +335,7 @@
     lead_ref, links_ref, last_ref, sum_ref, back_ref = refs[3 * sections + 7 :][:5]
     block_sems, info_sem, up_sem, links_sem, saved_sems, back_sems = refs[3 * sections + 12 :]
     p = p_ref[0]
-    _, rows, quarter = sum_ref.shape
+    _, _, rows, quarter = sum_ref.shape
     _, experts, _, half = block_ref.shape
     micro = up_ref.shape[0]
     n = experts * TILE
@@ -362,10 +362,10 @@
     ]
     for copy in [blocks[2], info] + lead + [up] + early + blocks[:2] + rest + [links]:
         copy.start()
-    out_row, in_row = iotas((2 * n, n))
-    within = out_row % (2 * experts)
-    order = in_row == (within % experts) * TILE + out_row // (2 * experts)
-    order = order.astype(BF16)
+    kept = micro * experts
+    out_row, in_row = iotas((4 * kept, n))
+    order = (out_row % experts) * TILE + out_row // (2 * kept) * micro + out_row % kept // experts
+    order = (in_row == order).astype(BF16)
     lane = lax.broadcasted_iota(jnp.int32, (rows, 128), 1)
     row, column = iotas((2 * sections, 128))
     eye = (row == column).astype(F32)
@@ -373,6 +373,16 @@
     last = block_ref[2].reshape(n, half)
     last_ref[...] = jnp.dot(order, last, preferred_element_type=F32).astype(BF16)
     info.wait()
+    for j in range(sections):
+        h, c = divmod(j, 2)
+        columns = slice(c * quarter, (c + 1) * quarter)
+        facts = info_ref[j, 2 * experts :, :]
+        gates = [facts[k : k + 1] for k in range(2)]
+        places = [facts[2 + k : 3 + k].astype(jnp.int32) for k in range(2)]
+        pick = split_pick(gates, places, n, kept)
+        received = last_ref[2 * h * kept : 2 * (h + 1) * kept, columns]
+        total = lax.dot_general(pick, received, TN, preferred_element_type=F32)
+        sum_ref[j] = total.reshape(micro, rows, quarter)
     for m in range(micro):
         if m == micro - 1:
             blocks[0].wait()
@@ -380,24 +390,21 @@
         for j in range(sections):
             h, c = divmod(j, 2)
             columns = slice(c * quarter, (c + 1) * quarter)
-            facts = info_ref[j, 2 * experts :, m * rows : (m + 1) * rows]
-            gates = [facts[k : k + 1] for k in range(2)]
-            places = [facts[2 + k : 3 + k].astype(jnp.int32) for k in range(2)]
-            start = (h * micro + m) * 2 * experts
-            pick = split_pick(gates, places, n + m * experts, experts)
-            received = last_ref[start : start + 2 * experts, columns]
-            total = lax.dot_general(pick, received, TN, preferred_element_type=F32)
             if m == micro - 1:
+                facts = info_ref[j, 2 * experts :, m * rows : (m + 1) * rows]
+                gates = [facts[k : k + 1] for k in range(2)]
+                places = [facts[2 + k : 3 + k].astype(jnp.int32) for k in range(2)]
                 main = block_ref[h, :, :, columns].reshape(n, quarter)
                 pick = split_pick(gates, places, 0, n)
-                total = total + lax.dot_general(
+                extra = lax.dot_general(
                     pick, jnp.concatenate([main, main], axis=0), TN, preferred_element_type=F32
                 )
             else:
                 if m == 0:
                     lead[j].wait()
-                total = total + lead_ref[j, m].astype(F32)
-            sum_ref[j] = total
+                extra = lead_ref[j, m].astype(F32)
+            total = sum_ref[j, m] + extra
+            sum_ref[j, m] = total
             back_ref[m, j] = total.astype(BF16)
         backs[m].start()
         if m == 0:
@@ -420,7 +427,7 @@
                 part = jnp.sum(part, axis=1, keepdims=True)
                 dots = jnp.where(lane == 2 * s + k, part, dots)
             if s > 0:
-                base = base + sum_ref[j]
+                base = base + sum_ref[j, m]
         dots = lax.dot_general(
             eye, dots, NT, precision=lax.Precision.HIGHEST, preferred_element_type=F32
         )
@@ -465,27 +472,32 @@
             pltpu.VMEM((sections,) + rest[0].shape, BF16),
             pltpu.VMEM((sections,) + lead[0].shape, BF16),
             pltpu.VMEM(links.shape, F32),
-            pltpu.VMEM((2 * experts * TILE, half), BF16),
-            pltpu.VMEM(part, F32),
+            pltpu.VMEM((4 * micro * experts, half), BF16),
+            pltpu.VMEM((sections, micro, rows, quarter), F32),
             pltpu.VMEM((micro,) + part, BF16),
             dma((3,)), dma, dma, dma, dma((3, sections)), dma((micro,)),
         ],
-        compiler_params=params(24),
+        compiler_params=params(32),
         name="tail_combine",
     )(p, *fetched)
 
 
 def dense_kernel(
-    micro, p_ref, sent_ref, info_ref, rows_ref, dense_hbm, part_hbm, dense_ref, part_ref, sems
+    micro, p_ref, sent_ref, info_hbm, rows_ref, dense_hbm, part_hbm, info_ref, dense_ref, part_ref, sems
 ):
+    copy = pltpu.make_async_copy(
+        info_hbm.at[:, pl.ds(0, info_ref.shape[1])], info_ref, sems.at[2]
+    )
+    copy.start()
     p = p_ref[0]
     sections = sent_ref.shape[0]
     tokens, width = rows_ref.shape
-    experts = (info_ref.shape[1] - 8) // 2
+    experts = info_ref.shape[1] // 2
     table = pairs(sections)
     given = sent_ref[0]
     for source in range(1, sections):
         given = given + sent_ref[source]
+    copy.wait()
     dots = {}
     own = jnp.zeros((experts, tokens), F32)
     for s in reversed(range(sections)):
@@ -523,30 +535,39 @@
     part = (experts // 8 * (width // 128), 8, 128)
     return pl.pallas_call(
         functools.partial(dense_kernel, micro),
-        in_specs=[SCALAR] + [WHOLE] * 3,
+        in_specs=[SCALAR, WHOLE, STAYS, WHOLE],
         out_specs=[STAYS] * 2,
         out_shape=[pltpu.HBM(dense, BF16), pltpu.HBM(part, BF16)],
         scratch_shapes=[
+            pltpu.VMEM((sections, 2 * experts, tokens), F32),
             pltpu.VMEM(dense, BF16),
             pltpu.VMEM(part, BF16),
-            pltpu.SemaphoreType.DMA((2,)),
+            pltpu.SemaphoreType.DMA((3,)),
         ],
         compiler_params=params(32),
         name="dense",
-    )(p, sent, info, normed)
-
-
-def grads_kernel(p_ref, up_ref, back_hbm, dense_ref, w_ref, *refs):
-    outs = refs[:-5]
-    back_ref, total_ref, turn_ref, back_sems, out_sems = refs[-5:]
+    )(p, sent, in_hbm(info), normed)
+
+
+def grads_kernel(p_ref, up_hbm, back_hbm, dense_hbm, w_hbm, *refs):
+    outs = refs[:-8]
+    up_ref, dense_ref, w_ref, back_ref, total_ref, turn_ref, in_sems, out_sems = refs[-8:]
     p = p_ref[0]
     sections, micro, rows, quarter = turn_ref.shape
     experts = w_ref.shape[1]
+    small = [
+        pltpu.make_async_copy(source, target, in_sems.at[micro + i])
+        for i, (source, target) in enumerate(
+            ((up_hbm, up_ref), (dense_hbm, dense_ref), (w_hbm, w_ref))
+        )
+    ]
     copies = [
-        pltpu.make_async_copy(back_hbm.at[:, m], back_ref.at[m], back_sems.at[m]) for m in range(micro)
-    ]
-    for copy in copies:
+        pltpu.make_async_copy(back_hbm.at[:, m], back_ref.at[m], in_sems.at[m]) for m in range(micro)
+    ]
+    for copy in small + copies:
         copy.start()
+    for copy in small:
+        copy.wait()
     total_ref[...] = up_ref[...].astype(F32)
     for s in reversed(range(sections)):
         j = (s - p) & (sections - 1)
@@ -570,19 +591,22 @@
     part = (micro, rows, quarter)
     return pl.pallas_call(
         grads_kernel,
-        in_specs=[SCALAR, WHOLE, STAYS, WHOLE, WHOLE],
+        in_specs=[SCALAR] + [STAYS] * 4,
         out_specs=[STAYS] * sections,
         out_shape=[pltpu.HBM(part, BF16)] * sections,
         scratch_shapes=[
+            pltpu.VMEM(part, BF16),
+            pltpu.VMEM(dense.shape, BF16),
+            pltpu.VMEM(w.shape, BF16),
             pltpu.VMEM((micro, sections, rows, quarter), BF16),
             pltpu.VMEM(part, F32),
             pltpu.VMEM((sections,) + part, BF16),
-            pltpu.SemaphoreType.DMA((micro,)),
+            pltpu.SemaphoreType.DMA((micro + 3,)),
             pltpu.SemaphoreType.DMA((sections,)),
         ],
         compiler_params=params(40),
         name="grads",
-    )(p, upstream, in_hbm(back), dense, w)
+    )(p, *[in_hbm(array) for array in (upstream, back, dense, w)])
 
 
 def total_kernel(parts_ref, out_hbm, out_ref, sem):

time: 187 us -> 184 us (0.984)
  local copies, waits for them, and re-layouts: 14.3 us -> 11.7 us
    unnamed x55 -> x47, local copies, waits for them, and re-layouts: 10.8 us -> 8.23 us
where the time goes in v8:
time: 184 us; the launch traced here: 183 us
  waiting for transfers between devices  72.4 us (39%)
  starting transfers between devices  57.8 us (31%)
  Pallas kernels  30.1 us (16%)
  local copies, waits for them, and re-layouts  11.7 us (6%)
  blocking collectives  9.65 us (5%)
    ppermute x21, waiting for transfers between devices, turned(): lax.ppermute(block, 'pipe', [(i, (i + distance) % n) for i in range(n)])  55 us
    ppermute x21, starting transfers between devices, turned(): lax.ppermute(block, 'pipe', [(i, (i + distance) % n) for i in range(n)])  29.9 us
    all_to_all x1, blocking collectives, on_device(): sent = lax.all_to_all(sent, 'pipe', 0, 0, tiled=True)  9.65 us
    all_to_all x1, starting transfers between devices, on_device(): lax.all_to_all(lead_pack(grads, micro - 1), 'expert', 0, 0, tiled=True)  8.77 us
    all_to_all x1, waiting for transfers between devices, on_device(): lax.all_to_all(lead_pack(grads, micro - 1), 'expert', 0, 0, tiled=True)  8.57 us
    unnamed x47, local copies, waits for them, and re-layouts  8.23 us
    all_to_all x1, starting transfers between devices, on_device(): partial = lax.all_to_all(partial, axes, 0, 0, tiled=True)  8 us
    all_to_all x1, starting transfers between devices, on_device(): total = lax.all_to_all(total_for_all(partial), axes, 0, 0, tiled=True)  6.4 us
  transfers between devices with their start and end apart: 25, of which 13 were waited for; matrix products, arithmetic and copies ran while one was open for 3% of the time, Pallas kernels for 10%

profile of v8, /device:TPU:8, one launch (start us, length us, event | category | flops | bytes accessed | tf_op | source)
XLA Modules:
  0.0 183.4 jit_solution(16259891090885703673)
XLA Ops:
  0.6 3.6 %lead_pack.1 = bf16[16,48,2048]{2,1,0:T(8,128)(2,1)} custom-call(bf16[4,9,16,4096]{3,2,1,0:T(8,128)(2,1)} %bitcast.55), custom_call_target="tpu_custom_call" | custom-call | tf_op jit(solution)/shard_map/lead_pack/pallas_call | solution.py:70
  4.3 8.8 %all-to-all-start = ((bf16[16,48,2048]{2,1,0:T(8,128)(2,1)}), bf16[16,48,2048]{2,1,0:T(8,128)(2,1)}, u32[]{:S(2)}, u32[]{:S(2)}) async-start(bf16[16,48,2048]{2,1,0:T(8,128)(2,1)} %lead_pack.1), calls=%async_computation | async-start | bytes 6291456 | tf_op jit(solution)/shard_map/all_to_all | solution.py:691
  14.3 3.1 %collective-permute-start.6 = (bf16[16,1024]{1,0:T(8,128)(2,1)S(1)}, bf16[16,1024]{1,0:T(8,128)(2,1)S(1)}, u32[]{:S(2)}, u32[]{:S(2)}) collective-permute-start(bf16[16,1024]{1,0:T(8,128)(2,1)S(1)} %get-tuple-element.127), channel_id=1, source_target_pairs={{0,192},{64,0},{128,64},{192,128},{1,193},{65,1},{129,65},{193,129... | collective-permute-start | bytes 98312 | tf_op jit(solution)/shard_map/ppermute | solution.py:665
  25.9 2.9 %collective-permute-start.9 = (bf16[12,16,1024]{2,1,0:T(8,128)(2,1)S(1)}, bf16[12,16,1024]{2,1,0:T(8,128)(2,1)S(1)}, u32[]{:S(2)}, u32[]{:S(2)}) collective-permute-start(bf16[12,16,1024]{2,1,0:T(8,128)(2,1)S(1)} %get-tuple-element.79), channel_id=1, source_target_pairs={{0,192},{64,0},{128,64},{192,128},{1,193},{65,1},{129,65},{193,129... | collective-permute-start | bytes 1179656 | tf_op jit(solution)/shard_map/ppermute | solution.py:665
  35.8 2.6 %collective-permute-done.9.refs_1_ = bf16[12,16,1024]{2,1,0:T(8,128)(2,1)S(1)} collective-permute-done((bf16[12,16,1024]{2,1,0:T(8,128)(2,1)S(1)}, bf16[12,16,1024]{2,1,0:T(8,128)(2,1)S(1)}, u32[]{:S(2)}, u32[]{:S(2)}) %collective-permute-start.9) | collective-permute-done | bytes 393248 | tf_op jit(solution)/shard_map/ppermute | solution.py:665
  38.4 6.1 %collective-permute-done.10.refs_2_ = bf16[12,16,1024]{2,1,0:T(8,128)(2,1)S(1)} collective-permute-done((bf16[12,16,1024]{2,1,0:T(8,128)(2,1)S(1)}, bf16[12,16,1024]{2,1,0:T(8,128)(2,1)S(1)}, u32[]{:S(2)}, u32[]{:S(2)}) %collective-permute-start.10) | collective-permute-done | bytes 393248 | tf_op jit(solution)/shard_map/ppermute | solution.py:665
  45.8 2.9 %collective-permute-start.12 = (bf16[2,3,48,1024]{3,2,1,0:T(8,128)(2,1)S(1)}, bf16[2,3,48,1024]{3,2,1,0:T(8,128)(2,1)S(1)}, u32[]{:S(2)}, u32[]{:S(2)}) collective-permute-start(bf16[2,3,48,1024]{3,2,1,0:T(8,128)(2,1)S(1)} %get-tuple-element.86), channel_id=1, source_target_pairs={{0,192},{64,0},{128,64},{192,128},{1,193},{65,1},{129,65},{193,129... | collective-permute-start | bytes 1769480 | tf_op jit(solution)/shard_map/ppermute | solution.py:665
  52.5 9.8 %collective-permute-done.12.refs_1_.refs_5_ = bf16[2,3,48,1024]{3,2,1,0:T(8,128)(2,1)S(1)} collective-permute-done((bf16[2,3,48,1024]{3,2,1,0:T(8,128)(2,1)S(1)}, bf16[2,3,48,1024]{3,2,1,0:T(8,128)(2,1)S(1)}, u32[]{:S(2)}, u32[]{:S(2)}) %collective-permute-start.12) | collective-permute-done | bytes 589856 | tf_op jit(solution)/shard_map/ppermute | solution.py:665
  63.2 11.5 %collective-permute-done.13.refs_2_.refs_6_ = bf16[2,3,48,1024]{3,2,1,0:T(8,128)(2,1)S(1)} collective-permute-done((bf16[2,3,48,1024]{3,2,1,0:T(8,128)(2,1)S(1)}, bf16[2,3,48,1024]{3,2,1,0:T(8,128)(2,1)S(1)}, u32[]{:S(2)}, u32[]{:S(2)}) %collective-permute-start.13) | collective-permute-done | bytes 589856 | tf_op jit(solution)/shard_map/ppermute | solution.py:665
  76.3 8.6 %all-to-all-done.received_hbm = bf16[16,48,2048]{2,1,0:T(8,128)(2,1)} async-done(((bf16[16,48,2048]{2,1,0:T(8,128)(2,1)}), bf16[16,48,2048]{2,1,0:T(8,128)(2,1)}, u32[]{:S(2)}, u32[]{:S(2)}) %all-to-all-start) | async-done | bytes 3145760 | tf_op jit(solution)/shard_map/all_to_all | solution.py:691
  84.8 4.7 %all-to-all-start.1 = ((bf16[16,24,2048]{2,1,0:T(8,128)(2,1)}), bf16[16,24,2048]{2,1,0:T(8,128)(2,1)}, u32[]{:S(2)}, u32[]{:S(2)}) async-start(bf16[16,24,2048]{2,1,0:T(8,128)(2,1)} %tail_pack.1), calls=%async_computation.1 | async-start | bytes 3145728 | tf_op jit(solution)/shard_map/all_to_all | solution.py:706
  94.0 4.0 %lead_combine.1 = (bf16[3,48,1024]{2,1,0:T(8,128)(2,1)}, bf16[3,48,1024]{2,1,0:T(8,128)(2,1)}, bf16[3,48,1024]{2,1,0:T(8,128)(2,1)}, bf16[3,48,1024]{2,1,0:T(8,128)(2,1)}) custom-call(s32[1]{0:T(128)} %bitcast.p_ref, bf16[16,48,2048]{2,1,0:T(8,128)(2,1)} %all-to-all-done.received_hbm, f32[4,8,96]{2,1,0:T(8,128)S(1)} %get-tuple-element.60.near_ref), custom_call_target="tpu_custom_call" | custom-call | tf_op jit(solution)/shard_map/lead_combine/pallas_call | solution.py:315
  104.1 15.5 %collective-permute-done.17.refs_7_.refs_11_ = bf16[2,1,48,1024]{3,2,1,0:T(8,128)(2,1)S(1)} collective-permute-done((bf16[2,1,48,1024]{3,2,1,0:T(8,128)(2,1)S(1)}, bf16[2,1,48,1024]{3,2,1,0:T(8,128)(2,1)S(1)}, u32[]{:S(2)}, u32[]{:S(2)}) %collective-permute-start.17) | collective-permute-done | bytes 196640 | tf_op jit(solution)/shard_map/ppermute | solution.py:665
  119.7 3.0 %coupling.1.links_hbm = f32[24,192]{1,0:T(8,128)S(1)} custom-call(s32[1]{0:T(128)} %bitcast.p_ref, bf16[4,16,1024]{2,1,0:T(8,128)(2,1)S(1)} %pad_maximum_fusion.1.w_ref.w_hbm, f32[4,40,192]{2,1,0:T(8,128)S(1)} %pad_maximum_fusion.info_ref.info_hbm, bf16[2,3,48,1024]{3,2,1,0:T(8,128)(2,1)S(1)} %copy-done.2, bf16[2,3,48,1024]{3,2,1,0:T(8,128)(2,1)S(1)} %copy-done.5, ...), custom_call_target="tpu_custom_call" | custom-call | tf_op jit(solution)/shard_map/coupling/pallas_call | solution.py:251
  124.8 2.6 %all-to-all-done.1.received_hbm = bf16[16,24,2048]{2,1,0:T(8,128)(2,1)} async-done(((bf16[16,24,2048]{2,1,0:T(8,128)(2,1)}), bf16[16,24,2048]{2,1,0:T(8,128)(2,1)}, u32[]{:S(2)}, u32[]{:S(2)}) %all-to-all-start.1) | async-done | bytes 1572896 | tf_op jit(solution)/shard_map/all_to_all | solution.py:706
  127.5 6.0 %tail_combine.1 = (bf16[4,4,48,1024]{3,2,1,0:T(8,128)(2,1)}, f32[4,32,192]{2,1,0:T(8,128)S(1)}) custom-call(s32[1]{0:T(128)} %bitcast.p_ref, bf16[16,24,2048]{2,1,0:T(8,128)(2,1)} %all-to-all-done.1.received_hbm, f32[4,40,192]{2,1,0:T(8,128)} %copy-done.3, bf16[4,48,1024]{2,1,0:T(8,128)(2,1)} %constant_dynamic-slice_fusion.up_hbm, f32[24,192]{1,0:T(8,128)} %copy-done.16, ...), custom_call_target="tpu_custom_call" | custom-call | tf_op jit(solution)/shard_map/tail_combine/pallas_call | solution.py:459
  133.5 9.7 %all_to_all.25.sent_ref = f32[4,32,192]{2,1,0:T(8,128)S(1)} all-to-all(f32[4,32,192]{2,1,0:T(8,128)S(1)} %get-tuple-element.110), channel_id=1, replica_groups=mesh['pipe'=4,'expert'=16,'dp'=4] {'pipe'}, dimensions={0} | all-to-all | bytes 196608 | tf_op jit(solution)/shard_map/all_to_all | solution.py:715
  145.0 8.0 %all-to-all-start.3 = ((bf16[64,8,128]{2,1,0:T(8,128)(2,1)}), bf16[64,8,128]{2,1,0:T(8,128)(2,1)S(1)}, u32[]{:S(2)}, u32[]{:S(2)}) async-start(bf16[64,8,128]{2,1,0:T(8,128)(2,1)} %get-tuple-element.117), calls=%async_computation.3 | async-start | bytes 262144 | tf_op jit(solution)/shard_map/all_to_all | solution.py:719
  153.0 3.3 %grads.1 = (bf16[4,48,1024]{2,1,0:T(8,128)(2,1)}, bf16[4,48,1024]{2,1,0:T(8,128)(2,1)}, bf16[4,48,1024]{2,1,0:T(8,128)(2,1)}, bf16[4,48,1024]{2,1,0:T(8,128)(2,1)}) custom-call(s32[1]{0:T(128)} %bitcast.p_ref, bf16[4,48,1024]{2,1,0:T(8,128)(2,1)} %constant_dynamic-slice_fusion.up_hbm, bf16[4,4,48,1024]{3,2,1,0:T(8,128)(2,1)} %get-tuple-element.109.back_hbm, ...), custom_call_target="tpu_custom_call" | custom-call | tf_op jit(solution)/shard_map/grads/pallas_call | solution.py:592
  156.6 3.3 %collective-permute-start.19 = (bf16[4,48,1024]{2,1,0:T(8,128)(2,1)}, bf16[4,48,1024]{2,1,0:T(8,128)(2,1)S(1)}, u32[]{:S(2)}, u32[]{:S(2)}) collective-permute-start(bf16[4,48,1024]{2,1,0:T(8,128)(2,1)} %get-tuple-element.115), channel_id=1, source_target_pairs={{0,128},{64,192},{128,0},{192,64},{1,129},{65,193},{129,1},{193,65... | collective-permute-start | bytes 1179656 | tf_op jit(solution)/shard_map/ppermute | solution.py:665
  160.5 3.7 %all-to-all-done.3.parts_ref = bf16[64,8,128]{2,1,0:T(8,128)(2,1)S(1)} async-done(((bf16[64,8,128]{2,1,0:T(8,128)(2,1)}), bf16[64,8,128]{2,1,0:T(8,128)(2,1)S(1)}, u32[]{:S(2)}, u32[]{:S(2)}) %all-to-all-start.3) | async-done | bytes 131104 | tf_op jit(solution)/shard_map/all_to_all | solution.py:719
  164.9 6.4 %all-to-all-start.4 = ((bf16[64,8,128]{2,1,0:T(8,128)(2,1)}), bf16[64,8,128]{2,1,0:T(8,128)(2,1)S(1)}, u32[]{:S(2)}, u32[]{:S(2)}) async-start(bf16[64,8,128]{2,1,0:T(8,128)(2,1)} %router_total.1), calls=%async_computation.4 | async-start | bytes 262144 | tf_op jit(solution)/shard_map/all_to_all | solution.py:722
  171.4 6.2 %collective-permute-done.20.refs_3_ = bf16[4,48,1024]{2,1,0:T(8,128)(2,1)S(1)} collective-permute-done((bf16[4,48,1024]{2,1,0:T(8,128)(2,1)}, bf16[4,48,1024]{2,1,0:T(8,128)(2,1)S(1)}, u32[]{:S(2)}, u32[]{:S(2)}) %collective-permute-start.20) | collective-permute-done | bytes 393248 | tf_op jit(solution)/shard_map/ppermute | solution.py:665
  177.5 2.7 %join.1 = bf16[4,48,4096]{2,1,0:T(8,128)(2,1)} custom-call(s32[1]{0:T(128)} %bitcast.p_ref, bf16[4,48,1024]{2,1,0:T(8,128)(2,1)} %get-tuple-element.113.refs_0_, bf16[4,48,1024]{2,1,0:T(8,128)(2,1)S(1)} %collective-permute-done.18.refs_1_, bf16[4,48,1024]{2,1,0:T(8,128)(2,1)S(1)} %collective-permute-done.19.refs_2_, ...), custom_call_target="tpu_custom_call" | custom-call | tf_op jit(solution)/shard_map/join/pallas_call | solution.py:649
  (96 shorter events, 43.7 us)
Async XLA Ops:
  4.3 80.6 %all-to-all-start = ((bf16[16,48,2048]{2,1,0:T(8,128)(2,1)}), bf16[16,48,2048]{2,1,0:T(8,128)(2,1)}, u32[]{:S(2)}, u32[]{:S(2)}) async-start(bf16[16,48,2048]{2,1,0:T(8,128)(2,1)} %lead_pack.1), calls=%async_computation | async-start | bytes 6291456 | tf_op jit(solution)/shard_map/all_to_all | solution.py:691
  13.8 7.1 %collective-permute-start.3 = (f32[40,192]{1,0:T(8,128)S(1)}, f32[40,192]{1,0:T(8,128)S(1)}, u32[]{:S(2)}, u32[]{:S(2)}) collective-permute-start(f32[40,192]{1,0:T(8,128)S(1)} %get-tuple-element.70), channel_id=1, source_target_pairs={{0,192},{64,0},{128,64},{192,128},{1,193},{65,1},{129,65},{193,129... | collective-permute-start | bytes 92168 | tf_op jit(solution)/shard_map/ppermute | solution.py:665
  14.3 11.7 %collective-permute-start.6 = (bf16[16,1024]{1,0:T(8,128)(2,1)S(1)}, bf16[16,1024]{1,0:T(8,128)(2,1)S(1)}, u32[]{:S(2)}, u32[]{:S(2)}) collective-permute-start(bf16[16,1024]{1,0:T(8,128)(2,1)S(1)} %get-tuple-element.127), channel_id=1, source_target_pairs={{0,192},{64,0},{128,64},{192,128},{1,193},{65,1},{129,65},{193,129... | collective-permute-start | bytes 98312 | tf_op jit(solution)/shard_map/ppermute | solution.py:665
  17.4 8.6 %collective-permute-start.7 = (bf16[16,1024]{1,0:T(8,128)(2,1)S(1)}, bf16[16,1024]{1,0:T(8,128)(2,1)S(1)}, u32[]{:S(2)}, u32[]{:S(2)}) collective-permute-start(bf16[16,1024]{1,0:T(8,128)(2,1)S(1)} %get-tuple-element.129), channel_id=1, source_target_pairs={{0,128},{64,192},{128,0},{192,64},{1,129},{65,193},{129,1},{193,65... | collective-permute-start | bytes 98312 | tf_op jit(solution)/shard_map/ppermute | solution.py:665
  17.4 8.6 %collective-permute-start.8 = (bf16[16,1024]{1,0:T(8,128)(2,1)S(1)}, bf16[16,1024]{1,0:T(8,128)(2,1)S(1)}, u32[]{:S(2)}, u32[]{:S(2)}) collective-permute-start(bf16[16,1024]{1,0:T(8,128)(2,1)S(1)} %get-tuple-element.126), channel_id=1, source_target_pairs={{0,64},{64,128},{128,192},{192,0},{1,65},{65,129},{129,193},{193,1... | collective-permute-start | bytes 98312 | tf_op jit(solution)/shard_map/ppermute | solution.py:665
  19.6 5.5 %collective-permute-start.4 = (f32[40,192]{1,0:T(8,128)S(1)}, f32[40,192]{1,0:T(8,128)S(1)}, u32[]{:S(2)}, u32[]{:S(2)}) collective-permute-start(f32[40,192]{1,0:T(8,128)S(1)} %get-tuple-element.70), channel_id=1, source_target_pairs={{0,128},{64,192},{128,0},{192,64},{1,129},{65,193},{129,1},{193,65... | collective-permute-start | bytes 92168 | tf_op jit(solution)/shard_map/ppermute | solution.py:665
  25.9 12.5 %collective-permute-start.9 = (bf16[12,16,1024]{2,1,0:T(8,128)(2,1)S(1)}, bf16[12,16,1024]{2,1,0:T(8,128)(2,1)S(1)}, u32[]{:S(2)}, u32[]{:S(2)}) collective-permute-start(bf16[12,16,1024]{2,1,0:T(8,128)(2,1)S(1)} %get-tuple-element.79), channel_id=1, source_target_pairs={{0,192},{64,0},{128,64},{192,128},{1,193},{65,1},{129,65},{193,129... | collective-permute-start | bytes 1179656 | tf_op jit(solution)/shard_map/ppermute | solution.py:665
  28.8 15.7 %collective-permute-start.10 = (bf16[12,16,1024]{2,1,0:T(8,128)(2,1)S(1)}, bf16[12,16,1024]{2,1,0:T(8,128)(2,1)S(1)}, u32[]{:S(2)}, u32[]{:S(2)}) collective-permute-start(bf16[12,16,1024]{2,1,0:T(8,128)(2,1)S(1)} %get-tuple-element.80), channel_id=1, source_target_pairs={{0,128},{64,192},{128,0},{192,64},{1,129},{65,193},{129,1},{193,65... | collective-permute-start | bytes 1179656 | tf_op jit(solution)/shard_map/ppermute | solution.py:665
  28.8 16.9 %collective-permute-start.11 = (bf16[12,16,1024]{2,1,0:T(8,128)(2,1)S(1)}, bf16[12,16,1024]{2,1,0:T(8,128)(2,1)S(1)}, u32[]{:S(2)}, u32[]{:S(2)}) collective-permute-start(bf16[12,16,1024]{2,1,0:T(8,128)(2,1)S(1)} %get-tuple-element.81), channel_id=1, source_target_pairs={{0,64},{64,128},{128,192},{192,0},{1,65},{65,129},{129,193},{193,1... | collective-permute-start | bytes 1179656 | tf_op jit(solution)/shard_map/ppermute | solution.py:665
  45.8 16.6 %collective-permute-start.12 = (bf16[2,3,48,1024]{3,2,1,0:T(8,128)(2,1)S(1)}, bf16[2,3,48,1024]{3,2,1,0:T(8,128)(2,1)S(1)}, u32[]{:S(2)}, u32[]{:S(2)}) collective-permute-start(bf16[2,3,48,1024]{3,2,1,0:T(8,128)(2,1)S(1)} %get-tuple-element.86), channel_id=1, source_target_pairs={{0,192},{64,0},{128,64},{192,128},{1,193},{65,1},{129,65},{193,129... | collective-permute-start | bytes 1769480 | tf_op jit(solution)/shard_map/ppermute | solution.py:665
  48.6 26.0 %collective-permute-start.13 = (bf16[2,3,48,1024]{3,2,1,0:T(8,128)(2,1)S(1)}, bf16[2,3,48,1024]{3,2,1,0:T(8,128)(2,1)S(1)}, u32[]{:S(2)}, u32[]{:S(2)}) collective-permute-start(bf16[2,3,48,1024]{3,2,1,0:T(8,128)(2,1)S(1)} %get-tuple-element.87), channel_id=1, source_target_pairs={{0,128},{64,192},{128,0},{192,64},{1,129},{65,193},{129,1},{193,65... | collective-permute-start | bytes 1769480 | tf_op jit(solution)/shard_map/ppermute | solution.py:665
  48.7 26.8 %collective-permute-start.14 = (bf16[2,3,48,1024]{3,2,1,0:T(8,128)(2,1)S(1)}, bf16[2,3,48,1024]{3,2,1,0:T(8,128)(2,1)S(1)}, u32[]{:S(2)}, u32[]{:S(2)}) collective-permute-start(bf16[2,3,48,1024]{3,2,1,0:T(8,128)(2,1)S(1)} %get-tuple-element.88), channel_id=1, source_target_pairs={{0,64},{64,128},{128,192},{192,0},{1,65},{65,129},{129,193},{193,1... | collective-permute-start | bytes 1769480 | tf_op jit(solution)/shard_map/ppermute | solution.py:665
  84.8 42.6 %all-to-all-start.1 = ((bf16[16,24,2048]{2,1,0:T(8,128)(2,1)}), bf16[16,24,2048]{2,1,0:T(8,128)(2,1)}, u32[]{:S(2)}, u32[]{:S(2)}) async-start(bf16[16,24,2048]{2,1,0:T(8,128)(2,1)} %tail_pack.1), calls=%async_computation.1 | async-start | bytes 3145728 | tf_op jit(solution)/shard_map/all_to_all | solution.py:706
  90.9 11.6 %collective-permute-start.15 = (bf16[2,1,48,1024]{3,2,1,0:T(8,128)(2,1)S(1)}, bf16[2,1,48,1024]{3,2,1,0:T(8,128)(2,1)S(1)}, u32[]{:S(2)}, u32[]{:S(2)}) collective-permute-start(bf16[2,1,48,1024]{3,2,1,0:T(8,128)(2,1)S(1)} %get-tuple-element.124), channel_id=1, source_target_pairs={{0,192},{64,0},{128,64},{192,128},{1,193},{65,1},{129,65},{193,129... | collective-permute-start | bytes 589832 | tf_op jit(solution)/shard_map/ppermute | solution.py:665
  91.4 12.7 %collective-permute-start.16 = (bf16[2,1,48,1024]{3,2,1,0:T(8,128)(2,1)S(1)}, bf16[2,1,48,1024]{3,2,1,0:T(8,128)(2,1)S(1)}, u32[]{:S(2)}, u32[]{:S(2)}) collective-permute-start(bf16[2,1,48,1024]{3,2,1,0:T(8,128)(2,1)S(1)} %get-tuple-element.123), channel_id=1, source_target_pairs={{0,128},{64,192},{128,0},{192,64},{1,129},{65,193},{129,1},{193,65... | collective-permute-start | bytes 589832 | tf_op jit(solution)/shard_map/ppermute | solution.py:665
  98.0 25.3 %collective-permute-start = (bf16[3,48,1024]{2,1,0:T(8,128)(2,1)}, bf16[3,48,1024]{2,1,0:T(8,128)(2,1)S(1)}, u32[]{:S(2)}, u32[]{:S(2)}) collective-permute-start(bf16[3,48,1024]{2,1,0:T(8,128)(2,1)} %get-tuple-element.62), channel_id=1, source_target_pairs={{0,192},{64,0},{128,64},{192,128},{1,193},{65,1},{129,65},{193,129... | collective-permute-start | bytes 884744 | tf_op jit(solution)/shard_map/ppermute | solution.py:665
  99.2 24.1 %collective-permute-start.1 = (bf16[3,48,1024]{2,1,0:T(8,128)(2,1)}, bf16[3,48,1024]{2,1,0:T(8,128)(2,1)S(1)}, u32[]{:S(2)}, u32[]{:S(2)}) collective-permute-start(bf16[3,48,1024]{2,1,0:T(8,128)(2,1)} %get-tuple-element.63), channel_id=1, source_target_pairs={{0,128},{64,192},{128,0},{192,64},{1,129},{65,193},{129,1},{193,65... | collective-permute-start | bytes 884744 | tf_op jit(solution)/shard_map/ppermute | solution.py:665
  101.5 21.9 %collective-permute-start.2 = (bf16[3,48,1024]{2,1,0:T(8,128)(2,1)}, bf16[3,48,1024]{2,1,0:T(8,128)(2,1)S(1)}, u32[]{:S(2)}, u32[]{:S(2)}) collective-permute-start(bf16[3,48,1024]{2,1,0:T(8,128)(2,1)} %get-tuple-element.64), channel_id=1, source_target_pairs={{0,64},{64,128},{128,192},{192,0},{1,65},{65,129},{129,193},{193,1... | collective-permute-start | bytes 884744 | tf_op jit(solution)/shard_map/ppermute | solution.py:665
  102.5 17.1 %collective-permute-start.17 = (bf16[2,1,48,1024]{3,2,1,0:T(8,128)(2,1)S(1)}, bf16[2,1,48,1024]{3,2,1,0:T(8,128)(2,1)S(1)}, u32[]{:S(2)}, u32[]{:S(2)}) collective-permute-start(bf16[2,1,48,1024]{3,2,1,0:T(8,128)(2,1)S(1)} %get-tuple-element.122), channel_id=1, source_target_pairs={{0,64},{64,128},{128,192},{192,0},{1,65},{65,129},{129,193},{193,1... | collective-permute-start | bytes 589832 | tf_op jit(solution)/shard_map/ppermute | solution.py:665
  145.0 19.2 %all-to-all-start.3 = ((bf16[64,8,128]{2,1,0:T(8,128)(2,1)}), bf16[64,8,128]{2,1,0:T(8,128)(2,1)S(1)}, u32[]{:S(2)}, u32[]{:S(2)}) async-start(bf16[64,8,128]{2,1,0:T(8,128)(2,1)} %get-tuple-element.117), calls=%async_computation.3 | async-start | bytes 262144 | tf_op jit(solution)/shard_map/all_to_all | solution.py:719
  156.3 15.0 %collective-permute-start.18 = (bf16[4,48,1024]{2,1,0:T(8,128)(2,1)}, bf16[4,48,1024]{2,1,0:T(8,128)(2,1)S(1)}, u32[]{:S(2)}, u32[]{:S(2)}) collective-permute-start(bf16[4,48,1024]{2,1,0:T(8,128)(2,1)} %get-tuple-element.114), channel_id=1, source_target_pairs={{0,64},{64,128},{128,192},{192,0},{1,65},{65,129},{129,193},{193,1... | collective-permute-start | bytes 1179656 | tf_op jit(solution)/shard_map/ppermute | solution.py:665
  156.6 14.7 %collective-permute-start.19 = (bf16[4,48,1024]{2,1,0:T(8,128)(2,1)}, bf16[4,48,1024]{2,1,0:T(8,128)(2,1)S(1)}, u32[]{:S(2)}, u32[]{:S(2)}) collective-permute-start(bf16[4,48,1024]{2,1,0:T(8,128)(2,1)} %get-tuple-element.115), channel_id=1, source_target_pairs={{0,128},{64,192},{128,0},{192,64},{1,129},{65,193},{129,1},{193,65... | collective-permute-start | bytes 1179656 | tf_op jit(solution)/shard_map/ppermute | solution.py:665
  159.9 17.6 %collective-permute-start.20 = (bf16[4,48,1024]{2,1,0:T(8,128)(2,1)}, bf16[4,48,1024]{2,1,0:T(8,128)(2,1)S(1)}, u32[]{:S(2)}, u32[]{:S(2)}) collective-permute-start(bf16[4,48,1024]{2,1,0:T(8,128)(2,1)} %get-tuple-element.116), channel_id=1, source_target_pairs={{0,192},{64,0},{128,64},{192,128},{1,193},{65,1},{129,65},{193,129... | collective-permute-start | bytes 1179656 | tf_op jit(solution)/shard_map/ppermute | solution.py:665
  164.9 17.8 %all-to-all-start.4 = ((bf16[64,8,128]{2,1,0:T(8,128)(2,1)}), bf16[64,8,128]{2,1,0:T(8,128)(2,1)S(1)}, u32[]{:S(2)}, u32[]{:S(2)}) async-start(bf16[64,8,128]{2,1,0:T(8,128)(2,1)} %router_total.1), calls=%async_computation.4 | async-start | bytes 262144 | tf_op jit(solution)/shard_map/all_to_all | solution.py:722
  (24 other events, 382.3 us)

commit v9 on v8

--- a/solution.py
+++ b/solution.py
@@ -331,9 +331,9 @@
 def tail_kernel(p_ref, received_hbm, info_hbm, up_hbm, links_hbm, *refs):
     sections = info_hbm.shape[0]
     lead_hbm, early_hbm, rest_hbm = [refs[i * sections : (i + 1) * sections] for i in range(3)]
-    back_hbm, sent_ref, block_ref, info_ref, up_ref, early_ref, rest_ref = refs[3 * sections :][:7]
-    lead_ref, links_ref, last_ref, sum_ref, back_ref = refs[3 * sections + 7 :][:5]
-    block_sems, info_sem, up_sem, links_sem, saved_sems, back_sems = refs[3 * sections + 12 :]
+    back_hbm, sent_ref, v_ref, block_ref, info_ref, up_ref, early_ref, rest_ref = refs[3 * sections :][:8]
+    lead_ref, links_ref, last_ref, sum_ref, back_ref = refs[3 * sections + 8 :][:5]
+    block_sems, info_sem, up_sem, links_sem, saved_sems, back_sems = refs[3 * sections + 13 :]
     p = p_ref[0]
     _, _, rows, quarter = sum_ref.shape
     _, experts, _, half = block_ref.shape
@@ -373,6 +373,7 @@
     last = block_ref[2].reshape(n, half)
     last_ref[...] = jnp.dot(order, last, preferred_element_type=F32).astype(BF16)
     info.wait()
+    v_ref[...] = info_ref[:, : 2 * experts]
     for j in range(sections):
         h, c = divmod(j, 2)
         columns = slice(c * quarter, (c + 1) * quarter)
@@ -459,10 +460,11 @@
     return pl.pallas_call(
         tail_kernel,
         in_specs=[SCALAR] + [STAYS] * len(fetched),
-        out_specs=[STAYS, WHOLE],
+        out_specs=[STAYS, WHOLE, WHOLE],
         out_shape=[
             pltpu.HBM((sections, micro, rows, quarter), BF16),
             jax.ShapeDtypeStruct((sections, 2 * sections + links.shape[0], micro * rows), F32),
+            jax.ShapeDtypeStruct((sections, 2 * experts, micro * rows), F32),
         ],
         scratch_shapes=[
             pltpu.VMEM((3, experts, TILE, half), BF16),
@@ -483,21 +485,16 @@
 
 
 def dense_kernel(
-    micro, p_ref, sent_ref, info_hbm, rows_ref, dense_hbm, part_hbm, info_ref, dense_ref, part_ref, sems
+    micro, p_ref, sent_ref, v_ref, rows_ref, dense_hbm, part_hbm, dense_ref, part_ref, sems
 ):
-    copy = pltpu.make_async_copy(
-        info_hbm.at[:, pl.ds(0, info_ref.shape[1])], info_ref, sems.at[2]
-    )
-    copy.start()
     p = p_ref[0]
     sections = sent_ref.shape[0]
     tokens, width = rows_ref.shape
-    experts = info_ref.shape[1] // 2
+    experts = v_ref.shape[1] // 2
     table = pairs(sections)
     given = sent_ref[0]
     for source in range(1, sections):
         given = given + sent_ref[source]
-    copy.wait()
     dots = {}
     own = jnp.zeros((experts, tokens), F32)
     for s in reversed(range(sections)):
@@ -510,7 +507,7 @@
                     row = 2 * sections + table[(s, k, upper, k2)]
                     value = value + given[row : row + 1, :] * dots[(upper, k2)]
             dots[(s, k)] = value
-            dense = dense + value * info_ref[j, k * experts : (k + 1) * experts, :]
+            dense = dense + value * v_ref[j, k * experts : (k + 1) * experts, :]
         dense_ref[s * experts : (s + 1) * experts, :] = dense.astype(BF16)
         own = jnp.where(p == s, dense, own)
     out_dense = pltpu.make_async_copy(dense_ref, dense_hbm, sems.at[0])
@@ -527,26 +524,25 @@
     out_part.wait()
 
 
-def dense_terms(p, sent, info, normed, micro):
+def dense_terms(p, sent, v, normed, micro):
     sections, _, tokens = sent.shape
     width = normed.shape[1]
-    experts = (info.shape[1] - 8) // 2
+    experts = v.shape[1] // 2
     dense = (sections * experts, tokens)
     part = (experts // 8 * (width // 128), 8, 128)
     return pl.pallas_call(
         functools.partial(dense_kernel, micro),
-        in_specs=[SCALAR, WHOLE, STAYS, WHOLE],
+        in_specs=[SCALAR, WHOLE, WHOLE, WHOLE],
         out_specs=[STAYS] * 2,
         out_shape=[pltpu.HBM(dense, BF16), pltpu.HBM(part, BF16)],
         scratch_shapes=[
-            pltpu.VMEM((sections, 2 * experts, tokens), F32),
             pltpu.VMEM(dense, BF16),
             pltpu.VMEM(part, BF16),
-            pltpu.SemaphoreType.DMA((3,)),
+            pltpu.SemaphoreType.DMA((2,)),
         ],
         compiler_params=params(32),
         name="dense",
-    )(p, sent, in_hbm(info), normed)
+    )(p, sent, v, normed)
 
 
 def grads_kernel(p_ref, up_hbm, back_hbm, dense_hbm, w_hbm, *refs):
@@ -711,9 +707,9 @@
     lead, info_all, w_all, early, rest, links, up = lax.optimization_barrier(
         (lead, info_all, w_all, early, rest, links, up)
     )
-    back, sent = tail_combine(p, tail, info_all, up, links, lead, early, rest)
+    back, sent, v = tail_combine(p, tail, info_all, up, links, lead, early, rest)
     sent = lax.all_to_all(sent, "pipe", 0, 0, tiled=True)
-    dense, partial = dense_terms(p, sent, info_all, normed, micro)
+    dense, partial = dense_terms(p, sent, v, normed, micro)
 
     axes = ("expert", "dp")
     partial = lax.all_to_all(partial, axes, 0, 0, tiled=True)

time: 184 us -> 183 us (level)
  no operation moved by 1% of the time
where the time goes in v9:
time: 183 us
  waiting for transfers between devices  72.4 us (40%)
  starting transfers between devices  57.8 us (32%)
  Pallas kernels  29.1 us (16%)
  local copies, waits for them, and re-layouts  11.7 us (6%)
  blocking collectives  9.67 us (5%)
    ppermute x21, waiting for transfers between devices, turned(): lax.ppermute(block, 'pipe', [(i, (i + distance) % n) for i in range(n)])  55 us
    ppermute x21, starting transfers between devices, turned(): lax.ppermute(block, 'pipe', [(i, (i + distance) % n) for i in range(n)])  29.9 us
    all_to_all x1, blocking collectives, on_device(): sent = lax.all_to_all(sent, 'pipe', 0, 0, tiled=True)  9.67 us
    all_to_all x1, starting transfers between devices, on_device(): lax.all_to_all(lead_pack(grads, micro - 1), 'expert', 0, 0, tiled=True)  8.77 us
    all_to_all x1, waiting for transfers between devices, on_device(): lax.all_to_all(lead_pack(grads, micro - 1), 'expert', 0, 0, tiled=True)  8.57 us
    unnamed x47, local copies, waits for them, and re-layouts  8.23 us
    all_to_all x1, starting transfers between devices, on_device(): partial = lax.all_to_all(partial, axes, 0, 0, tiled=True)  7.99 us
    all_to_all x1, starting transfers between devices, on_device(): total = lax.all_to_all(total_for_all(partial), axes, 0, 0, tiled=True)  6.4 us
  transfers between devices with their start and end apart: 25, of which 13 were waited for; matrix products, arithmetic and copies ran while one was open for 3% of the time, Pallas kernels for 10%

profile of v9, /device:TPU:8, one launch (start us, length us, event | category | flops | bytes accessed | tf_op | source)
XLA Modules:
  0.0 182.5 jit_solution(5867994644363730048)
XLA Ops:
  0.6 3.6 %lead_pack.1 = bf16[16,48,2048]{2,1,0:T(8,128)(2,1)} custom-call(bf16[4,9,16,4096]{3,2,1,0:T(8,128)(2,1)} %bitcast.55), custom_call_target="tpu_custom_call" | custom-call | tf_op jit(solution)/shard_map/lead_pack/pallas_call | solution.py:70
  4.3 8.8 %all-to-all-start = ((bf16[16,48,2048]{2,1,0:T(8,128)(2,1)}), bf16[16,48,2048]{2,1,0:T(8,128)(2,1)}, u32[]{:S(2)}, u32[]{:S(2)}) async-start(bf16[16,48,2048]{2,1,0:T(8,128)(2,1)} %lead_pack.1), calls=%async_computation | async-start | bytes 6291456 | tf_op jit(solution)/shard_map/all_to_all | solution.py:687
  14.3 3.1 %collective-permute-start.6 = (bf16[16,1024]{1,0:T(8,128)(2,1)S(1)}, bf16[16,1024]{1,0:T(8,128)(2,1)S(1)}, u32[]{:S(2)}, u32[]{:S(2)}) collective-permute-start(bf16[16,1024]{1,0:T(8,128)(2,1)S(1)} %get-tuple-element.129), channel_id=1, source_target_pairs={{0,192},{64,0},{128,64},{192,128},{1,193},{65,1},{129,65},{193,129... | collective-permute-start | bytes 98312 | tf_op jit(solution)/shard_map/ppermute | solution.py:661
  25.9 2.9 %collective-permute-start.9 = (bf16[12,16,1024]{2,1,0:T(8,128)(2,1)S(1)}, bf16[12,16,1024]{2,1,0:T(8,128)(2,1)S(1)}, u32[]{:S(2)}, u32[]{:S(2)}) collective-permute-start(bf16[12,16,1024]{2,1,0:T(8,128)(2,1)S(1)} %get-tuple-element.80), channel_id=1, source_target_pairs={{0,192},{64,0},{128,64},{192,128},{1,193},{65,1},{129,65},{193,129... | collective-permute-start | bytes 1179656 | tf_op jit(solution)/shard_map/ppermute | solution.py:661
  35.8 2.6 %collective-permute-done.9.refs_1_ = bf16[12,16,1024]{2,1,0:T(8,128)(2,1)S(1)} collective-permute-done((bf16[12,16,1024]{2,1,0:T(8,128)(2,1)S(1)}, bf16[12,16,1024]{2,1,0:T(8,128)(2,1)S(1)}, u32[]{:S(2)}, u32[]{:S(2)}) %collective-permute-start.9) | collective-permute-done | bytes 393248 | tf_op jit(solution)/shard_map/ppermute | solution.py:661
  38.4 6.1 %collective-permute-done.10.refs_2_ = bf16[12,16,1024]{2,1,0:T(8,128)(2,1)S(1)} collective-permute-done((bf16[12,16,1024]{2,1,0:T(8,128)(2,1)S(1)}, bf16[12,16,1024]{2,1,0:T(8,128)(2,1)S(1)}, u32[]{:S(2)}, u32[]{:S(2)}) %collective-permute-start.10) | collective-permute-done | bytes 393248 | tf_op jit(solution)/shard_map/ppermute | solution.py:661
  45.8 2.9 %collective-permute-start.12 = (bf16[2,3,48,1024]{3,2,1,0:T(8,128)(2,1)S(1)}, bf16[2,3,48,1024]{3,2,1,0:T(8,128)(2,1)S(1)}, u32[]{:S(2)}, u32[]{:S(2)}) collective-permute-start(bf16[2,3,48,1024]{3,2,1,0:T(8,128)(2,1)S(1)} %get-tuple-element.87), channel_id=1, source_target_pairs={{0,192},{64,0},{128,64},{192,128},{1,193},{65,1},{129,65},{193,129... | collective-permute-start | bytes 1769480 | tf_op jit(solution)/shard_map/ppermute | solution.py:661
  52.5 9.8 %collective-permute-done.12.refs_1_.refs_5_ = bf16[2,3,48,1024]{3,2,1,0:T(8,128)(2,1)S(1)} collective-permute-done((bf16[2,3,48,1024]{3,2,1,0:T(8,128)(2,1)S(1)}, bf16[2,3,48,1024]{3,2,1,0:T(8,128)(2,1)S(1)}, u32[]{:S(2)}, u32[]{:S(2)}) %collective-permute-start.12) | collective-permute-done | bytes 589856 | tf_op jit(solution)/shard_map/ppermute | solution.py:661
  63.2 11.5 %collective-permute-done.13.refs_2_.refs_6_ = bf16[2,3,48,1024]{3,2,1,0:T(8,128)(2,1)S(1)} collective-permute-done((bf16[2,3,48,1024]{3,2,1,0:T(8,128)(2,1)S(1)}, bf16[2,3,48,1024]{3,2,1,0:T(8,128)(2,1)S(1)}, u32[]{:S(2)}, u32[]{:S(2)}) %collective-permute-start.13) | collective-permute-done | bytes 589856 | tf_op jit(solution)/shard_map/ppermute | solution.py:661
  76.3 8.6 %all-to-all-done.received_hbm = bf16[16,48,2048]{2,1,0:T(8,128)(2,1)} async-done(((bf16[16,48,2048]{2,1,0:T(8,128)(2,1)}), bf16[16,48,2048]{2,1,0:T(8,128)(2,1)}, u32[]{:S(2)}, u32[]{:S(2)}) %all-to-all-start) | async-done | bytes 3145760 | tf_op jit(solution)/shard_map/all_to_all | solution.py:687
  84.8 4.7 %all-to-all-start.1 = ((bf16[16,24,2048]{2,1,0:T(8,128)(2,1)}), bf16[16,24,2048]{2,1,0:T(8,128)(2,1)}, u32[]{:S(2)}, u32[]{:S(2)}) async-start(bf16[16,24,2048]{2,1,0:T(8,128)(2,1)} %tail_pack.1), calls=%async_computation.1 | async-start | bytes 3145728 | tf_op jit(solution)/shard_map/all_to_all | solution.py:702
  94.0 4.0 %lead_combine.1 = (bf16[3,48,1024]{2,1,0:T(8,128)(2,1)}, bf16[3,48,1024]{2,1,0:T(8,128)(2,1)}, bf16[3,48,1024]{2,1,0:T(8,128)(2,1)}, bf16[3,48,1024]{2,1,0:T(8,128)(2,1)}) custom-call(s32[1]{0:T(128)} %bitcast.p_ref, bf16[16,48,2048]{2,1,0:T(8,128)(2,1)} %all-to-all-done.received_hbm, f32[4,8,96]{2,1,0:T(8,128)S(1)} %get-tuple-element.61.near_ref), custom_call_target="tpu_custom_call" | custom-call | tf_op jit(solution)/shard_map/lead_combine/pallas_call | solution.py:315
  104.1 15.5 %collective-permute-done.17.refs_7_.refs_11_ = bf16[2,1,48,1024]{3,2,1,0:T(8,128)(2,1)S(1)} collective-permute-done((bf16[2,1,48,1024]{3,2,1,0:T(8,128)(2,1)S(1)}, bf16[2,1,48,1024]{3,2,1,0:T(8,128)(2,1)S(1)}, u32[]{:S(2)}, u32[]{:S(2)}) %collective-permute-start.17) | collective-permute-done | bytes 196640 | tf_op jit(solution)/shard_map/ppermute | solution.py:661
  119.7 3.0 %coupling.1.links_hbm = f32[24,192]{1,0:T(8,128)S(1)} custom-call(s32[1]{0:T(128)} %bitcast.p_ref, bf16[4,16,1024]{2,1,0:T(8,128)(2,1)S(1)} %pad_maximum_fusion.1.w_ref.w_hbm, f32[4,40,192]{2,1,0:T(8,128)S(1)} %pad_maximum_fusion.info_ref.info_hbm, bf16[2,3,48,1024]{3,2,1,0:T(8,128)(2,1)S(1)} %copy-done.2, bf16[2,3,48,1024]{3,2,1,0:T(8,128)(2,1)S(1)} %copy-done.4, ...), custom_call_target="tpu_custom_call" | custom-call | tf_op jit(solution)/shard_map/coupling/pallas_call | solution.py:251
  124.8 2.6 %all-to-all-done.1.received_hbm = bf16[16,24,2048]{2,1,0:T(8,128)(2,1)} async-done(((bf16[16,24,2048]{2,1,0:T(8,128)(2,1)}), bf16[16,24,2048]{2,1,0:T(8,128)(2,1)}, u32[]{:S(2)}, u32[]{:S(2)}) %all-to-all-start.1) | async-done | bytes 1572896 | tf_op jit(solution)/shard_map/all_to_all | solution.py:702
  127.5 6.0 %tail_combine.1 = (bf16[4,4,48,1024]{3,2,1,0:T(8,128)(2,1)}, f32[4,32,192]{2,1,0:T(8,128)S(1)}, f32[4,32,192]{2,1,0:T(8,128)S(1)}) custom-call(s32[1]{0:T(128)} %bitcast.p_ref, bf16[16,24,2048]{2,1,0:T(8,128)(2,1)} %all-to-all-done.1.received_hbm, f32[4,40,192]{2,1,0:T(8,128)} %copy-done.10, bf16[4,48,1024]{2,1,0:T(8,128)(2,1)} %constant_dynamic-slice_fusion.up_hbm, ...), custom_call_target="tpu_custom_call" | custom-call | tf_op jit(solution)/shard_map/tail_combine/pallas_call | solution.py:460
  133.4 9.7 %all_to_all.25.sent_ref = f32[4,32,192]{2,1,0:T(8,128)S(1)} all-to-all(f32[4,32,192]{2,1,0:T(8,128)S(1)} %get-tuple-element.111), channel_id=1, replica_groups=mesh['pipe'=4,'expert'=16,'dp'=4] {'pipe'}, dimensions={0} | all-to-all | bytes 196608 | tf_op jit(solution)/shard_map/all_to_all | solution.py:711
  144.1 8.0 %all-to-all-start.3 = ((bf16[64,8,128]{2,1,0:T(8,128)(2,1)}), bf16[64,8,128]{2,1,0:T(8,128)(2,1)S(1)}, u32[]{:S(2)}, u32[]{:S(2)}) async-start(bf16[64,8,128]{2,1,0:T(8,128)(2,1)} %get-tuple-element.119), calls=%async_computation.3 | async-start | bytes 262144 | tf_op jit(solution)/shard_map/all_to_all | solution.py:715
  152.1 3.3 %grads.1 = (bf16[4,48,1024]{2,1,0:T(8,128)(2,1)}, bf16[4,48,1024]{2,1,0:T(8,128)(2,1)}, bf16[4,48,1024]{2,1,0:T(8,128)(2,1)}, bf16[4,48,1024]{2,1,0:T(8,128)(2,1)}) custom-call(s32[1]{0:T(128)} %bitcast.p_ref, bf16[4,48,1024]{2,1,0:T(8,128)(2,1)} %constant_dynamic-slice_fusion.up_hbm, bf16[4,4,48,1024]{3,2,1,0:T(8,128)(2,1)} %get-tuple-element.110.back_hbm, ...), custom_call_target="tpu_custom_call" | custom-call | tf_op jit(solution)/shard_map/grads/pallas_call | solution.py:588
  155.7 3.3 %collective-permute-start.19 = (bf16[4,48,1024]{2,1,0:T(8,128)(2,1)}, bf16[4,48,1024]{2,1,0:T(8,128)(2,1)S(1)}, u32[]{:S(2)}, u32[]{:S(2)}) collective-permute-start(bf16[4,48,1024]{2,1,0:T(8,128)(2,1)} %get-tuple-element.117), channel_id=1, source_target_pairs={{0,128},{64,192},{128,0},{192,64},{1,129},{65,193},{129,1},{193,65... | collective-permute-start | bytes 1179656 | tf_op jit(solution)/shard_map/ppermute | solution.py:661
  159.6 3.7 %all-to-all-done.3.parts_ref = bf16[64,8,128]{2,1,0:T(8,128)(2,1)S(1)} async-done(((bf16[64,8,128]{2,1,0:T(8,128)(2,1)}), bf16[64,8,128]{2,1,0:T(8,128)(2,1)S(1)}, u32[]{:S(2)}, u32[]{:S(2)}) %all-to-all-start.3) | async-done | bytes 131104 | tf_op jit(solution)/shard_map/all_to_all | solution.py:715
  164.0 6.4 %all-to-all-start.4 = ((bf16[64,8,128]{2,1,0:T(8,128)(2,1)}), bf16[64,8,128]{2,1,0:T(8,128)(2,1)S(1)}, u32[]{:S(2)}, u32[]{:S(2)}) async-start(bf16[64,8,128]{2,1,0:T(8,128)(2,1)} %router_total.1), calls=%async_computation.4 | async-start | bytes 262144 | tf_op jit(solution)/shard_map/all_to_all | solution.py:718
  170.5 6.1 %collective-permute-done.20.refs_3_ = bf16[4,48,1024]{2,1,0:T(8,128)(2,1)S(1)} collective-permute-done((bf16[4,48,1024]{2,1,0:T(8,128)(2,1)}, bf16[4,48,1024]{2,1,0:T(8,128)(2,1)S(1)}, u32[]{:S(2)}, u32[]{:S(2)}) %collective-permute-start.20) | collective-permute-done | bytes 393248 | tf_op jit(solution)/shard_map/ppermute | solution.py:661
  176.6 2.7 %join.1 = bf16[4,48,4096]{2,1,0:T(8,128)(2,1)} custom-call(s32[1]{0:T(128)} %bitcast.p_ref, bf16[4,48,1024]{2,1,0:T(8,128)(2,1)} %get-tuple-element.115.refs_0_, bf16[4,48,1024]{2,1,0:T(8,128)(2,1)S(1)} %collective-permute-done.18.refs_1_, bf16[4,48,1024]{2,1,0:T(8,128)(2,1)S(1)} %collective-permute-done.19.refs_2_, ...), custom_call_target="tpu_custom_call" | custom-call | tf_op jit(solution)/shard_map/join/pallas_call | solution.py:645
  (96 shorter events, 42.8 us)
Async XLA Ops:
  4.3 80.6 %all-to-all-start = ((bf16[16,48,2048]{2,1,0:T(8,128)(2,1)}), bf16[16,48,2048]{2,1,0:T(8,128)(2,1)}, u32[]{:S(2)}, u32[]{:S(2)}) async-start(bf16[16,48,2048]{2,1,0:T(8,128)(2,1)} %lead_pack.1), calls=%async_computation | async-start | bytes 6291456 | tf_op jit(solution)/shard_map/all_to_all | solution.py:687
  13.8 7.1 %collective-permute-start.3 = (f32[40,192]{1,0:T(8,128)S(1)}, f32[40,192]{1,0:T(8,128)S(1)}, u32[]{:S(2)}, u32[]{:S(2)}) collective-permute-start(f32[40,192]{1,0:T(8,128)S(1)} %get-tuple-element.71), channel_id=1, source_target_pairs={{0,192},{64,0},{128,64},{192,128},{1,193},{65,1},{129,65},{193,129... | collective-permute-start | bytes 92168 | tf_op jit(solution)/shard_map/ppermute | solution.py:661
  14.3 11.7 %collective-permute-start.6 = (bf16[16,1024]{1,0:T(8,128)(2,1)S(1)}, bf16[16,1024]{1,0:T(8,128)(2,1)S(1)}, u32[]{:S(2)}, u32[]{:S(2)}) collective-permute-start(bf16[16,1024]{1,0:T(8,128)(2,1)S(1)} %get-tuple-element.129), channel_id=1, source_target_pairs={{0,192},{64,0},{128,64},{192,128},{1,193},{65,1},{129,65},{193,129... | collective-permute-start | bytes 98312 | tf_op jit(solution)/shard_map/ppermute | solution.py:661
  17.4 8.6 %collective-permute-start.7 = (bf16[16,1024]{1,0:T(8,128)(2,1)S(1)}, bf16[16,1024]{1,0:T(8,128)(2,1)S(1)}, u32[]{:S(2)}, u32[]{:S(2)}) collective-permute-start(bf16[16,1024]{1,0:T(8,128)(2,1)S(1)} %get-tuple-element.131), channel_id=1, source_target_pairs={{0,128},{64,192},{128,0},{192,64},{1,129},{65,193},{129,1},{193,65... | collective-permute-start | bytes 98312 | tf_op jit(solution)/shard_map/ppermute | solution.py:661
  17.4 8.6 %collective-permute-start.8 = (bf16[16,1024]{1,0:T(8,128)(2,1)S(1)}, bf16[16,1024]{1,0:T(8,128)(2,1)S(1)}, u32[]{:S(2)}, u32[]{:S(2)}) collective-permute-start(bf16[16,1024]{1,0:T(8,128)(2,1)S(1)} %get-tuple-element.128), channel_id=1, source_target_pairs={{0,64},{64,128},{128,192},{192,0},{1,65},{65,129},{129,193},{193,1... | collective-permute-start | bytes 98312 | tf_op jit(solution)/shard_map/ppermute | solution.py:661
  19.6 5.5 %collective-permute-start.4 = (f32[40,192]{1,0:T(8,128)S(1)}, f32[40,192]{1,0:T(8,128)S(1)}, u32[]{:S(2)}, u32[]{:S(2)}) collective-permute-start(f32[40,192]{1,0:T(8,128)S(1)} %get-tuple-element.71), channel_id=1, source_target_pairs={{0,128},{64,192},{128,0},{192,64},{1,129},{65,193},{129,1},{193,65... | collective-permute-start | bytes 92168 | tf_op jit(solution)/shard_map/ppermute | solution.py:661
  25.9 12.5 %collective-permute-start.9 = (bf16[12,16,1024]{2,1,0:T(8,128)(2,1)S(1)}, bf16[12,16,1024]{2,1,0:T(8,128)(2,1)S(1)}, u32[]{:S(2)}, u32[]{:S(2)}) collective-permute-start(bf16[12,16,1024]{2,1,0:T(8,128)(2,1)S(1)} %get-tuple-element.80), channel_id=1, source_target_pairs={{0,192},{64,0},{128,64},{192,128},{1,193},{65,1},{129,65},{193,129... | collective-permute-start | bytes 1179656 | tf_op jit(solution)/shard_map/ppermute | solution.py:661
  28.8 15.7 %collective-permute-start.10 = (bf16[12,16,1024]{2,1,0:T(8,128)(2,1)S(1)}, bf16[12,16,1024]{2,1,0:T(8,128)(2,1)S(1)}, u32[]{:S(2)}, u32[]{:S(2)}) collective-permute-start(bf16[12,16,1024]{2,1,0:T(8,128)(2,1)S(1)} %get-tuple-element.81), channel_id=1, source_target_pairs={{0,128},{64,192},{128,0},{192,64},{1,129},{65,193},{129,1},{193,65... | collective-permute-start | bytes 1179656 | tf_op jit(solution)/shard_map/ppermute | solution.py:661
  28.8 16.9 %collective-permute-start.11 = (bf16[12,16,1024]{2,1,0:T(8,128)(2,1)S(1)}, bf16[12,16,1024]{2,1,0:T(8,128)(2,1)S(1)}, u32[]{:S(2)}, u32[]{:S(2)}) collective-permute-start(bf16[12,16,1024]{2,1,0:T(8,128)(2,1)S(1)} %get-tuple-element.82), channel_id=1, source_target_pairs={{0,64},{64,128},{128,192},{192,0},{1,65},{65,129},{129,193},{193,1... | collective-permute-start | bytes 1179656 | tf_op jit(solution)/shard_map/ppermute | solution.py:661
  45.8 16.6 %collective-permute-start.12 = (bf16[2,3,48,1024]{3,2,1,0:T(8,128)(2,1)S(1)}, bf16[2,3,48,1024]{3,2,1,0:T(8,128)(2,1)S(1)}, u32[]{:S(2)}, u32[]{:S(2)}) collective-permute-start(bf16[2,3,48,1024]{3,2,1,0:T(8,128)(2,1)S(1)} %get-tuple-element.87), channel_id=1, source_target_pairs={{0,192},{64,0},{128,64},{192,128},{1,193},{65,1},{129,65},{193,129... | collective-permute-start | bytes 1769480 | tf_op jit(solution)/shard_map/ppermute | solution.py:661
  48.6 26.0 %collective-permute-start.13 = (bf16[2,3,48,1024]{3,2,1,0:T(8,128)(2,1)S(1)}, bf16[2,3,48,1024]{3,2,1,0:T(8,128)(2,1)S(1)}, u32[]{:S(2)}, u32[]{:S(2)}) collective-permute-start(bf16[2,3,48,1024]{3,2,1,0:T(8,128)(2,1)S(1)} %get-tuple-element.88), channel_id=1, source_target_pairs={{0,128},{64,192},{128,0},{192,64},{1,129},{65,193},{129,1},{193,65... | collective-permute-start | bytes 1769480 | tf_op jit(solution)/shard_map/ppermute | solution.py:661
  48.7 26.8 %collective-permute-start.14 = (bf16[2,3,48,1024]{3,2,1,0:T(8,128)(2,1)S(1)}, bf16[2,3,48,1024]{3,2,1,0:T(8,128)(2,1)S(1)}, u32[]{:S(2)}, u32[]{:S(2)}) collective-permute-start(bf16[2,3,48,1024]{3,2,1,0:T(8,128)(2,1)S(1)} %get-tuple-element.89), channel_id=1, source_target_pairs={{0,64},{64,128},{128,192},{192,0},{1,65},{65,129},{129,193},{193,1... | collective-permute-start | bytes 1769480 | tf_op jit(solution)/shard_map/ppermute | solution.py:661
  84.8 42.6 %all-to-all-start.1 = ((bf16[16,24,2048]{2,1,0:T(8,128)(2,1)}), bf16[16,24,2048]{2,1,0:T(8,128)(2,1)}, u32[]{:S(2)}, u32[]{:S(2)}) async-start(bf16[16,24,2048]{2,1,0:T(8,128)(2,1)} %tail_pack.1), calls=%async_computation.1 | async-start | bytes 3145728 | tf_op jit(solution)/shard_map/all_to_all | solution.py:702
  90.9 11.6 %collective-permute-start.15 = (bf16[2,1,48,1024]{3,2,1,0:T(8,128)(2,1)S(1)}, bf16[2,1,48,1024]{3,2,1,0:T(8,128)(2,1)S(1)}, u32[]{:S(2)}, u32[]{:S(2)}) collective-permute-start(bf16[2,1,48,1024]{3,2,1,0:T(8,128)(2,1)S(1)} %get-tuple-element.126), channel_id=1, source_target_pairs={{0,192},{64,0},{128,64},{192,128},{1,193},{65,1},{129,65},{193,129... | collective-permute-start | bytes 589832 | tf_op jit(solution)/shard_map/ppermute | solution.py:661
  91.4 12.7 %collective-permute-start.16 = (bf16[2,1,48,1024]{3,2,1,0:T(8,128)(2,1)S(1)}, bf16[2,1,48,1024]{3,2,1,0:T(8,128)(2,1)S(1)}, u32[]{:S(2)}, u32[]{:S(2)}) collective-permute-start(bf16[2,1,48,1024]{3,2,1,0:T(8,128)(2,1)S(1)} %get-tuple-element.125), channel_id=1, source_target_pairs={{0,128},{64,192},{128,0},{192,64},{1,129},{65,193},{129,1},{193,65... | collective-permute-start | bytes 589832 | tf_op jit(solution)/shard_map/ppermute | solution.py:661
  98.0 25.3 %collective-permute-start = (bf16[3,48,1024]{2,1,0:T(8,128)(2,1)}, bf16[3,48,1024]{2,1,0:T(8,128)(2,1)S(1)}, u32[]{:S(2)}, u32[]{:S(2)}) collective-permute-start(bf16[3,48,1024]{2,1,0:T(8,128)(2,1)} %get-tuple-element.63), channel_id=1, source_target_pairs={{0,192},{64,0},{128,64},{192,128},{1,193},{65,1},{129,65},{193,129... | collective-permute-start | bytes 884744 | tf_op jit(solution)/shard_map/ppermute | solution.py:661
  99.2 24.1 %collective-permute-start.1 = (bf16[3,48,1024]{2,1,0:T(8,128)(2,1)}, bf16[3,48,1024]{2,1,0:T(8,128)(2,1)S(1)}, u32[]{:S(2)}, u32[]{:S(2)}) collective-permute-start(bf16[3,48,1024]{2,1,0:T(8,128)(2,1)} %get-tuple-element.64), channel_id=1, source_target_pairs={{0,128},{64,192},{128,0},{192,64},{1,129},{65,193},{129,1},{193,65... | collective-permute-start | bytes 884744 | tf_op jit(solution)/shard_map/ppermute | solution.py:661
  101.5 21.9 %collective-permute-start.2 = (bf16[3,48,1024]{2,1,0:T(8,128)(2,1)}, bf16[3,48,1024]{2,1,0:T(8,128)(2,1)S(1)}, u32[]{:S(2)}, u32[]{:S(2)}) collective-permute-start(bf16[3,48,1024]{2,1,0:T(8,128)(2,1)} %get-tuple-element.65), channel_id=1, source_target_pairs={{0,64},{64,128},{128,192},{192,0},{1,65},{65,129},{129,193},{193,1... | collective-permute-start | bytes 884744 | tf_op jit(solution)/shard_map/ppermute | solution.py:661
  102.5 17.1 %collective-permute-start.17 = (bf16[2,1,48,1024]{3,2,1,0:T(8,128)(2,1)S(1)}, bf16[2,1,48,1024]{3,2,1,0:T(8,128)(2,1)S(1)}, u32[]{:S(2)}, u32[]{:S(2)}) collective-permute-start(bf16[2,1,48,1024]{3,2,1,0:T(8,128)(2,1)S(1)} %get-tuple-element.124), channel_id=1, source_target_pairs={{0,64},{64,128},{128,192},{192,0},{1,65},{65,129},{129,193},{193,1... | collective-permute-start | bytes 589832 | tf_op jit(solution)/shard_map/ppermute | solution.py:661
  144.1 19.1 %all-to-all-start.3 = ((bf16[64,8,128]{2,1,0:T(8,128)(2,1)}), bf16[64,8,128]{2,1,0:T(8,128)(2,1)S(1)}, u32[]{:S(2)}, u32[]{:S(2)}) async-start(bf16[64,8,128]{2,1,0:T(8,128)(2,1)} %get-tuple-element.119), calls=%async_computation.3 | async-start | bytes 262144 | tf_op jit(solution)/shard_map/all_to_all | solution.py:715
  155.4 15.0 %collective-permute-start.18 = (bf16[4,48,1024]{2,1,0:T(8,128)(2,1)}, bf16[4,48,1024]{2,1,0:T(8,128)(2,1)S(1)}, u32[]{:S(2)}, u32[]{:S(2)}) collective-permute-start(bf16[4,48,1024]{2,1,0:T(8,128)(2,1)} %get-tuple-element.116), channel_id=1, source_target_pairs={{0,64},{64,128},{128,192},{192,0},{1,65},{65,129},{129,193},{193,1... | collective-permute-start | bytes 1179656 | tf_op jit(solution)/shard_map/ppermute | solution.py:661
  155.7 14.7 %collective-permute-start.19 = (bf16[4,48,1024]{2,1,0:T(8,128)(2,1)}, bf16[4,48,1024]{2,1,0:T(8,128)(2,1)S(1)}, u32[]{:S(2)}, u32[]{:S(2)}) collective-permute-start(bf16[4,48,1024]{2,1,0:T(8,128)(2,1)} %get-tuple-element.117), channel_id=1, source_target_pairs={{0,128},{64,192},{128,0},{192,64},{1,129},{65,193},{129,1},{193,65... | collective-permute-start | bytes 1179656 | tf_op jit(solution)/shard_map/ppermute | solution.py:661
  159.0 17.6 %collective-permute-start.20 = (bf16[4,48,1024]{2,1,0:T(8,128)(2,1)}, bf16[4,48,1024]{2,1,0:T(8,128)(2,1)S(1)}, u32[]{:S(2)}, u32[]{:S(2)}) collective-permute-start(bf16[4,48,1024]{2,1,0:T(8,128)(2,1)} %get-tuple-element.118), channel_id=1, source_target_pairs={{0,192},{64,0},{128,64},{192,128},{1,193},{65,1},{129,65},{193,129... | collective-permute-start | bytes 1179656 | tf_op jit(solution)/shard_map/ppermute | solution.py:661
  164.0 17.8 %all-to-all-start.4 = ((bf16[64,8,128]{2,1,0:T(8,128)(2,1)}), bf16[64,8,128]{2,1,0:T(8,128)(2,1)S(1)}, u32[]{:S(2)}, u32[]{:S(2)}) async-start(bf16[64,8,128]{2,1,0:T(8,128)(2,1)} %router_total.1), calls=%async_computation.4 | async-start | bytes 262144 | tf_op jit(solution)/shard_map/all_to_all | solution.py:718
  (24 other events, 382.3 us)

commit v10 on v9

--- a/solution.py
+++ b/solution.py
@@ -711,7 +711,7 @@
     sent = lax.all_to_all(sent, "pipe", 0, 0, tiled=True)
     dense, partial = dense_terms(p, sent, v, normed, micro)
 
-    axes = ("expert", "dp")
+    axes = ("dp", "expert")
     partial = lax.all_to_all(partial, axes, 0, 0, tiled=True)
     outs = grads_of(p, up, back, dense, w_all)
     blocks = [turned(out, d) if d else out for d, out in enumerate(outs)]

time: 183 us -> 183 us (level)
  waiting for transfers between devices: 72.4 us -> 70.3 us
where the time goes in v10:
time: 183 us; the launch traced here: 182 us
  waiting for transfers between devices  70.3 us (38%)
  starting transfers between devices  58.9 us (32%)
  Pallas kernels  29.1 us (16%)
  local copies, waits for them, and re-layouts  11.7 us (6%)
  blocking collectives  9.67 us (5%)
    ppermute x21, waiting for transfers between devices, turned(): lax.ppermute(block, 'pipe', [(i, (i + distance) % n) for i in range(n)])  54.9 us
    ppermute x21, starting transfers between devices, turned(): lax.ppermute(block, 'pipe', [(i, (i + distance) % n) for i in range(n)])  29.9 us
    all_to_all x1, blocking collectives, on_device(): sent = lax.all_to_all(sent, 'pipe', 0, 0, tiled=True)  9.67 us
    all_to_all x1, starting transfers between devices, on_device(): lax.all_to_all(lead_pack(grads, micro - 1), 'expert', 0, 0, tiled=True)  8.77 us
    all_to_all x1, waiting for transfers between devices, on_device(): lax.all_to_all(lead_pack(grads, micro - 1), 'expert', 0, 0, tiled=True)  8.57 us
    unnamed x47, local copies, waits for them, and re-layouts  8.23 us
    all_to_all x1, starting transfers between devices, on_device(): partial = lax.all_to_all(partial, axes, 0, 0, tiled=True)  7.99 us
    all_to_all x1, starting transfers between devices, on_device(): total = lax.all_to_all(total_for_all(partial), axes, 0, 0, tiled=True)  7.5 us
  transfers between devices with their start and end apart: 25, of which 13 were waited for; matrix products, arithmetic and copies ran while one was open for 3% of the time, Pallas kernels for 10%

profile of v10, /device:TPU:8, one launch (start us, length us, event | category | flops | bytes accessed | tf_op | source)
XLA Modules:
  0.0 181.5 jit_solution(12434130002073756871)
XLA Ops:
  0.6 3.6 %lead_pack.1 = bf16[16,48,2048]{2,1,0:T(8,128)(2,1)} custom-call(bf16[4,9,16,4096]{3,2,1,0:T(8,128)(2,1)} %bitcast.55), custom_call_target="tpu_custom_call" | custom-call | tf_op jit(solution)/shard_map/lead_pack/pallas_call | solution.py:70
  4.3 8.8 %all-to-all-start = ((bf16[16,48,2048]{2,1,0:T(8,128)(2,1)}), bf16[16,48,2048]{2,1,0:T(8,128)(2,1)}, u32[]{:S(2)}, u32[]{:S(2)}) async-start(bf16[16,48,2048]{2,1,0:T(8,128)(2,1)} %lead_pack.1), calls=%async_computation | async-start | bytes 6291456 | tf_op jit(solution)/shard_map/all_to_all | solution.py:687
  14.3 3.1 %collective-permute-start.6 = (bf16[16,1024]{1,0:T(8,128)(2,1)S(1)}, bf16[16,1024]{1,0:T(8,128)(2,1)S(1)}, u32[]{:S(2)}, u32[]{:S(2)}) collective-permute-start(bf16[16,1024]{1,0:T(8,128)(2,1)S(1)} %get-tuple-element.129), channel_id=1, source_target_pairs={{0,192},{64,0},{128,64},{192,128},{1,193},{65,1},{129,65},{193,129... | collective-permute-start | bytes 98312 | tf_op jit(solution)/shard_map/ppermute | solution.py:661
  25.9 2.9 %collective-permute-start.9 = (bf16[12,16,1024]{2,1,0:T(8,128)(2,1)S(1)}, bf16[12,16,1024]{2,1,0:T(8,128)(2,1)S(1)}, u32[]{:S(2)}, u32[]{:S(2)}) collective-permute-start(bf16[12,16,1024]{2,1,0:T(8,128)(2,1)S(1)} %get-tuple-element.80), channel_id=1, source_target_pairs={{0,192},{64,0},{128,64},{192,128},{1,193},{65,1},{129,65},{193,129... | collective-permute-start | bytes 1179656 | tf_op jit(solution)/shard_map/ppermute | solution.py:661
  35.8 2.6 %collective-permute-done.9.refs_1_ = bf16[12,16,1024]{2,1,0:T(8,128)(2,1)S(1)} collective-permute-done((bf16[12,16,1024]{2,1,0:T(8,128)(2,1)S(1)}, bf16[12,16,1024]{2,1,0:T(8,128)(2,1)S(1)}, u32[]{:S(2)}, u32[]{:S(2)}) %collective-permute-start.9) | collective-permute-done | bytes 393248 | tf_op jit(solution)/shard_map/ppermute | solution.py:661
  38.4 6.1 %collective-permute-done.10.refs_2_ = bf16[12,16,1024]{2,1,0:T(8,128)(2,1)S(1)} collective-permute-done((bf16[12,16,1024]{2,1,0:T(8,128)(2,1)S(1)}, bf16[12,16,1024]{2,1,0:T(8,128)(2,1)S(1)}, u32[]{:S(2)}, u32[]{:S(2)}) %collective-permute-start.10) | collective-permute-done | bytes 393248 | tf_op jit(solution)/shard_map/ppermute | solution.py:661
  45.8 2.9 %collective-permute-start.12 = (bf16[2,3,48,1024]{3,2,1,0:T(8,128)(2,1)S(1)}, bf16[2,3,48,1024]{3,2,1,0:T(8,128)(2,1)S(1)}, u32[]{:S(2)}, u32[]{:S(2)}) collective-permute-start(bf16[2,3,48,1024]{3,2,1,0:T(8,128)(2,1)S(1)} %get-tuple-element.87), channel_id=1, source_target_pairs={{0,192},{64,0},{128,64},{192,128},{1,193},{65,1},{129,65},{193,129... | collective-permute-start | bytes 1769480 | tf_op jit(solution)/shard_map/ppermute | solution.py:661
  52.5 9.8 %collective-permute-done.12.refs_1_.refs_5_ = bf16[2,3,48,1024]{3,2,1,0:T(8,128)(2,1)S(1)} collective-permute-done((bf16[2,3,48,1024]{3,2,1,0:T(8,128)(2,1)S(1)}, bf16[2,3,48,1024]{3,2,1,0:T(8,128)(2,1)S(1)}, u32[]{:S(2)}, u32[]{:S(2)}) %collective-permute-start.12) | collective-permute-done | bytes 589856 | tf_op jit(solution)/shard_map/ppermute | solution.py:661
  63.2 11.5 %collective-permute-done.13.refs_2_.refs_6_ = bf16[2,3,48,1024]{3,2,1,0:T(8,128)(2,1)S(1)} collective-permute-done((bf16[2,3,48,1024]{3,2,1,0:T(8,128)(2,1)S(1)}, bf16[2,3,48,1024]{3,2,1,0:T(8,128)(2,1)S(1)}, u32[]{:S(2)}, u32[]{:S(2)}) %collective-permute-start.13) | collective-permute-done | bytes 589856 | tf_op jit(solution)/shard_map/ppermute | solution.py:661
  76.3 8.6 %all-to-all-done.received_hbm = bf16[16,48,2048]{2,1,0:T(8,128)(2,1)} async-done(((bf16[16,48,2048]{2,1,0:T(8,128)(2,1)}), bf16[16,48,2048]{2,1,0:T(8,128)(2,1)}, u32[]{:S(2)}, u32[]{:S(2)}) %all-to-all-start) | async-done | bytes 3145760 | tf_op jit(solution)/shard_map/all_to_all | solution.py:687
  84.8 4.7 %all-to-all-start.1 = ((bf16[16,24,2048]{2,1,0:T(8,128)(2,1)}), bf16[16,24,2048]{2,1,0:T(8,128)(2,1)}, u32[]{:S(2)}, u32[]{:S(2)}) async-start(bf16[16,24,2048]{2,1,0:T(8,128)(2,1)} %tail_pack.1), calls=%async_computation.1 | async-start | bytes 3145728 | tf_op jit(solution)/shard_map/all_to_all | solution.py:702
  94.0 4.0 %lead_combine.1 = (bf16[3,48,1024]{2,1,0:T(8,128)(2,1)}, bf16[3,48,1024]{2,1,0:T(8,128)(2,1)}, bf16[3,48,1024]{2,1,0:T(8,128)(2,1)}, bf16[3,48,1024]{2,1,0:T(8,128)(2,1)}) custom-call(s32[1]{0:T(128)} %bitcast.p_ref, bf16[16,48,2048]{2,1,0:T(8,128)(2,1)} %all-to-all-done.received_hbm, f32[4,8,96]{2,1,0:T(8,128)S(1)} %get-tuple-element.61.near_ref), custom_call_target="tpu_custom_call" | custom-call | tf_op jit(solution)/shard_map/lead_combine/pallas_call | solution.py:315
  104.1 15.5 %collective-permute-done.17.refs_7_.refs_11_ = bf16[2,1,48,1024]{3,2,1,0:T(8,128)(2,1)S(1)} collective-permute-done((bf16[2,1,48,1024]{3,2,1,0:T(8,128)(2,1)S(1)}, bf16[2,1,48,1024]{3,2,1,0:T(8,128)(2,1)S(1)}, u32[]{:S(2)}, u32[]{:S(2)}) %collective-permute-start.17) | collective-permute-done | bytes 196640 | tf_op jit(solution)/shard_map/ppermute | solution.py:661
  119.7 3.0 %coupling.1.links_hbm = f32[24,192]{1,0:T(8,128)S(1)} custom-call(s32[1]{0:T(128)} %bitcast.p_ref, bf16[4,16,1024]{2,1,0:T(8,128)(2,1)S(1)} %pad_maximum_fusion.1.w_ref.w_hbm, f32[4,40,192]{2,1,0:T(8,128)S(1)} %pad_maximum_fusion.info_ref.info_hbm, bf16[2,3,48,1024]{3,2,1,0:T(8,128)(2,1)S(1)} %copy-done.2, bf16[2,3,48,1024]{3,2,1,0:T(8,128)(2,1)S(1)} %copy-done.4, ...), custom_call_target="tpu_custom_call" | custom-call | tf_op jit(solution)/shard_map/coupling/pallas_call | solution.py:251
  124.8 2.6 %all-to-all-done.1.received_hbm = bf16[16,24,2048]{2,1,0:T(8,128)(2,1)} async-done(((bf16[16,24,2048]{2,1,0:T(8,128)(2,1)}), bf16[16,24,2048]{2,1,0:T(8,128)(2,1)}, u32[]{:S(2)}, u32[]{:S(2)}) %all-to-all-start.1) | async-done | bytes 1572896 | tf_op jit(solution)/shard_map/all_to_all | solution.py:702
  127.5 6.0 %tail_combine.1 = (bf16[4,4,48,1024]{3,2,1,0:T(8,128)(2,1)}, f32[4,32,192]{2,1,0:T(8,128)S(1)}, f32[4,32,192]{2,1,0:T(8,128)S(1)}) custom-call(s32[1]{0:T(128)} %bitcast.p_ref, bf16[16,24,2048]{2,1,0:T(8,128)(2,1)} %all-to-all-done.1.received_hbm, f32[4,40,192]{2,1,0:T(8,128)} %copy-done.10, bf16[4,48,1024]{2,1,0:T(8,128)(2,1)} %constant_dynamic-slice_fusion.up_hbm, ...), custom_call_target="tpu_custom_call" | custom-call | tf_op jit(solution)/shard_map/tail_combine/pallas_call | solution.py:460
  133.4 9.7 %all_to_all.25.sent_ref = f32[4,32,192]{2,1,0:T(8,128)S(1)} all-to-all(f32[4,32,192]{2,1,0:T(8,128)S(1)} %get-tuple-element.111), channel_id=1, replica_groups=mesh['pipe'=4,'expert'=16,'dp'=4] {'pipe'}, dimensions={0} | all-to-all | bytes 196608 | tf_op jit(solution)/shard_map/all_to_all | solution.py:711
  144.1 8.0 %all-to-all-start.3 = ((bf16[64,8,128]{2,1,0:T(8,128)(2,1)}), bf16[64,8,128]{2,1,0:T(8,128)(2,1)S(1)}, u32[]{:S(2)}, u32[]{:S(2)}) async-start(bf16[64,8,128]{2,1,0:T(8,128)(2,1)} %get-tuple-element.119), calls=%async_computation.3 | async-start | bytes 262144 | tf_op jit(solution)/shard_map/all_to_all | solution.py:715
  152.1 3.3 %grads.1 = (bf16[4,48,1024]{2,1,0:T(8,128)(2,1)}, bf16[4,48,1024]{2,1,0:T(8,128)(2,1)}, bf16[4,48,1024]{2,1,0:T(8,128)(2,1)}, bf16[4,48,1024]{2,1,0:T(8,128)(2,1)}) custom-call(s32[1]{0:T(128)} %bitcast.p_ref, bf16[4,48,1024]{2,1,0:T(8,128)(2,1)} %constant_dynamic-slice_fusion.up_hbm, bf16[4,4,48,1024]{3,2,1,0:T(8,128)(2,1)} %get-tuple-element.110.back_hbm, ...), custom_call_target="tpu_custom_call" | custom-call | tf_op jit(solution)/shard_map/grads/pallas_call | solution.py:588
  155.7 3.3 %collective-permute-start.19 = (bf16[4,48,1024]{2,1,0:T(8,128)(2,1)}, bf16[4,48,1024]{2,1,0:T(8,128)(2,1)S(1)}, u32[]{:S(2)}, u32[]{:S(2)}) collective-permute-start(bf16[4,48,1024]{2,1,0:T(8,128)(2,1)} %get-tuple-element.117), channel_id=1, source_target_pairs={{0,128},{64,192},{128,0},{192,64},{1,129},{65,193},{129,1},{193,65... | collective-permute-start | bytes 1179656 | tf_op jit(solution)/shard_map/ppermute | solution.py:661
  159.6 2.6 %all-to-all-done.3.parts_ref = bf16[64,8,128]{2,1,0:T(8,128)(2,1)S(1)} async-done(((bf16[64,8,128]{2,1,0:T(8,128)(2,1)}), bf16[64,8,128]{2,1,0:T(8,128)(2,1)S(1)}, u32[]{:S(2)}, u32[]{:S(2)}) %all-to-all-start.3) | async-done | bytes 131104 | tf_op jit(solution)/shard_map/all_to_all | solution.py:715
  163.0 7.5 %all-to-all-start.4 = ((bf16[64,8,128]{2,1,0:T(8,128)(2,1)}), bf16[64,8,128]{2,1,0:T(8,128)(2,1)S(1)}, u32[]{:S(2)}, u32[]{:S(2)}) async-start(bf16[64,8,128]{2,1,0:T(8,128)(2,1)} %router_total.1), calls=%async_computation.4 | async-start | bytes 262144 | tf_op jit(solution)/shard_map/all_to_all | solution.py:718
  170.5 6.1 %collective-permute-done.20.refs_3_ = bf16[4,48,1024]{2,1,0:T(8,128)(2,1)S(1)} collective-permute-done((bf16[4,48,1024]{2,1,0:T(8,128)(2,1)}, bf16[4,48,1024]{2,1,0:T(8,128)(2,1)S(1)}, u32[]{:S(2)}, u32[]{:S(2)}) %collective-permute-start.20) | collective-permute-done | bytes 393248 | tf_op jit(solution)/shard_map/ppermute | solution.py:661
  176.6 2.7 %join.1 = bf16[4,48,4096]{2,1,0:T(8,128)(2,1)} custom-call(s32[1]{0:T(128)} %bitcast.p_ref, bf16[4,48,1024]{2,1,0:T(8,128)(2,1)} %get-tuple-element.115.refs_0_, bf16[4,48,1024]{2,1,0:T(8,128)(2,1)S(1)} %collective-permute-done.18.refs_1_, bf16[4,48,1024]{2,1,0:T(8,128)(2,1)S(1)} %collective-permute-done.19.refs_2_, ...), custom_call_target="tpu_custom_call" | custom-call | tf_op jit(solution)/shard_map/join/pallas_call | solution.py:645
  (96 shorter events, 41.8 us)
Async XLA Ops:
  4.3 80.6 %all-to-all-start = ((bf16[16,48,2048]{2,1,0:T(8,128)(2,1)}), bf16[16,48,2048]{2,1,0:T(8,128)(2,1)}, u32[]{:S(2)}, u32[]{:S(2)}) async-start(bf16[16,48,2048]{2,1,0:T(8,128)(2,1)} %lead_pack.1), calls=%async_computation | async-start | bytes 6291456 | tf_op jit(solution)/shard_map/all_to_all | solution.py:687
  13.8 7.1 %collective-permute-start.3 = (f32[40,192]{1,0:T(8,128)S(1)}, f32[40,192]{1,0:T(8,128)S(1)}, u32[]{:S(2)}, u32[]{:S(2)}) collective-permute-start(f32[40,192]{1,0:T(8,128)S(1)} %get-tuple-element.71), channel_id=1, source_target_pairs={{0,192},{64,0},{128,64},{192,128},{1,193},{65,1},{129,65},{193,129... | collective-permute-start | bytes 92168 | tf_op jit(solution)/shard_map/ppermute | solution.py:661
  14.3 11.7 %collective-permute-start.6 = (bf16[16,1024]{1,0:T(8,128)(2,1)S(1)}, bf16[16,1024]{1,0:T(8,128)(2,1)S(1)}, u32[]{:S(2)}, u32[]{:S(2)}) collective-permute-start(bf16[16,1024]{1,0:T(8,128)(2,1)S(1)} %get-tuple-element.129), channel_id=1, source_target_pairs={{0,192},{64,0},{128,64},{192,128},{1,193},{65,1},{129,65},{193,129... | collective-permute-start | bytes 98312 | tf_op jit(solution)/shard_map/ppermute | solution.py:661
  17.4 8.6 %collective-permute-start.7 = (bf16[16,1024]{1,0:T(8,128)(2,1)S(1)}, bf16[16,1024]{1,0:T(8,128)(2,1)S(1)}, u32[]{:S(2)}, u32[]{:S(2)}) collective-permute-start(bf16[16,1024]{1,0:T(8,128)(2,1)S(1)} %get-tuple-element.131), channel_id=1, source_target_pairs={{0,128},{64,192},{128,0},{192,64},{1,129},{65,193},{129,1},{193,65... | collective-permute-start | bytes 98312 | tf_op jit(solution)/shard_map/ppermute | solution.py:661
  17.4 8.6 %collective-permute-start.8 = (bf16[16,1024]{1,0:T(8,128)(2,1)S(1)}, bf16[16,1024]{1,0:T(8,128)(2,1)S(1)}, u32[]{:S(2)}, u32[]{:S(2)}) collective-permute-start(bf16[16,1024]{1,0:T(8,128)(2,1)S(1)} %get-tuple-element.128), channel_id=1, source_target_pairs={{0,64},{64,128},{128,192},{192,0},{1,65},{65,129},{129,193},{193,1... | collective-permute-start | bytes 98312 | tf_op jit(solution)/shard_map/ppermute | solution.py:661
  19.6 5.5 %collective-permute-start.4 = (f32[40,192]{1,0:T(8,128)S(1)}, f32[40,192]{1,0:T(8,128)S(1)}, u32[]{:S(2)}, u32[]{:S(2)}) collective-permute-start(f32[40,192]{1,0:T(8,128)S(1)} %get-tuple-element.71), channel_id=1, source_target_pairs={{0,128},{64,192},{128,0},{192,64},{1,129},{65,193},{129,1},{193,65... | collective-permute-start | bytes 92168 | tf_op jit(solution)/shard_map/ppermute | solution.py:661
  25.9 12.5 %collective-permute-start.9 = (bf16[12,16,1024]{2,1,0:T(8,128)(2,1)S(1)}, bf16[12,16,1024]{2,1,0:T(8,128)(2,1)S(1)}, u32[]{:S(2)}, u32[]{:S(2)}) collective-permute-start(bf16[12,16,1024]{2,1,0:T(8,128)(2,1)S(1)} %get-tuple-element.80), channel_id=1, source_target_pairs={{0,192},{64,0},{128,64},{192,128},{1,193},{65,1},{129,65},{193,129... | collective-permute-start | bytes 1179656 | tf_op jit(solution)/shard_map/ppermute | solution.py:661
  28.8 15.7 %collective-permute-start.10 = (bf16[12,16,1024]{2,1,0:T(8,128)(2,1)S(1)}, bf16[12,16,1024]{2,1,0:T(8,128)(2,1)S(1)}, u32[]{:S(2)}, u32[]{:S(2)}) collective-permute-start(bf16[12,16,1024]{2,1,0:T(8,128)(2,1)S(1)} %get-tuple-element.81), channel_id=1, source_target_pairs={{0,128},{64,192},{128,0},{192,64},{1,129},{65,193},{129,1},{193,65... | collective-permute-start | bytes 1179656 | tf_op jit(solution)/shard_map/ppermute | solution.py:661
  28.8 16.9 %collective-permute-start.11 = (bf16[12,16,1024]{2,1,0:T(8,128)(2,1)S(1)}, bf16[12,16,1024]{2,1,0:T(8,128)(2,1)S(1)}, u32[]{:S(2)}, u32[]{:S(2)}) collective-permute-start(bf16[12,16,1024]{2,1,0:T(8,128)(2,1)S(1)} %get-tuple-element.82), channel_id=1, source_target_pairs={{0,64},{64,128},{128,192},{192,0},{1,65},{65,129},{129,193},{193,1... | collective-permute-start | bytes 1179656 | tf_op jit(solution)/shard_map/ppermute | solution.py:661
  45.8 16.6 %collective-permute-start.12 = (bf16[2,3,48,1024]{3,2,1,0:T(8,128)(2,1)S(1)}, bf16[2,3,48,1024]{3,2,1,0:T(8,128)(2,1)S(1)}, u32[]{:S(2)}, u32[]{:S(2)}) collective-permute-start(bf16[2,3,48,1024]{3,2,1,0:T(8,128)(2,1)S(1)} %get-tuple-element.87), channel_id=1, source_target_pairs={{0,192},{64,0},{128,64},{192,128},{1,193},{65,1},{129,65},{193,129... | collective-permute-start | bytes 1769480 | tf_op jit(solution)/shard_map/ppermute | solution.py:661
  48.6 26.0 %collective-permute-start.13 = (bf16[2,3,48,1024]{3,2,1,0:T(8,128)(2,1)S(1)}, bf16[2,3,48,1024]{3,2,1,0:T(8,128)(2,1)S(1)}, u32[]{:S(2)}, u32[]{:S(2)}) collective-permute-start(bf16[2,3,48,1024]{3,2,1,0:T(8,128)(2,1)S(1)} %get-tuple-element.88), channel_id=1, source_target_pairs={{0,128},{64,192},{128,0},{192,64},{1,129},{65,193},{129,1},{193,65... | collective-permute-start | bytes 1769480 | tf_op jit(solution)/shard_map/ppermute | solution.py:661
  48.7 26.8 %collective-permute-start.14 = (bf16[2,3,48,1024]{3,2,1,0:T(8,128)(2,1)S(1)}, bf16[2,3,48,1024]{3,2,1,0:T(8,128)(2,1)S(1)}, u32[]{:S(2)}, u32[]{:S(2)}) collective-permute-start(bf16[2,3,48,1024]{3,2,1,0:T(8,128)(2,1)S(1)} %get-tuple-element.89), channel_id=1, source_target_pairs={{0,64},{64,128},{128,192},{192,0},{1,65},{65,129},{129,193},{193,1... | collective-permute-start | bytes 1769480 | tf_op jit(solution)/shard_map/ppermute | solution.py:661
  84.8 42.6 %all-to-all-start.1 = ((bf16[16,24,2048]{2,1,0:T(8,128)(2,1)}), bf16[16,24,2048]{2,1,0:T(8,128)(2,1)}, u32[]{:S(2)}, u32[]{:S(2)}) async-start(bf16[16,24,2048]{2,1,0:T(8,128)(2,1)} %tail_pack.1), calls=%async_computation.1 | async-start | bytes 3145728 | tf_op jit(solution)/shard_map/all_to_all | solution.py:702
  90.9 11.6 %collective-permute-start.15 = (bf16[2,1,48,1024]{3,2,1,0:T(8,128)(2,1)S(1)}, bf16[2,1,48,1024]{3,2,1,0:T(8,128)(2,1)S(1)}, u32[]{:S(2)}, u32[]{:S(2)}) collective-permute-start(bf16[2,1,48,1024]{3,2,1,0:T(8,128)(2,1)S(1)} %get-tuple-element.126), channel_id=1, source_target_pairs={{0,192},{64,0},{128,64},{192,128},{1,193},{65,1},{129,65},{193,129... | collective-permute-start | bytes 589832 | tf_op jit(solution)/shard_map/ppermute | solution.py:661
  91.4 12.7 %collective-permute-start.16 = (bf16[2,1,48,1024]{3,2,1,0:T(8,128)(2,1)S(1)}, bf16[2,1,48,1024]{3,2,1,0:T(8,128)(2,1)S(1)}, u32[]{:S(2)}, u32[]{:S(2)}) collective-permute-start(bf16[2,1,48,1024]{3,2,1,0:T(8,128)(2,1)S(1)} %get-tuple-element.125), channel_id=1, source_target_pairs={{0,128},{64,192},{128,0},{192,64},{1,129},{65,193},{129,1},{193,65... | collective-permute-start | bytes 589832 | tf_op jit(solution)/shard_map/ppermute | solution.py:661
  98.0 25.3 %collective-permute-start = (bf16[3,48,1024]{2,1,0:T(8,128)(2,1)}, bf16[3,48,1024]{2,1,0:T(8,128)(2,1)S(1)}, u32[]{:S(2)}, u32[]{:S(2)}) collective-permute-start(bf16[3,48,1024]{2,1,0:T(8,128)(2,1)} %get-tuple-element.63), channel_id=1, source_target_pairs={{0,192},{64,0},{128,64},{192,128},{1,193},{65,1},{129,65},{193,129... | collective-permute-start | bytes 884744 | tf_op jit(solution)/shard_map/ppermute | solution.py:661
  99.2 24.1 %collective-permute-start.1 = (bf16[3,48,1024]{2,1,0:T(8,128)(2,1)}, bf16[3,48,1024]{2,1,0:T(8,128)(2,1)S(1)}, u32[]{:S(2)}, u32[]{:S(2)}) collective-permute-start(bf16[3,48,1024]{2,1,0:T(8,128)(2,1)} %get-tuple-element.64), channel_id=1, source_target_pairs={{0,128},{64,192},{128,0},{192,64},{1,129},{65,193},{129,1},{193,65... | collective-permute-start | bytes 884744 | tf_op jit(solution)/shard_map/ppermute | solution.py:661
  101.5 21.9 %collective-permute-start.2 = (bf16[3,48,1024]{2,1,0:T(8,128)(2,1)}, bf16[3,48,1024]{2,1,0:T(8,128)(2,1)S(1)}, u32[]{:S(2)}, u32[]{:S(2)}) collective-permute-start(bf16[3,48,1024]{2,1,0:T(8,128)(2,1)} %get-tuple-element.65), channel_id=1, source_target_pairs={{0,64},{64,128},{128,192},{192,0},{1,65},{65,129},{129,193},{193,1... | collective-permute-start | bytes 884744 | tf_op jit(solution)/shard_map/ppermute | solution.py:661
  102.5 17.1 %collective-permute-start.17 = (bf16[2,1,48,1024]{3,2,1,0:T(8,128)(2,1)S(1)}, bf16[2,1,48,1024]{3,2,1,0:T(8,128)(2,1)S(1)}, u32[]{:S(2)}, u32[]{:S(2)}) collective-permute-start(bf16[2,1,48,1024]{3,2,1,0:T(8,128)(2,1)S(1)} %get-tuple-element.124), channel_id=1, source_target_pairs={{0,64},{64,128},{128,192},{192,0},{1,65},{65,129},{129,193},{193,1... | collective-permute-start | bytes 589832 | tf_op jit(solution)/shard_map/ppermute | solution.py:661
  144.1 18.1 %all-to-all-start.3 = ((bf16[64,8,128]{2,1,0:T(8,128)(2,1)}), bf16[64,8,128]{2,1,0:T(8,128)(2,1)S(1)}, u32[]{:S(2)}, u32[]{:S(2)}) async-start(bf16[64,8,128]{2,1,0:T(8,128)(2,1)} %get-tuple-element.119), calls=%async_computation.3 | async-start | bytes 262144 | tf_op jit(solution)/shard_map/all_to_all | solution.py:715
  155.4 15.1 %collective-permute-start.18 = (bf16[4,48,1024]{2,1,0:T(8,128)(2,1)}, bf16[4,48,1024]{2,1,0:T(8,128)(2,1)S(1)}, u32[]{:S(2)}, u32[]{:S(2)}) collective-permute-start(bf16[4,48,1024]{2,1,0:T(8,128)(2,1)} %get-tuple-element.116), channel_id=1, source_target_pairs={{0,64},{64,128},{128,192},{192,0},{1,65},{65,129},{129,193},{193,1... | collective-permute-start | bytes 1179656 | tf_op jit(solution)/shard_map/ppermute | solution.py:661
  155.7 14.8 %collective-permute-start.19 = (bf16[4,48,1024]{2,1,0:T(8,128)(2,1)}, bf16[4,48,1024]{2,1,0:T(8,128)(2,1)S(1)}, u32[]{:S(2)}, u32[]{:S(2)}) collective-permute-start(bf16[4,48,1024]{2,1,0:T(8,128)(2,1)} %get-tuple-element.117), channel_id=1, source_target_pairs={{0,128},{64,192},{128,0},{192,64},{1,129},{65,193},{129,1},{193,65... | collective-permute-start | bytes 1179656 | tf_op jit(solution)/shard_map/ppermute | solution.py:661
  159.0 17.6 %collective-permute-start.20 = (bf16[4,48,1024]{2,1,0:T(8,128)(2,1)}, bf16[4,48,1024]{2,1,0:T(8,128)(2,1)S(1)}, u32[]{:S(2)}, u32[]{:S(2)}) collective-permute-start(bf16[4,48,1024]{2,1,0:T(8,128)(2,1)} %get-tuple-element.118), channel_id=1, source_target_pairs={{0,192},{64,0},{128,64},{192,128},{1,193},{65,1},{129,65},{193,129... | collective-permute-start | bytes 1179656 | tf_op jit(solution)/shard_map/ppermute | solution.py:661
  163.0 17.8 %all-to-all-start.4 = ((bf16[64,8,128]{2,1,0:T(8,128)(2,1)}), bf16[64,8,128]{2,1,0:T(8,128)(2,1)S(1)}, u32[]{:S(2)}, u32[]{:S(2)}) async-start(bf16[64,8,128]{2,1,0:T(8,128)(2,1)} %router_total.1), calls=%async_computation.4 | async-start | bytes 262144 | tf_op jit(solution)/shard_map/all_to_all | solution.py:718
  (24 other events, 382.3 us)
